TPU v7x, 32 devices: a whole 2x2x4 slice. The times are simulated.
32 devices in a mesh: dp: 8 (over y, x, core), mp: 4 (over z).
Axes of the slice: x: 2, y: 2, z: 4, core: 2. Of those that a mesh axis runs over, the one named last changes fastest.
Arguments:
- tokens: bfloat16 [8, 1024, 1536], P('dp', 'mp'), may hold values from -6 to 6
- attn_gain: bfloat16 [1536], P('dp'), may hold values from 0.5 to 1.5
- w_query: bfloat16 [1536, 1536], P('dp', 'mp'), may hold values from -0.5 to 0.5
- key_weight: bfloat16 [1536, 512], P('dp', 'mp'), may hold values from -0.5 to 0.5
- value_weight: bfloat16 [1536, 512], P('dp', 'mp'), may hold values from -0.15625 to 0.15625
- w_output: bfloat16 [1536, 1536], P('dp', 'mp'), may hold values from -1.75 to 1.75
- router: bfloat16 [1536, 24], P('dp'), may hold values from -0.078125 to 0.078125
- moe_gain: bfloat16 [1536], P('dp'), may hold values from 0.5 to 1.5
- w_in: bfloat16 [1536, 24, 2, 512], P('dp', None, None, 'mp'), may hold values from -0.15625 to 0.15625
- w_out: bfloat16 [1536, 24, 512], P('dp', None, 'mp'), may hold values from -5 to 5
- segments: int32 [8, 1024], P('dp'), may hold values from 0 to 7, never falling along the last dimension, each value on 1 to 512 neighbouring positions
- routes: int32 [8, 1024, 8], P('dp'), may hold values from 0 to 23, all different within a row; in each aligned block of 1024 rows (0 to 1023, 1024 to 2047, ..., all dimensions but the last counted through in order) at most 384 rows name the same one
- cotangent: bfloat16 [8, 1024, 1536], P('dp', 'mp'), may hold values from -6 to 6
Outputs:
- layer_out: bfloat16 [8, 1024, 1536], P('dp', 'mp')
- grad_tokens: float32 [8, 1024, 1536], P('dp', 'mp')
- grad_attn_gain: float32 [1536], P('dp')
- grad_query: float32 [1536, 1536], P('dp', 'mp')
- grad_key: float32 [1536, 512], P('dp', 'mp')
- grad_value: float32 [1536, 512], P('dp', 'mp')
- grad_output: float32 [1536, 1536], P('dp', 'mp')
- grad_router: float32 [1536, 24], P('dp')
- grad_moe_gain: float32 [1536], P('dp')
- grad_w_in: float32 [1536, 24, 2, 512], P('dp', None, None, 'mp')
- grad_w_out: float32 [1536, 24, 512], P('dp', None, 'mp')
Inputs may be any that keep to these rules, and one draw needn't show every extreme that they name: `segments`: within a sequence segment numbers never fall; each document has 1 to 512 tokens, and one has exactly 512. `routes`: A token's 8 experts differ. Within one sequence at most 384 token-choice pairs name one expert, a bound that some block reaches.
All inputs are finite; a program needn't handle non-finite values.
Results may differ from a plain program's by a relative error of at most 0.025.
Values may be sent and summed in bfloat16 or wider, within the bound.
No kernel may reach another device: no remote copies, remote signals or barrier semaphores. Data moves between devices by JAX's collectives and lax.ppermute only.
A program may use at most 320 MiB of HBM per device.

v0:
```python
import jax
import jax.numpy as jnp
from jax import lax
from jax.sharding import PartitionSpec as P

HEAD_SIZE = 64
CAP = 384


RESID = 0.22
ATTN_MULT = 0.015625
EPS = 1e-06
ROPE_BASE = 10000.0
NEG = -1e30
HIGHEST = lax.Precision.HIGHEST


def norm_scale(values, gain_vec):
    inverse = lax.rsqrt(jnp.mean(values * values, -1, keepdims=True) + EPS)
    return (values * inverse * gain_vec, inverse)


def norm_back(grad_in, values, inverse, gain_vec):
    scaled = grad_in * gain_vec
    back_grad = inverse * (
        scaled - values * inverse * inverse * jnp.mean(scaled * values, -1, keepdims=True)
    )
    gain_grad = jnp.sum(grad_in * values * inverse, 0)
    return (back_grad, gain_grad)


def apply_rotary(values, head_count, forward):
    length = values.shape[0]
    shaped = values.reshape(length, head_count, HEAD_SIZE)
    half_size = HEAD_SIZE // 2
    frequency = ROPE_BASE ** (-jnp.arange(half_size).astype(jnp.float32) * 2.0 / HEAD_SIZE)
    angles = jnp.arange(length).astype(jnp.float32)[:, None] * frequency[None, :]
    cosine = jnp.cos(angles)[:, None, :]
    sine_part = jnp.sin(angles)[:, None, :]
    if not forward:
        sine_part = -sine_part
    front_half = shaped[:, :, :half_size]
    back_half = shaped[:, :, half_size:]
    turned = jnp.concatenate(
        [front_half * cosine - back_half * sine_part, back_half * cosine + front_half * sine_part],
        -1,
    )
    return turned.reshape(length, head_count * HEAD_SIZE)


def dispatch(route_ids, experts, capacity):
    length, top_count = route_ids.shape
    flat_ids = route_ids.reshape(-1)
    onehot = (flat_ids[:, None] == jnp.arange(experts, dtype=jnp.int32)[None, :]).astype(jnp.int32)
    rank_of = jnp.sum((jnp.cumsum(onehot, 0) - onehot) * onehot, 1)
    slot_of = flat_ids * capacity + rank_of
    slot_owner = (
        jnp.full((experts * capacity,), length * top_count, jnp.int32)
        .at[slot_of]
        .set(jnp.arange(length * top_count, dtype=jnp.int32))
    )
    return (slot_of, slot_owner)


def block_scores(query_block, row_start, heads_of_keys, doc_ids, rows_per_block):
    length = heads_of_keys.shape[0]
    scores = ATTN_MULT * jnp.einsum(
        "qgjd,kgd->gjqk", query_block, heads_of_keys, preferred_element_type=jnp.float32
    )
    positions = jnp.arange(length, dtype=jnp.int32)
    row_pos = row_start + jnp.arange(rows_per_block, dtype=jnp.int32)
    row_docs = lax.dynamic_slice_in_dim(doc_ids, row_start, rows_per_block)
    visible = (positions[None, :] <= row_pos[:, None]) & (doc_ids[None, :] == row_docs[:, None])
    return jnp.where(visible, scores, NEG)


def attend_forward(query_rows, incoming_keys, incoming_values, doc_ids):
    length = incoming_keys.shape[0]
    rows_per_block = min(512, length)
    kv_heads = incoming_keys.shape[1] // HEAD_SIZE
    grouping_width = query_rows.shape[1] // incoming_keys.shape[1]
    blocks_of_queries = query_rows.reshape(
        length // rows_per_block, rows_per_block, kv_heads, grouping_width, HEAD_SIZE
    )
    heads_of_keys = incoming_keys.reshape(length, kv_heads, HEAD_SIZE)
    heads_of_values = incoming_values.reshape(length, kv_heads, HEAD_SIZE)

    def one_block(block_item):
        query_block, row_start = block_item
        scores = block_scores(query_block, row_start, heads_of_keys, doc_ids, rows_per_block)
        largest = jnp.max(scores, -1, keepdims=True)
        expo = jnp.exp(scores - largest)
        totals = jnp.sum(expo, -1, keepdims=True)
        probability = (expo / totals).astype(jnp.bfloat16)
        output = jnp.einsum(
            "gjqk,kgd->qgjd", probability, heads_of_values, preferred_element_type=jnp.float32
        )
        return (output.reshape(rows_per_block, -1), largest + jnp.log(totals))

    starts = jnp.arange(length // rows_per_block, dtype=jnp.int32) * rows_per_block
    outputs, log_totals = lax.map(one_block, (blocks_of_queries, starts))
    return (outputs.reshape(length, -1), log_totals)


def attend_backward(query_rows, incoming_keys, incoming_values, doc_ids, attended_grad, log_totals):
    length = incoming_keys.shape[0]
    rows_per_block = min(512, length)
    kv_heads = incoming_keys.shape[1] // HEAD_SIZE
    grouping_width = query_rows.shape[1] // incoming_keys.shape[1]
    blocks = length // rows_per_block
    blocks_of_queries = query_rows.reshape(
        blocks, rows_per_block, kv_heads, grouping_width, HEAD_SIZE
    )
    grad_blocks = attended_grad.reshape(blocks, rows_per_block, kv_heads, grouping_width, HEAD_SIZE)
    heads_of_keys = incoming_keys.reshape(length, kv_heads, HEAD_SIZE)
    heads_of_values = incoming_values.reshape(length, kv_heads, HEAD_SIZE)

    def one_block(carry, block_item):
        key_sum, value_sum = carry
        query_block, grad_block, log_block, row_start = block_item
        scores = block_scores(query_block, row_start, heads_of_keys, doc_ids, rows_per_block)
        probability = jnp.exp(scores - log_block)
        prob_low = probability.astype(jnp.bfloat16)
        prob_grad = jnp.einsum(
            "qgjd,kgd->gjqk", grad_block, heads_of_values, preferred_element_type=jnp.float32
        )
        row_dot = jnp.sum(probability * prob_grad, -1, keepdims=True)
        score_grad = (probability * (prob_grad - row_dot)).astype(jnp.bfloat16)
        value_sum = value_sum + jnp.einsum(
            "gjqk,qgjd->kgd", prob_low, grad_block, preferred_element_type=jnp.float32
        )
        key_sum = key_sum + ATTN_MULT * jnp.einsum(
            "gjqk,qgjd->kgd", score_grad, query_block, preferred_element_type=jnp.float32
        )
        query_part = ATTN_MULT * jnp.einsum(
            "gjqk,kgd->qgjd", score_grad, heads_of_keys, preferred_element_type=jnp.float32
        )
        return ((key_sum, value_sum), query_part.reshape(rows_per_block, -1))

    zero_heads = jnp.zeros((length, kv_heads, HEAD_SIZE), jnp.float32)
    starts = jnp.arange(blocks, dtype=jnp.int32) * rows_per_block
    (key_sum, value_sum), query_parts = lax.scan(
        one_block, (zero_heads, zero_heads), (blocks_of_queries, grad_blocks, log_totals, starts)
    )
    return (
        query_parts.reshape(length, -1),
        key_sum.reshape(length, -1),
        value_sum.reshape(length, -1),
    )


def contract_rows(left, right):
    return lax.dot_general(
        left, right, (((0,), (0,)), ((), ())), preferred_element_type=jnp.float32
    )


def contract_cols(left, right):
    return lax.dot_general(
        left, right, (((1,), (1,)), ((), ())), preferred_element_type=jnp.float32
    )


def body(
    tokens,
    attn_gain,
    w_query,
    key_weight,
    value_weight,
    w_output,
    router,
    moe_gain,
    w_in,
    w_out,
    segments,
    routes,
    cotangent,
):
    resid_in = tokens[0].astype(jnp.float32)
    doc_ids = segments[0]
    route_ids = routes[0]
    length = doc_ids.shape[0]
    width = resid_in.shape[1]
    experts = router.shape[1]
    top_count = route_ids.shape[1]
    capacity = CAP
    col_width = 512
    col_starts = jnp.arange(width // col_width, dtype=jnp.int32) * col_width
    attn_g, query_w, key_matrix, value_w, output_w, router_w, moe_g = (
        lax.all_gather(attn_gain, "dp", axis=0, tiled=True),
        lax.all_gather(w_query, "dp", axis=0, tiled=True),
        lax.all_gather(key_weight, "dp", axis=0, tiled=True),
        lax.all_gather(value_weight, "dp", axis=0, tiled=True),
        lax.all_gather(w_output, "dp", axis=0, tiled=True),
        lax.all_gather(router, "dp", axis=0, tiled=True),
        lax.all_gather(moe_gain, "dp", axis=0, tiled=True),
    )
    in_w, out_w = (
        lax.all_gather(w_in, "dp", axis=0, tiled=True),
        lax.all_gather(w_out, "dp", axis=0, tiled=True),
    )
    attn_gf = attn_g.astype(jnp.float32)
    moe_gf = moe_g.astype(jnp.float32)
    router_f = router_w.astype(jnp.float32)
    query_heads = query_w.shape[1] // HEAD_SIZE
    heads_of_keys = key_matrix.shape[1] // HEAD_SIZE
    attention_normed, inverse_a = norm_scale(resid_in, attn_gf)
    attention_normed = attention_normed.astype(jnp.bfloat16)
    normed_all = lax.all_gather(attention_normed, "mp", axis=0, tiled=True)
    query_rows = apply_rotary(
        jnp.dot(normed_all, query_w, preferred_element_type=jnp.float32), query_heads, True
    ).astype(jnp.bfloat16)
    rotated_keys = apply_rotary(
        jnp.dot(normed_all, key_matrix, preferred_element_type=jnp.float32), heads_of_keys, True
    ).astype(jnp.bfloat16)
    values_r = jnp.dot(normed_all, value_w, preferred_element_type=jnp.float32).astype(jnp.bfloat16)
    attended, log_totals = attend_forward(query_rows, rotated_keys, values_r, doc_ids)
    attended = attended.astype(jnp.bfloat16)
    attn_branch = lax.psum_scatter(
        contract_cols(attended, output_w), "mp", scatter_dimension=0, tiled=True
    )
    middle = resid_in + RESID * attn_branch
    normed_m, inverse_m = norm_scale(middle, moe_gf)
    normed_m = normed_m.astype(jnp.bfloat16)
    moe_all = lax.all_gather(normed_m, "mp", axis=0, tiled=True)
    logits = jnp.dot(moe_all, router_w, preferred_element_type=jnp.float32)
    chosen = route_ids[:, :, None] == jnp.arange(experts, dtype=jnp.int32)[None, None, :]
    picked = jnp.sum(jnp.where(chosen, logits[:, None, :], 0.0), -1)
    gates = jax.nn.softmax(picked, -1)
    slot_of, slot_owner = dispatch(route_ids, experts, capacity)
    table = slot_owner // top_count
    padded = jnp.concatenate([moe_all, jnp.zeros((1, width), jnp.bfloat16)], 0)
    dispatched = padded[table].reshape(experts, capacity, width)
    gate_up = jnp.einsum("ecd,dejf->ecjf", dispatched, in_w, preferred_element_type=jnp.float32)
    gate_part = gate_up[:, :, 0]
    up_part = gate_up[:, :, 1]
    activated = (jax.nn.silu(gate_part) * up_part).astype(jnp.bfloat16)

    def combine_cols(col_start):
        piece = lax.dynamic_slice_in_dim(out_w, col_start, col_width, 0)
        expert_out = jnp.einsum(
            "ecf,def->ecd", activated, piece, preferred_element_type=jnp.float32
        ).reshape(-1, col_width)
        per_choice = expert_out[slot_of].reshape(length, top_count, col_width)
        return jnp.sum(gates[:, :, None] * per_choice, 1)

    combined = jnp.moveaxis(lax.map(combine_cols, col_starts), 0, 1).reshape(length, width)
    moe_branch = lax.psum_scatter(
        combined.astype(jnp.bfloat16), "mp", scatter_dimension=0, tiled=True
    ).astype(jnp.float32)
    layer_out = (middle + RESID * moe_branch).astype(jnp.bfloat16)
    cot_f = cotangent[0].astype(jnp.float32)
    moe_grad = (RESID * cot_f).astype(jnp.bfloat16)
    moe_grad_all = lax.all_gather(moe_grad, "mp", axis=0, tiled=True)
    in_back, out_back = (in_w, out_w)
    filled = slot_owner < length * top_count
    gate_pad = jnp.concatenate([gates.reshape(-1), jnp.zeros((1,), jnp.float32)], 0)
    slot_gate = jnp.where(filled, gate_pad[slot_owner], 0.0).reshape(experts, capacity, 1)
    grad_pad = jnp.concatenate([moe_grad_all, jnp.zeros((1, width), jnp.bfloat16)], 0)
    slot_plain = grad_pad[table].reshape(experts, capacity, width)
    slot_grad = (slot_gate * slot_plain.astype(jnp.float32)).astype(jnp.bfloat16)
    plain_back = jnp.einsum(
        "ecd,def->ecf", slot_plain, out_back, preferred_element_type=jnp.float32
    )
    slot_choice = jnp.sum(activated.astype(jnp.float32) * plain_back, -1).reshape(-1)
    act_grad = jnp.einsum("ecd,def->ecf", slot_grad, out_back, preferred_element_type=jnp.float32)
    sigmoid_g = jax.nn.sigmoid(gate_part)
    gate_grad = act_grad * up_part * sigmoid_g * (1.0 + gate_part * (1.0 - sigmoid_g))
    up_grad = act_grad * gate_part * sigmoid_g
    gate_up_grad = jnp.stack([gate_grad, up_grad], 2).astype(jnp.bfloat16)

    def token_cols(col_start):
        piece = lax.dynamic_slice_in_dim(in_back, col_start, col_width, 0)
        slot_in = jnp.einsum(
            "ecjf,dejf->ecd", gate_up_grad, piece, preferred_element_type=jnp.float32
        ).reshape(-1, col_width)
        return jnp.sum(slot_in[slot_of].reshape(length, top_count, col_width), 1)

    expert_back = jnp.moveaxis(lax.map(token_cols, col_starts), 0, 1).reshape(length, width)
    choice_grad = slot_choice[slot_of].reshape(length, top_count)
    picked_grad = gates * (choice_grad - jnp.sum(gates * choice_grad, -1, keepdims=True))
    logit_grad = jnp.sum(jnp.where(chosen, picked_grad[:, :, None], 0.0), 1)
    router_part = jnp.dot(moe_all.astype(jnp.float32).T, logit_grad, precision=HIGHEST)
    normed_m_grad = expert_back + jnp.dot(logit_grad, router_f.T, precision=HIGHEST)
    normed_m_shard = lax.psum_scatter(normed_m_grad, "mp", scatter_dimension=0, tiled=True)
    in_cols = w_in.shape[1] * w_in.shape[2] * w_in.shape[3]
    row_count = w_in.shape[0] * lax.axis_size("dp")
    columns = grad_pad
    plain = columns[table].reshape(experts, capacity, row_count)
    outputs = (slot_gate * plain.astype(jnp.float32)).astype(jnp.bfloat16)
    columns = padded
    inputs = columns[table].reshape(experts, capacity, row_count)
    weight_grads = lax.psum_scatter(
        jnp.concatenate(
            [
                jnp.einsum(
                    "ecd,ecjf->dejf", inputs, gate_up_grad, preferred_element_type=jnp.float32
                ).reshape(row_count, -1),
                jnp.einsum(
                    "ecd,ecf->def", outputs, activated, preferred_element_type=jnp.float32
                ).reshape(row_count, -1),
            ],
            1,
        ).astype(jnp.bfloat16),
        "dp",
        scatter_dimension=0,
        tiled=True,
    ).astype(jnp.float32)
    grad_w_in = weight_grads[:, :in_cols].reshape(w_in.shape)
    grad_w_out = weight_grads[:, in_cols:].reshape(w_out.shape)
    middle_back, moe_gain_part = norm_back(normed_m_shard, middle, inverse_m, moe_gf)
    middle_grad = cot_f + middle_back
    attn_grad = (RESID * middle_grad).astype(jnp.bfloat16)
    attn_grad_all = lax.all_gather(attn_grad, "mp", axis=0, tiled=True)
    output_part = contract_rows(attn_grad_all, attended)
    attended_grad = jnp.dot(attn_grad_all, output_w, preferred_element_type=jnp.float32).astype(
        jnp.bfloat16
    )
    query_grad, key_grad, value_grad = attend_backward(
        query_rows, rotated_keys, values_r, doc_ids, attended_grad, log_totals
    )
    query_grad = apply_rotary(query_grad, query_heads, False).astype(jnp.bfloat16)
    key_grad = apply_rotary(key_grad, heads_of_keys, False).astype(jnp.bfloat16)
    value_grad = value_grad.astype(jnp.bfloat16)
    normed_a_grad = (
        contract_cols(query_grad, query_w)
        + contract_cols(key_grad, key_matrix)
        + contract_cols(value_grad, value_w)
    )
    normed_a_shard = lax.psum_scatter(
        normed_a_grad.astype(jnp.bfloat16), "mp", scatter_dimension=0, tiled=True
    ).astype(jnp.float32)
    query_part = contract_rows(normed_all, query_grad)
    key_part = contract_rows(normed_all, key_grad)
    value_part = contract_rows(normed_all, value_grad)
    input_back, attn_gain_part = norm_back(normed_a_shard, resid_in, inverse_a, attn_gf)
    grad_tokens = middle_grad + input_back
    router_sum, attn_gain_sum, moe_gain_sum = (
        lax.psum(router_part.astype(jnp.bfloat16), "mp").astype(jnp.float32),
        lax.psum(attn_gain_part.astype(jnp.bfloat16), "mp").astype(jnp.float32),
        lax.psum(moe_gain_part.astype(jnp.bfloat16), "mp").astype(jnp.float32),
    )
    grad_attn_gain, grad_query, grad_key, grad_value, grad_output, grad_router, grad_moe_gain = (
        lax.psum_scatter(
            attn_gain_sum.astype(jnp.bfloat16), "dp", scatter_dimension=0, tiled=True
        ).astype(jnp.float32),
        lax.psum_scatter(
            query_part.astype(jnp.bfloat16), "dp", scatter_dimension=0, tiled=True
        ).astype(jnp.float32),
        lax.psum_scatter(
            key_part.astype(jnp.bfloat16), "dp", scatter_dimension=0, tiled=True
        ).astype(jnp.float32),
        lax.psum_scatter(
            value_part.astype(jnp.bfloat16), "dp", scatter_dimension=0, tiled=True
        ).astype(jnp.float32),
        lax.psum_scatter(
            output_part.astype(jnp.bfloat16), "dp", scatter_dimension=0, tiled=True
        ).astype(jnp.float32),
        lax.psum_scatter(
            router_sum.astype(jnp.bfloat16), "dp", scatter_dimension=0, tiled=True
        ).astype(jnp.float32),
        lax.psum_scatter(
            moe_gain_sum.astype(jnp.bfloat16), "dp", scatter_dimension=0, tiled=True
        ).astype(jnp.float32),
    )
    return (
        layer_out[None],
        grad_tokens[None],
        grad_attn_gain,
        grad_query,
        grad_key,
        grad_value,
        grad_output,
        grad_router,
        grad_moe_gain,
        grad_w_in,
        grad_w_out,
    )


def solution(mesh):
    placed = (
        P("dp", "mp", None),
        P("dp"),
        P("dp", "mp"),
        P("dp", "mp"),
        P("dp", "mp"),
        P("dp", "mp"),
        P("dp", None),
        P("dp"),
        P("dp", None, None, "mp"),
        P("dp", None, "mp"),
        P("dp", None),
        P("dp", None, None),
        P("dp", "mp", None),
    )
    return jax.shard_map(
        body,
        mesh=mesh,
        in_specs=placed,
        out_specs=(
            P("dp", "mp", None),
            P("dp", "mp", None),
            P("dp"),
            P("dp", "mp"),
            P("dp", "mp"),
            P("dp", "mp"),
            P("dp", "mp"),
            P("dp", None),
            P("dp"),
            P("dp", None, None, "mp"),
            P("dp", None, "mp"),
        ),
        check_vma=False,
    )
```

profile of v0, /device:TPU:0, one launch (start us, length us, event | category | flops | bytes accessed | tf_op | source)
XLA Modules:
  0.0 1777.9 jit_solution(8305624295881236619)
XLA Ops:
  11.7 15.5 all-reduce.7
  33.0 8.9 all_gather.42
  41.9 10.4 all_gather.43
  53.6 49.2 %all-gather.10.cloned.1.call-done = bf16[1024,1536]{1,0:T(8,128)(2,1)} async-done(((bf16[256,1536]{1,0:T(8,128)(2,1)}), bf16[1024,1536]{1,0:T(8,128)(2,1)}) %all-gather.10.cloned.1.call-update) | async-done | bytes 3145744 | tf_op jit(solution)/shard_map/all_gather | solution.py:209
  116.4 37.5 %while.51 = (s32[]{:T(128)}, bf16[2,512,384]{2,1,0:T(8,128)(2,1)}, f32[2,2,3,512,1]{3,2,1,4,0:T(4,128)}, s32[2]{0:T(128)}, s32[1,1024]{1,0:T(1,128)}, /*index=5*...) while((s32[]{:T(128)}, bf16[2,512,384]{2,1,0:T(8,128)(2,1)}, ...), condition=%wide.region_4.5_spmd.clone, body=%wide.region_1.4_spmd.sunk.clone | while | flops 844625408 | bytes 50187496 | solution.py:101
  154.0 6.1 fusion.92
  162.3 107.3 %reduce-scatter.15.cloned.1.call-done = f32[256,1536]{1,0:T(8,128)} async-done(((f32[1024,1536]{1,0:T(8,128)}), f32[256,1536]{1,0:T(8,128)}) %reduce-scatter.15.cloned.1.call-update) | async-done | bytes 1572880 | tf_op jit(solution)/shard_map/reduce_scatter | solution.py:219
  279.3 7.6 reduce-window.6
  288.3 9.2 all-gather
  298.6 30.5 %scatter_custom_fusion = s32[9216]{0:T(1024)S(1)} fusion(s32[8192]{0:T(1024)S(1)} %bitcast.457, s32[8192]{0:T(1024)S(1)} %iota.124, s32[]{:T(128)} %constant.93.clone.1), kind=kCustom, calls=%fused_computation.182 | custom fusion | bytes 36868 | tf_op jit(solution)/shard_map/scatter | solution.py:60
  337.2 41.8 %gather_fusion.4 = bf16[9216,1536]{1,0:T(8,128)(2,1)} fusion(bf16[1025,1536]{1,0:T(8,128)(2,1)S(1)} %concatenate.33, s32[9216]{0:T(1024)S(1)} %get-tuple-element.487), kind=kCustom, calls=%fused_computation.4 | custom fusion | bytes 56659968 | tf_op jit(solution)/shard_map/gather | solution.py:260
  379.1 20.3 %all-gather.16.cloned.1.call-done = bf16[1024,1536]{1,0:T(8,128)(2,1)} async-done(((bf16[256,1536]{1,0:T(8,128)(2,1)}), bf16[1024,1536]{1,0:T(8,128)(2,1)}) %all-gather.16.cloned.1.call-update) | async-done | bytes 3145744 | tf_op jit(solution)/shard_map/all_gather | solution.py:225
  401.5 41.9 %gather_fusion.2 = bf16[9216,1536]{1,0:T(8,128)(2,1)} fusion(bf16[1025,1536]{1,0:T(8,128)(2,1)S(1)} %concatenate.31, s32[9216]{0:T(1024)S(1)} %get-tuple-element.487), kind=kCustom, calls=%fused_computation.2 | custom fusion | bytes 56659968 | tf_op jit(solution)/shard_map/gather | solution.py:233
  447.3 52.0 %all-gather.20.cloned.1.call-done = bf16[1536,24,2,128]{3,0,2,1:T(8,128)(2,1)} async-done(((bf16[192,24,2,128]{3,0,2,1:T(8,128)(2,1)}), bf16[1536,24,2,128]{3,0,2,1:T(8,128)(2,1)}) %all-gather.20.cloned.1.call-update) | async-done | bytes 18874384 | tf_op jit(solution)/shard_map/all_gather | solution.py:199
  499.2 22.4 %fusion.94 = f32[24,384,2,128]{1,3,2,0:T(8,128)} fusion(bf16[24,384,1536,1]{2,1,3,0:T(8,128)(2,1)} %bitcast.424, bf16[1536,24,2,128]{3,0,2,1:T(8,128)(2,1)} %all-gather.20.cloned.1.call-done), kind=kOutput, calls=%fused_computation.200 | convolution fusion | flops 7247757312 | bytes 56623104 | tf_op jit(solution)/shard_map/ecd,dejf->ecjf/dot_general | solution.py:234
  526.1 34.5 %all-gather.18.cloned.1.call-done = bf16[1536,24,128]{2,0,1:T(8,128)(2,1)} async-done(((bf16[192,24,128]{2,0,1:T(8,128)(2,1)}), bf16[1536,24,128]{2,0,1:T(8,128)(2,1)}) %all-gather.18.cloned.1.call-update) | async-done | bytes 9437200 | tf_op jit(solution)/shard_map/all_gather | solution.py:200
  560.6 15.3 multiply_reduce_fusion
  575.9 45.5 %gather_fusion.5 = f32[8192]{0:T(1024)S(1)} fusion(f32[9216]{0:T(1024)S(1)} %reshape.394, s32[8192]{0:T(1024)S(1)} %copy-done.57), kind=kCustom, calls=%fused_computation.5 | custom fusion | bytes 98304 | tf_op jit(solution)/shard_map/gather | solution.py:280
  623.3 51.2 %gather_fusion.3 = f32[9216]{0:T(1024)S(1)} fusion(f32[8193]{0:T(1024)S(1)} %pad_maximum_fusion.6, s32[9216]{0:T(1024)S(1)} %copy-done.54), kind=kCustom, calls=%fused_computation.3 | custom fusion | bytes 110592 | tf_op jit(solution)/shard_map/gather | solution.py:258
  674.5 19.6 %fusion.60 = (bf16[24,384,1,128]{1,3,0,2:T(8,128)(2,1)S(1)}, bf16[24,384,1,128]{1,3,0,2:T(8,128)(2,1)}) fusion(f32[24,384,2,128]{1,3,2,0:T(8,128)} %fusion.94, bf16[1536,24,128]{2,0,1:T(8,128)(2,1)} %all-gather.18.cloned.1.call-done, bf16[24,384,1536]{2,1,0:T(8,128)(2,1)} %bitcast.430, f32[24,384]{1,0:T(8,128)S(1)} %mul.558), kind=kOutput, calls=%fused_computation.108 | convolution fusion | flops 3681681408 | bytes 51941376 | tf_op jit(solution)/shard_map/ecd,def->ecf/dot_general | solution.py:266
  698.4 6.7 copy.107
  705.9 213.0 %while.53 = (s32[]{:T(128)}, f32[3,1024,512]{1,2,0:T(8,128)}, s32[3]{0:T(128)S(1)}, bf16[1536,24,2,128]{3,0,2,1:T(8,128)(2,1)}, bf16[24,384,2,128]{3,1,2,0:T(8,128)(2,1)}, /*index=5*/s32[8192]{0:T(1024)S(1)}) while((s32[]{:T(128)}, f32[3,1024,512]{1,2,0:T(8,128)}, s32[3]{0:T(128)S(1)}, bf16[1536,24,2,128]{3,0,2,1:T(8,128)(2,1)}, ...), condition=%wide.region_20.21_spmd.clone, body=%wide.region_18.20_spmd.sunk.clone | while | flops 2419621888 | bytes 90866296 | solution.py:279
  708.4 13.3 fusion.199
  721.8 41.3 %gather_fusion.1 = f32[8192,512]{1,0:T(8,128)} fusion(f32[9216,512]{1,0:T(8,128)} %bitcast.421, s32[8192]{0:T(1024)S(1)} %broadcast_clamp_fusion.8), kind=kCustom, calls=%fused_computation.1.clone.1.clone | custom fusion | bytes 33587200 | tf_op jit(solution)/shard_map/while/body/eval_jaxpr/gather | solution.py:277
  763.1 8.8 bitcast_reduce_fusion.7
  779.3 13.3 fusion.199
  792.7 41.3 %gather_fusion.1 = f32[8192,512]{1,0:T(8,128)} fusion(f32[9216,512]{1,0:T(8,128)} %bitcast.421, s32[8192]{0:T(1024)S(1)} %broadcast_clamp_fusion.8), kind=kCustom, calls=%fused_computation.1.clone.1.clone | custom fusion | bytes 33587200 | tf_op jit(solution)/shard_map/while/body/eval_jaxpr/gather | solution.py:277
  834.0 8.8 bitcast_reduce_fusion.7
  850.3 13.4 fusion.199
  863.8 41.3 %gather_fusion.1 = f32[8192,512]{1,0:T(8,128)} fusion(f32[9216,512]{1,0:T(8,128)} %bitcast.421, s32[8192]{0:T(1024)S(1)} %broadcast_clamp_fusion.8), kind=kCustom, calls=%fused_computation.1.clone.1.clone | custom fusion | bytes 33587200 | tf_op jit(solution)/shard_map/while/body/eval_jaxpr/gather | solution.py:277
  905.1 8.8 bitcast_reduce_fusion.7
  918.9 6.6 copy.111
  925.5 6.5 convolution_add_fusion
  932.0 110.8 %reduce-scatter.19.cloned.1.call-done = f32[256,1536]{1,0:T(8,128)} async-done(((f32[1024,1536]{1,0:T(8,128)}), f32[256,1536]{1,0:T(8,128)}) %reduce-scatter.19.cloned.1.call-update) | async-done | bytes 1572880 | tf_op jit(solution)/shard_map/reduce_scatter | solution.py:285
  1053.1 59.8 %all-gather.24.cloned.1.call-done = bf16[1024,1536]{1,0:T(8,128)(2,1)} async-done(((bf16[256,1536]{1,0:T(8,128)(2,1)}), bf16[1024,1536]{1,0:T(8,128)(2,1)}) %all-gather.24.cloned.1.call-update) | async-done | bytes 3145744 | tf_op jit(solution)/shard_map/all_gather | solution.py:314
  1119.6 111.0 %while.54 = (s32[]{:T(128)}, f32[1024,2,64]{0,2,1:T(8,128)}, f32[1024,2,64]{0,2,1:T(8,128)}, f32[2,512,384]{1,0,2:T(2,128)}, bf16[2,512,2,3,64]{1,4,3,2,0:T(8,12...) while((s32[]{:T(128)}, f32[1024,2,64]{0,2,1:T(8,128)}, ...), condition=%wide.region_28.29_spmd.clone.clone, body=%wide.region_26.28_spmd.clone.sunk.clone | while | flops 2062874112 | bytes 184658256 | solution.py:142
  1128.4 7.5 fusion.210
  1136.0 6.8 fusion.211
  1148.3 14.9 dynamic_update_slice.37
  1168.1 6.4 fusion.213
  1183.8 7.5 fusion.210
  1191.2 6.8 fusion.211
  1203.5 14.9 dynamic_update_slice.37
  1223.4 6.4 fusion.213
  1239.5 5.0 convolution_convert_fusion.1
  1264.7 200.3 %while.52 = (s32[]{:T(128)}, bf16[3,1024,512]{1,2,0:T(8,128)(2,1)}, f32[1024,8]{1,0:T(8,128)S(1)}, s32[3]{0:T(128)S(1)}, bf16[1536,24,128]{2,0,1:T(8,128)(2,1)},...) while((s32[]{:T(128)}, bf16[3,1024,512]{1,2,0:T(8,128)(2,1)}, f32[1024,8]{1,0:T(8,128)S(1)}, ...), condition=%wide.region_16.17_spmd.clone, body=%wide.region_14.16_spmd.sunk.clone | while | flops 1215856640 | bytes 80151168 | solution.py:247
  1267.3 11.7 fusion.195
  1279.0 41.5 %gather_fusion = f32[8192,512]{1,0:T(8,128)} fusion(f32[9216,512]{1,0:T(8,128)} %bitcast.422, s32[8192]{0:T(1024)S(1)} %broadcast_clamp_fusion.7), kind=kCustom, calls=%fused_computation.clone.1.clone | custom fusion | bytes 33587200 | tf_op jit(solution)/shard_map/while/body/eval_jaxpr/gather | solution.py:244
  1320.5 9.4 fusion.196
  1334.1 11.7 fusion.195
  1345.8 41.3 %gather_fusion = f32[8192,512]{1,0:T(8,128)} fusion(f32[9216,512]{1,0:T(8,128)} %bitcast.422, s32[8192]{0:T(1024)S(1)} %broadcast_clamp_fusion.7), kind=kCustom, calls=%fused_computation.clone.1.clone | custom fusion | bytes 33587200 | tf_op jit(solution)/shard_map/while/body/eval_jaxpr/gather | solution.py:244
  1387.2 9.6 fusion.196
  1400.9 11.7 fusion.195
  1412.7 41.4 %gather_fusion = f32[8192,512]{1,0:T(8,128)} fusion(f32[9216,512]{1,0:T(8,128)} %bitcast.422, s32[8192]{0:T(1024)S(1)} %broadcast_clamp_fusion.7), kind=kCustom, calls=%fused_computation.clone.1.clone | custom fusion | bytes 33587200 | tf_op jit(solution)/shard_map/while/body/eval_jaxpr/gather | solution.py:244
  1454.1 9.4 fusion.196
  1470.2 15.9 fusion.58
  1486.1 22.5 %convolution_convert_fusion = bf16[24,2,128,1536]{3,2,1,0:T(8,128)(2,1)} fusion(bf16[24,384,2,128]{3,1,2,0:T(8,128)(2,1)} %get-tuple-element.917, bf16[24,384,1536,1]{2,1,3,0:T(8,128)(2,1)} %bitcast.425), kind=kOutput, calls=%fused_computation.86 | convolution fusion | flops 7257194496 | bytes 51904512 | tf_op jit(solution)/shard_map/ecd,ecjf->dejf/dot_general | solution.py:296
  1508.5 29.0 %pad_maximum_fusion = bf16[1536,9216]{0,1:T(8,128)(2,1)} fusion(bf16[1536,3072]{0,1:T(8,128)(2,1)} %bitcast.437, bf16[1536,6144]{0,1:T(8,128)(2,1)} %bitcast.427), kind=kLoop, calls=%fused_computation.83 | loop fusion | flops 56623104 | bytes 56623104 | tf_op jit(solution)/shard_map/concatenate | solution.py:294
  1537.5 36.7 %copy.128 = bf16[1536,9216]{1,0:T(8,128)(2,1)} copy(bf16[1536,9216]{0,1:T(8,128)(2,1)} %pad_maximum_fusion) | data formatting | bytes 56623104
  1584.2 13.6 all-reduce.6
  1598.0 16.7 all-reduce.8
  1620.7 125.3 %reduce-scatter.31.cloned.1.call-done = bf16[192,9216]{1,0:T(8,128)(2,1)} async-done(((bf16[1536,9216]{1,0:T(8,128)(2,1)}), bf16[192,9216]{1,0:T(8,128)(2,1)}) %reduce-scatter.31.cloned.1.call-update) | async-done | bytes 3538960
  1750.4 6.3 copy.154
  1756.6 8.1 copy.117
  (384 shorter events, 233.1 us)
Async XLA Ops:
  7.2 46.4 %all-gather.12.cloned.1.call-start = ((), (), s32[]{:S(2)}) async-start(), calls=%async_computation.11 | async-start | bytes 1327104 | tf_op jit(solution)/shard_map/all_gather | solution.py:191
  7.9 94.8 %all-gather.10.cloned.1.call-start = ((), (), s32[]{:S(2)}) async-start(), calls=%async_computation.10 | async-start | bytes 3932160 | tf_op jit(solution)/shard_map/all_gather | solution.py:209
  31.6 122.3 %all-gather.14.cloned.1.call-start = ((), (), s32[]{:S(2)}) async-start(), calls=%async_computation.12 | async-start | bytes 1327104 | tf_op jit(solution)/shard_map/all_gather | solution.py:194
  32.3 237.3 %reduce-scatter.15.cloned.1.call-start = ((), (), s32[]{:S(2)}) async-start(), calls=%async_computation.13 | async-start | bytes 7864320 | tf_op jit(solution)/shard_map/reduce_scatter | solution.py:219
  41.9 71.4 %copy-start.27 = (bf16[1536,128]{1,0:T(8,128)(2,1)}, bf16[1536,128]{1,0:T(8,128)(2,1)S(1)}, u32[]{:S(2)}) copy-start(bf16[1536,128]{1,0:T(8,128)(2,1)S(1)} %all_gather.42) | copy-start | bytes 1179652
  106.4 6.8 copy-start.2
  148.5 4.5 copy-start.37
  154.0 6.1 copy-start.4
  160.1 109.6 %copy-start.12 = (bf16[1,256,1536]{2,1,0:T(8,128)(2,1)S(1)}, bf16[1,256,1536]{2,1,0:T(8,128)(2,1)}, u32[]{:S(2)}) copy-start(bf16[1,256,1536]{2,1,0:T(8,128)(2,1)} %param.21) | copy-start | bytes 2359300
  160.1 175.1 %all-gather.22.cloned.1.call-start = ((), (), s32[]{:S(2)}) async-start(), calls=%async_computation.18 | async-start | bytes 3932160 | tf_op jit(solution)/shard_map/all_gather | solution.py:254
  162.2 111.5 %copy-start.36 = (bf16[192,24,2,128]{3,2,1,0:T(2,128)(2,1)S(1)}, bf16[192,24,2,128]{3,2,1,0:T(2,128)(2,1)}, u32[]{:S(2)}) copy-start(bf16[192,24,2,128]{3,2,1,0:T(2,128)(2,1)} %param.29) | copy-start | bytes 7077892
  162.2 237.1 %all-gather.16.cloned.1.call-start = ((), (), s32[]{:S(2)}) async-start(), calls=%async_computation.14 | async-start | bytes 3932160 | tf_op jit(solution)/shard_map/all_gather | solution.py:225
  162.3 113.5 %copy-start.51 = (f32[1536]{0:T(1024)}, f32[1536]{0:T(1024)S(1)}, u32[]{:S(2)}) copy-start(f32[1536]{0:T(1024)S(1)} %convert_element_type.259) | copy-start | bytes 18436
  273.6 4.8 copy-start.46
  273.6 225.6 %all-gather.20.cloned.1.call-start = ((), (), s32[]{:S(2)}) async-start(), calls=%async_computation.16 | async-start | bytes 21233664 | tf_op jit(solution)/shard_map/all_gather | solution.py:199
  275.8 12.5 copy-start.66
  275.8 284.8 %all-gather.18.cloned.1.call-start = ((), (), s32[]{:S(2)}) async-start(), calls=%async_computation.15 | async-start | bytes 10616832 | tf_op jit(solution)/shard_map/all_gather | solution.py:200
  278.4 764.5 %reduce-scatter.19.cloned.1.call-start = ((), (), s32[]{:S(2)}) async-start(), calls=%async_computation.19 | async-start | bytes 7864320 | tf_op jit(solution)/shard_map/reduce_scatter | solution.py:285
  297.6 145.7 %copy-start.44 = (bf16[1536,24]{0,1:T(8,128)(2,1)}, bf16[1536,24]{0,1:T(8,128)(2,1)S(1)}, u32[]{:S(2)}) copy-start(bf16[1536,24]{0,1:T(8,128)(2,1)S(1)} %reshape.469) | copy-start | bytes 221188
  526.1 34.5 %copy-start.17 = (bf16[24,384,128]{1,2,0:T(8,128)(2,1)}, bf16[24,384,128]{1,2,0:T(8,128)(2,1)S(1)}, u32[]{:S(2)}) copy-start(bf16[24,384,128]{1,2,0:T(8,128)(2,1)S(1)} %multiply_convert_fusion.7) | copy-start | bytes 7077892
  560.6 15.3 copy-start.57
  575.9 47.3 %copy-start.54 = (s32[9216]{0:T(1024)S(1)}, s32[9216]{0:T(1024)}, u32[]{:S(2)}) copy-start(s32[9216]{0:T(1024)} %get-tuple-element.486) | copy-start | bytes 110596
  623.2 51.2 %copy-start.50 = (s32[9216]{0:T(1024)S(1)}, s32[9216]{0:T(1024)}, u32[]{:S(2)}) copy-start(s32[9216]{0:T(1024)} %copy-done.49) | copy-start | bytes 110596
  674.5 19.6 %copy-start.58 = (f32[24,384]{1,0:T(8,128)}, f32[24,384]{1,0:T(8,128)S(1)}, u32[]{:S(2)}) copy-start(f32[24,384]{1,0:T(8,128)S(1)} %mul.558) | copy-start | bytes 110596
  698.4 7.4 copy-start.25
  698.4 7.4 copy-start.69
  918.8 6.6 copy-start.43
  918.9 6.6 copy-start.45
  931.9 110.9 %copy-start.8 = (f32[256,1536]{1,0:T(8,128)S(1)}, f32[256,1536]{1,0:T(8,128)}, u32[]{:S(2)}) copy-start(f32[256,1536]{1,0:T(8,128)} %copy-done.7) | copy-start | bytes 4718596
  931.9 110.9 %copy-start.52 = (f32[1536]{0:T(1024)S(1)}, f32[1536]{0:T(1024)}, u32[]{:S(2)}) copy-start(f32[1536]{0:T(1024)} %copy-done.51) | copy-start | bytes 18436
  931.9 110.9 %copy-start.61 = (f32[256]{0:T(256)S(1)}, f32[256]{0:T(256)}, u32[]{:S(2)}) copy-start(f32[256]{0:T(256)} %copy-done.60) | copy-start | bytes 3076
  931.9 113.9 %copy-start.21 = (bf16[1,256,1536]{2,1,0:T(8,128)(2,1)S(1)}, bf16[1,256,1536]{2,1,0:T(8,128)(2,1)}, u32[]{:S(2)}) copy-start(bf16[1,256,1536]{2,1,0:T(8,128)(2,1)} %param.33) | copy-start | bytes 2359300
  932.0 180.9 %all-gather.24.cloned.1.call-start = ((), (), s32[]{:S(2)}) async-start(), calls=%async_computation.20 | async-start | bytes 3932160 | tf_op jit(solution)/shard_map/all_gather | solution.py:314
  1048.7 64.2 %copy-start.40 = (bf16[1536,384]{1,0:T(8,128)(2,1)S(1)}, bf16[1536,384]{1,0:T(8,128)(2,1)}, u32[]{:S(2)}) copy-start(bf16[1536,384]{1,0:T(8,128)(2,1)} %all-gather.14.cloned.1.call-done) | copy-start | bytes 3538948
  1048.7 526.4 %reduce-scatter.33.cloned.1.call-start = ((), (), s32[]{:S(2)}) async-start(), calls=%async_computation.27 | async-start | bytes 442368
  1053.1 66.5 %copy-start.5 = (bf16[1024,2,64]{0,2,1:T(8,128)(2,1)S(1)}, bf16[1024,2,64]{0,2,1:T(8,128)(2,1)}, u32[]{:S(2)}) copy-start(bf16[1024,2,64]{0,2,1:T(8,128)(2,1)} %copy-done.4) | copy-start | bytes 786436
  1053.1 66.5 %copy-start.6 = (bf16[2,512,2,3,64]{1,4,3,2,0:T(8,128)(2,1)S(1)}, bf16[2,512,2,3,64]{1,4,3,2,0:T(8,128)(2,1)}, u32[]{:S(2)}) copy-start(bf16[2,512,2,3,64]{1,4,3,2,0:T(8,128)(2,1)} %get-tuple-element.922) | copy-start | bytes 2359300
  1053.1 66.5 %copy-start.16 = (bf16[1024,2,64]{0,2,1:T(8,128)(2,1)S(1)}, bf16[1024,2,64]{0,2,1:T(8,128)(2,1)}, u32[]{:S(2)}) copy-start(bf16[1024,2,64]{0,2,1:T(8,128)(2,1)} %get-tuple-element.936) | copy-start | bytes 786436
  1053.1 523.0 %reduce-scatter.25.cloned.1.call-start = ((), (), s32[]{:S(2)}) async-start(), calls=%async_computation.23 | async-start | bytes 442368 | tf_op jit(solution)/shard_map/reduce_scatter | solution.py:350
  1119.6 111.0 %copy-start.33 = (f32[1024,32]{0,1:T(8,128)S(1)}, f32[1024,32]{0,1:T(8,128)}, u32[]{:S(2)}) copy-start(f32[1024,32]{0,1:T(8,128)} %get-tuple-element.490) | copy-start | bytes 393220
  1127.7 8.3 copy-start
  1163.2 4.9 copy-start.47
  1183.0 8.3 copy-start
  1218.5 4.9 copy-start.47
  1230.6 7.0 copy-start.3
  1235.6 342.0 %reduce-scatter.27.cloned.1.call-start = ((), (), s32[]{:S(2)}) async-start(), calls=%async_computation.24 | async-start | bytes 442368 | tf_op jit(solution)/shard_map/reduce_scatter | solution.py:353
  1239.4 339.6 %reduce-scatter.29.cloned.1.call-start = ((), (), s32[]{:S(2)}) async-start(), calls=%async_computation.25 | async-start | bytes 1327104 | tf_op jit(solution)/shard_map/reduce_scatter | solution.py:356
  1244.5 336.2 %reduce-scatter.23.cloned.1.call-start = ((), (), s32[]{:S(2)}) async-start(), calls=%async_computation.22 | async-start | bytes 1327104 | tf_op jit(solution)/shard_map/reduce_scatter | solution.py:347
  1253.4 4.9 copy-start.28
  1253.4 328.9 %reduce-scatter.21.cloned.1.call-start = ((), (), s32[]{:S(2)}) async-start(), calls=%async_computation.21 | async-start | bytes 3932160 | tf_op jit(solution)/shard_map/reduce_scatter | solution.py:330
  1264.5 352.0 %reduce-scatter.17.cloned.1.call-start = ((), (), s32[]{:S(2)}) async-start(), calls=%async_computation.17 | async-start | bytes 3932160 | tf_op jit(solution)/shard_map/reduce_scatter | solution.py:248
  1465.1 5.1 copy-start.19
  1465.1 5.1 copy-start.59
  1469.9 276.1 %reduce-scatter.31.cloned.1.call-start = ((), (), s32[]{:S(2)}) async-start(), calls=%async_computation.26 | async-start | bytes 31850496
  1574.2 8.1 copy-start.13
  1574.2 8.1 copy-start.56
  1574.2 8.1 copy-start.65
  1574.2 10.0 copy-start.63
  1574.2 42.2 %copy-start.9 = (f32[256,1536]{1,0:T(8,128)S(1)}, f32[256,1536]{1,0:T(8,128)}, u32[]{:S(2)}) copy-start(f32[256,1536]{1,0:T(8,128)} %copy-done.7) | copy-start | bytes 4718596
  1574.3 42.2 %copy-start.22 = (bf16[1,256,1536]{2,1,0:T(8,128)(2,1)S(1)}, bf16[1,256,1536]{2,1,0:T(8,128)(2,1)}, u32[]{:S(2)}) copy-start(bf16[1,256,1536]{2,1,0:T(8,128)(2,1)} %param.33) | copy-start | bytes 2359300
  1574.3 42.2 %copy-start.53 = (f32[1536]{0:T(1024)S(1)}, f32[1536]{0:T(1024)}, u32[]{:S(2)}) copy-start(f32[1536]{0:T(1024)} %copy-done.51) | copy-start | bytes 18436
  1574.3 42.2 %copy-start.62 = (f32[256]{0:T(256)S(1)}, f32[256]{0:T(256)}, u32[]{:S(2)}) copy-start(f32[256]{0:T(256)} %copy-done.60) | copy-start | bytes 3076
  1574.3 42.2 %copy-start.68 = (f32[256]{0:T(256)S(1)}, f32[256]{0:T(256)}, u32[]{:S(2)}) copy-start(f32[256]{0:T(256)} %copy-done.67) | copy-start | bytes 3076
  1756.6 8.1 copy-start.14
  (32 other events, 67.9 us)
Sparse Core Ops, SparseCore 0:
  9.9 26.9 all-gather.11
  39.0 63.6 all-gather.9
  104.6 22.6 all-gather.13
  160.2 109.3 reduce-scatter.14
  271.0 64.0 all-gather.21
  337.1 62.1 all-gather.15
  401.8 97.3 all-gather.19
  501.7 58.8 all-gather.17
  932.1 110.7 reduce-scatter.18
  1048.8 64.0 all-gather.23
  1116.0 32.4 reduce-scatter.32
  1235.7 32.4 reduce-scatter.24
  1271.3 33.8 reduce-scatter.26
  1308.2 36.7 reduce-scatter.28
  1349.0 36.7 reduce-scatter.22
  1388.6 60.2 reduce-scatter.20
  1470.0 58.5 reduce-scatter.16
  1574.4 171.4 reduce-scatter.30
where the time goes:
time: 1790 us; the launch traced here: 1780 us
  local copies, waits for them, and re-layouts  649 us (36%)
  waiting for transfers between devices  564 us (32%)
  matrix products  281 us (16%)
  other arithmetic  170 us (9%)
  blocking collectives  74.3 us (4%)
  loops' own time  20.3 us (1%)
    unnamed x20, waiting for transfers between devices  127 us
    gather x3, local copies, waits for them, and re-layouts, combine_cols(): per_choice = expert_out[slot_of].reshape(length, top_count, col_width)  124 us
    gather x3, local copies, waits for them, and re-layouts, token_cols(): return jnp.sum(slot_in[slot_of].reshape(length, top_count, col_width), 1)  124 us
    reduce_scatter x1, waiting for transfers between devices, body(): lax.psum_scatter(normed_m_grad, 'mp', scatter_dimension=0, tiled=True)  111 us
    reduce_scatter x1, waiting for transfers between devices, body(): lax.psum_scatter(contract_cols(attended, output_w), 'mp', scatter_dimensi...  107 us
    unnamed x147, local copies, waits for them, and re-layouts  72.3 us
    all_gather x1, waiting for transfers between devices, body(): attn_grad_all = lax.all_gather(attn_grad, 'mp', axis=0, tiled=True)  59.8 us
    all_gather x1, waiting for transfers between devices, body(): lax.all_gather(w_in, 'dp', axis=0, tiled=True)  52 us
  transfers between devices with their start and end apart: 18, of which 9 were waited for; matrix products, arithmetic and copies ran while one was open for 39% of the time, Pallas kernels for 0%

commit v1 on v0

v1 whole, which is shorter than its diff:
```python
import functools

import jax
import jax.numpy as jnp
from jax import lax
from jax.experimental import pallas as pl
from jax.experimental.pallas import tpu as pltpu
from jax.sharding import Mesh
from jax.sharding import PartitionSpec as P

HEAD = 64
RESID = 0.22
ATTN_MULT = 0.015625
EPS = 1e-06
ROPE_BASE = 10000.0
NEG = -1e30
F32 = jnp.float32
BF16 = jnp.bfloat16
BLK = 256
VMEM_CAP = 60 * 1024 * 1024


def nt(left, right):
    return lax.dot_general(left, right, (((1,), (1,)), ((), ())), preferred_element_type=F32)


def tn(left, right):
    return lax.dot_general(left, right, (((0,), (0,)), ((), ())), preferred_element_type=F32)


def nn(left, right):
    return jnp.dot(left, right, preferred_element_type=F32)


def rope_cols(values, cosine, sine):
    lane = lax.broadcasted_iota(jnp.int32, cosine.shape, 1)
    low = (lane % HEAD) < (HEAD // 2)
    pieces = []
    for start in range(0, values.shape[1], 128):
        piece = values[:, start : start + 128]
        turned = jnp.where(low, pltpu.roll(piece, 96, 1), pltpu.roll(piece, 32, 1))
        pieces.append(piece * cosine + turned * sine)
    return pieces[0] if len(pieces) == 1 else jnp.concatenate(pieces, 1)


def seen(kc, i, kdoc_ref, qdoc, group):
    kdoc = kdoc_ref[pl.ds(pl.multiple_of(kc * BLK, BLK), BLK), :]
    kpos = kc * BLK + lax.broadcasted_iota(jnp.int32, (BLK, 1), 0)
    qpos = i * BLK + lax.broadcasted_iota(jnp.int32, (1, BLK), 1)
    visible = (kpos <= qpos) & (kdoc == qdoc)
    return jnp.where(visible, 0.0, NEG)


def attn_fwd_kernel(
    tok_ref, gain_ref, w_ref, cos_ref, sin_ref, kdoc_ref, qdoc_ref,
    na_ref, q_ref, k_ref, v_ref, att_ref, lse_ref, s_scr, *, q_heads, kv_heads,
):
    i = pl.program_id(0)
    group = q_heads // kv_heads
    tok = tok_ref[...].astype(F32)
    inv = lax.rsqrt(jnp.mean(tok * tok, -1, keepdims=True) + EPS)
    na = (tok * inv * gain_ref[...]).astype(BF16)
    na_ref[...] = na
    qkv = nn(na, w_ref[...])
    qk_cols = (q_heads + kv_heads) * HEAD
    roped = rope_cols(qkv[:, :qk_cols], cos_ref[...], sin_ref[...]).astype(BF16)
    vals = qkv[:, qk_cols:].astype(BF16)
    rows = pl.ds(pl.multiple_of(i * BLK, BLK), BLK)
    heads = [roped[:, h * HEAD : (h + 1) * HEAD] for h in range(q_heads + kv_heads)]
    for h in range(q_heads):
        q_ref[h] = heads[h]
    for g in range(kv_heads):
        k_ref[g, rows, :] = heads[q_heads + g]
        v_ref[g, rows, :] = vals[:, g * HEAD : (g + 1) * HEAD]
    lo = jnp.maximum(i - 2, 0)
    qdoc = qdoc_ref[...]
    for g in range(kv_heads):
        qs = jnp.concatenate(heads[g * group : (g + 1) * group], 0)

        def scores(kc, top, g=g, qs=qs):
            keys = k_ref[g, pl.ds(pl.multiple_of(kc * BLK, BLK), BLK), :]
            bias = seen(kc, i, kdoc_ref, qdoc, group)
            s = nt(keys, qs) * ATTN_MULT + jnp.concatenate([bias] * group, 1)
            s_scr[kc - lo] = s
            return jnp.maximum(top, jnp.max(s, 0, keepdims=True))

        top = lax.fori_loop(lo, i + 1, scores, jnp.full((1, group * BLK), NEG, F32))

        def mix(kc, carry, g=g, top=top):
            total, out = carry
            e = jnp.exp(s_scr[kc - lo] - top)
            vv = v_ref[g, pl.ds(pl.multiple_of(kc * BLK, BLK), BLK), :]
            return total + jnp.sum(e, 0, keepdims=True), out + tn(vv, e.astype(BF16))

        total, out = lax.fori_loop(
            lo, i + 1, mix, (jnp.zeros((1, group * BLK), F32), jnp.zeros((HEAD, group * BLK), F32))
        )
        out = out / total
        lse_ref[0, g : g + 1, :] = top + jnp.log(total)
        for j in range(group):
            h = g * group + j
            att_ref[:, h * HEAD : (h + 1) * HEAD] = out[:, j * BLK : (j + 1) * BLK].T.astype(BF16)


def attn_fwd(tokens, gain, pack, cosine, sine, kdoc, qdoc, q_heads, kv_heads):
    length, width = tokens.shape
    blocks = length // BLK
    cols = (q_heads + 2 * kv_heads) * HEAD
    group = q_heads // kv_heads
    fixed = lambda i: (0, 0)
    fixed3 = lambda i: (0, 0, 0)
    row = lambda i: (i, 0)
    return pl.pallas_call(
        functools.partial(attn_fwd_kernel, q_heads=q_heads, kv_heads=kv_heads),
        grid=(blocks,),
        in_specs=[
            pl.BlockSpec((BLK, width), row),
            pl.BlockSpec((1, width), fixed),
            pl.BlockSpec((width, cols), fixed),
            pl.BlockSpec((BLK, 128), row),
            pl.BlockSpec((BLK, 128), row),
            pl.BlockSpec((length, 1), fixed),
            pl.BlockSpec((1, BLK), lambda i: (0, i)),
        ],
        out_specs=[
            pl.BlockSpec((BLK, width), row),
            pl.BlockSpec((q_heads, BLK, HEAD), lambda i: (0, i, 0)),
            pl.BlockSpec((kv_heads, length, HEAD), fixed3),
            pl.BlockSpec((kv_heads, length, HEAD), fixed3),
            pl.BlockSpec((BLK, q_heads * HEAD), row),
            pl.BlockSpec((1, kv_heads, group * BLK), lambda i: (i, 0, 0)),
        ],
        out_shape=[
            jax.ShapeDtypeStruct((length, width), BF16),
            jax.ShapeDtypeStruct((q_heads, length, HEAD), BF16),
            jax.ShapeDtypeStruct((kv_heads, length, HEAD), BF16),
            jax.ShapeDtypeStruct((kv_heads, length, HEAD), BF16),
            jax.ShapeDtypeStruct((length, q_heads * HEAD), BF16),
            jax.ShapeDtypeStruct((blocks, kv_heads, group * BLK), F32),
        ],
        scratch_shapes=[pltpu.VMEM((3, BLK, group * BLK), F32)],
        compiler_params=pltpu.CompilerParams(
            dimension_semantics=("arbitrary",), vmem_limit_bytes=VMEM_CAP
        ),
        cost_estimate=pl.CostEstimate(
            flops=2 * length * width * cols + 8 * length * 768 * q_heads * HEAD,
            transcendentals=length * 640 * q_heads,
            bytes_accessed=4 * length * width + 2 * width * cols,
        ),
        name="attn_fwd",
    )(tokens, gain, pack, cosine, sine, kdoc, qdoc)


def attn_bwd_kernel(
    ag_ref, wo_ref, q_ref, k_ref, v_ref, att_ref, lse_ref, cos_ref, sin_ref, kdoc_ref, qdoc_ref,
    dq_ref, dkv_ref, dk_scr, dv_scr, *, q_heads, kv_heads,
):
    i = pl.program_id(0)
    group = q_heads // kv_heads

    @pl.when(i == 0)
    def _():
        dk_scr[...] = jnp.zeros_like(dk_scr)
        dv_scr[...] = jnp.zeros_like(dv_scr)

    do = nn(ag_ref[...], wo_ref[...]).astype(BF16)
    lo = jnp.maximum(i - 2, 0)
    qdoc = qdoc_ref[...]
    att = att_ref[...]
    dq_heads = []
    for g in range(kv_heads):
        span = range(g * group, (g + 1) * group)
        qs = jnp.concatenate([q_ref[h] for h in span], 0)
        dos = jnp.concatenate([do[:, h * HEAD : (h + 1) * HEAD] for h in span], 0)
        outs = jnp.concatenate([att[:, h * HEAD : (h + 1) * HEAD] for h in span], 0)
        dot_row = jnp.sum((dos.astype(F32) * outs.astype(F32)).T, 0, keepdims=True)
        lse = lse_ref[0, g : g + 1, :]

        def chunk(kc, dq, g=g, qs=qs, dos=dos, dot_row=dot_row, lse=lse):
            rows = pl.ds(pl.multiple_of(kc * BLK, BLK), BLK)
            keys = k_ref[g, rows, :]
            vals = v_ref[g, rows, :]
            bias = seen(kc, i, kdoc_ref, qdoc, group)
            s = nt(keys, qs) * ATTN_MULT + jnp.concatenate([bias] * group, 1)
            prob = jnp.exp(s - lse)
            dprob = nt(vals, dos)
            ds = (prob * (dprob - dot_row)).astype(BF16)
            dv_scr[g, rows, :] += nn(prob.astype(BF16), dos)
            dk_scr[g, rows, :] += nn(ds, qs)
            return dq + tn(keys, ds)

        dq = lax.fori_loop(lo, i + 1, chunk, jnp.zeros((HEAD, group * BLK), F32))
        for j in range(group):
            dq_heads.append(dq[:, j * BLK : (j + 1) * BLK].T)
    rows = pl.ds(pl.multiple_of(i * BLK, BLK), BLK)
    dq_all = jnp.concatenate(dq_heads, 1) * ATTN_MULT
    dq_ref[...] = rope_cols(dq_all, cos_ref[rows, :], -sin_ref[rows, :]).astype(BF16)

    @pl.when(i == pl.num_programs(0) - 1)
    def _():
        dk = jnp.concatenate([dk_scr[g] for g in range(kv_heads)], 1) * ATTN_MULT
        kcols = kv_heads * HEAD
        dkv_ref[:, :kcols] = rope_cols(dk, cos_ref[...], -sin_ref[...]).astype(BF16)
        dkv_ref[:, kcols:] = jnp.concatenate([dv_scr[g] for g in range(kv_heads)], 1).astype(BF16)


def attn_bwd(ag, wo, q, k, v, att, lse, cosine, sine, kdoc, qdoc):
    length, width = ag.shape
    q_heads, kv_heads = q.shape[0], k.shape[0]
    blocks = length // BLK
    group = q_heads // kv_heads
    fixed = lambda i: (0, 0)
    fixed3 = lambda i: (0, 0, 0)
    row = lambda i: (i, 0)
    return pl.pallas_call(
        functools.partial(attn_bwd_kernel, q_heads=q_heads, kv_heads=kv_heads),
        grid=(blocks,),
        in_specs=[
            pl.BlockSpec((BLK, width), row),
            pl.BlockSpec((width, q_heads * HEAD), fixed),
            pl.BlockSpec((q_heads, BLK, HEAD), lambda i: (0, i, 0)),
            pl.BlockSpec((kv_heads, length, HEAD), fixed3),
            pl.BlockSpec((kv_heads, length, HEAD), fixed3),
            pl.BlockSpec((BLK, q_heads * HEAD), row),
            pl.BlockSpec((1, kv_heads, group * BLK), lambda i: (i, 0, 0)),
            pl.BlockSpec((length, 128), fixed),
            pl.BlockSpec((length, 128), fixed),
            pl.BlockSpec((length, 1), fixed),
            pl.BlockSpec((1, BLK), lambda i: (0, i)),
        ],
        out_specs=[
            pl.BlockSpec((BLK, q_heads * HEAD), row),
            pl.BlockSpec((length, 2 * kv_heads * HEAD), fixed),
        ],
        out_shape=[
            jax.ShapeDtypeStruct((length, q_heads * HEAD), BF16),
            jax.ShapeDtypeStruct((length, 2 * kv_heads * HEAD), BF16),
        ],
        scratch_shapes=[
            pltpu.VMEM((kv_heads, length, HEAD), F32),
            pltpu.VMEM((kv_heads, length, HEAD), F32),
        ],
        compiler_params=pltpu.CompilerParams(
            dimension_semantics=("arbitrary",), vmem_limit_bytes=VMEM_CAP
        ),
        cost_estimate=pl.CostEstimate(
            flops=2 * length * width * q_heads * HEAD + 20 * length * 768 * q_heads * HEAD,
            transcendentals=length * 640 * q_heads,
            bytes_accessed=2 * length * width + 2 * width * q_heads * HEAD,
        ),
        name="attn_bwd",
    )(ag, wo, q, k, v, att, lse, cosine, sine, kdoc, qdoc)


def mid_kernel(
    att_ref, wo_ref, tok_ref, gain_ref, small_ref, routes_ref, mid_ref, nm_ref, gate_ref, *, experts
):
    branch = nt(att_ref[0], wo_ref[0])
    for m in range(1, att_ref.shape[0]):
        branch += nt(att_ref[m], wo_ref[m])
    middle = tok_ref[...].astype(F32) + RESID * branch
    mid_ref[...] = middle
    inv = lax.rsqrt(jnp.mean(middle * middle, -1, keepdims=True) + EPS)
    nm = (middle * inv * gain_ref[...]).astype(BF16)
    nm_ref[...] = nm
    logits = nn(nm, small_ref[...])
    lane = lax.broadcasted_iota(jnp.int32, logits.shape, 1)
    chosen = lane == routes_ref[:, 0:1]
    for c in range(1, routes_ref.shape[1]):
        chosen = chosen | (lane == routes_ref[:, c : c + 1])
    logits = jnp.where(chosen, logits, NEG)
    e = jnp.exp(logits - jnp.max(logits, -1, keepdims=True))
    gate_ref[...] = e / jnp.sum(e, -1, keepdims=True)


def mid_fwd(att_all, wo_all, tokens, gain, pack, small_at, routes, experts):
    length, width = tokens.shape
    parts, _, cols = att_all.shape
    blocks = length // BLK
    fixed = lambda i: (0, 0)
    row = lambda i: (i, 0)
    return pl.pallas_call(
        functools.partial(mid_kernel, experts=experts),
        grid=(blocks,),
        in_specs=[
            pl.BlockSpec((parts, BLK, cols), lambda i: (0, i, 0)),
            pl.BlockSpec((parts, width, cols), lambda i: (0, 0, 0)),
            pl.BlockSpec((BLK, width), row),
            pl.BlockSpec((1, width), fixed),
            pl.BlockSpec((width, 128), lambda i: (0, small_at)),
            pl.BlockSpec((BLK, routes.shape[1]), row),
        ],
        out_specs=[
            pl.BlockSpec((BLK, width), row),
            pl.BlockSpec((BLK, width), row),
            pl.BlockSpec((BLK, 128), row),
        ],
        out_shape=[
            jax.ShapeDtypeStruct((length, width), F32),
            jax.ShapeDtypeStruct((length, width), BF16),
            jax.ShapeDtypeStruct((length, 128), F32),
        ],
        compiler_params=pltpu.CompilerParams(
            dimension_semantics=("arbitrary",), vmem_limit_bytes=VMEM_CAP
        ),
        cost_estimate=pl.CostEstimate(
            flops=2 * length * width * cols * parts,
            transcendentals=length * 128,
            bytes_accessed=10 * length * width + 2 * width * cols * parts,
        ),
        name="mid_fwd",
    )(att_all, wo_all, tokens, gain, pack, routes)


def gate_cols(gates, first):
    lane = lax.broadcasted_iota(jnp.int32, gates.shape, 1)
    return [
        jnp.sum(jnp.where(lane == first + k, gates, 0.0), -1, keepdims=True) for k in range(2)
    ]


def moe_fwd_kernel(base_ref, x_ref, w_ref, gate_ref, h_ref, gact_ref):
    p = pl.program_id(1)
    h = nn(x_ref[...], w_ref[...])
    h_ref[...] = h.astype(BF16)
    cols = gate_cols(gate_ref[...], base_ref[0] + 2 * p)
    for k in range(2):
        gate = h[:, 256 * k : 256 * k + 128]
        up = h[:, 256 * k + 128 : 256 * k + 256]
        act = gate * jax.nn.sigmoid(gate) * up
        gact_ref[:, 128 * k : 128 * k + 128] = (cols[k] * act).astype(BF16)


def moe_fwd(base, x, w_in, gates, rows):
    length, width = x.shape
    cols = w_in.shape[1]
    return pl.pallas_call(
        moe_fwd_kernel,
        grid_spec=pltpu.PrefetchScalarGridSpec(
            num_scalar_prefetch=1,
            grid=(length // rows, cols // 512),
            in_specs=[
                pl.BlockSpec((rows, width), lambda i, p, b: (i, 0)),
                pl.BlockSpec((width, 512), lambda i, p, b: (0, p)),
                pl.BlockSpec((rows, 128), lambda i, p, b: (i, 0)),
            ],
            out_specs=[
                pl.BlockSpec((rows, 512), lambda i, p, b: (i, p)),
                pl.BlockSpec((rows, 256), lambda i, p, b: (i, p)),
            ],
        ),
        out_shape=[
            jax.ShapeDtypeStruct((length, cols), BF16),
            jax.ShapeDtypeStruct((length, cols // 2), BF16),
        ],
        compiler_params=pltpu.CompilerParams(
            dimension_semantics=("arbitrary", "arbitrary"), vmem_limit_bytes=VMEM_CAP
        ),
        cost_estimate=pl.CostEstimate(
            flops=2 * length * width * cols,
            transcendentals=length * cols // 2,
            bytes_accessed=2 * length * (width + cols + cols // 2) + 4 * width * cols,
        ),
        name="moe_fwd",
    )(base, x, w_in, gates)


def moe_bwd_kernel(base_ref, g_ref, w_ref, gate_ref, h_ref, gug_ref, choice_ref):
    p = pl.program_id(1)
    first = base_ref[0] + 2 * p
    plain = nn(g_ref[...], w_ref[...])
    cols = gate_cols(gate_ref[...], first)

    @pl.when(p == 0)
    def _():
        choice_ref[...] = jnp.zeros_like(choice_ref)

    lane = lax.broadcasted_iota(jnp.int32, choice_ref.shape, 1)
    add = jnp.zeros(choice_ref.shape, F32)
    for k in range(2):
        gate = h_ref[:, 256 * k : 256 * k + 128].astype(F32)
        up = h_ref[:, 256 * k + 128 : 256 * k + 256].astype(F32)
        part = plain[:, 128 * k : 128 * k + 128]
        sig = jax.nn.sigmoid(gate)
        silu = gate * sig
        add = jnp.where(lane == first + k, jnp.sum(silu * up * part, -1, keepdims=True), add)
        act_grad = cols[k] * part
        gug_ref[:, 256 * k : 256 * k + 128] = (
            act_grad * up * sig * (1.0 + gate * (1.0 - sig))
        ).astype(BF16)
        gug_ref[:, 256 * k + 128 : 256 * k + 256] = (act_grad * silu).astype(BF16)
    choice_ref[...] += add


def moe_bwd(base, g, w_out, gates, h, rows):
    length, width = g.shape
    cols = h.shape[1]
    return pl.pallas_call(
        moe_bwd_kernel,
        grid_spec=pltpu.PrefetchScalarGridSpec(
            num_scalar_prefetch=1,
            grid=(length // rows, cols // 512),
            in_specs=[
                pl.BlockSpec((rows, width), lambda i, p, b: (i, 0)),
                pl.BlockSpec((width, 256), lambda i, p, b: (0, p)),
                pl.BlockSpec((rows, 128), lambda i, p, b: (i, 0)),
                pl.BlockSpec((rows, 512), lambda i, p, b: (i, p)),
            ],
            out_specs=[
                pl.BlockSpec((rows, 512), lambda i, p, b: (i, p)),
                pl.BlockSpec((rows, 128), lambda i, p, b: (i, 0)),
            ],
        ),
        out_shape=[
            jax.ShapeDtypeStruct((length, cols), BF16),
            jax.ShapeDtypeStruct((length, 128), F32),
        ],
        compiler_params=pltpu.CompilerParams(
            dimension_semantics=("arbitrary", "arbitrary"), vmem_limit_bytes=VMEM_CAP
        ),
        cost_estimate=pl.CostEstimate(
            flops=length * width * cols,
            transcendentals=length * cols // 2,
            bytes_accessed=2 * length * (width + 2 * cols) + 2 * width * cols,
        ),
        name="moe_bwd",
    )(base, g, w_out, gates, h)


def swap(value, axis, bit, size):
    return lax.ppermute(value, axis, [(i, i ^ bit) for i in range(size)])


def reorder(value, q, quads):
    if quads != 4:
        return value
    n = value.shape[-1] // 4
    b = [value[..., k * n : (k + 1) * n] for k in range(4)]
    odd = (q & 1) == 1
    far = (q & 2) == 2
    c = [jnp.where(odd, b[k ^ 1], b[k]) for k in range(4)]
    return jnp.concatenate([jnp.where(far, c[k ^ 2], c[k]) for k in range(4)], -1)


def gather_rows(value, quads):
    if quads != 4:
        return lax.all_gather(value, "q", axis=0, tiled=True)
    half = value.shape[0] // 2
    from_x = swap(value, "q", 1, 4)
    from_y = swap(value, "q", 2, 4)
    diag_a = swap(from_x[:half], "q", 2, 4)
    diag_b = swap(from_y[half:], "q", 1, 4)
    return jnp.concatenate([value, from_x, from_y, diag_a, diag_b], 0)


def scatter_rows(value, quads):
    if quads != 4:
        return lax.psum_scatter(value, "q", scatter_dimension=0, tiled=True).astype(F32)
    n = value.shape[0] // 4
    half = n // 2
    own, to_x, to_y, diag = (value[k * n : (k + 1) * n] for k in range(4))
    via_x = swap(diag[:half], "q", 1, 4)
    via_y = swap(diag[half:], "q", 2, 4)
    to_y = jnp.concatenate([(to_y[:half].astype(F32) + via_x.astype(F32)).astype(BF16), to_y[half:]], 0)
    to_x = jnp.concatenate([to_x[:half], (to_x[half:].astype(F32) + via_y.astype(F32)).astype(BF16)], 0)
    from_x = swap(to_x, "q", 1, 4)
    from_y = swap(to_y, "q", 2, 4)
    return own.astype(F32) + from_x.astype(F32) + from_y.astype(F32)


def both_cores(mine, c):
    other = swap(mine, "c", 1, 2)
    first = c == 0
    return jnp.concatenate([jnp.where(first, mine, other), jnp.where(first, other, mine)], 0)


def body(
    tokens, attn_gain, w_query, key_weight, value_weight, w_output, router, moe_gain, w_in, w_out,
    segments, routes, cotangent, *, quads,
):
    q = lax.axis_index("q")
    c = lax.axis_index("c")
    length = segments.shape[1]
    width = tokens.shape[2]
    rows = w_query.shape[0]
    experts = router.shape[1]
    half_e = experts // 2
    ff = w_out.shape[2]
    q_heads = w_query.shape[1] // HEAD
    kv_heads = key_weight.shape[1] // HEAD
    q_cols, kv_cols = q_heads * HEAD, kv_heads * HEAD
    qkv_cols = q_cols + 2 * kv_cols
    mp = lax.axis_size("mp")

    doc_row = segments
    doc_col = segments.reshape(length, 1)
    lane = jnp.arange(128, dtype=jnp.int32) % (HEAD // 2)
    freq = ROPE_BASE ** (-lane.astype(F32) * 2.0 / HEAD)
    angles = jnp.arange(length).astype(F32)[:, None] * freq[None, :]
    cosine = jnp.cos(angles)
    upper = (jnp.arange(128, dtype=jnp.int32) % HEAD) < (HEAD // 2)
    sine = jnp.where(upper[None, :], -jnp.sin(angles), jnp.sin(angles))

    tok_own = reorder(tokens[0], q, quads)
    cot_own = reorder(cotangent[0], q, quads)
    tok_all = lax.all_gather(tok_own, "mp", axis=0, tiled=True)

    pad = jnp.zeros((rows, 128 - experts - 2), BF16)
    pack = jnp.concatenate(
        [w_query, key_weight, value_weight, router, attn_gain[:, None], moe_gain[:, None], pad], 1
    )
    pack = gather_rows(both_cores(pack, c), quads)
    small_at = qkv_cols // 128
    gains = pack[:, qkv_cols + experts : qkv_cols + experts + 2].astype(F32)
    attn_g = gains[:, 0].reshape(1, width)
    moe_g = gains[:, 1].reshape(1, width)
    wo_pieces = lax.all_gather(w_output, "mp", axis=0, tiled=False)
    wo_pieces = wo_pieces.transpose(1, 0, 2).reshape(rows, mp * q_cols)
    wo_rows = gather_rows(both_cores(wo_pieces, c), quads)
    wo_all = wo_rows.reshape(width, mp, q_cols).transpose(1, 0, 2)

    in_halves = w_in.reshape(rows, 2, half_e * 2 * ff)
    out_halves = w_out.reshape(rows, 2, half_e * ff)

    def half_rows(halves):
        mine = lax.dynamic_index_in_dim(halves, c, 1, keepdims=False)
        give = lax.dynamic_index_in_dim(halves, 1 - c, 1, keepdims=False)
        other = swap(give, "c", 1, 2)
        first = c == 0
        return jnp.concatenate([jnp.where(first, mine, other), jnp.where(first, other, mine)], 0)

    in_full = gather_rows(half_rows(in_halves), quads)
    out_full = gather_rows(half_rows(out_halves), quads)

    normed_a, q_r, k_r, v_r, attended, lse = attn_fwd(
        tok_all, attn_g, pack, cosine, sine, doc_col, doc_row, q_heads, kv_heads
    )
    att_all = lax.all_gather(attended, "mp", axis=0, tiled=False)
    middle, normed_m, gates = mid_fwd(
        att_all, wo_all, tok_all, moe_g, pack, small_at, routes[0], experts
    )

    x2 = jnp.concatenate([normed_m, swap(normed_m, "c", 1, 2)], 0)
    gates2 = jnp.concatenate([gates, swap(gates, "c", 1, 2)], 0)
    base = (c * half_e).astype(jnp.int32).reshape(1)
    hidden, gact = moe_fwd(base, x2, in_full, gates2, length)

    moe_grad = (RESID * cot_own.astype(F32)).astype(BF16)
    grad_all = lax.all_gather(moe_grad, "mp", axis=0, tiled=True)
    g2 = jnp.concatenate([grad_all, swap(grad_all, "c", 1, 2)], 0)
    gug, choice2 = moe_bwd(base, g2, out_full, gates2, hidden, length)

    back2 = nt(gug, in_full).astype(BF16)
    back_other = swap(back2[length:], "c", 1, 2)
    choice = choice2[:length] + swap(choice2[length:], "c", 1, 2)
    gates_c = gates * choice
    logit_grad = (gates_c - gates * jnp.sum(gates_c, -1, keepdims=True)).astype(BF16)
    router_all = pack[:, small_at * 128 :]
    normed_m_grad = (
        back2[:length].astype(F32) + back_other.astype(F32) + nt(logit_grad, router_all)
    ).astype(BF16)
    m_grad = lax.psum_scatter(normed_m_grad, "mp", scatter_dimension=0, tiled=True).astype(F32)

    combined2 = nt(gact, out_full).astype(BF16)
    comb_other = swap(combined2[length:], "c", 1, 2)
    combined = (combined2[:length].astype(F32) + comb_other.astype(F32)).astype(BF16)
    moe_branch = lax.psum_scatter(combined, "mp", scatter_dimension=0, tiled=True).astype(F32)

    own_at = lax.axis_index("mp") * (length // mp)
    middle_own = lax.dynamic_slice_in_dim(middle, own_at, length // mp, 0)
    layer_out = (middle_own + RESID * moe_branch).astype(BF16)

    in_part = tn(x2, gug).astype(BF16)
    out_part = tn(g2, gact).astype(BF16)
    in_sum = scatter_rows(in_part, quads).astype(BF16)
    out_sum = scatter_rows(out_part, quads).astype(BF16)

    def own_rows(total):
        mine = lax.dynamic_slice_in_dim(total, c * rows, rows, 0)
        give = lax.dynamic_slice_in_dim(total, (1 - c) * rows, rows, 0)
        other = swap(give, "c", 1, 2)
        first = c == 0
        return jnp.concatenate([jnp.where(first, mine, other), jnp.where(first, other, mine)], 1)

    grad_in = own_rows(in_sum).astype(F32)
    grad_out = own_rows(out_sum).astype(F32)

    inv_m = lax.rsqrt(jnp.mean(middle_own * middle_own, -1, keepdims=True) + EPS)
    scaled = m_grad * moe_g
    middle_grad = cot_own.astype(F32) + inv_m * (
        scaled - middle_own * inv_m * inv_m * jnp.mean(scaled * middle_own, -1, keepdims=True)
    )
    attn_grad = (RESID * middle_grad).astype(BF16)
    ag_all = lax.all_gather(attn_grad, "mp", axis=0, tiled=True)

    wo_own = lax.dynamic_index_in_dim(wo_all, lax.axis_index("mp"), 0, keepdims=False)
    dq, dkv = attn_bwd(ag_all, wo_own, q_r, k_r, v_r, attended, lse, cosine, sine, doc_col, doc_row)
    normed_a_grad = nt(dq, pack[:, :q_cols]) + nt(dkv, pack[:, q_cols:qkv_cols])
    a_grad = lax.psum_scatter(
        normed_a_grad.astype(BF16), "mp", scatter_dimension=0, tiled=True
    ).astype(F32)
    tok_f = tok_own.astype(F32)
    inv_a = lax.rsqrt(jnp.mean(tok_f * tok_f, -1, keepdims=True) + EPS)
    scaled = a_grad * attn_g
    grad_tokens = middle_grad + inv_a * (
        scaled - tok_f * inv_a * inv_a * jnp.mean(scaled * tok_f, -1, keepdims=True)
    )

    parts = jnp.concatenate(
        [
            tn(normed_a, dq).astype(BF16),
            tn(normed_a, dkv).astype(BF16),
            tn(ag_all, attended).astype(BF16),
            tn(normed_m, logit_grad).astype(BF16),
        ],
        1,
    )
    cols = parts.shape[1]
    by_core = parts.reshape(width // (2 * rows), 2, rows, cols)
    mine = lax.dynamic_index_in_dim(by_core, c, 1, keepdims=False)
    give = lax.dynamic_index_in_dim(by_core, 1 - c, 1, keepdims=False)
    pair = (mine.astype(F32) + swap(give, "c", 1, 2).astype(F32)).astype(BF16)
    sums = scatter_rows(pair.reshape(width // 2, cols), quads)
    grad_query = sums[:, :q_cols]
    grad_kv = sums[:, q_cols:qkv_cols]
    grad_output = sums[:, qkv_cols : qkv_cols + q_cols]
    router_part = sums[:, qkv_cols + q_cols : qkv_cols + q_cols + experts]

    attn_gain_part = (
        jnp.sum(grad_query * w_query.astype(F32), 1)
        + jnp.sum(grad_kv[:, :kv_cols] * key_weight.astype(F32), 1)
        + jnp.sum(grad_kv[:, kv_cols:] * value_weight.astype(F32), 1)
    ) / attn_gain.astype(F32)
    moe_gain_part = (
        jnp.sum(grad_in * w_in.reshape(rows, -1).astype(F32), 1)
        + jnp.sum(router_part * router.astype(F32), 1)
    ) / moe_gain.astype(F32)
    tiny = jnp.concatenate([router_part, attn_gain_part[:, None], moe_gain_part[:, None]], 1)
    total = tiny
    for k in range(1, mp):
        total = total + lax.ppermute(tiny, "mp", [(i, (i + k) % mp) for i in range(mp)])

    return (
        reorder(layer_out, q, quads)[None],
        reorder(grad_tokens, q, quads)[None],
        total[:, experts],
        grad_query,
        grad_kv[:, :kv_cols],
        grad_kv[:, kv_cols:],
        grad_output,
        total[:, :experts],
        total[:, experts + 1],
        grad_in.reshape(w_in.shape),
        grad_out.reshape(w_out.shape),
    )


def solution(mesh):
    dp, mp = mesh.shape["dp"], mesh.shape["mp"]
    quads = dp // 2
    split = Mesh(mesh.devices.reshape(quads, 2, mp), ("q", "c", "mp"))
    d = ("q", "c")
    placed = (
        P(d, "mp", None),
        P(d),
        P(d, "mp"),
        P(d, "mp"),
        P(d, "mp"),
        P(d, "mp"),
        P(d, None),
        P(d),
        P(d, None, None, "mp"),
        P(d, None, "mp"),
        P(d, None),
        P(d, None, None),
        P(d, "mp", None),
    )
    return jax.shard_map(
        functools.partial(body, quads=quads),
        mesh=split,
        in_specs=placed,
        out_specs=(
            P(d, "mp", None),
            P(d, "mp", None),
            P(d),
            P(d, "mp"),
            P(d, "mp"),
            P(d, "mp"),
            P(d, "mp"),
            P(d, None),
            P(d),
            P(d, None, None, "mp"),
            P(d, None, "mp"),
        ),
        check_vma=False,
    )
```

time: 1790 us -> 738 us (0.41)
  local copies, waits for them, and re-layouts: 649 us -> 132 us
  waiting for transfers between devices: 564 us -> 221 us
  matrix products: 281 us -> 94.4 us
  Pallas kernels: 0 us -> 114 us
  other arithmetic: 170 us -> 87.6 us
  blocking collectives: 74.3 us -> 24 us
  starting transfers between devices: 1.38 us -> 38.2 us
  loops' own time: 20.3 us -> 0 us
    gather x10 -> x0, local copies, waits for them, and re-layouts: 429 us -> none  [the longest x3 124 us: combine_cols(): per_choice = expert_out[slot_of].reshape(length, top_count, col_width)]
    all_gather x8 -> x4, waiting for transfers between devices: 219 us -> 22.4 us  [the longest x1 22.4 us: body(): ag_all = lax.all_gather(attn_grad, 'mp', axis=0, tiled=True)]
    dot_general x40 -> x11, matrix products: 281 us -> 94.4 us  [the longest x5 49.5 us: nt(): lax.dot_general(left, right, (((1,), (1,)), ((), ())), preferred_element_...]
    ppermute x0 -> x44, waiting for transfers between devices: none -> 153 us  [the longest x41 153 us: swap(): return lax.ppermute(value, axis, [(i, i ^ bit) for i in range(size)])]
    unnamed x20 -> x7, waiting for transfers between devices: 127 us -> 0.11 us
    pallas_call x0 -> x5, Pallas kernels: none -> 114 us  [the longest x1 27.9 us: moe_fwd(): pl.pallas_call(moe_fwd_kernel, grid_spec=pltpu.PrefetchScalarGridSpec(num...]
    reduce_scatter x1, waiting for transfers between devices: 111 us -> 0.01 us  [body(): lax.psum_scatter(normed_m_grad, 'mp', scatter_dimension=0, tiled=True)]
    reduce_scatter x7 -> x2, waiting for transfers between devices: 107 us -> 45 us  [the longest x1 43.2 us: body(): lax.psum_scatter(combined, 'mp', scatter_dimension=0, tiled=True)]
  transfers between devices with their start and end apart: 18 -> 51, of which waited for: 9 -> 18; matrix products, arithmetic and copies ran while one was open for 39% -> 36% of each run, Pallas kernels for 0% -> 8%
where the time goes in v1:
time: 738 us; the launch traced here: 726 us
  waiting for transfers between devices  221 us (30%)
  local copies, waits for them, and re-layouts  132 us (18%)
  Pallas kernels  114 us (15%)
  matrix products  94.4 us (13%)
  other arithmetic  87.6 us (12%)
  starting transfers between devices  38.2 us (5%)
  blocking collectives  24 us (3%)
  between operations  15.5 us (2%)
    ppermute x41, waiting for transfers between devices, swap(): return lax.ppermute(value, axis, [(i, i ^ bit) for i in range(size)])  153 us
    unnamed x170, local copies, waits for them, and re-layouts  53.7 us
    dot_general x5, matrix products, nt(): lax.dot_general(left, right, (((1,), (1,)), ((), ())), preferred_element_...  49.5 us
    dot_general x6, matrix products, tn(): lax.dot_general(left, right, (((0,), (0,)), ((), ())), preferred_element_...  45 us
    reduce_scatter x1, waiting for transfers between devices, body(): lax.psum_scatter(combined, 'mp', scatter_dimension=0, tiled=True)  43.2 us
    ppermute x41, starting transfers between devices, swap(): return lax.ppermute(value, axis, [(i, i ^ bit) for i in range(size)])  34.4 us
    pallas_call x1, Pallas kernels, moe_fwd(): pl.pallas_call(moe_fwd_kernel, grid_spec=pltpu.PrefetchScalarGridSpec(num...  27.9 us
    pallas_call x1, Pallas kernels, moe_bwd(): pl.pallas_call(moe_bwd_kernel, grid_spec=pltpu.PrefetchScalarGridSpec(num...  26.3 us
  transfers between devices with their start and end apart: 51, of which 18 were waited for; matrix products, arithmetic and copies ran while one was open for 36% of the time, Pallas kernels for 8%

profile of v1, /device:TPU:0, one launch (start us, length us, event | category | flops | bytes accessed | tf_op | source)
XLA Modules:
  0.0 725.7 jit_solution(2208318432497271989)
XLA Ops:
  14.4 24.0 %all-gather.1 = bf16[768,384]{1,0:T(8,128)(2,1)S(1)} all-gather(bf16[192,384]{1,0:T(8,128)(2,1)S(1)} %copy-done.57), channel_id=3, replica_groups=mesh['q'=4,'c'=2,'mp'=4] {'mp'}, dimensions={0}, use_global_device_ids=true | all-gather | bytes 737280 | tf_op jit(solution)/shard_map/all_gather | solution.py:517
  40.2 2.4 constant_dynamic-slice_fusion.4
  44.0 7.3 %reshape.131 = bf16[192,2,3072]{2,1,0:T(2,128)(2,1)} reshape(bf16[192,24,2,128]{3,2,1,0:T(2,128)(2,1)} %param.21) | data formatting | bytes 4718592 | tf_op jit(solution)/shard_map/reshape | solution.py:522
  51.4 7.3 %constant_dynamic-slice_fusion.6 = (bf16[192,1,3072]{2,1,0:T(2,128)(2,1)S(1)}, bf16[192,1,3072]{2,1,0:T(2,128)(2,1)S(1)}) fusion(bf16[192,2,3072]{2,1,0:T(2,128)(2,1)} %reshape.131, s32[]{:T(128)S(6)} %select_n.278, s32[]{:T(128)S(6)} %select_n.279), kind=kLoop, calls=%fused_computation.177 | loop fusion | bytes 4718600 | tf_op jit(solution)/shard_map/jit(dynamic_index_in_dim)/dynamic_slice | solution.py:526
  65.9 3.3 negate_select_fusion
  71.8 2.2 constant_dynamic-update-slice_fusion.11
  74.0 6.5 collective-permute-done.1
  84.3 2.3 collective-permute-done.2
  90.1 2.2 collective-permute-done.3
  98.1 20.9 %attn_fwd.1 = (bf16[1024,1536]{1,0:T(8,128)(2,1)}, bf16[6,1024,64]{2,1,0:T(8,128)(2,1)}, bf16[2,1024,64]{2,1,0:T(8,128)(2,1)}, bf16[2,1024,64]{2,1,0:T(8,128)(2,...) custom-call(bf16[1024,1536]{1,0:T(8,128)(2,1)} %all-gather.7.cloned.1.call-done.tok_ref, ...), custom_call_target="tpu_custom_call" | custom-call | flops 4429185024 | bytes 8257536 | tf_op jit(solution)/shard_map/attn_fwd/pallas_call | solution.py:113
  119.1 2.7 constant_dynamic-update-slice_fusion.10
  130.0 3.1 constant_dynamic-update-slice_fusion.18
  138.0 14.3 %collective-permute-done.19 = bf16[384,1536]{1,0:T(8,128)(2,1)} collective-permute-done((bf16[384,1536]{1,0:T(8,128)(2,1)}, bf16[384,1536]{1,0:T(8,128)(2,1)}, u32[]{:S(2)}, u32[]{:S(2)}) %collective-permute-start.19) | collective-permute-done | bytes 1179680 | tf_op jit(solution)/shard_map/ppermute | solution.py:431
  155.8 21.7 %collective-permute-done.7 = bf16[384,1536]{1,0:T(8,128)(2,1)} collective-permute-done((bf16[384,1536]{1,0:T(8,128)(2,1)}, bf16[384,1536]{1,0:T(8,128)(2,1)}, u32[]{:S(2)}, u32[]{:S(2)}) %collective-permute-start.7) | collective-permute-done | bytes 1179680 | tf_op jit(solution)/shard_map/ppermute | solution.py:431
  185.4 2.4 constant_dynamic-update-slice_fusion.24
  187.8 2.4 constant_dynamic-update-slice_fusion.9
  191.0 2.4 constant_dynamic-update-slice_fusion.8
  193.5 44.2 %collective-permute-done.8 = bf16[192,1536]{1,0:T(8,128)(2,1)} collective-permute-done((bf16[192,1536]{1,0:T(8,128)(2,1)S(1)}, bf16[192,1536]{1,0:T(8,128)(2,1)}, u32[]{:S(2)}, u32[]{:S(2)}) %collective-permute-start.8) | collective-permute-done | bytes 589856 | tf_op jit(solution)/shard_map/ppermute | solution.py:431
  239.6 12.0 %collective-permute-done.9 = bf16[192,1536]{1,0:T(8,128)(2,1)} collective-permute-done((bf16[192,1536]{1,0:T(8,128)(2,1)}, bf16[192,1536]{1,0:T(8,128)(2,1)}, u32[]{:S(2)}, u32[]{:S(2)}) %collective-permute-start.9) | collective-permute-done | bytes 589856 | tf_op jit(solution)/shard_map/ppermute | solution.py:431
  253.9 4.9 copy.168
  258.9 14.5 %mid_fwd.1 = (f32[1024,1536]{1,0:T(8,128)}, bf16[1024,1536]{1,0:T(8,128)(2,1)}, f32[1024,128]{1,0:T(8,128)}) custom-call(bf16[4,1024,384]{2,1,0:T(8,128)(2,1)} %bitcast.114, bf16[4,1536,384]{2,1,0:T(8,128)(2,1)} %bitcast.99, bf16[1024,1536]{1,0:T(8,128)(2,1)} %all-gather.7.cloned.1.call-done.tok_ref, f32[1,1536]{1,0:T(1,128)} %reshape_squeeze.7.gain_ref, ...), custom_call_target="tpu_custom_call" | custom-call | flops 4831838208 | bytes 20447232 | tf_op jit(solution)/shard_map/mid_fwd/pallas_call | solution.py:282
  281.5 3.4 constant_dynamic-update-slice_fusion.16
  285.1 17.8 %collective-permute-done.14 = bf16[192,3072]{1,0:T(8,128)(2,1)S(1)} collective-permute-done((bf16[192,3072]{1,0:T(8,128)(2,1)S(1)}, bf16[192,3072]{1,0:T(8,128)(2,1)S(1)}, u32[]{:S(2)}, u32[]{:S(2)}) %collective-permute-start.14) | collective-permute-done | bytes 1179680 | tf_op jit(solution)/shard_map/ppermute | solution.py:431
  304.0 3.5 collective-permute-done.15
  308.6 2.2 constant_dynamic-update-slice_fusion.28.g_ref
  314.6 2.7 copy-done.34
  317.2 27.9 %moe_fwd.1 = (bf16[2048,3072]{1,0:T(8,128)(2,1)}, bf16[2048,1536]{1,0:T(8,128)(2,1)}) custom-call(s32[1]{0:T(128)} %bitcast.7.base_ref, bf16[2048,1536]{1,0:T(8,128)(2,1)} %copy-done.34, bf16[1536,3072]{1,0:T(8,128)(2,1)} %constant_dynamic-update-slice_fusion.14.w_ref, f32[2048,128]{1,0:T(8,128)} %copy-done.51), custom_call_target="tpu_custom_call" | custom-call | flops 19327352832 | bytes 44040192 | tf_op jit(solution)/shard_map/moe_fwd/pallas_call | solution.py:337
  345.2 26.3 %moe_bwd.1 = (bf16[2048,3072]{1,0:T(8,128)(2,1)}, f32[2048,128]{1,0:T(8,128)}) custom-call(s32[1]{0:T(128)} %bitcast.7.base_ref, bf16[2048,1536]{1,0:T(8,128)(2,1)} %copy-done.33, bf16[1536,1536]{1,0:T(8,128)(2,1)} %constant_dynamic-update-slice_fusion.22.w_ref, f32[2048,128]{1,0:T(8,128)} %copy-done.51, bf16[2048,3072]{1,0:T(8,128)(2,1)} %get-tuple-element.31.h_ref), custom_call_target="tpu_custom_call" | custom-call | flops 9663676416 | bytes 40894464 | tf_op jit(solution)/shard_map/moe_bwd/pallas_call | solution.py:398
  371.4 25.1 %convolution_convert_fusion.1 = bf16[2048,1536]{1,0:T(8,128)(2,1)S(1)} fusion(bf16[2048,3072]{1,0:T(8,128)(2,1)} %get-tuple-element.32, bf16[1536,3072]{1,0:T(8,128)(2,1)} %constant_dynamic-update-slice_fusion.14.w_ref), kind=kOutput, calls=%fused_computation.1 | convolution fusion | flops 19330498560 | bytes 28311552 | tf_op jit(solution)/shard_map/dot_general | solution.py:24
  398.3 5.0 collective-permute-done.25
  404.4 3.7 add_convert_fusion.1
  408.2 13.5 %convolution_convert_fusion.2 = bf16[2048,1536]{1,0:T(8,128)(2,1)S(1)} fusion(bf16[2048,1536]{1,0:T(8,128)(2,1)} %get-tuple-element.30, bf16[1536,1536]{1,0:T(8,128)(2,1)} %constant_dynamic-update-slice_fusion.22.w_ref), kind=kOutput, calls=%fused_computation.2 | convolution fusion | flops 9666822144 | bytes 17301504 | tf_op jit(solution)/shard_map/dot_general | solution.py:24
  421.9 2.3 copy-done.6
  426.9 3.1 collective-permute-done.22
  430.1 5.4 add_convert_fusion.2
  435.5 14.2 %convolution_convert_fusion.3 = bf16[1536,1536]{1,0:T(8,128)(2,1)S(1)} fusion(bf16[2048,1536]{1,0:T(8,128)(2,1)} %copy-done.33, bf16[2048,1536]{1,0:T(8,128)(2,1)} %get-tuple-element.30), kind=kOutput, calls=%fused_computation.3 | convolution fusion | flops 9666035712 | bytes 17301504 | tf_op jit(solution)/shard_map/dot_general | solution.py:28
  454.3 24.4 %convolution_convert_fusion = bf16[1536,3072]{1,0:T(8,128)(2,1)S(1)} fusion(bf16[2048,1536]{1,0:T(8,128)(2,1)} %copy-done.34, bf16[2048,3072]{1,0:T(8,128)(2,1)} %get-tuple-element.32), kind=kOutput, calls=%fused_computation | convolution fusion | flops 19332071424 | bytes 28311552 | tf_op jit(solution)/shard_map/dot_general | solution.py:28
  478.8 2.0 fusion.26
  480.8 2.3 copy-done.2
  485.4 2.1 multiply_reduce_fusion.2
  487.5 43.2 %reduce-scatter.4.cloned.1.call-done = bf16[256,1536]{1,0:T(8,128)(2,1)} async-done(((bf16[1024,1536]{1,0:T(8,128)(2,1)}), bf16[256,1536]{1,0:T(8,128)(2,1)}) %reduce-scatter.4.cloned.1.call-update) | async-done | bytes 786448 | tf_op jit(solution)/shard_map/reduce_scatter | solution.py:567
  530.7 4.2 multiply_convert_fusion
  540.6 2.5 dynamic-slice_bitcast_fusion.1.wo_ref
  544.5 3.2 add_convert_fusion.6
  547.7 17.3 %collective-permute-done.42 = bf16[384,1536]{1,0:T(8,128)(2,1)S(1)} collective-permute-done((bf16[384,1536]{1,0:T(8,128)(2,1)S(1)}, bf16[384,1536]{1,0:T(8,128)(2,1)S(1)}, u32[]{:S(2)}, u32[]{:S(2)}) %collective-permute-start.42) | collective-permute-done | bytes 1179680 | tf_op jit(solution)/shard_map/ppermute | solution.py:431
  576.2 22.4 %all-gather.11.cloned.1.call-done.ag_ref = bf16[1024,1536]{1,0:T(8,128)(2,1)} async-done(((bf16[256,1536]{1,0:T(8,128)(2,1)}), bf16[1024,1536]{1,0:T(8,128)(2,1)}) %all-gather.11.cloned.1.call-update) | async-done | bytes 3145744 | tf_op jit(solution)/shard_map/all_gather | solution.py:594
  598.6 24.0 %attn_bwd.1 = (bf16[1024,384]{1,0:T(8,128)(2,1)}, bf16[1024,256]{1,0:T(8,128)(2,1)}) custom-call(bf16[1024,1536]{1,0:T(8,128)(2,1)} %all-gather.11.cloned.1.call-done.ag_ref, bf16[1536,384]{1,0:T(8,128)(2,1)} %dynamic-slice_bitcast_fusion.1.wo_ref, bf16[6,1024,64]{2,1,0:T(8,128)(2,1)} %get-tuple-element.34.q_ref, ...), custom_call_target="tpu_custom_call" | custom-call | flops 7247757312 | bytes 4325376 | tf_op jit(solution)/shard_map/attn_bwd/pallas_call | solution.py:215
  622.6 2.1 convolution_convert_fusion.6
  628.7 3.7 copy.128
  632.3 3.5 constant_dynamic-slice_fusion.2
  635.8 4.3 add_convert_fusion.3
  643.1 2.5 copy.146
  645.6 2.4 fusion.11
  648.0 4.8 add_convert_fusion
  652.8 2.6 copy.130
  655.5 3.2 fusion
  662.7 3.3 broadcast_select_fusion.1
  665.9 3.3 concatenate.114
  669.3 4.0 concatenate.115
  675.3 2.2 pad_maximum_fusion.11
  677.4 2.1 copy.131
  679.5 2.1 pad_maximum_fusion.12
  681.6 2.1 copy.133
  685.4 8.8 %multiply_reduce_fusion = (f32[192]{0:T(256)S(1)}, f32[192,24,2,128]{3,2,1,0:T(2,128)}) fusion(bf16[192,24,2,128]{3,2,1,0:T(2,128)(2,1)S(1)} %copy-done, bf16[192,12,2,128]{3,2,1,0:T(2,128)(2,1)} %concatenate.115, bf16[192,12,2,128]{3,2,1,0:T(2,128)(2,1)S(1)} %concatenate.114), kind=kLoop, calls=%fused_computation.10 | loop fusion | flops 5898048 | bytes 9437952 | tf_op jit(solution)/shard_map/reduce_sum | solution.py:635
  (343 shorter events, 146.6 us)
Async XLA Ops:
  7.2 90.9 %all-gather.7.cloned.1.call-start = ((), (), s32[]{:S(2)}) async-start(), calls=%async_computation.3 | async-start | bytes 3932160 | tf_op jit(solution)/shard_map/all_gather | solution.py:506
  10.6 227.1 %all-gather.9.cloned.1.call-start = ((), (), s32[]{:S(2)}) async-start(), calls=%async_computation.5 | async-start | bytes 3932160 | tf_op jit(solution)/shard_map/all_gather | solution.py:549
  11.9 48.2 %collective-permute-start = (bf16[192,768]{1,0:T(8,128)(2,1)}, bf16[192,768]{1,0:T(8,128)(2,1)}, u32[]{:S(2)}, u32[]{:S(2)}) collective-permute-start(bf16[192,768]{1,0:T(8,128)(2,1)} %concatenate.94), channel_id=1, source_target_pairs={{0,4},{4,0},{1,5},{5,1},{2,6},{6,2},{3,7},{7,3},{8,12},{12,8},{9,1... | collective-permute-start | bytes 884744 | tf_op jit(solution)/shard_map/ppermute | solution.py:431
  13.3 26.5 %copy-start.35 = (bf16[192,24,128]{2,1,0:T(8,128)(2,1)S(1)}, bf16[192,24,128]{2,1,0:T(8,128)(2,1)}, u32[]{:S(2)}) copy-start(bf16[192,24,128]{2,1,0:T(8,128)(2,1)} %param.22) | copy-start | bytes 3538948
  14.3 244.5 %all-gather.13.cloned.1.call-start = ((), (), s32[]{:S(2)}) async-start(), calls=%async_computation.9 | async-start | bytes 3932160 | tf_op jit(solution)/shard_map/all_gather | solution.py:538
  39.8 32.0 %collective-permute-start.5 = (bf16[192,1536]{1,0:T(8,128)(2,1)}, bf16[192,1536]{1,0:T(8,128)(2,1)}, u32[]{:S(2)}, u32[]{:S(2)}) collective-permute-start(bf16[192,1536]{1,0:T(8,128)(2,1)} %bitcast.37), channel_id=1, source_target_pairs={{0,4},{4,0},{1,5},{5,1},{2,6},{6,2},{3,7},{7,3},{8,12},{12,8},{9,1... | collective-permute-start | bytes 1769480 | tf_op jit(solution)/shard_map/ppermute | solution.py:431
  43.5 39.6 %collective-permute-start.17 = (bf16[192,1536]{1,0:T(8,128)(2,1)}, bf16[192,1536]{1,0:T(8,128)(2,1)}, u32[]{:S(2)}, u32[]{:S(2)}) collective-permute-start(bf16[192,1536]{1,0:T(8,128)(2,1)} %bitcast.97), channel_id=1, source_target_pairs={{0,4},{4,0},{1,5},{5,1},{2,6},{6,2},{3,7},{7,3},{8,12},{12,8},{9,1... | collective-permute-start | bytes 1769480 | tf_op jit(solution)/shard_map/ppermute | solution.py:431
  60.0 68.2 %collective-permute-start.11 = (bf16[192,3072]{1,0:T(8,128)(2,1)}, bf16[192,3072]{1,0:T(8,128)(2,1)}, u32[]{:S(2)}, u32[]{:S(2)}) collective-permute-start(bf16[192,3072]{1,0:T(8,128)(2,1)} %bitcast.96), channel_id=1, source_target_pairs={{0,4},{4,0},{1,5},{5,1},{2,6},{6,2},{3,7},{7,3},{8,12},{12,8},{9,1... | collective-permute-start | bytes 3538952 | tf_op jit(solution)/shard_map/ppermute | solution.py:431
  64.4 16.0 %collective-permute-start.1 = (bf16[384,768]{1,0:T(8,128)(2,1)}, bf16[384,768]{1,0:T(8,128)(2,1)}, u32[]{:S(2)}, u32[]{:S(2)}) collective-permute-start(bf16[384,768]{1,0:T(8,128)(2,1)} %pad_maximum_fusion.10), channel_id=1, source_target_pairs={{0,8},{8,0},{16,24},{24,16},{1,9},{9,1},{17,25},{25,17},{2,10},{10... | collective-permute-start | bytes 1769480 | tf_op jit(solution)/shard_map/ppermute | solution.py:431
  70.2 16.4 %collective-permute-start.2 = (bf16[384,768]{1,0:T(8,128)(2,1)}, bf16[384,768]{1,0:T(8,128)(2,1)S(1)}, u32[]{:S(2)}, u32[]{:S(2)}) collective-permute-start(bf16[384,768]{1,0:T(8,128)(2,1)} %pad_maximum_fusion.10), channel_id=1, source_target_pairs={{0,16},{8,24},{16,0},{24,8},{1,17},{9,25},{17,1},{25,9},{2,18},{10... | collective-permute-start | bytes 1769480 | tf_op jit(solution)/shard_map/ppermute | solution.py:431
  81.5 10.8 %collective-permute-start.3 = (bf16[192,768]{1,0:T(8,128)(2,1)S(1)}, bf16[192,768]{1,0:T(8,128)(2,1)S(1)}, u32[]{:S(2)}, u32[]{:S(2)}) collective-permute-start(bf16[192,768]{1,0:T(8,128)(2,1)S(1)} %slice.318), channel_id=1, source_target_pairs={{0,16},{8,24},{16,0},{24,8},{1,17},{9,25},{17,1},{25,9},{2,18},{10... | collective-permute-start | bytes 884744 | tf_op jit(solution)/shard_map/ppermute | solution.py:431
  86.6 7.7 %collective-permute-start.4 = (bf16[192,768]{1,0:T(8,128)(2,1)S(1)}, bf16[192,768]{1,0:T(8,128)(2,1)S(1)}, u32[]{:S(2)}, u32[]{:S(2)}) collective-permute-start(bf16[192,768]{1,0:T(8,128)(2,1)S(1)} %slice.319), channel_id=1, source_target_pairs={{0,8},{8,0},{16,24},{24,16},{1,9},{9,1},{17,25},{25,17},{2,10},{10... | collective-permute-start | bytes 884744 | tf_op jit(solution)/shard_map/ppermute | solution.py:431
  96.9 40.4 %copy-start.60 = (f32[1536]{0:T(1024)}, f32[1536]{0:T(1024)S(1)}, u32[]{:S(2)}) copy-start(f32[1536]{0:T(1024)S(1)} %get-tuple-element.102) | copy-start | bytes 18436
  119.1 366.3 %reduce-scatter.6.cloned.1.call-start = ((), (), s32[]{:S(2)}) async-start(), calls=%async_computation.6 | async-start | bytes 3932160 | tf_op jit(solution)/shard_map/reduce_scatter | solution.py:562
  123.1 29.2 %collective-permute-start.19 = (bf16[384,1536]{1,0:T(8,128)(2,1)}, bf16[384,1536]{1,0:T(8,128)(2,1)}, u32[]{:S(2)}, u32[]{:S(2)}) collective-permute-start(bf16[384,1536]{1,0:T(8,128)(2,1)} %pad_maximum_fusion.5), channel_id=1, source_target_pairs={{0,16},{8,24},{16,0},{24,8},{1,17},{9,25},{17,1},{25,9},{2,18},{10... | collective-permute-start | bytes 3538952 | tf_op jit(solution)/shard_map/ppermute | solution.py:431
  124.6 58.0 %collective-permute-start.18 = (bf16[384,1536]{1,0:T(8,128)(2,1)}, bf16[384,1536]{1,0:T(8,128)(2,1)S(1)}, u32[]{:S(2)}, u32[]{:S(2)}) collective-permute-start(bf16[384,1536]{1,0:T(8,128)(2,1)} %pad_maximum_fusion.5), channel_id=1, source_target_pairs={{0,8},{8,0},{16,24},{24,16},{1,9},{9,1},{17,25},{25,17},{2,10},{10... | collective-permute-start | bytes 3538952 | tf_op jit(solution)/shard_map/ppermute | solution.py:431
  126.2 51.3 %collective-permute-start.7 = (bf16[384,1536]{1,0:T(8,128)(2,1)}, bf16[384,1536]{1,0:T(8,128)(2,1)}, u32[]{:S(2)}, u32[]{:S(2)}) collective-permute-start(bf16[384,1536]{1,0:T(8,128)(2,1)} %pad_maximum_fusion.4), channel_id=1, source_target_pairs={{0,16},{8,24},{16,0},{24,8},{1,17},{9,25},{17,1},{25,9},{2,18},{10... | collective-permute-start | bytes 3538952 | tf_op jit(solution)/shard_map/ppermute | solution.py:431
  127.2 53.3 %collective-permute-start.6 = (bf16[384,1536]{1,0:T(8,128)(2,1)}, bf16[384,1536]{1,0:T(8,128)(2,1)}, u32[]{:S(2)}, u32[]{:S(2)}) collective-permute-start(bf16[384,1536]{1,0:T(8,128)(2,1)} %pad_maximum_fusion.4), channel_id=1, source_target_pairs={{0,8},{8,0},{16,24},{24,16},{1,9},{9,1},{17,25},{25,17},{2,10},{10... | collective-permute-start | bytes 3538952 | tf_op jit(solution)/shard_map/ppermute | solution.py:431
  134.6 139.7 %collective-permute-start.12 = (bf16[384,3072]{1,0:T(8,128)(2,1)}, bf16[384,3072]{1,0:T(8,128)(2,1)S(1)}, u32[]{:S(2)}, u32[]{:S(2)}) collective-permute-start(bf16[384,3072]{1,0:T(8,128)(2,1)} %pad_maximum_fusion.1), channel_id=1, source_target_pairs={{0,8},{8,0},{16,24},{24,16},{1,9},{9,1},{17,25},{25,17},{2,10},{10... | collective-permute-start | bytes 7077896 | tf_op jit(solution)/shard_map/ppermute | solution.py:431
  152.3 125.7 %collective-permute-start.13 = (bf16[384,3072]{1,0:T(8,128)(2,1)}, bf16[384,3072]{1,0:T(8,128)(2,1)}, u32[]{:S(2)}, u32[]{:S(2)}) collective-permute-start(bf16[384,3072]{1,0:T(8,128)(2,1)} %pad_maximum_fusion.1), channel_id=1, source_target_pairs={{0,16},{8,24},{16,0},{24,8},{1,17},{9,25},{17,1},{25,9},{2,18},{10... | collective-permute-start | bytes 7077896 | tf_op jit(solution)/shard_map/ppermute | solution.py:431
  177.6 98.5 %collective-permute-start.21 = (bf16[192,1536]{1,0:T(8,128)(2,1)}, bf16[192,1536]{1,0:T(8,128)(2,1)}, u32[]{:S(2)}, u32[]{:S(2)}) collective-permute-start(bf16[192,1536]{1,0:T(8,128)(2,1)} %slice.328), channel_id=1, source_target_pairs={{0,8},{8,0},{16,24},{24,16},{1,9},{9,1},{17,25},{25,17},{2,10},{10... | collective-permute-start | bytes 1769480 | tf_op jit(solution)/shard_map/ppermute | solution.py:431
  180.5 71.0 %collective-permute-start.9 = (bf16[192,1536]{1,0:T(8,128)(2,1)}, bf16[192,1536]{1,0:T(8,128)(2,1)}, u32[]{:S(2)}, u32[]{:S(2)}) collective-permute-start(bf16[192,1536]{1,0:T(8,128)(2,1)} %slice.323), channel_id=1, source_target_pairs={{0,8},{8,0},{16,24},{24,16},{1,9},{9,1},{17,25},{25,17},{2,10},{10... | collective-permute-start | bytes 1769480 | tf_op jit(solution)/shard_map/ppermute | solution.py:431
  182.6 55.0 %collective-permute-start.8 = (bf16[192,1536]{1,0:T(8,128)(2,1)S(1)}, bf16[192,1536]{1,0:T(8,128)(2,1)}, u32[]{:S(2)}, u32[]{:S(2)}) collective-permute-start(bf16[192,1536]{1,0:T(8,128)(2,1)S(1)} %slice.322), channel_id=1, source_target_pairs={{0,16},{8,24},{16,0},{24,8},{1,17},{9,25},{17,1},{25,9},{2,18},{10... | collective-permute-start | bytes 1769480 | tf_op jit(solution)/shard_map/ppermute | solution.py:431
  191.0 60.5 %copy-start.45 = (bf16[192,1536]{1,0:T(8,128)(2,1)S(1)}, bf16[192,1536]{1,0:T(8,128)(2,1)}, u32[]{:S(2)}) copy-start(bf16[192,1536]{1,0:T(8,128)(2,1)} %slice.327) | copy-start | bytes 1769476
  237.6 71.0 %collective-permute-start.23 = (bf16[1024,1536]{1,0:T(8,128)(2,1)}, bf16[1024,1536]{1,0:T(8,128)(2,1)}, u32[]{:S(2)}, u32[]{:S(2)}) collective-permute-start(bf16[1024,1536]{1,0:T(8,128)(2,1)} %all-gather.9.cloned.1.call-done), channel_id=1, source_target_pairs={{0,4},{4,0},{1,5},{5,1},{2,6},{6,2},{3,7},{7,3},{8,12},{12,8},{9,1... | collective-permute-start | bytes 9437192 | tf_op jit(solution)/shard_map/ppermute | solution.py:431
  251.5 21.9 %collective-permute-start.20 = (bf16[192,1536]{1,0:T(8,128)(2,1)S(1)}, bf16[192,1536]{1,0:T(8,128)(2,1)S(1)}, u32[]{:S(2)}, u32[]{:S(2)}) collective-permute-start(bf16[192,1536]{1,0:T(8,128)(2,1)S(1)} %copy-done.45), channel_id=1, source_target_pairs={{0,16},{8,24},{16,0},{24,8},{1,17},{9,25},{17,1},{25,9},{2,18},{10... | collective-permute-start | bytes 1769480 | tf_op jit(solution)/shard_map/ppermute | solution.py:431
  273.4 40.2 %collective-permute-start.10 = (bf16[1024,1536]{1,0:T(8,128)(2,1)}, bf16[1024,1536]{1,0:T(8,128)(2,1)S(1)}, u32[]{:S(2)}, u32[]{:S(2)}) collective-permute-start(bf16[1024,1536]{1,0:T(8,128)(2,1)} %get-tuple-element.28), channel_id=1, source_target_pairs={{0,4},{4,0},{1,5},{5,1},{2,6},{6,2},{3,7},{7,3},{8,12},{12,8},{9,1... | collective-permute-start | bytes 9437192 | tf_op jit(solution)/shard_map/ppermute | solution.py:431
  274.4 28.4 %collective-permute-start.14 = (bf16[192,3072]{1,0:T(8,128)(2,1)S(1)}, bf16[192,3072]{1,0:T(8,128)(2,1)S(1)}, u32[]{:S(2)}, u32[]{:S(2)}) collective-permute-start(bf16[192,3072]{1,0:T(8,128)(2,1)S(1)} %slice.325), channel_id=1, source_target_pairs={{0,16},{8,24},{16,0},{24,8},{1,17},{9,25},{17,1},{25,9},{2,18},{10... | collective-permute-start | bytes 3538952 | tf_op jit(solution)/shard_map/ppermute | solution.py:431
  279.3 28.2 %collective-permute-start.15 = (bf16[192,3072]{1,0:T(8,128)(2,1)S(1)}, bf16[192,3072]{1,0:T(8,128)(2,1)S(1)}, u32[]{:S(2)}, u32[]{:S(2)}) collective-permute-start(bf16[192,3072]{1,0:T(8,128)(2,1)S(1)} %slice.326), channel_id=1, source_target_pairs={{0,8},{8,0},{16,24},{24,16},{1,9},{9,1},{17,25},{25,17},{2,10},{10... | collective-permute-start | bytes 3538952 | tf_op jit(solution)/shard_map/ppermute | solution.py:431
  285.1 23.5 %copy-start.7 = (f32[1024,128]{1,0:T(8,128)S(1)}, f32[1024,128]{1,0:T(8,128)}, u32[]{:S(2)}) copy-start(f32[1024,128]{1,0:T(8,128)} %get-tuple-element.29) | copy-start | bytes 1572868
  308.6 5.0 collective-permute-start.16
  396.8 6.9 collective-permute-start.24
  397.8 5.4 collective-permute-start.25
  408.2 122.5 %reduce-scatter.4.cloned.1.call-start = ((), (), s32[]{:S(2)}) async-start(), calls=%async_computation.4 | async-start | bytes 3932160 | tf_op jit(solution)/shard_map/reduce_scatter | solution.py:567
  424.3 5.8 collective-permute-start.22
  435.4 163.2 %all-gather.11.cloned.1.call-start = ((), (), s32[]{:S(2)}) async-start(), calls=%async_computation.7 | async-start | bytes 3932160 | tf_op jit(solution)/shard_map/all_gather | solution.py:594
  452.6 82.9 %collective-permute-start.41 = (bf16[192,1536]{1,0:T(8,128)(2,1)}, bf16[192,1536]{1,0:T(8,128)(2,1)}, u32[]{:S(2)}, u32[]{:S(2)}) collective-permute-start(bf16[192,1536]{1,0:T(8,128)(2,1)} %get-tuple-element.133), channel_id=1, source_target_pairs={{0,8},{8,0},{16,24},{24,16},{1,9},{9,1},{17,25},{25,17},{2,10},{10... | collective-permute-start | bytes 1769480 | tf_op jit(solution)/shard_map/ppermute | solution.py:431
  453.2 82.3 %collective-permute-start.39 = (bf16[192,1536]{1,0:T(8,128)(2,1)}, bf16[192,1536]{1,0:T(8,128)(2,1)}, u32[]{:S(2)}, u32[]{:S(2)}) collective-permute-start(bf16[192,1536]{1,0:T(8,128)(2,1)} %get-tuple-element.134), channel_id=1, source_target_pairs={{0,16},{8,24},{16,0},{24,8},{1,17},{9,25},{17,1},{25,9},{2,18},{10... | collective-permute-start | bytes 1769480 | tf_op jit(solution)/shard_map/ppermute | solution.py:431
  483.2 47.6 %copy-start.28 = (bf16[256,384]{1,0:T(8,128)(2,1)S(1)}, bf16[256,384]{1,0:T(8,128)(2,1)}, u32[]{:S(2)}) copy-start(bf16[256,384]{1,0:T(8,128)(2,1)} %copy-done.27) | copy-start | bytes 589828
  483.2 47.6 %copy-start.30 = (bf16[256,384]{1,0:T(8,128)(2,1)S(1)}, bf16[256,384]{1,0:T(8,128)(2,1)}, u32[]{:S(2)}) copy-start(bf16[256,384]{1,0:T(8,128)(2,1)} %copy-done.29) | copy-start | bytes 589828
  483.2 61.3 %collective-permute-start.33 = (bf16[192,3072]{1,0:T(8,128)(2,1)}, bf16[192,3072]{1,0:T(8,128)(2,1)}, u32[]{:S(2)}, u32[]{:S(2)}) collective-permute-start(bf16[192,3072]{1,0:T(8,128)(2,1)} %get-tuple-element.126), channel_id=1, source_target_pairs={{0,8},{8,0},{16,24},{24,16},{1,9},{9,1},{17,25},{25,17},{2,10},{10... | collective-permute-start | bytes 3538952 | tf_op jit(solution)/shard_map/ppermute | solution.py:431
  484.0 60.5 %collective-permute-start.31 = (bf16[192,3072]{1,0:T(8,128)(2,1)}, bf16[192,3072]{1,0:T(8,128)(2,1)}, u32[]{:S(2)}, u32[]{:S(2)}) collective-permute-start(bf16[192,3072]{1,0:T(8,128)(2,1)} %get-tuple-element.127), channel_id=1, source_target_pairs={{0,16},{8,24},{16,0},{24,8},{1,17},{9,25},{17,1},{25,9},{2,18},{10... | collective-permute-start | bytes 3538952 | tf_op jit(solution)/shard_map/ppermute | solution.py:431
  485.4 45.3 %copy-start.21 = (bf16[256,1536]{1,0:T(8,128)(2,1)S(1)}, bf16[256,1536]{1,0:T(8,128)(2,1)}, u32[]{:S(2)}) copy-start(bf16[256,1536]{1,0:T(8,128)(2,1)} %reduce-scatter.6.cloned.1.call-done) | copy-start | bytes 2359300
  534.9 179.0 %reduce-scatter.8.cloned.1.call-start = ((), (), s32[]{:S(2)}) async-start(), calls=%async_computation.8 | async-start | bytes 3932160 | tf_op jit(solution)/shard_map/reduce_scatter | solution.py:599
  537.5 27.6 %collective-permute-start.42 = (bf16[384,1536]{1,0:T(8,128)(2,1)S(1)}, bf16[384,1536]{1,0:T(8,128)(2,1)S(1)}, u32[]{:S(2)}, u32[]{:S(2)}) collective-permute-start(bf16[384,1536]{1,0:T(8,128)(2,1)S(1)} %pad_maximum_fusion.7), channel_id=1, source_target_pairs={{0,16},{8,24},{16,0},{24,8},{1,17},{9,25},{17,1},{25,9},{2,18},{10... | collective-permute-start | bytes 3538952 | tf_op jit(solution)/shard_map/ppermute | solution.py:431
  539.1 27.3 %collective-permute-start.40 = (bf16[384,1536]{1,0:T(8,128)(2,1)S(1)}, bf16[384,1536]{1,0:T(8,128)(2,1)S(1)}, u32[]{:S(2)}, u32[]{:S(2)}) collective-permute-start(bf16[384,1536]{1,0:T(8,128)(2,1)S(1)} %pad_maximum_fusion.6), channel_id=1, source_target_pairs={{0,8},{8,0},{16,24},{24,16},{1,9},{9,1},{17,25},{25,17},{2,10},{10... | collective-permute-start | bytes 3538952 | tf_op jit(solution)/shard_map/ppermute | solution.py:431
  568.2 5.2 collective-permute-start.43
  569.8 66.0 %collective-permute-start.34 = (bf16[384,3072]{1,0:T(8,128)(2,1)}, bf16[384,3072]{1,0:T(8,128)(2,1)}, u32[]{:S(2)}, u32[]{:S(2)}) collective-permute-start(bf16[384,3072]{1,0:T(8,128)(2,1)} %pad_maximum_fusion.3), channel_id=1, source_target_pairs={{0,16},{8,24},{16,0},{24,8},{1,17},{9,25},{17,1},{25,9},{2,18},{10... | collective-permute-start | bytes 7077896 | tf_op jit(solution)/shard_map/ppermute | solution.py:431
  571.9 63.9 %collective-permute-start.32 = (bf16[384,3072]{1,0:T(8,128)(2,1)}, bf16[384,3072]{1,0:T(8,128)(2,1)}, u32[]{:S(2)}, u32[]{:S(2)}) collective-permute-start(bf16[384,3072]{1,0:T(8,128)(2,1)} %pad_maximum_fusion.2), channel_id=1, source_target_pairs={{0,8},{8,0},{16,24},{24,16},{1,9},{9,1},{17,25},{25,17},{2,10},{10... | collective-permute-start | bytes 7077896 | tf_op jit(solution)/shard_map/ppermute | solution.py:431
  598.6 24.0 %copy-start.70 = (bf16[1024,1536]{1,0:T(8,128)(2,1)S(1)}, bf16[1024,1536]{1,0:T(8,128)(2,1)}, u32[]{:S(2)}) copy-start(bf16[1024,1536]{1,0:T(8,128)(2,1)} %get-tuple-element.40) | copy-start | bytes 9437188
  635.8 17.0 %collective-permute-start.26 = (bf16[4,192,1152]{2,1,0:T(8,128)(2,1)}, bf16[4,192,1152]{2,1,0:T(8,128)(2,1)S(1)}, u32[]{:S(2)}, u32[]{:S(2)}) collective-permute-start(bf16[4,192,1152]{2,1,0:T(8,128)(2,1)} %get-tuple-element.140), channel_id=1, source_target_pairs={{0,4},{4,0},{1,5},{5,1},{2,6},{6,2},{3,7},{7,3},{8,12},{12,8},{9,1... | collective-permute-start | bytes 5308424 | tf_op jit(solution)/shard_map/ppermute | solution.py:431
  642.6 20.1 %collective-permute-start.35 = (bf16[192,3072]{1,0:T(8,128)(2,1)}, bf16[192,3072]{1,0:T(8,128)(2,1)}, u32[]{:S(2)}, u32[]{:S(2)}) collective-permute-start(bf16[192,3072]{1,0:T(8,128)(2,1)} %constant_dynamic-slice_fusion.1), channel_id=1, source_target_pairs={{0,4},{4,0},{1,5},{5,1},{2,6},{6,2},{3,7},{7,3},{8,12},{12,8},{9,1... | collective-permute-start | bytes 3538952 | tf_op jit(solution)/shard_map/ppermute | solution.py:431
  658.7 14.6 %copy-start.1 = (bf16[4,192,1152]{1,2,0:T(8,128)(2,1)}, bf16[4,192,1152]{1,2,0:T(8,128)(2,1)S(1)}, u32[]{:S(2)}) copy-start(bf16[4,192,1152]{1,2,0:T(8,128)(2,1)S(1)} %fusion) | copy-start | bytes 5308420
  660.0 13.3 %collective-permute-start.29 = (bf16[96,1152]{0,1:T(8,128)(2,1)}, bf16[96,1152]{0,1:T(8,128)(2,1)}, u32[]{:S(2)}, u32[]{:S(2)}) collective-permute-start(bf16[96,1152]{0,1:T(8,128)(2,1)} %get-tuple-element.145), channel_id=1, source_target_pairs={{0,8},{8,0},{16,24},{24,16},{1,9},{9,1},{17,25},{25,17},{2,10},{10... | collective-permute-start | bytes 663560 | tf_op jit(solution)/shard_map/ppermute | solution.py:431
  661.2 12.1 %collective-permute-start.27 = (bf16[96,1152]{0,1:T(8,128)(2,1)}, bf16[96,1152]{0,1:T(8,128)(2,1)}, u32[]{:S(2)}, u32[]{:S(2)}) collective-permute-start(bf16[96,1152]{0,1:T(8,128)(2,1)} %get-tuple-element.146), channel_id=1, source_target_pairs={{0,16},{8,24},{16,0},{24,8},{1,17},{9,25},{17,1},{25,9},{2,18},{10... | collective-permute-start | bytes 663560 | tf_op jit(solution)/shard_map/ppermute | solution.py:431
  683.7 11.8 %collective-permute-start.30 = (bf16[192,1152]{1,0:T(8,128)(2,1)}, bf16[192,1152]{1,0:T(8,128)(2,1)}, u32[]{:S(2)}, u32[]{:S(2)}) collective-permute-start(bf16[192,1152]{1,0:T(8,128)(2,1)} %copy.133), channel_id=1, source_target_pairs={{0,16},{8,24},{16,0},{24,8},{1,17},{9,25},{17,1},{25,9},{2,18},{10... | collective-permute-start | bytes 1327112 | tf_op jit(solution)/shard_map/ppermute | solution.py:431
  684.3 12.6 %collective-permute-start.28 = (bf16[192,1152]{1,0:T(8,128)(2,1)}, bf16[192,1152]{1,0:T(8,128)(2,1)}, u32[]{:S(2)}, u32[]{:S(2)}) collective-permute-start(bf16[192,1152]{1,0:T(8,128)(2,1)} %copy.131), channel_id=1, source_target_pairs={{0,8},{8,0},{16,24},{24,16},{1,9},{9,1},{17,25},{25,17},{2,10},{10... | collective-permute-start | bytes 1327112 | tf_op jit(solution)/shard_map/ppermute | solution.py:431
  700.3 13.6 %copy-start.10 = (bf16[256,384]{1,0:T(8,128)(2,1)S(1)}, bf16[256,384]{1,0:T(8,128)(2,1)}, u32[]{:S(2)}) copy-start(bf16[256,384]{1,0:T(8,128)(2,1)} %copy-done.9) | copy-start | bytes 589828
  700.3 13.6 %copy-start.12 = (bf16[256,384]{1,0:T(8,128)(2,1)S(1)}, bf16[256,384]{1,0:T(8,128)(2,1)}, u32[]{:S(2)}) copy-start(bf16[256,384]{1,0:T(8,128)(2,1)} %copy-done.11) | copy-start | bytes 589828
  700.3 13.6 %copy-start.14 = (bf16[256,384]{1,0:T(8,128)(2,1)S(1)}, bf16[256,384]{1,0:T(8,128)(2,1)}, u32[]{:S(2)}) copy-start(bf16[256,384]{1,0:T(8,128)(2,1)} %copy-done.13) | copy-start | bytes 589828
  700.3 13.6 %copy-start.16 = (bf16[256,384]{1,0:T(8,128)(2,1)S(1)}, bf16[256,384]{1,0:T(8,128)(2,1)}, u32[]{:S(2)}) copy-start(bf16[256,384]{1,0:T(8,128)(2,1)} %copy-done.15) | copy-start | bytes 589828
  701.1 9.0 %collective-permute-start.37 = (f32[192,26]{0,1:T(8,128)}, f32[192,26]{0,1:T(8,128)}, u32[]{:S(2)}, u32[]{:S(2)}) collective-permute-start(f32[192,26]{0,1:T(8,128)} %pad_maximum_fusion.13), channel_id=1, source_target_pairs={{0,2},{1,3},{2,0},{3,1},{4,6},{5,7},{6,4},{7,5},{8,10},{9,11},{10,... | collective-permute-start | bytes 59912 | tf_op jit(solution)/shard_map/ppermute | solution.py:641
  702.1 8.0 %collective-permute-start.38 = (f32[192,26]{0,1:T(8,128)}, f32[192,26]{0,1:T(8,128)}, u32[]{:S(2)}, u32[]{:S(2)}) collective-permute-start(f32[192,26]{0,1:T(8,128)} %pad_maximum_fusion.13), channel_id=1, source_target_pairs={{0,3},{1,0},{2,1},{3,2},{4,7},{5,4},{6,5},{7,6},{8,11},{9,8},{10,9... | collective-permute-start | bytes 59912 | tf_op jit(solution)/shard_map/ppermute | solution.py:641
  702.6 7.5 %collective-permute-start.36 = (f32[192,26]{0,1:T(8,128)}, f32[192,26]{0,1:T(8,128)}, u32[]{:S(2)}, u32[]{:S(2)}) collective-permute-start(f32[192,26]{0,1:T(8,128)} %pad_maximum_fusion.13), channel_id=1, source_target_pairs={{0,1},{1,2},{2,3},{3,0},{4,5},{5,6},{6,7},{7,4},{8,9},{9,10},{10,1... | collective-permute-start | bytes 59912 | tf_op jit(solution)/shard_map/ppermute | solution.py:641
  (58 other events, 210.0 us)
Sparse Core Ops, SparseCore 0:
  10.7 71.3 all-gather.6
  83.7 63.7 all-gather.8
  149.7 62.1 all-gather.12
  408.3 59.9 reduce-scatter.5
  470.4 60.2 reduce-scatter.3
  535.1 63.5 all-gather.10
  652.9 60.9 reduce-scatter.7

commit v2 on v1

--- a/solution.py
+++ b/solution.py
@@ -30,6 +30,14 @@
 
 def nn(left, right):
     return jnp.dot(left, right, preferred_element_type=F32)
+
+
+def cost(flops, transcendentals, bytes_accessed, scale=1):
+    return pl.CostEstimate(
+        flops=flops // scale,
+        transcendentals=transcendentals // scale,
+        bytes_accessed=bytes_accessed // scale,
+    )
 
 
 def rope_cols(values, cosine, sine):
@@ -142,17 +150,18 @@
         compiler_params=pltpu.CompilerParams(
             dimension_semantics=("arbitrary",), vmem_limit_bytes=VMEM_CAP
         ),
-        cost_estimate=pl.CostEstimate(
+        cost_estimate=cost(
             flops=2 * length * width * cols + 8 * length * 768 * q_heads * HEAD,
             transcendentals=length * 640 * q_heads,
             bytes_accessed=4 * length * width + 2 * width * cols,
+            scale=100,
         ),
         name="attn_fwd",
     )(tokens, gain, pack, cosine, sine, kdoc, qdoc)
 
 
 def attn_bwd_kernel(
-    ag_ref, wo_ref, q_ref, k_ref, v_ref, att_ref, lse_ref, cos_ref, sin_ref, kdoc_ref, qdoc_ref,
+    do_ref, q_ref, k_ref, v_ref, att_ref, lse_ref, cos_ref, sin_ref, kdoc_ref, qdoc_ref,
     dq_ref, dkv_ref, dk_scr, dv_scr, *, q_heads, kv_heads,
 ):
     i = pl.program_id(0)
@@ -163,7 +172,7 @@
         dk_scr[...] = jnp.zeros_like(dk_scr)
         dv_scr[...] = jnp.zeros_like(dv_scr)
 
-    do = nn(ag_ref[...], wo_ref[...]).astype(BF16)
+    do = do_ref[...]
     lo = jnp.maximum(i - 2, 0)
     qdoc = qdoc_ref[...]
     att = att_ref[...]
@@ -204,8 +213,8 @@
         dkv_ref[:, kcols:] = jnp.concatenate([dv_scr[g] for g in range(kv_heads)], 1).astype(BF16)
 
 
-def attn_bwd(ag, wo, q, k, v, att, lse, cosine, sine, kdoc, qdoc):
-    length, width = ag.shape
+def attn_bwd(do, q, k, v, att, lse, cosine, sine, kdoc, qdoc):
+    length = do.shape[0]
     q_heads, kv_heads = q.shape[0], k.shape[0]
     blocks = length // BLK
     group = q_heads // kv_heads
@@ -216,8 +225,7 @@
         functools.partial(attn_bwd_kernel, q_heads=q_heads, kv_heads=kv_heads),
         grid=(blocks,),
         in_specs=[
-            pl.BlockSpec((BLK, width), row),
-            pl.BlockSpec((width, q_heads * HEAD), fixed),
+            pl.BlockSpec((BLK, q_heads * HEAD), row),
             pl.BlockSpec((q_heads, BLK, HEAD), lambda i: (0, i, 0)),
             pl.BlockSpec((kv_heads, length, HEAD), fixed3),
             pl.BlockSpec((kv_heads, length, HEAD), fixed3),
@@ -243,21 +251,21 @@
         compiler_params=pltpu.CompilerParams(
             dimension_semantics=("arbitrary",), vmem_limit_bytes=VMEM_CAP
         ),
-        cost_estimate=pl.CostEstimate(
-            flops=2 * length * width * q_heads * HEAD + 20 * length * 768 * q_heads * HEAD,
+        cost_estimate=cost(
+            flops=20 * length * 768 * q_heads * HEAD,
             transcendentals=length * 640 * q_heads,
-            bytes_accessed=2 * length * width + 2 * width * q_heads * HEAD,
+            bytes_accessed=8 * length * q_heads * HEAD,
         ),
         name="attn_bwd",
-    )(ag, wo, q, k, v, att, lse, cosine, sine, kdoc, qdoc)
+    )(do, q, k, v, att, lse, cosine, sine, kdoc, qdoc)
 
 
 def mid_kernel(
-    att_ref, wo_ref, tok_ref, gain_ref, small_ref, routes_ref, mid_ref, nm_ref, gate_ref, *, experts
+    att_ref, wo_ref, tok_ref, gain_ref, small_ref, routes_ref, mid_ref, nm_ref, gate_ref, flat_ref
 ):
-    branch = nt(att_ref[0], wo_ref[0])
-    for m in range(1, att_ref.shape[0]):
-        branch += nt(att_ref[m], wo_ref[m])
+    att = jnp.concatenate([att_ref[k] for k in range(att_ref.shape[0])], 1)
+    flat_ref[...] = att
+    branch = nt(att, wo_ref[...])
     middle = tok_ref[...].astype(F32) + RESID * branch
     mid_ref[...] = middle
     inv = lax.rsqrt(jnp.mean(middle * middle, -1, keepdims=True) + EPS)
@@ -273,18 +281,18 @@
     gate_ref[...] = e / jnp.sum(e, -1, keepdims=True)
 
 
-def mid_fwd(att_all, wo_all, tokens, gain, pack, small_at, routes, experts):
+def mid_fwd(att_all, wo_rows, tokens, gain, pack, small_at, routes):
     length, width = tokens.shape
     parts, _, cols = att_all.shape
     blocks = length // BLK
     fixed = lambda i: (0, 0)
     row = lambda i: (i, 0)
     return pl.pallas_call(
-        functools.partial(mid_kernel, experts=experts),
+        mid_kernel,
         grid=(blocks,),
         in_specs=[
             pl.BlockSpec((parts, BLK, cols), lambda i: (0, i, 0)),
-            pl.BlockSpec((parts, width, cols), lambda i: (0, 0, 0)),
+            pl.BlockSpec((width, parts * cols), fixed),
             pl.BlockSpec((BLK, width), row),
             pl.BlockSpec((1, width), fixed),
             pl.BlockSpec((width, 128), lambda i: (0, small_at)),
@@ -294,22 +302,124 @@
             pl.BlockSpec((BLK, width), row),
             pl.BlockSpec((BLK, width), row),
             pl.BlockSpec((BLK, 128), row),
+            pl.BlockSpec((BLK, parts * cols), row),
         ],
         out_shape=[
             jax.ShapeDtypeStruct((length, width), F32),
             jax.ShapeDtypeStruct((length, width), BF16),
             jax.ShapeDtypeStruct((length, 128), F32),
+            jax.ShapeDtypeStruct((length, parts * cols), BF16),
         ],
         compiler_params=pltpu.CompilerParams(
             dimension_semantics=("arbitrary",), vmem_limit_bytes=VMEM_CAP
         ),
-        cost_estimate=pl.CostEstimate(
+        cost_estimate=cost(
             flops=2 * length * width * cols * parts,
             transcendentals=length * 128,
             bytes_accessed=10 * length * width + 2 * width * cols * parts,
+            scale=100,
         ),
         name="mid_fwd",
-    )(att_all, wo_all, tokens, gain, pack, routes)
+    )(att_all, wo_rows, tokens, gain, pack, routes)
+
+
+def norm_back(n_grad, values, gain):
+    inv = lax.rsqrt(jnp.mean(values * values, -1, keepdims=True) + EPS)
+    scaled = n_grad * gain
+    return inv * (scaled - values * (inv * inv) * jnp.mean(scaled * values, -1, keepdims=True))
+
+
+def back_mid_kernel(
+    own_ref, back_ref, recv_ref, lg_ref, small_ref, mid_ref, gain_ref, cot_ref, wo_ref, ag_ref, p_ref
+):
+    n_grad = back_ref[...].astype(F32) + recv_ref[...].astype(F32) + nt(lg_ref[...], small_ref[...])
+    grad = norm_back(n_grad, mid_ref[...], gain_ref[...])
+    own = (pl.program_id(0) == own_ref[0]).astype(F32)
+    ag = (RESID * (grad + own * cot_ref[...].astype(F32))).astype(BF16)
+    ag_ref[...] = ag
+    out = nn(ag, wo_ref[...]).astype(BF16)
+    cols = p_ref.shape[2]
+    for k in range(p_ref.shape[0]):
+        p_ref[k] = out[:, k * cols : (k + 1) * cols]
+
+
+def back_mid(own, back, recv, logit_grad, pack, small_at, middle, gain, cot, wo_rows, parts):
+    length, width = middle.shape
+    blocks = length // BLK
+    cols = wo_rows.shape[1] // parts
+    fixed = lambda i, o: (0, 0)
+    row = lambda i, o: (i, 0)
+    return pl.pallas_call(
+        back_mid_kernel,
+        grid_spec=pltpu.PrefetchScalarGridSpec(
+            num_scalar_prefetch=1,
+            grid=(blocks,),
+            in_specs=[
+                pl.BlockSpec((BLK, width), row),
+                pl.BlockSpec((BLK, width), row),
+                pl.BlockSpec((BLK, 128), row),
+                pl.BlockSpec((width, 128), lambda i, o: (0, small_at)),
+                pl.BlockSpec((BLK, width), row),
+                pl.BlockSpec((1, width), fixed),
+                pl.BlockSpec((BLK, width), fixed),
+                pl.BlockSpec((width, parts * cols), fixed),
+            ],
+            out_specs=[
+                pl.BlockSpec((BLK, width), row),
+                pl.BlockSpec((parts, BLK, cols), lambda i, o: (0, i, 0)),
+            ],
+        ),
+        out_shape=[
+            jax.ShapeDtypeStruct((length, width), BF16),
+            jax.ShapeDtypeStruct((parts, length, cols), BF16),
+        ],
+        compiler_params=pltpu.CompilerParams(
+            dimension_semantics=("arbitrary",), vmem_limit_bytes=VMEM_CAP
+        ),
+        cost_estimate=cost(
+            flops=2 * length * width * cols * parts,
+            transcendentals=0,
+            bytes_accessed=12 * length * width + 2 * width * cols * parts,
+        ),
+        name="back_mid",
+    )(own, back, recv, logit_grad, pack, middle, gain, cot, wo_rows)
+
+
+def back_end_kernel(dq_ref, dkv_ref, w_ref, tok_ref, gain_ref, ag_ref, out_ref):
+    d_all = jnp.concatenate([dq_ref[...], dkv_ref[...]], 1)
+    n_grad = nt(d_all, w_ref[...])
+    grad = norm_back(n_grad, tok_ref[...].astype(F32), gain_ref[...])
+    out_ref[...] = (grad + ag_ref[...].astype(F32) * (1.0 / RESID)).astype(BF16)
+
+
+def back_end(dq, dkv, pack, tokens, gain, ag):
+    length, width = tokens.shape
+    cols = dq.shape[1] + dkv.shape[1]
+    fixed = lambda i: (0, 0)
+    row = lambda i: (i, 0)
+    return pl.pallas_call(
+        back_end_kernel,
+        grid=(length // BLK,),
+        in_specs=[
+            pl.BlockSpec((BLK, dq.shape[1]), row),
+            pl.BlockSpec((BLK, dkv.shape[1]), row),
+            pl.BlockSpec((width, cols), fixed),
+            pl.BlockSpec((BLK, width), row),
+            pl.BlockSpec((1, width), fixed),
+            pl.BlockSpec((BLK, width), row),
+        ],
+        out_specs=pl.BlockSpec((BLK, width), row),
+        out_shape=jax.ShapeDtypeStruct((length, width), BF16),
+        compiler_params=pltpu.CompilerParams(
+            dimension_semantics=("arbitrary",), vmem_limit_bytes=VMEM_CAP
+        ),
+        cost_estimate=cost(
+            flops=2 * length * width * cols,
+            transcendentals=0,
+            bytes_accessed=6 * length * width + 2 * width * cols,
+        ),
+        name="back_end",
+    )(dq, dkv, pack, tokens, gain, ag)
 
 
 def gate_cols(gates, first):
@@ -356,10 +466,11 @@
         compiler_params=pltpu.CompilerParams(
             dimension_semantics=("arbitrary", "arbitrary"), vmem_limit_bytes=VMEM_CAP
         ),
-        cost_estimate=pl.CostEstimate(
+        cost_estimate=cost(
             flops=2 * length * width * cols,
             transcendentals=length * cols // 2,
             bytes_accessed=2 * length * (width + cols + cols // 2) + 4 * width * cols,
+            scale=100,
         ),
         name="moe_fwd",
     )(base, x, w_in, gates)
@@ -418,13 +529,45 @@
         compiler_params=pltpu.CompilerParams(
             dimension_semantics=("arbitrary", "arbitrary"), vmem_limit_bytes=VMEM_CAP
         ),
-        cost_estimate=pl.CostEstimate(
+        cost_estimate=cost(
             flops=length * width * cols,
             transcendentals=length * cols // 2,
             bytes_accessed=2 * length * (width + 2 * cols) + 2 * width * cols,
         ),
         name="moe_bwd",
     )(base, g, w_out, gates, h)
+
+
+def tn_pair_kernel(left_ref, left2_ref, right_ref, right2_ref, out_ref):
+    out_ref[...] = (tn(left_ref[...], right_ref[...]) + tn(left2_ref[...], right2_ref[...])).astype(BF16)
+
+
+def tn_pair(left, left2, right, right2):
+    length, width = left.shape
+    cols = right.shape[1]
+    tall, wide = width // 2, 512
+    return pl.pallas_call(
+        tn_pair_kernel,
+        grid=(width // tall, cols // wide),
+        in_specs=[
+            pl.BlockSpec((length, tall), lambda i, j: (0, i)),
+            pl.BlockSpec((length, tall), lambda i, j: (0, i)),
+            pl.BlockSpec((length, wide), lambda i, j: (0, j)),
+            pl.BlockSpec((length, wide), lambda i, j: (0, j)),
+        ],
+        out_specs=pl.BlockSpec((tall, wide), lambda i, j: (i, j)),
+        out_shape=jax.ShapeDtypeStruct((width, cols), BF16),
+        compiler_params=pltpu.CompilerParams(
+            dimension_semantics=("arbitrary", "arbitrary"), vmem_limit_bytes=VMEM_CAP
+        ),
+        cost_estimate=cost(
+            flops=4 * length * width * cols,
+            transcendentals=0,
+            bytes_accessed=4 * length * (width + 2 * cols),
+            scale=100,
+        ),
+        name="weight_grad",
+    )(left, left2, right, right2)
 
 
 def swap(value, axis, bit, size):
@@ -442,36 +585,98 @@
     return jnp.concatenate([jnp.where(far, c[k ^ 2], c[k]) for k in range(4)], -1)
 
 
+def gather_first(value, quads):
+    if quads != 4:
+        return (lax.all_gather(value, "q", axis=0, tiled=True),)
+    half = value.shape[0] // 2
+    return swap(value[:half], "q", 1, 4), swap(value[half:], "q", 2, 4)
+
+
+def gather_rest(value, quads):
+    if quads != 4:
+        return ()
+    half = value.shape[0] // 2
+    return swap(value[half:], "q", 1, 4), swap(value[:half], "q", 2, 4)
+
+
+def gather_last(value, first, rest, quads):
+    if quads != 4:
+        return first[0]
+    diag_a = swap(first[0], "q", 2, 4)
+    diag_b = swap(first[1], "q", 1, 4)
+    return jnp.concatenate([value, first[0], rest[0], rest[1], first[1], diag_a, diag_b], 0)
+
+
 def gather_rows(value, quads):
+    return gather_last(value, gather_first(value, quads), gather_rest(value, quads), quads)
+
+
+def scatter_first(value, quads):
     if quads != 4:
-        return lax.all_gather(value, "q", axis=0, tiled=True)
-    half = value.shape[0] // 2
-    from_x = swap(value, "q", 1, 4)
-    from_y = swap(value, "q", 2, 4)
-    diag_a = swap(from_x[:half], "q", 2, 4)
-    diag_b = swap(from_y[half:], "q", 1, 4)
-    return jnp.concatenate([value, from_x, from_y, diag_a, diag_b], 0)
+        return (value,)
+    n = value.shape[0] // 8
+    part = [value[k * n : (k + 1) * n] for k in range(8)]
+    from_x = swap(jnp.concatenate([part[2], part[6]], 0), "q", 1, 4)
+    from_y = swap(jnp.concatenate([part[5], part[7]], 0), "q", 2, 4)
+    return value, from_x, from_y
+
+
+def scatter_second(first, quads):
+    if quads != 4:
+        return lax.psum_scatter(first[0], "q", scatter_dimension=0, tiled=True).astype(F32)
+    value, from_x, from_y = first
+    n = value.shape[0] // 8
+    give_y = (value[4 * n : 5 * n].astype(F32) + from_x[n:].astype(F32)).astype(BF16)
+    give_x = (value[3 * n : 4 * n].astype(F32) + from_y[n:].astype(F32)).astype(BF16)
+    give_x, give_y = lax.optimization_barrier((give_x, give_y))
+    low = swap(give_y, "q", 2, 4)
+    high = swap(give_x, "q", 1, 4)
+    value, from_x, from_y = all_after((value, from_x, from_y), low, high)
+    return jnp.concatenate(
+        [
+            value[:n].astype(F32) + from_x[:n].astype(F32) + low.astype(F32),
+            value[n : 2 * n].astype(F32) + from_y[:n].astype(F32) + high.astype(F32),
+        ],
+        0,
+    )
 
 
 def scatter_rows(value, quads):
-    if quads != 4:
-        return lax.psum_scatter(value, "q", scatter_dimension=0, tiled=True).astype(F32)
-    n = value.shape[0] // 4
-    half = n // 2
-    own, to_x, to_y, diag = (value[k * n : (k + 1) * n] for k in range(4))
-    via_x = swap(diag[:half], "q", 1, 4)
-    via_y = swap(diag[half:], "q", 2, 4)
-    to_y = jnp.concatenate([(to_y[:half].astype(F32) + via_x.astype(F32)).astype(BF16), to_y[half:]], 0)
-    to_x = jnp.concatenate([to_x[:half], (to_x[half:].astype(F32) + via_y.astype(F32)).astype(BF16)], 0)
-    from_x = swap(to_x, "q", 1, 4)
-    from_y = swap(to_y, "q", 2, 4)
-    return own.astype(F32) + from_x.astype(F32) + from_y.astype(F32)
-
-
-def both_cores(mine, c):
-    other = swap(mine, "c", 1, 2)
+    return scatter_second(scatter_first(value, quads), quads)
+
+
+def after(value, *others):
+    return lax.optimization_barrier((value, *others))[0]
+
+
+def all_after(values, *others):
+    return lax.optimization_barrier((*values, *others))[: len(values)]
+
+
+def to_halves(mine, give, c):
+    other = swap(give, "c", 1, 2)
     first = c == 0
     return jnp.concatenate([jnp.where(first, mine, other), jnp.where(first, other, mine)], 0)
+
+
+def from_halves(total, rows, c):
+    mine = lax.dynamic_slice_in_dim(total, c * rows, rows, 0)
+    give = lax.dynamic_slice_in_dim(total, (1 - c) * rows, rows, 0)
+    other = swap(give, "c", 1, 2)
+    first = c == 0
+    return jnp.where(first, mine, other), jnp.where(first, other, mine), mine, other
+
+
+def column_halves(value, c):
+    n = value.shape[1] // 2
+    mine = jnp.where(c == 0, value[:, :n], value[:, n:])
+    give = jnp.where(c == 0, value[:, n:], value[:, :n])
+    return mine, give
+
+
+def whole_columns(half, c):
+    other = swap(half, "c", 1, 2)
+    return jnp.where(c == 0, half, other), jnp.where(c == 0, other, half)
 
 
 def body(
@@ -480,6 +685,7 @@
 ):
     q = lax.axis_index("q")
     c = lax.axis_index("c")
+    m = lax.axis_index("mp")
     length = segments.shape[1]
     width = tokens.shape[2]
     rows = w_query.shape[0]
@@ -492,6 +698,22 @@
     qkv_cols = q_cols + 2 * kv_cols
     mp = lax.axis_size("mp")
 
+    tok_own = reorder(tokens[0], q, quads)
+    tok_all = lax.all_gather(tok_own, "mp", axis=0, tiled=True)
+
+    pad = jnp.zeros((rows, 128 - experts - 2), BF16)
+    pack = jnp.concatenate(
+        [w_query, key_weight, value_weight, router, attn_gain[:, None], moe_gain[:, None], pad], 1
+    )
+    pack_pair = to_halves(*column_halves(pack, c), c)
+    pack_first = gather_first(pack_pair, quads)
+    pack_half = gather_last(pack_pair, pack_first, gather_rest(pack_pair, quads), quads)
+    pack = jnp.concatenate(whole_columns(pack_half, c), 1)
+    small_at = qkv_cols // 128
+    gains = pack[:, qkv_cols + experts : qkv_cols + experts + 2].astype(F32)
+    attn_g = gains[:, 0].reshape(1, width)
+    moe_g = gains[:, 1].reshape(1, width)
+
     doc_row = segments
     doc_col = segments.reshape(length, 1)
     lane = jnp.arange(128, dtype=jnp.int32) % (HEAD // 2)
@@ -501,138 +723,131 @@
     upper = (jnp.arange(128, dtype=jnp.int32) % HEAD) < (HEAD // 2)
     sine = jnp.where(upper[None, :], -jnp.sin(angles), jnp.sin(angles))
 
-    tok_own = reorder(tokens[0], q, quads)
-    cot_own = reorder(cotangent[0], q, quads)
-    tok_all = lax.all_gather(tok_own, "mp", axis=0, tiled=True)
-
-    pad = jnp.zeros((rows, 128 - experts - 2), BF16)
-    pack = jnp.concatenate(
-        [w_query, key_weight, value_weight, router, attn_gain[:, None], moe_gain[:, None], pad], 1
-    )
-    pack = gather_rows(both_cores(pack, c), quads)
-    small_at = qkv_cols // 128
-    gains = pack[:, qkv_cols + experts : qkv_cols + experts + 2].astype(F32)
-    attn_g = gains[:, 0].reshape(1, width)
-    moe_g = gains[:, 1].reshape(1, width)
-    wo_pieces = lax.all_gather(w_output, "mp", axis=0, tiled=False)
-    wo_pieces = wo_pieces.transpose(1, 0, 2).reshape(rows, mp * q_cols)
-    wo_rows = gather_rows(both_cores(wo_pieces, c), quads)
-    wo_all = wo_rows.reshape(width, mp, q_cols).transpose(1, 0, 2)
-
-    in_halves = w_in.reshape(rows, 2, half_e * 2 * ff)
-    out_halves = w_out.reshape(rows, 2, half_e * ff)
-
-    def half_rows(halves):
-        mine = lax.dynamic_index_in_dim(halves, c, 1, keepdims=False)
-        give = lax.dynamic_index_in_dim(halves, 1 - c, 1, keepdims=False)
-        other = swap(give, "c", 1, 2)
-        first = c == 0
-        return jnp.concatenate([jnp.where(first, mine, other), jnp.where(first, other, mine)], 0)
-
-    in_full = gather_rows(half_rows(in_halves), quads)
-    out_full = gather_rows(half_rows(out_halves), quads)
+    def half_rows(value):
+        mine = lax.dynamic_slice_in_dim(value, c * half_e, half_e, 1).reshape(rows, -1)
+        give = lax.dynamic_slice_in_dim(value, (1 - c) * half_e, half_e, 1).reshape(rows, -1)
+        return to_halves(mine, give, c), mine, give
+
+    in_pair, in_kept, in_gave = half_rows(after(w_in, pack_pair))
+    out_pair, _, _ = half_rows(after(w_out, in_pair))
+    in_src = after(in_pair, *pack_first)
+    in_got = gather_first(in_src, quads)
+    in_rest = gather_rest(after(in_src, *in_got), quads)
 
     normed_a, q_r, k_r, v_r, attended, lse = attn_fwd(
-        tok_all, attn_g, pack, cosine, sine, doc_col, doc_row, q_heads, kv_heads
-    )
-    att_all = lax.all_gather(attended, "mp", axis=0, tiled=False)
-    middle, normed_m, gates = mid_fwd(
-        att_all, wo_all, tok_all, moe_g, pack, small_at, routes[0], experts
-    )
-
-    x2 = jnp.concatenate([normed_m, swap(normed_m, "c", 1, 2)], 0)
-    gates2 = jnp.concatenate([gates, swap(gates, "c", 1, 2)], 0)
+        tok_all, attn_g, after(pack, *in_got), cosine, sine, doc_col, doc_row, q_heads, kv_heads
+    )
+
+    wo_pad = jnp.concatenate([w_output, jnp.zeros((rows, 5 * 64), BF16)], 1)
+    wo_cols = lax.all_gather(after(wo_pad, tok_all, pack), "mp", axis=0, tiled=False)
+    wo_cols = jnp.concatenate([wo_cols[j, :, :q_cols] for j in range(mp)], 1)
+    wo_pair = to_halves(*column_halves(after(wo_cols, attended), c), c)
+    in_full = gather_last(in_pair, in_got, in_rest, quads)
+    wo_src = after(wo_pair, in_full)
+    wo_got, wo_rest = gather_first(wo_src, quads), gather_rest(wo_src, quads)
+    out_src = after(out_pair, *wo_got, *wo_rest)
+    out_got, out_rest = gather_first(out_src, quads), gather_rest(out_src, quads)
+    wo_half = gather_last(wo_src, wo_got, wo_rest, quads)
+    wo_rows = jnp.concatenate(whole_columns(wo_half, c), 1)
+    out_full = gather_last(out_src, out_got, out_rest, quads)
+
+    att_all = lax.all_gather(after(attended, *in_rest), "mp", axis=0, tiled=False)
+    middle, normed_m, gates, att_flat = mid_fwd(
+        after(att_all, in_full, *out_got, *out_rest), wo_rows, tok_all, moe_g, pack, small_at, routes[0]
+    )
+
+    cot_own = lax.optimization_barrier(reorder(cotangent[0], q, quads))
+    moe_grad = (RESID * cot_own.astype(F32)).astype(BF16)
+    grad_all = lax.all_gather(after(moe_grad, attended), "mp", axis=0, tiled=True)
+
+    x_own = normed_m
+    x_other = swap(normed_m, "c", 1, 2)
+    gates_other = swap(gates, "c", 1, 2)
     base = (c * half_e).astype(jnp.int32).reshape(1)
-    hidden, gact = moe_fwd(base, x2, in_full, gates2, length)
-
-    moe_grad = (RESID * cot_own.astype(F32)).astype(BF16)
-    grad_all = lax.all_gather(moe_grad, "mp", axis=0, tiled=True)
-    g2 = jnp.concatenate([grad_all, swap(grad_all, "c", 1, 2)], 0)
-    gug, choice2 = moe_bwd(base, g2, out_full, gates2, hidden, length)
-
-    back2 = nt(gug, in_full).astype(BF16)
-    back_other = swap(back2[length:], "c", 1, 2)
-    choice = choice2[:length] + swap(choice2[length:], "c", 1, 2)
+    hid_own, gact_own = moe_fwd(base, x_own, in_full, gates, length)
+    x_other, _ = lax.optimization_barrier((x_other, gact_own))
+    hid_other, gact_other = moe_fwd(base, x_other, in_full, gates_other, length)
+    comb_give = nt(gact_other, out_full).astype(BF16)
+    comb_recv = swap(comb_give, "c", 1, 2)
+    comb_own = nt(after(gact_own, comb_give), out_full)
+    combined = (comb_own + comb_recv.astype(F32)).astype(BF16)
+    moe_branch = lax.psum_scatter(combined, "mp", scatter_dimension=0, tiled=True).astype(F32)
+
+    g_other = swap(grad_all, "c", 1, 2)
+    gug_own, choice_own = moe_bwd(base, grad_all, out_full, gates, after(hid_own, combined), length)
+    gug_other, choice_other = moe_bwd(
+        base, g_other, out_full, gates_other, after(hid_other, gug_own), length
+    )
+    choice = choice_own + swap(choice_other, "c", 1, 2)
+    out_part = tn_pair(grad_all, g_other, *all_after((gact_own, gact_other), gug_other))
+    out_first = scatter_first(out_part, quads)
+    back_give = nt(after(gug_other, out_part), in_full).astype(BF16)
+    back_recv = swap(back_give, "c", 1, 2)
+    back_own = nt(after(gug_own, back_give), in_full).astype(BF16)
     gates_c = gates * choice
     logit_grad = (gates_c - gates * jnp.sum(gates_c, -1, keepdims=True)).astype(BF16)
-    router_all = pack[:, small_at * 128 :]
-    normed_m_grad = (
-        back2[:length].astype(F32) + back_other.astype(F32) + nt(logit_grad, router_all)
+    ag, p_part = back_mid(
+        m.astype(jnp.int32).reshape(1), back_own, back_recv, logit_grad, pack, small_at,
+        after(middle, moe_branch, *out_first[1:]), moe_g, cot_own, wo_rows, mp,
+    )
+    attended_grad = lax.psum_scatter(p_part, "mp", scatter_dimension=0, tiled=False)
+
+    out_sum = scatter_second(all_after(out_first, ag), quads).astype(BF16)
+    in_part = tn_pair(x_own, x_other, *all_after((gug_own, gug_other), ag))
+    att_late = after(att_flat, in_part)
+    half_cols = att_flat.shape[1] // 2
+    wo_mine = tn(ag, jnp.where(c == 0, att_late[:, :half_cols], att_late[:, half_cols:]))
+    wo_give = tn(ag, jnp.where(c == 0, att_late[:, half_cols:], att_late[:, :half_cols]))
+    wo_part = (wo_mine + swap(wo_give.astype(BF16), "c", 1, 2).astype(F32)).astype(BF16)
+    in_first = scatter_first(in_part, quads)
+    layer_out = (
+        lax.dynamic_slice_in_dim(middle, m * (length // mp), length // mp, 0) + RESID * moe_branch
     ).astype(BF16)
-    m_grad = lax.psum_scatter(normed_m_grad, "mp", scatter_dimension=0, tiled=True).astype(F32)
-
-    combined2 = nt(gact, out_full).astype(BF16)
-    comb_other = swap(combined2[length:], "c", 1, 2)
-    combined = (combined2[:length].astype(F32) + comb_other.astype(F32)).astype(BF16)
-    moe_branch = lax.psum_scatter(combined, "mp", scatter_dimension=0, tiled=True).astype(F32)
-
-    own_at = lax.axis_index("mp") * (length // mp)
-    middle_own = lax.dynamic_slice_in_dim(middle, own_at, length // mp, 0)
-    layer_out = (middle_own + RESID * moe_branch).astype(BF16)
-
-    in_part = tn(x2, gug).astype(BF16)
-    out_part = tn(g2, gact).astype(BF16)
-    in_sum = scatter_rows(in_part, quads).astype(BF16)
-    out_sum = scatter_rows(out_part, quads).astype(BF16)
-
-    def own_rows(total):
-        mine = lax.dynamic_slice_in_dim(total, c * rows, rows, 0)
-        give = lax.dynamic_slice_in_dim(total, (1 - c) * rows, rows, 0)
-        other = swap(give, "c", 1, 2)
-        first = c == 0
-        return jnp.concatenate([jnp.where(first, mine, other), jnp.where(first, other, mine)], 1)
-
-    grad_in = own_rows(in_sum).astype(F32)
-    grad_out = own_rows(out_sum).astype(F32)
-
-    inv_m = lax.rsqrt(jnp.mean(middle_own * middle_own, -1, keepdims=True) + EPS)
-    scaled = m_grad * moe_g
-    middle_grad = cot_own.astype(F32) + inv_m * (
-        scaled - middle_own * inv_m * inv_m * jnp.mean(scaled * middle_own, -1, keepdims=True)
-    )
-    attn_grad = (RESID * middle_grad).astype(BF16)
-    ag_all = lax.all_gather(attn_grad, "mp", axis=0, tiled=True)
-
-    wo_own = lax.dynamic_index_in_dim(wo_all, lax.axis_index("mp"), 0, keepdims=False)
-    dq, dkv = attn_bwd(ag_all, wo_own, q_r, k_r, v_r, attended, lse, cosine, sine, doc_col, doc_row)
-    normed_a_grad = nt(dq, pack[:, :q_cols]) + nt(dkv, pack[:, q_cols:qkv_cols])
-    a_grad = lax.psum_scatter(
-        normed_a_grad.astype(BF16), "mp", scatter_dimension=0, tiled=True
-    ).astype(F32)
-    tok_f = tok_own.astype(F32)
-    inv_a = lax.rsqrt(jnp.mean(tok_f * tok_f, -1, keepdims=True) + EPS)
-    scaled = a_grad * attn_g
-    grad_tokens = middle_grad + inv_a * (
-        scaled - tok_f * inv_a * inv_a * jnp.mean(scaled * tok_f, -1, keepdims=True)
-    )
-
-    parts = jnp.concatenate(
-        [
-            tn(normed_a, dq).astype(BF16),
-            tn(normed_a, dkv).astype(BF16),
-            tn(ag_all, attended).astype(BF16),
-            tn(normed_m, logit_grad).astype(BF16),
-        ],
-        1,
-    )
-    cols = parts.shape[1]
-    by_core = parts.reshape(width // (2 * rows), 2, rows, cols)
-    mine = lax.dynamic_index_in_dim(by_core, c, 1, keepdims=False)
-    give = lax.dynamic_index_in_dim(by_core, 1 - c, 1, keepdims=False)
+
+    dq, dkv = attn_bwd(
+        after(attended_grad, out_sum), q_r, k_r, v_r, attended, lse, cosine, sine, doc_col, doc_row
+    )
+    end_part = back_end(dq, dkv, pack, tok_all, attn_g, ag)
+    grad_tokens = lax.psum_scatter(end_part, "mp", scatter_dimension=0, tiled=True).astype(F32)
+
+    in_sum = scatter_second(all_after(in_first, end_part), quads).astype(BF16)
+    wo_sum = scatter_rows(after(wo_part, end_part), quads).astype(BF16)
+
+    dq_late, dkv_late = after(dq, end_part), after(dkv, end_part)
+    part = jnp.concatenate(
+        [tn(normed_a, dq_late), tn(normed_a, dkv_late), tn(normed_m, logit_grad)], 1
+    ).astype(BF16)
+    mine, give = column_halves(part, c)
     pair = (mine.astype(F32) + swap(give, "c", 1, 2).astype(F32)).astype(BF16)
-    sums = scatter_rows(pair.reshape(width // 2, cols), quads)
+    pair_sum = scatter_second(all_after(scatter_first(pair, quads), in_sum), quads).astype(BF16)
+    sums = jnp.concatenate(from_halves(after(pair_sum, wo_sum), rows, c)[:2], 1)
+    sums = sums.astype(F32)
     grad_query = sums[:, :q_cols]
-    grad_kv = sums[:, q_cols:qkv_cols]
-    grad_output = sums[:, qkv_cols : qkv_cols + q_cols]
-    router_part = sums[:, qkv_cols + q_cols : qkv_cols + q_cols + experts]
+    grad_key = sums[:, q_cols : q_cols + kv_cols]
+    grad_value = sums[:, q_cols + kv_cols : qkv_cols]
+    router_part = sums[:, qkv_cols : qkv_cols + experts]
+
+    wo_own_rows = jnp.concatenate(from_halves(wo_sum, rows, c)[:2], 1)
+    grad_output = lax.dynamic_slice_in_dim(wo_own_rows, m * q_cols, q_cols, 1).astype(F32)
+    for k in range(1, mp):
+        send = lax.dynamic_slice_in_dim(wo_own_rows, ((m + k) % mp) * q_cols, q_cols, 1)
+        grad_output = grad_output + lax.ppermute(
+            send, "mp", [(i, (i + k) % mp) for i in range(mp)]
+        ).astype(F32)
+
+    in_0, in_1, in_mine, in_other = from_halves(in_sum, rows, c)
+    out_0, out_1, _, _ = from_halves(out_sum, rows, c)
+    grad_in = jnp.concatenate([in_0, in_1], 1).astype(F32)
+    grad_out = jnp.concatenate([out_0, out_1], 1).astype(F32)
 
     attn_gain_part = (
         jnp.sum(grad_query * w_query.astype(F32), 1)
-        + jnp.sum(grad_kv[:, :kv_cols] * key_weight.astype(F32), 1)
-        + jnp.sum(grad_kv[:, kv_cols:] * value_weight.astype(F32), 1)
+        + jnp.sum(grad_key * key_weight.astype(F32), 1)
+        + jnp.sum(grad_value * value_weight.astype(F32), 1)
     ) / attn_gain.astype(F32)
     moe_gain_part = (
-        jnp.sum(grad_in * w_in.reshape(rows, -1).astype(F32), 1)
+        jnp.sum(in_mine.astype(F32) * in_kept.astype(F32), 1)
+        + jnp.sum(in_other.astype(F32) * in_gave.astype(F32), 1)
         + jnp.sum(router_part * router.astype(F32), 1)
     ) / moe_gain.astype(F32)
     tiny = jnp.concatenate([router_part, attn_gain_part[:, None], moe_gain_part[:, None]], 1)
@@ -645,8 +860,8 @@
         reorder(grad_tokens, q, quads)[None],
         total[:, experts],
         grad_query,
-        grad_kv[:, :kv_cols],
-        grad_kv[:, kv_cols:],
+        grad_key,
+        grad_value,
         grad_output,
         total[:, :experts],
         total[:, experts + 1],

time: 738 us -> 656 us (0.89)
  local copies, waits for them, and re-layouts: 132 us -> 64.5 us
  Pallas kernels: 114 us -> 178 us
  matrix products: 94.4 us -> 62.6 us
  starting transfers between devices: 38.2 us -> 62.8 us
  blocking collectives: 24 us -> 0 us
  other arithmetic: 87.6 us -> 66.1 us
  waiting for transfers between devices: 221 us -> 201 us
    pallas_call x1 -> x5, Pallas kernels: 14.5 us -> 78.2 us  [the longest x2 42.8 us: tn_pair(): pl.pallas_call(tn_pair_kernel, grid=(width // tall, cols // wide), in_spe...]
    reduce_scatter x1, waiting for transfers between devices: 43.2 us -> 0.01 us  [body(): lax.psum_scatter(combined, 'mp', scatter_dimension=0, tiled=True)]
    dot_general x6 -> x5, matrix products: 45 us -> 16 us  [tn(): lax.dot_general(left, right, (((0,), (0,)), ((), ())), preferred_element_...]
    all_gather x1 -> x0, blocking collectives: 24 us -> none  [body(): wo_pieces = lax.all_gather(w_output, 'mp', axis=0, tiled=False)]
    ppermute x41 -> x58, waiting for transfers between devices: 153 us -> 176 us  [swap(): return lax.ppermute(value, axis, [(i, i ^ bit) for i in range(size)])]
    unnamed x170 -> x125, local copies, waits for them, and re-layouts: 53.7 us -> 34.4 us
    all_gather x3, waiting for transfers between devices: 22.4 us -> 6.23 us  [the longest x1 5.49 us: body(): lax.all_gather(after(attended, *in_rest), 'mp', axis=0, tiled=False)]
    concatenate x14 -> x9, local copies, waits for them, and re-layouts: 24.1 us -> 9.72 us  [the longest x2 4.52 us: body(): grad_out = jnp.concatenate([out_0, out_1], 1).astype(F32)]
  transfers between devices with their start and end apart: 51 -> 71, of which waited for: 18 -> 35; matrix products, arithmetic and copies ran while one was open for 36% -> 26% of each run, Pallas kernels for 8% -> 25%
where the time goes in v2:
time: 656 us; the launch traced here: 650 us
  waiting for transfers between devices  201 us (31%)
  Pallas kernels  178 us (27%)
  other arithmetic  66.1 us (10%)
  local copies, waits for them, and re-layouts  64.5 us (10%)
  starting transfers between devices  62.8 us (10%)
  matrix products  62.6 us (10%)
  between operations  15.4 us (2%)
    ppermute x58, waiting for transfers between devices, swap(): return lax.ppermute(value, axis, [(i, i ^ bit) for i in range(size)])  176 us
    dot_general x4, matrix products, nt(): lax.dot_general(left, right, (((1,), (1,)), ((), ())), preferred_element_...  46.7 us
    ppermute x58, starting transfers between devices, swap(): return lax.ppermute(value, axis, [(i, i ^ bit) for i in range(size)])  46 us
    pallas_call x2, Pallas kernels, tn_pair(): pl.pallas_call(tn_pair_kernel, grid=(width // tall, cols // wide), in_spe...  42.8 us
    unnamed x125, local copies, waits for them, and re-layouts  34.4 us
    pallas_call x2, Pallas kernels, moe_fwd(): pl.pallas_call(moe_fwd_kernel, grid_spec=pltpu.PrefetchScalarGridSpec(num...  30 us
    pallas_call x2, Pallas kernels, moe_bwd(): pl.pallas_call(moe_bwd_kernel, grid_spec=pltpu.PrefetchScalarGridSpec(num...  28.3 us
    pallas_call x1, Pallas kernels, attn_fwd(): pl.pallas_call(functools.partial(attn_fwd_kernel, q_heads=q_heads, kv_hea...  20.9 us
  transfers between devices with their start and end apart: 71, of which 35 were waited for; matrix products, arithmetic and copies ran while one was open for 26% of the time, Pallas kernels for 25%

profile of v2, /device:TPU:0, one launch (start us, length us, event | category | flops | bytes accessed | tf_op | source)
XLA Modules:
  0.0 650.3 jit_solution(7601486998961481120)
XLA Ops:
  12.7 3.2 constant_dynamic-slice_fusion.3
  22.4 2.3 collective-permute-start.2
  32.7 1.8 collective-permute-start.5
  47.7 3.1 negate_select_fusion
  52.3 22.4 %collective-permute-done.9 = bf16[192,3072]{1,0:T(8,128)(2,1)S(1)} collective-permute-done((bf16[192,3072]{1,0:T(8,128)(2,1)S(1)}, bf16[192,3072]{1,0:T(8,128)(2,1)S(1)}, u32[]{:S(2)}, u32[]{:S(2)}) %collective-permute-start.9) | collective-permute-done | bytes 1179680 | tf_op jit(solution)/shard_map/ppermute | solution.py:574
  84.0 7.7 %all-gather.7.cloned.1.call-done.tok_ref = bf16[1024,1536]{1,0:T(8,128)(2,1)} async-done(((bf16[256,1536]{1,0:T(8,128)(2,1)}), bf16[1024,1536]{1,0:T(8,128)(2,1)}) %all-gather.7.cloned.1.call-update) | async-done | bytes 3145744 | tf_op jit(solution)/shard_map/all_gather | solution.py:702
  92.9 13.1 %collective-permute-done.11 = bf16[192,3072]{1,0:T(8,128)(2,1)} collective-permute-done((bf16[192,3072]{1,0:T(8,128)(2,1)}, bf16[192,3072]{1,0:T(8,128)(2,1)}, u32[]{:S(2)}, u32[]{:S(2)}) %collective-permute-start.11) | collective-permute-done | bytes 1179680 | tf_op jit(solution)/shard_map/ppermute | solution.py:574
  106.0 2.4 constant_dynamic-update-slice_fusion.12
  108.5 2.4 constant_dynamic-update-slice_fusion.11
  112.0 18.9 %collective-permute-done.13 = bf16[192,3072]{1,0:T(8,128)(2,1)} collective-permute-done((bf16[192,3072]{1,0:T(8,128)(2,1)S(1)}, bf16[192,3072]{1,0:T(8,128)(2,1)}, u32[]{:S(2)}, u32[]{:S(2)}) %collective-permute-start.13) | collective-permute-done | bytes 1179680 | tf_op jit(solution)/shard_map/ppermute | solution.py:574
  130.9 2.4 constant_dynamic-update-slice_fusion.9
  133.3 20.9 %attn_fwd.1 = (bf16[1024,1536]{1,0:T(8,128)(2,1)}, bf16[6,1024,64]{2,1,0:T(8,128)(2,1)}, bf16[2,1024,64]{2,1,0:T(8,128)(2,1)}, bf16[2,1024,64]{2,1,0:T(8,128)(2,...) custom-call(bf16[1024,1536]{1,0:T(8,128)(2,1)} %all-gather.7.cloned.1.call-done.tok_ref, ...), custom_call_target="tpu_custom_call" | custom-call | flops 44291848 | bytes 82575 | tf_op jit(solution)/shard_map/attn_fwd/pallas_call | solution.py:121
  162.9 4.7 collective-permute-done.17
  169.7 4.2 collective-permute-done.19
  174.9 5.1 collective-permute-done.25
  186.6 1.8 copy.56
  188.9 9.9 %collective-permute-done.21 = bf16[192,1536]{1,0:T(8,128)(2,1)S(1)} collective-permute-done((bf16[192,1536]{1,0:T(8,128)(2,1)}, bf16[192,1536]{1,0:T(8,128)(2,1)S(1)}, u32[]{:S(2)}, u32[]{:S(2)}) %collective-permute-start.21) | collective-permute-done | bytes 589856 | tf_op jit(solution)/shard_map/ppermute | solution.py:574
  200.1 11.1 %collective-permute-done.23 = bf16[192,1536]{1,0:T(8,128)(2,1)} collective-permute-done((bf16[192,1536]{1,0:T(8,128)(2,1)}, bf16[192,1536]{1,0:T(8,128)(2,1)}, u32[]{:S(2)}, u32[]{:S(2)}) %collective-permute-start.23) | collective-permute-done | bytes 589856 | tf_op jit(solution)/shard_map/ppermute | solution.py:574
  212.1 5.5 all-gather.11.cloned.1.call-done
  217.6 2.0 broadcast_select_fusion.1
  219.6 2.6 pad_maximum_fusion.wo_ref
  222.1 12.9 %mid_fwd.1 = (f32[1024,1536]{1,0:T(8,128)}, bf16[1024,1536]{1,0:T(8,128)(2,1)}, f32[1024,128]{1,0:T(8,128)}, bf16[1024,1536]{1,0:T(8,128)(2,1)}) custom-call(bf16[4,1024,384]{2,1,0:T(8,128)(2,1)} %bitcast.55, bf16[1536,1536]{1,0:T(8,128)(2,1)} %pad_maximum_fusion.wo_ref, bf16[1024,1536]{1,0:T(8,128)(2,1)} %all-gather.7.cloned.1.call-done.tok_ref, ...), custom_call_target="tpu_custom_call" | custom-call | flops 48318384 | bytes 204472 | tf_op jit(solution)/shard_map/mid_fwd/pallas_call | solution.py:290
  245.5 10.3 %collective-permute-done.30 = bf16[192,1536]{1,0:T(8,128)(2,1)S(1)} collective-permute-done((bf16[192,1536]{1,0:T(8,128)(2,1)S(1)}, bf16[192,1536]{1,0:T(8,128)(2,1)S(1)}, u32[]{:S(2)}, u32[]{:S(2)}) %collective-permute-start.30) | collective-permute-done | bytes 589856 | tf_op jit(solution)/shard_map/ppermute | solution.py:574
  257.0 2.1 copy-done.32
  259.1 15.0 %moe_fwd.2 = (bf16[1024,3072]{1,0:T(8,128)(2,1)}, bf16[1024,1536]{1,0:T(8,128)(2,1)}) custom-call(s32[1]{0:T(128)} %bitcast.9.base_ref, bf16[1024,1536]{1,0:T(8,128)(2,1)} %get-tuple-element.102.x_ref.left_ref, bf16[1536,3072]{1,0:T(8,128)(2,1)} %constant_dynamic-update-slice_fusion.8.w_ref, f32[1024,128]{1,0:T(8,128)} %get-tuple-element.103.gate_ref), custom_call_target="tpu_custom_call" | custom-call | flops 96636768 | bytes 314572 | tf_op jit(solution)/shard_map/moe_fwd/pallas_call | solution.py:447
  275.8 15.0 %moe_fwd.3 = (bf16[1024,3072]{1,0:T(8,128)(2,1)}, bf16[1024,1536]{1,0:T(8,128)(2,1)}) custom-call(s32[1]{0:T(128)} %bitcast.9.base_ref, bf16[1024,1536]{1,0:T(8,128)(2,1)} %copy-done.4, bf16[1536,3072]{1,0:T(8,128)(2,1)} %constant_dynamic-update-slice_fusion.8.w_ref, f32[1024,128]{1,0:T(8,128)} %collective-permute-done.29.gate_ref), custom_call_target="tpu_custom_call" | custom-call | flops 96636768 | bytes 314572 | tf_op jit(solution)/shard_map/moe_fwd/pallas_call | solution.py:447
  290.8 9.4 %convolution_convert_fusion.2 = bf16[1024,1536]{1,0:T(8,128)(2,1)} fusion(bf16[1024,1536]{1,0:T(8,128)(2,1)} %get-tuple-element.116.right2_ref, bf16[1536,1536]{1,0:T(8,128)(2,1)} %copy-done.32), kind=kOutput, calls=%fused_computation.5 | convolution fusion | flops 4833411072 | bytes 11010048 | tf_op jit(solution)/shard_map/dot_general | solution.py:24
  301.6 4.5 collective-permute-done.32
  306.2 9.3 %add_convert_fusion = bf16[1024,1536]{1,0:T(8,128)(2,1)} fusion(bf16[1024,1536]{1,0:T(8,128)(2,1)} %collective-permute-done.32, bf16[1024,1536]{1,0:T(8,128)(2,1)S(1)} %copy-done.12, bf16[1536,1536]{1,0:T(8,128)(2,1)} %copy-done.32), kind=kOutput, calls=%fused_computation | convolution fusion | flops 4836556800 | bytes 14155776 | tf_op jit(solution)/shard_map/dot_general | solution.py:24
  315.4 10.5 %reduce-scatter.6.cloned.1.call-start = ((), (), s32[]{:S(2)}) async-start(), calls=%async_computation.6 | async-start | bytes 3932160 | tf_op jit(solution)/shard_map/reduce_scatter | solution.py:793
  325.9 14.2 %moe_bwd.2 = (bf16[1024,3072]{1,0:T(8,128)(2,1)}, f32[1024,128]{1,0:T(8,128)}) custom-call(s32[1]{0:T(128)} %bitcast.9.base_ref, bf16[1024,1536]{1,0:T(8,128)(2,1)} %all-gather.9.cloned.1.call-done.g_ref.left_ref, bf16[1536,1536]{1,0:T(8,128)(2,1)} %copy-done.32, f32[1024,128]{1,0:T(8,128)} %get-tuple-element.103.gate_ref, ...), custom_call_target="tpu_custom_call" | custom-call | flops 4831838208 | bytes 25165824 | tf_op jit(solution)/shard_map/moe_bwd/pallas_call | solution.py:509
  340.1 14.2 %moe_bwd.3 = (bf16[1024,3072]{1,0:T(8,128)(2,1)}, f32[1024,128]{1,0:T(8,128)}) custom-call(s32[1]{0:T(128)} %bitcast.9.base_ref, bf16[1024,1536]{1,0:T(8,128)(2,1)} %collective-permute-done.33.g_ref.left2_ref, bf16[1536,1536]{1,0:T(8,128)(2,1)} %copy-done.32, f32[1024,128]{1,0:T(8,128)} %collective-permute-done.29.gate_ref, ...), custom_call_target="tpu_custom_call" | custom-call | flops 4831838208 | bytes 25165824 | tf_op jit(solution)/shard_map/moe_bwd/pallas_call | solution.py:509
  354.3 15.5 %weight_grad.2 = bf16[1536,1536]{1,0:T(8,128)(2,1)} custom-call(bf16[1024,1536]{1,0:T(8,128)(2,1)} %all-gather.9.cloned.1.call-done.g_ref.left_ref, bf16[1024,1536]{1,0:T(8,128)(2,1)} %collective-permute-done.33.g_ref.left2_ref, bf16[1024,1536]{1,0:T(8,128)(2,1)} %get-tuple-element.115.right_ref, bf16[1024,1536]{1,0:T(8,128)(2,1)} %get-tuple-element.116.right2_ref), custom_call_target="tpu_custom_call" | custom-call | flops 96636768 | bytes 188743 | tf_op jit(solution)/shard_map/weight_grad/pallas_call | solution.py:549
  369.8 14.3 %convolution_convert_fusion.1 = bf16[1024,1536]{1,0:T(8,128)(2,1)S(1)} fusion(bf16[1024,3072]{1,0:T(8,128)(2,1)} %get-tuple-element.143.right2_ref, bf16[1536,3072]{1,0:T(8,128)(2,1)} %constant_dynamic-update-slice_fusion.8.w_ref), kind=kOutput, calls=%fused_computation.4 | convolution fusion | flops 9665249280 | bytes 18874368 | tf_op jit(solution)/shard_map/dot_general | solution.py:24
  387.7 13.7 %convolution_convert_fusion.back_ref = bf16[1024,1536]{1,0:T(8,128)(2,1)} fusion(bf16[1024,3072]{1,0:T(8,128)(2,1)S(1)} %bitcast.54, bf16[1536,3072]{1,0:T(8,128)(2,1)} %constant_dynamic-update-slice_fusion.8.w_ref), kind=kOutput, calls=%fused_computation.3 | convolution fusion | flops 9665249280 | bytes 18874368 | tf_op jit(solution)/shard_map/dot_general | solution.py:24
  402.6 11.1 %collective-permute-done.36 = bf16[384,1536]{1,0:T(8,128)(2,1)S(1)} collective-permute-done((bf16[384,1536]{1,0:T(8,128)(2,1)S(1)}, bf16[384,1536]{1,0:T(8,128)(2,1)S(1)}, u32[]{:S(2)}, u32[]{:S(2)}) %collective-permute-start.36) | collective-permute-done | bytes 1179680 | tf_op jit(solution)/shard_map/ppermute | solution.py:574
  416.0 13.4 %back_mid.1 = (bf16[1024,1536]{1,0:T(8,128)(2,1)}, bf16[4,1024,384]{2,1,0:T(8,128)(2,1)}) custom-call(s32[1]{0:T(128)} %bitcast.11.own_ref, bf16[1024,1536]{1,0:T(8,128)(2,1)} %convolution_convert_fusion.back_ref, bf16[1024,1536]{1,0:T(8,128)(2,1)} %collective-permute-done.34.recv_ref, bf16[1024,128]{1,0:T(8,128)(2,1)} %subtract_convert_fusion.lg_ref, ...), custom_call_target="tpu_custom_call" | custom-call | flops 4831838208 | bytes 23592960 | tf_op jit(solution)/shard_map/back_mid/pallas_call | solution.py:352
  429.5 1.8 copy-done
  431.3 1.8 convolution_convert_fusion.6
  433.2 27.2 %weight_grad.3 = bf16[1536,3072]{1,0:T(8,128)(2,1)} custom-call(bf16[1024,1536]{1,0:T(8,128)(2,1)} %get-tuple-element.102.x_ref.left_ref, bf16[1024,1536]{1,0:T(8,128)(2,1)} %copy-done.4, bf16[1024,3072]{1,0:T(8,128)(2,1)} %get-tuple-element.142.right_ref, bf16[1024,3072]{1,0:T(8,128)(2,1)} %get-tuple-element.143.right2_ref), custom_call_target="tpu_custom_call" | custom-call | flops 193273536 | bytes 314572 | tf_op jit(solution)/shard_map/weight_grad/pallas_call | solution.py:549
  460.5 6.0 convolution_convert_fusion.3
  470.4 13.5 %collective-permute-done.39 = bf16[192,1536]{1,0:T(8,128)(2,1)S(1)} collective-permute-done((bf16[192,1536]{1,0:T(8,128)(2,1)S(1)}, bf16[192,1536]{1,0:T(8,128)(2,1)S(1)}, u32[]{:S(2)}, u32[]{:S(2)}) %collective-permute-start.39) | collective-permute-done | bytes 589856 | tf_op jit(solution)/shard_map/ppermute | solution.py:574
  493.7 2.2 concatenate.158
  496.0 2.3 concatenate.157
  498.3 3.3 maximum_convert_fusion.1
  501.6 5.3 add_convert_fusion.1
  506.8 1.8 add_convert_fusion.7
  509.7 20.5 %attn_bwd.1 = (bf16[1024,384]{1,0:T(8,128)(2,1)}, bf16[1024,256]{1,0:T(8,128)(2,1)}) custom-call(bf16[1024,384]{1,0:T(8,128)(2,1)} %bitcast.70, bf16[6,1024,64]{2,1,0:T(8,128)(2,1)} %get-tuple-element.133.q_ref, bf16[2,1024,64]{2,1,0:T(8,128)(2,1)} %get-tuple-element.134.k_ref, bf16[2,1024,64]{2,1,0:T(8,128)(2,1)} %get-tuple-element.135.v_ref, ...), custom_call_target="tpu_custom_call" | custom-call | flops 6039797760 | bytes 3145728 | tf_op jit(solution)/shard_map/attn_bwd/pallas_call | solution.py:224
  530.2 9.1 %back_end.1 = bf16[1024,1536]{1,0:T(8,128)(2,1)} custom-call(bf16[1024,384]{1,0:T(8,128)(2,1)} %get-tuple-element.140.dq_ref, bf16[1024,256]{1,0:T(8,128)(2,1)} %get-tuple-element.141.dkv_ref, bf16[1536,768]{1,0:T(8,128)(2,1)} %pad_maximum_fusion.2.w_ref.small_ref, bf16[1024,1536]{1,0:T(8,128)(2,1)} %all-gather.7.cloned.1.call-done.tok_ref, ...), custom_call_target="tpu_custom_call" | custom-call | flops 2013265920 | bytes 11403264 | tf_op jit(solution)/shard_map/back_end/pallas_call | solution.py:400
  544.7 1.8 broadcast_select_fusion.6
  546.6 9.7 %collective-permute-done.50 = bf16[384,768]{1,0:T(8,128)(2,1)S(1)} collective-permute-done((bf16[384,768]{1,0:T(8,128)(2,1)S(1)}, bf16[384,768]{1,0:T(8,128)(2,1)S(1)}, u32[]{:S(2)}, u32[]{:S(2)}) %collective-permute-start.50) | collective-permute-done | bytes 589856 | tf_op jit(solution)/shard_map/ppermute | solution.py:574
  559.2 2.5 add_convert_fusion.4
  564.0 3.3 collective-permute-done.53
  571.9 20.7 %collective-permute-done.46 = bf16[192,3072]{1,0:T(8,128)(2,1)S(1)} collective-permute-done((bf16[192,3072]{1,0:T(8,128)(2,1)S(1)}, bf16[192,3072]{1,0:T(8,128)(2,1)S(1)}, u32[]{:S(2)}, u32[]{:S(2)}) %collective-permute-start.46) | collective-permute-done | bytes 1179680 | tf_op jit(solution)/shard_map/ppermute | solution.py:574
  593.4 2.8 add_convert_fusion.2
  596.3 1.8 fusion.9
  598.8 1.9 collective-permute-start.48
  602.6 1.9 collective-permute-done.47
  605.2 2.5 collective-permute-done.62
  607.7 8.3 %collective-permute-done.61 = bf16[192,384]{1,0:T(8,128)(2,1)S(1)} collective-permute-done((bf16[192,384]{1,0:T(8,128)(2,1)S(1)}, bf16[192,384]{1,0:T(8,128)(2,1)S(1)}, u32[]{:S(2)}, u32[]{:S(2)}) %collective-permute-start.61) | collective-permute-done | bytes 147488 | tf_op jit(solution)/shard_map/ppermute | solution.py:834
  624.1 2.1 broadcast_select_fusion.3
  627.7 2.2 collective-permute-start.57
  629.9 2.0 collective-permute-start.56
  633.8 4.6 maximum_convert_fusion
  (341 shorter events, 139.0 us)
Async XLA Ops:
  7.2 84.5 %all-gather.7.cloned.1.call-start = ((), (), s32[]{:S(2)}) async-start(), calls=%async_computation.3 | async-start | bytes 3932160 | tf_op jit(solution)/shard_map/all_gather | solution.py:702
  11.3 7.7 %collective-permute-start = (bf16[192,384]{1,0:T(8,128)(2,1)}, bf16[192,384]{1,0:T(8,128)(2,1)}, u32[]{:S(2)}, u32[]{:S(2)}) collective-permute-start(bf16[192,384]{1,0:T(8,128)(2,1)} %broadcast_select_fusion.49), channel_id=1, source_target_pairs={{0,4},{4,0},{1,5},{5,1},{2,6},{6,2},{3,7},{7,3},{8,12},{12,8},{9,1... | collective-permute-start | bytes 442376 | tf_op jit(solution)/shard_map/ppermute | solution.py:574
  17.6 25.2 %collective-permute-start.8 = (bf16[192,3072]{1,0:T(8,128)(2,1)}, bf16[192,3072]{1,0:T(8,128)(2,1)S(1)}, u32[]{:S(2)}, u32[]{:S(2)}) collective-permute-start(bf16[192,3072]{1,0:T(8,128)(2,1)} %reshape.78), channel_id=1, source_target_pairs={{0,4},{4,0},{1,5},{5,1},{2,6},{6,2},{3,7},{7,3},{8,12},{12,8},{9,1... | collective-permute-start | bytes 3538952 | tf_op jit(solution)/shard_map/ppermute | solution.py:574
  22.4 15.2 %collective-permute-start.2 = (bf16[192,384]{1,0:T(8,128)(2,1)}, bf16[192,384]{1,0:T(8,128)(2,1)}, u32[]{:S(2)}, u32[]{:S(2)}) collective-permute-start(bf16[192,384]{1,0:T(8,128)(2,1)} %get-tuple-element.208), channel_id=1, source_target_pairs={{0,8},{8,0},{16,24},{24,16},{1,9},{9,1},{17,25},{25,17},{2,10},{10... | collective-permute-start | bytes 442376 | tf_op jit(solution)/shard_map/ppermute | solution.py:574
  24.7 11.4 %collective-permute-start.4 = (bf16[192,384]{1,0:T(8,128)(2,1)}, bf16[192,384]{1,0:T(8,128)(2,1)}, u32[]{:S(2)}, u32[]{:S(2)}) collective-permute-start(bf16[192,384]{1,0:T(8,128)(2,1)} %get-tuple-element.208), channel_id=1, source_target_pairs={{0,16},{8,24},{16,0},{24,8},{1,17},{9,25},{17,1},{25,9},{2,18},{10... | collective-permute-start | bytes 442376 | tf_op jit(solution)/shard_map/ppermute | solution.py:574
  26.3 6.5 collective-permute-start.1
  27.8 126.8 %all-gather.13.cloned.1.call-start = ((), (), s32[]{:S(2)}) async-start(), calls=%async_computation.9 | async-start | bytes 1474560 | tf_op jit(solution)/shard_map/all_gather | solution.py:742
  31.6 7.6 %collective-permute-start.3 = (bf16[192,384]{1,0:T(8,128)(2,1)}, bf16[192,384]{1,0:T(8,128)(2,1)S(1)}, u32[]{:S(2)}, u32[]{:S(2)}) collective-permute-start(bf16[192,384]{1,0:T(8,128)(2,1)} %get-tuple-element.210), channel_id=1, source_target_pairs={{0,16},{8,24},{16,0},{24,8},{1,17},{9,25},{17,1},{25,9},{2,18},{10... | collective-permute-start | bytes 442376 | tf_op jit(solution)/shard_map/ppermute | solution.py:574
  32.7 8.7 %collective-permute-start.5 = (bf16[192,384]{1,0:T(8,128)(2,1)}, bf16[192,384]{1,0:T(8,128)(2,1)S(1)}, u32[]{:S(2)}, u32[]{:S(2)}) collective-permute-start(bf16[192,384]{1,0:T(8,128)(2,1)} %collective-permute-done.1), channel_id=1, source_target_pairs={{0,16},{8,24},{16,0},{24,8},{1,17},{9,25},{17,1},{25,9},{2,18},{10... | collective-permute-start | bytes 442376 | tf_op jit(solution)/shard_map/ppermute | solution.py:574
  42.8 8.0 %collective-permute-start.7 = (bf16[1536,384]{1,0:T(8,128)(2,1)}, bf16[1536,384]{1,0:T(8,128)(2,1)S(1)}, u32[]{:S(2)}, u32[]{:S(2)}) collective-permute-start(bf16[1536,384]{1,0:T(8,128)(2,1)} %constant_dynamic-update-slice_fusion), channel_id=1, source_target_pairs={{0,4},{4,0},{1,5},{5,1},{2,6},{6,2},{3,7},{7,3},{8,12},{12,8},{9,1... | collective-permute-start | bytes 3538952 | tf_op jit(solution)/shard_map/ppermute | solution.py:574
  46.2 28.4 %collective-permute-start.9 = (bf16[192,3072]{1,0:T(8,128)(2,1)S(1)}, bf16[192,3072]{1,0:T(8,128)(2,1)S(1)}, u32[]{:S(2)}, u32[]{:S(2)}) collective-permute-start(bf16[192,3072]{1,0:T(8,128)(2,1)S(1)} %get-tuple-element.240), channel_id=1, source_target_pairs={{0,8},{8,0},{16,24},{24,16},{1,9},{9,1},{17,25},{25,17},{2,10},{10... | collective-permute-start | bytes 3538952 | tf_op jit(solution)/shard_map/ppermute | solution.py:574
  47.2 28.1 %collective-permute-start.10 = (bf16[192,3072]{1,0:T(8,128)(2,1)S(1)}, bf16[192,3072]{1,0:T(8,128)(2,1)S(1)}, u32[]{:S(2)}, u32[]{:S(2)}) collective-permute-start(bf16[192,3072]{1,0:T(8,128)(2,1)S(1)} %get-tuple-element.239), channel_id=1, source_target_pairs={{0,16},{8,24},{16,0},{24,8},{1,17},{9,25},{17,1},{25,9},{2,18},{10... | collective-permute-start | bytes 3538952 | tf_op jit(solution)/shard_map/ppermute | solution.py:574
  76.8 29.2 %collective-permute-start.11 = (bf16[192,3072]{1,0:T(8,128)(2,1)}, bf16[192,3072]{1,0:T(8,128)(2,1)}, u32[]{:S(2)}, u32[]{:S(2)}) collective-permute-start(bf16[192,3072]{1,0:T(8,128)(2,1)} %get-tuple-element.238), channel_id=1, source_target_pairs={{0,8},{8,0},{16,24},{24,16},{1,9},{9,1},{17,25},{25,17},{2,10},{10... | collective-permute-start | bytes 3538952 | tf_op jit(solution)/shard_map/ppermute | solution.py:574
  78.2 30.3 %collective-permute-start.12 = (bf16[192,3072]{1,0:T(8,128)(2,1)}, bf16[192,3072]{1,0:T(8,128)(2,1)}, u32[]{:S(2)}, u32[]{:S(2)}) collective-permute-start(bf16[192,3072]{1,0:T(8,128)(2,1)} %get-tuple-element.237), channel_id=1, source_target_pairs={{0,16},{8,24},{16,0},{24,8},{1,17},{9,25},{17,1},{25,9},{2,18},{10... | collective-permute-start | bytes 3538952 | tf_op jit(solution)/shard_map/ppermute | solution.py:574
  81.6 49.3 %collective-permute-start.13 = (bf16[192,3072]{1,0:T(8,128)(2,1)S(1)}, bf16[192,3072]{1,0:T(8,128)(2,1)}, u32[]{:S(2)}, u32[]{:S(2)}) collective-permute-start(bf16[192,3072]{1,0:T(8,128)(2,1)S(1)} %collective-permute-done.9), channel_id=1, source_target_pairs={{0,16},{8,24},{16,0},{24,8},{1,17},{9,25},{17,1},{25,9},{2,18},{10... | collective-permute-start | bytes 3538952 | tf_op jit(solution)/shard_map/ppermute | solution.py:574
  83.2 72.8 %collective-permute-start.14 = (bf16[192,3072]{1,0:T(8,128)(2,1)S(1)}, bf16[192,3072]{1,0:T(8,128)(2,1)S(1)}, u32[]{:S(2)}, u32[]{:S(2)}) collective-permute-start(bf16[192,3072]{1,0:T(8,128)(2,1)S(1)} %collective-permute-done.10), channel_id=1, source_target_pairs={{0,8},{8,0},{16,24},{24,16},{1,9},{9,1},{17,25},{25,17},{2,10},{10... | collective-permute-start | bytes 3538952 | tf_op jit(solution)/shard_map/ppermute | solution.py:574
  91.7 125.8 %all-gather.11.cloned.1.call-start = ((), (), s32[]{:S(2)}) async-start(), calls=%async_computation.8 | async-start | bytes 3932160 | tf_op jit(solution)/shard_map/all_gather | solution.py:754
  154.3 146.6 %all-gather.9.cloned.1.call-start = ((), (), s32[]{:S(2)}) async-start(), calls=%async_computation.5 | async-start | bytes 3932160 | tf_op jit(solution)/shard_map/all_gather | solution.py:761
  157.7 9.9 %collective-permute-start.17 = (bf16[192,768]{1,0:T(8,128)(2,1)S(1)}, bf16[192,768]{1,0:T(8,128)(2,1)S(1)}, u32[]{:S(2)}, u32[]{:S(2)}) collective-permute-start(bf16[192,768]{1,0:T(8,128)(2,1)S(1)} %get-tuple-element.289), channel_id=1, source_target_pairs={{0,8},{8,0},{16,24},{24,16},{1,9},{9,1},{17,25},{25,17},{2,10},{10... | collective-permute-start | bytes 884744 | tf_op jit(solution)/shard_map/ppermute | solution.py:574
  158.6 9.9 %collective-permute-start.18 = (bf16[192,768]{1,0:T(8,128)(2,1)S(1)}, bf16[192,768]{1,0:T(8,128)(2,1)S(1)}, u32[]{:S(2)}, u32[]{:S(2)}) collective-permute-start(bf16[192,768]{1,0:T(8,128)(2,1)S(1)} %get-tuple-element.288), channel_id=1, source_target_pairs={{0,16},{8,24},{16,0},{24,8},{1,17},{9,25},{17,1},{25,9},{2,18},{10... | collective-permute-start | bytes 884744 | tf_op jit(solution)/shard_map/ppermute | solution.py:574
  159.1 14.8 %collective-permute-start.19 = (bf16[192,768]{1,0:T(8,128)(2,1)S(1)}, bf16[192,768]{1,0:T(8,128)(2,1)S(1)}, u32[]{:S(2)}, u32[]{:S(2)}) collective-permute-start(bf16[192,768]{1,0:T(8,128)(2,1)S(1)} %get-tuple-element.288), channel_id=1, source_target_pairs={{0,8},{8,0},{16,24},{24,16},{1,9},{9,1},{17,25},{25,17},{2,10},{10... | collective-permute-start | bytes 884744 | tf_op jit(solution)/shard_map/ppermute | solution.py:574
  161.2 18.9 %collective-permute-start.15 = (bf16[192,1536]{1,0:T(8,128)(2,1)S(1)}, bf16[192,1536]{1,0:T(8,128)(2,1)S(1)}, u32[]{:S(2)}, u32[]{:S(2)}) collective-permute-start(bf16[192,1536]{1,0:T(8,128)(2,1)S(1)} %bitcast.61), channel_id=1, source_target_pairs={{0,4},{4,0},{1,5},{5,1},{2,6},{6,2},{3,7},{7,3},{8,12},{12,8},{9,1... | collective-permute-start | bytes 1769480 | tf_op jit(solution)/shard_map/ppermute | solution.py:574
  161.3 13.5 %collective-permute-start.20 = (bf16[192,768]{1,0:T(8,128)(2,1)S(1)}, bf16[192,768]{1,0:T(8,128)(2,1)S(1)}, u32[]{:S(2)}, u32[]{:S(2)}) collective-permute-start(bf16[192,768]{1,0:T(8,128)(2,1)S(1)} %get-tuple-element.289), channel_id=1, source_target_pairs={{0,16},{8,24},{16,0},{24,8},{1,17},{9,25},{17,1},{25,9},{2,18},{10... | collective-permute-start | bytes 884744 | tf_op jit(solution)/shard_map/ppermute | solution.py:574
  167.6 12.4 %collective-permute-start.25 = (bf16[192,768]{1,0:T(8,128)(2,1)S(1)}, bf16[192,768]{1,0:T(8,128)(2,1)S(1)}, u32[]{:S(2)}, u32[]{:S(2)}) collective-permute-start(bf16[192,768]{1,0:T(8,128)(2,1)S(1)} %collective-permute-done.17), channel_id=1, source_target_pairs={{0,16},{8,24},{16,0},{24,8},{1,17},{9,25},{17,1},{25,9},{2,18},{10... | collective-permute-start | bytes 884744 | tf_op jit(solution)/shard_map/ppermute | solution.py:574
  168.5 11.5 %collective-permute-start.26 = (bf16[192,768]{1,0:T(8,128)(2,1)S(1)}, bf16[192,768]{1,0:T(8,128)(2,1)S(1)}, u32[]{:S(2)}, u32[]{:S(2)}) collective-permute-start(bf16[192,768]{1,0:T(8,128)(2,1)S(1)} %collective-permute-done.18), channel_id=1, source_target_pairs={{0,8},{8,0},{16,24},{24,16},{1,9},{9,1},{17,25},{25,17},{2,10},{10... | collective-permute-start | bytes 884744 | tf_op jit(solution)/shard_map/ppermute | solution.py:574
  180.1 37.5 %collective-permute-start.27 = (bf16[1536,768]{1,0:T(8,128)(2,1)S(1)}, bf16[1536,768]{1,0:T(8,128)(2,1)}, u32[]{:S(2)}, u32[]{:S(2)}) collective-permute-start(bf16[1536,768]{1,0:T(8,128)(2,1)S(1)} %constant_dynamic-update-slice_fusion.16), channel_id=1, source_target_pairs={{0,4},{4,0},{1,5},{5,1},{2,6},{6,2},{3,7},{7,3},{8,12},{12,8},{9,1... | collective-permute-start | bytes 7077896 | tf_op jit(solution)/shard_map/ppermute | solution.py:574
  182.5 16.3 %collective-permute-start.21 = (bf16[192,1536]{1,0:T(8,128)(2,1)}, bf16[192,1536]{1,0:T(8,128)(2,1)S(1)}, u32[]{:S(2)}, u32[]{:S(2)}) collective-permute-start(bf16[192,1536]{1,0:T(8,128)(2,1)} %get-tuple-element.262), channel_id=1, source_target_pairs={{0,8},{8,0},{16,24},{24,16},{1,9},{9,1},{17,25},{25,17},{2,10},{10... | collective-permute-start | bytes 1769480 | tf_op jit(solution)/shard_map/ppermute | solution.py:574
  183.7 16.4 %collective-permute-start.22 = (bf16[192,1536]{1,0:T(8,128)(2,1)}, bf16[192,1536]{1,0:T(8,128)(2,1)S(1)}, u32[]{:S(2)}, u32[]{:S(2)}) collective-permute-start(bf16[192,1536]{1,0:T(8,128)(2,1)} %get-tuple-element.261), channel_id=1, source_target_pairs={{0,16},{8,24},{16,0},{24,8},{1,17},{9,25},{17,1},{25,9},{2,18},{10... | collective-permute-start | bytes 1769480 | tf_op jit(solution)/shard_map/ppermute | solution.py:574
  184.2 27.0 %collective-permute-start.23 = (bf16[192,1536]{1,0:T(8,128)(2,1)}, bf16[192,1536]{1,0:T(8,128)(2,1)}, u32[]{:S(2)}, u32[]{:S(2)}) collective-permute-start(bf16[192,1536]{1,0:T(8,128)(2,1)} %get-tuple-element.261), channel_id=1, source_target_pairs={{0,8},{8,0},{16,24},{24,16},{1,9},{9,1},{17,25},{25,17},{2,10},{10... | collective-permute-start | bytes 1769480 | tf_op jit(solution)/shard_map/ppermute | solution.py:574
  185.0 27.0 %collective-permute-start.24 = (bf16[192,1536]{1,0:T(8,128)(2,1)}, bf16[192,1536]{1,0:T(8,128)(2,1)}, u32[]{:S(2)}, u32[]{:S(2)}) collective-permute-start(bf16[192,1536]{1,0:T(8,128)(2,1)} %get-tuple-element.262), channel_id=1, source_target_pairs={{0,16},{8,24},{16,0},{24,8},{1,17},{9,25},{17,1},{25,9},{2,18},{10... | collective-permute-start | bytes 1769480 | tf_op jit(solution)/shard_map/ppermute | solution.py:574
  235.0 39.1 %collective-permute-start.28 = (bf16[1024,1536]{1,0:T(8,128)(2,1)}, bf16[1024,1536]{1,0:T(8,128)(2,1)S(1)}, u32[]{:S(2)}, u32[]{:S(2)}) collective-permute-start(bf16[1024,1536]{1,0:T(8,128)(2,1)} %get-tuple-element.102.x_ref.left_ref), channel_id=1, source_target_pairs={{0,4},{4,0},{1,5},{5,1},{2,6},{6,2},{3,7},{7,3},{8,12},{12,8},{9,1... | collective-permute-start | bytes 9437192 | tf_op jit(solution)/shard_map/ppermute | solution.py:574
  238.4 268.4 %reduce-scatter.4.cloned.1.call-start = ((), (), s32[]{:S(2)}) async-start(), calls=%async_computation.4 | async-start | bytes 3932160 | tf_op jit(solution)/shard_map/reduce_scatter | solution.py:774
  240.0 15.8 %collective-permute-start.30 = (bf16[192,1536]{1,0:T(8,128)(2,1)S(1)}, bf16[192,1536]{1,0:T(8,128)(2,1)S(1)}, u32[]{:S(2)}, u32[]{:S(2)}) collective-permute-start(bf16[192,1536]{1,0:T(8,128)(2,1)S(1)} %copy-done.29), channel_id=1, source_target_pairs={{0,16},{8,24},{16,0},{24,8},{1,17},{9,25},{17,1},{25,9},{2,18},{10... | collective-permute-start | bytes 1769480 | tf_op jit(solution)/shard_map/ppermute | solution.py:574
  241.5 15.4 %collective-permute-start.31 = (bf16[192,1536]{1,0:T(8,128)(2,1)S(1)}, bf16[192,1536]{1,0:T(8,128)(2,1)S(1)}, u32[]{:S(2)}, u32[]{:S(2)}) collective-permute-start(bf16[192,1536]{1,0:T(8,128)(2,1)S(1)} %copy-done.27), channel_id=1, source_target_pairs={{0,8},{8,0},{16,24},{24,16},{1,9},{9,1},{17,25},{25,17},{2,10},{10... | collective-permute-start | bytes 1769480 | tf_op jit(solution)/shard_map/ppermute | solution.py:574
  245.3 28.8 %collective-permute-start.29 = (f32[1024,128]{1,0:T(8,128)S(1)}, f32[1024,128]{1,0:T(8,128)}, u32[]{:S(2)}, u32[]{:S(2)}) collective-permute-start(f32[1024,128]{1,0:T(8,128)S(1)} %copy-done.7), channel_id=1, source_target_pairs={{0,4},{4,0},{1,5},{5,1},{2,6},{6,2},{3,7},{7,3},{8,12},{12,8},{9,1... | collective-permute-start | bytes 1572872 | tf_op jit(solution)/shard_map/ppermute | solution.py:574
  300.9 39.2 %collective-permute-start.33 = (bf16[1024,1536]{1,0:T(8,128)(2,1)}, bf16[1024,1536]{1,0:T(8,128)(2,1)}, u32[]{:S(2)}, u32[]{:S(2)}) collective-permute-start(bf16[1024,1536]{1,0:T(8,128)(2,1)} %all-gather.9.cloned.1.call-done.g_ref.left_ref), channel_id=1, source_target_pairs={{0,4},{4,0},{1,5},{5,1},{2,6},{6,2},{3,7},{7,3},{8,12},{12,8},{9,1... | collective-permute-start | bytes 9437192 | tf_op jit(solution)/shard_map/ppermute | solution.py:574
  315.4 194.3 %reduce-scatter.6.cloned.1.call-start = ((), (), s32[]{:S(2)}) async-start(), calls=%async_computation.6 | async-start | bytes 3932160 | tf_op jit(solution)/shard_map/reduce_scatter | solution.py:793
  384.1 30.9 %collective-permute-start.34 = (bf16[1024,1536]{1,0:T(8,128)(2,1)S(1)}, bf16[1024,1536]{1,0:T(8,128)(2,1)}, u32[]{:S(2)}, u32[]{:S(2)}) collective-permute-start(bf16[1024,1536]{1,0:T(8,128)(2,1)S(1)} %convolution_convert_fusion.1), channel_id=1, source_target_pairs={{0,4},{4,0},{1,5},{5,1},{2,6},{6,2},{3,7},{7,3},{8,12},{12,8},{9,1... | collective-permute-start | bytes 9437192 | tf_op jit(solution)/shard_map/ppermute | solution.py:574
  385.1 16.3 %collective-permute-start.35 = (f32[1024,128]{1,0:T(8,128)S(1)}, f32[1024,128]{1,0:T(8,128)S(1)}, u32[]{:S(2)}, u32[]{:S(2)}) collective-permute-start(f32[1024,128]{1,0:T(8,128)S(1)} %copy-done.41), channel_id=1, source_target_pairs={{0,4},{4,0},{1,5},{5,1},{2,6},{6,2},{3,7},{7,3},{8,12},{12,8},{9,1... | collective-permute-start | bytes 1572872 | tf_op jit(solution)/shard_map/ppermute | solution.py:574
  385.4 28.2 %collective-permute-start.36 = (bf16[384,1536]{1,0:T(8,128)(2,1)S(1)}, bf16[384,1536]{1,0:T(8,128)(2,1)S(1)}, u32[]{:S(2)}, u32[]{:S(2)}) collective-permute-start(bf16[384,1536]{1,0:T(8,128)(2,1)S(1)} %pad_maximum_fusion.8), channel_id=1, source_target_pairs={{0,8},{8,0},{16,24},{24,16},{1,9},{9,1},{17,25},{25,17},{2,10},{10... | collective-permute-start | bytes 3538952 | tf_op jit(solution)/shard_map/ppermute | solution.py:574
  387.1 28.0 %collective-permute-start.37 = (bf16[384,1536]{1,0:T(8,128)(2,1)S(1)}, bf16[384,1536]{1,0:T(8,128)(2,1)S(1)}, u32[]{:S(2)}, u32[]{:S(2)}) collective-permute-start(bf16[384,1536]{1,0:T(8,128)(2,1)S(1)} %pad_maximum_fusion.9), channel_id=1, source_target_pairs={{0,16},{8,24},{16,0},{24,8},{1,17},{9,25},{17,1},{25,9},{2,18},{10... | collective-permute-start | bytes 3538952 | tf_op jit(solution)/shard_map/ppermute | solution.py:574
  429.5 211.0 %reduce-scatter.8.cloned.1.call-start = ((), (), s32[]{:S(2)}) async-start(), calls=%async_computation.7 | async-start | bytes 3932160 | tf_op jit(solution)/shard_map/reduce_scatter | solution.py:811
  466.5 35.1 %collective-permute-start.49 = (bf16[1536,768]{1,0:T(8,128)(2,1)}, bf16[1536,768]{1,0:T(8,128)(2,1)}, u32[]{:S(2)}, u32[]{:S(2)}) collective-permute-start(bf16[1536,768]{1,0:T(8,128)(2,1)} %convolution_convert_fusion.3), channel_id=1, source_target_pairs={{0,4},{4,0},{1,5},{5,1},{2,6},{6,2},{3,7},{7,3},{8,12},{12,8},{9,1... | collective-permute-start | bytes 7077896 | tf_op jit(solution)/shard_map/ppermute | solution.py:574
  468.1 15.8 %collective-permute-start.39 = (bf16[192,1536]{1,0:T(8,128)(2,1)S(1)}, bf16[192,1536]{1,0:T(8,128)(2,1)S(1)}, u32[]{:S(2)}, u32[]{:S(2)}) collective-permute-start(bf16[192,1536]{1,0:T(8,128)(2,1)S(1)} %get-tuple-element.128), channel_id=1, source_target_pairs={{0,8},{8,0},{16,24},{24,16},{1,9},{9,1},{17,25},{25,17},{2,10},{10... | collective-permute-start | bytes 1769480 | tf_op jit(solution)/shard_map/ppermute | solution.py:574
  469.2 15.5 %collective-permute-start.38 = (bf16[192,1536]{1,0:T(8,128)(2,1)S(1)}, bf16[192,1536]{1,0:T(8,128)(2,1)S(1)}, u32[]{:S(2)}, u32[]{:S(2)}) collective-permute-start(bf16[192,1536]{1,0:T(8,128)(2,1)S(1)} %get-tuple-element.127), channel_id=1, source_target_pairs={{0,16},{8,24},{16,0},{24,8},{1,17},{9,25},{17,1},{25,9},{2,18},{10... | collective-permute-start | bytes 1769480 | tf_op jit(solution)/shard_map/ppermute | solution.py:574
  488.5 58.1 %collective-permute-start.43 = (bf16[384,3072]{1,0:T(8,128)(2,1)}, bf16[384,3072]{1,0:T(8,128)(2,1)}, u32[]{:S(2)}, u32[]{:S(2)}) collective-permute-start(bf16[384,3072]{1,0:T(8,128)(2,1)} %pad_maximum_fusion.4), channel_id=1, source_target_pairs={{0,8},{8,0},{16,24},{24,16},{1,9},{9,1},{17,25},{25,17},{2,10},{10... | collective-permute-start | bytes 7077896 | tf_op jit(solution)/shard_map/ppermute | solution.py:574
  490.9 55.7 %collective-permute-start.44 = (bf16[384,3072]{1,0:T(8,128)(2,1)}, bf16[384,3072]{1,0:T(8,128)(2,1)}, u32[]{:S(2)}, u32[]{:S(2)}) collective-permute-start(bf16[384,3072]{1,0:T(8,128)(2,1)} %pad_maximum_fusion.5), channel_id=1, source_target_pairs={{0,16},{8,24},{16,0},{24,8},{1,17},{9,25},{17,1},{25,9},{2,18},{10... | collective-permute-start | bytes 7077896 | tf_op jit(solution)/shard_map/ppermute | solution.py:574
  541.0 15.2 %collective-permute-start.50 = (bf16[384,768]{1,0:T(8,128)(2,1)S(1)}, bf16[384,768]{1,0:T(8,128)(2,1)S(1)}, u32[]{:S(2)}, u32[]{:S(2)}) collective-permute-start(bf16[384,768]{1,0:T(8,128)(2,1)S(1)} %pad_maximum_fusion.16), channel_id=1, source_target_pairs={{0,8},{8,0},{16,24},{24,16},{1,9},{9,1},{17,25},{25,17},{2,10},{10... | collective-permute-start | bytes 1769480 | tf_op jit(solution)/shard_map/ppermute | solution.py:574
  541.8 15.3 %collective-permute-start.51 = (bf16[384,768]{1,0:T(8,128)(2,1)S(1)}, bf16[384,768]{1,0:T(8,128)(2,1)S(1)}, u32[]{:S(2)}, u32[]{:S(2)}) collective-permute-start(bf16[384,768]{1,0:T(8,128)(2,1)S(1)} %pad_maximum_fusion.17), channel_id=1, source_target_pairs={{0,16},{8,24},{16,0},{24,8},{1,17},{9,25},{17,1},{25,9},{2,18},{10... | collective-permute-start | bytes 1769480 | tf_op jit(solution)/shard_map/ppermute | solution.py:574
  546.5 22.3 %collective-permute-start.40 = (bf16[1536,384]{1,0:T(8,128)(2,1)S(1)}, bf16[1536,384]{1,0:T(8,128)(2,1)S(1)}, u32[]{:S(2)}, u32[]{:S(2)}) collective-permute-start(bf16[1536,384]{1,0:T(8,128)(2,1)S(1)} %get-tuple-element.298), channel_id=1, source_target_pairs={{0,4},{4,0},{1,5},{5,1},{2,6},{6,2},{3,7},{7,3},{8,12},{12,8},{9,1... | collective-permute-start | bytes 3538952 | tf_op jit(solution)/shard_map/ppermute | solution.py:574
  557.3 10.0 %collective-permute-start.53 = (bf16[192,768]{1,0:T(8,128)(2,1)S(1)}, bf16[192,768]{1,0:T(8,128)(2,1)S(1)}, u32[]{:S(2)}, u32[]{:S(2)}) collective-permute-start(bf16[192,768]{1,0:T(8,128)(2,1)S(1)} %get-tuple-element.164), channel_id=1, source_target_pairs={{0,8},{8,0},{16,24},{24,16},{1,9},{9,1},{17,25},{25,17},{2,10},{10... | collective-permute-start | bytes 884744 | tf_op jit(solution)/shard_map/ppermute | solution.py:574
  558.5 9.7 %collective-permute-start.52 = (bf16[192,768]{1,0:T(8,128)(2,1)S(1)}, bf16[192,768]{1,0:T(8,128)(2,1)S(1)}, u32[]{:S(2)}, u32[]{:S(2)}) collective-permute-start(bf16[192,768]{1,0:T(8,128)(2,1)S(1)} %get-tuple-element.163), channel_id=1, source_target_pairs={{0,16},{8,24},{16,0},{24,8},{1,17},{9,25},{17,1},{25,9},{2,18},{10... | collective-permute-start | bytes 884744 | tf_op jit(solution)/shard_map/ppermute | solution.py:574
  561.7 30.9 %collective-permute-start.46 = (bf16[192,3072]{1,0:T(8,128)(2,1)S(1)}, bf16[192,3072]{1,0:T(8,128)(2,1)S(1)}, u32[]{:S(2)}, u32[]{:S(2)}) collective-permute-start(bf16[192,3072]{1,0:T(8,128)(2,1)S(1)} %get-tuple-element.148), channel_id=1, source_target_pairs={{0,8},{8,0},{16,24},{24,16},{1,9},{9,1},{17,25},{25,17},{2,10},{10... | collective-permute-start | bytes 3538952 | tf_op jit(solution)/shard_map/ppermute | solution.py:574
  563.1 30.3 %collective-permute-start.45 = (bf16[192,3072]{1,0:T(8,128)(2,1)S(1)}, bf16[192,3072]{1,0:T(8,128)(2,1)S(1)}, u32[]{:S(2)}, u32[]{:S(2)}) collective-permute-start(bf16[192,3072]{1,0:T(8,128)(2,1)S(1)} %get-tuple-element.147), channel_id=1, source_target_pairs={{0,16},{8,24},{16,0},{24,8},{1,17},{9,25},{17,1},{25,9},{2,18},{10... | collective-permute-start | bytes 3538952 | tf_op jit(solution)/shard_map/ppermute | solution.py:574
  568.7 32.0 %collective-permute-start.59 = (bf16[192,768]{1,0:T(8,128)(2,1)S(1)}, bf16[192,768]{1,0:T(8,128)(2,1)S(1)}, u32[]{:S(2)}, u32[]{:S(2)}) collective-permute-start(bf16[192,768]{1,0:T(8,128)(2,1)S(1)} %fusion.13), channel_id=1, source_target_pairs={{0,4},{4,0},{1,5},{5,1},{2,6},{6,2},{3,7},{7,3},{8,12},{12,8},{9,1... | collective-permute-start | bytes 884744 | tf_op jit(solution)/shard_map/ppermute | solution.py:574
  569.4 28.8 %collective-permute-start.41 = (bf16[384,384]{1,0:T(8,128)(2,1)S(1)}, bf16[384,384]{1,0:T(8,128)(2,1)S(1)}, u32[]{:S(2)}, u32[]{:S(2)}) collective-permute-start(bf16[384,384]{1,0:T(8,128)(2,1)S(1)} %pad_maximum_fusion.18), channel_id=1, source_target_pairs={{0,8},{8,0},{16,24},{24,16},{1,9},{9,1},{17,25},{25,17},{2,10},{10... | collective-permute-start | bytes 884744 | tf_op jit(solution)/shard_map/ppermute | solution.py:574
  570.6 27.5 %collective-permute-start.42 = (bf16[384,384]{1,0:T(8,128)(2,1)S(1)}, bf16[384,384]{1,0:T(8,128)(2,1)S(1)}, u32[]{:S(2)}, u32[]{:S(2)}) collective-permute-start(bf16[384,384]{1,0:T(8,128)(2,1)S(1)} %pad_maximum_fusion.19), channel_id=1, source_target_pairs={{0,16},{8,24},{16,0},{24,8},{1,17},{9,25},{17,1},{25,9},{2,18},{10... | collective-permute-start | bytes 884744 | tf_op jit(solution)/shard_map/ppermute | solution.py:574
  598.1 25.9 %collective-permute-start.55 = (bf16[192,3072]{1,0:T(8,128)(2,1)}, bf16[192,3072]{1,0:T(8,128)(2,1)S(1)}, u32[]{:S(2)}, u32[]{:S(2)}) collective-permute-start(bf16[192,3072]{1,0:T(8,128)(2,1)} %fusion.9), channel_id=1, source_target_pairs={{0,4},{4,0},{1,5},{5,1},{2,6},{6,2},{3,7},{7,3},{8,12},{12,8},{9,1... | collective-permute-start | bytes 3538952 | tf_op jit(solution)/shard_map/ppermute | solution.py:574
  602.1 13.8 %collective-permute-start.61 = (bf16[192,384]{1,0:T(8,128)(2,1)S(1)}, bf16[192,384]{1,0:T(8,128)(2,1)S(1)}, u32[]{:S(2)}, u32[]{:S(2)}) collective-permute-start(bf16[192,384]{1,0:T(8,128)(2,1)S(1)} %get-tuple-element.286), channel_id=1, source_target_pairs={{0,2},{1,3},{2,0},{3,1},{4,6},{5,7},{6,4},{7,5},{8,10},{9,11},{10,... | collective-permute-start | bytes 442376 | tf_op jit(solution)/shard_map/ppermute | solution.py:834
  604.5 11.4 %collective-permute-start.60 = (bf16[192,384]{1,0:T(8,128)(2,1)S(1)}, bf16[192,384]{1,0:T(8,128)(2,1)S(1)}, u32[]{:S(2)}, u32[]{:S(2)}) collective-permute-start(bf16[192,384]{1,0:T(8,128)(2,1)S(1)} %get-tuple-element.285), channel_id=1, source_target_pairs={{0,1},{1,2},{2,3},{3,0},{4,5},{5,6},{6,7},{7,4},{8,9},{9,10},{10,1... | collective-permute-start | bytes 442376 | tf_op jit(solution)/shard_map/ppermute | solution.py:834
  605.1 11.7 %collective-permute-start.54 = (bf16[192,384]{1,0:T(8,128)(2,1)S(1)}, bf16[192,384]{1,0:T(8,128)(2,1)S(1)}, u32[]{:S(2)}, u32[]{:S(2)}) collective-permute-start(bf16[192,384]{1,0:T(8,128)(2,1)S(1)} %constant_dynamic-slice_fusion), channel_id=1, source_target_pairs={{0,4},{4,0},{1,5},{5,1},{2,6},{6,2},{3,7},{7,3},{8,12},{12,8},{9,1... | collective-permute-start | bytes 442376 | tf_op jit(solution)/shard_map/ppermute | solution.py:574
  627.6 10.9 %collective-permute-start.58 = (f32[192,26]{0,1:T(8,128)}, f32[192,26]{0,1:T(8,128)}, u32[]{:S(2)}, u32[]{:S(2)}) collective-permute-start(f32[192,26]{0,1:T(8,128)} %pad_maximum_fusion.21), channel_id=1, source_target_pairs={{0,3},{1,0},{2,1},{3,2},{4,7},{5,4},{6,5},{7,6},{8,11},{9,8},{10,9... | collective-permute-start | bytes 59912 | tf_op jit(solution)/shard_map/ppermute | solution.py:856
  627.7 10.7 %collective-permute-start.57 = (f32[192,26]{0,1:T(8,128)}, f32[192,26]{0,1:T(8,128)}, u32[]{:S(2)}, u32[]{:S(2)}) collective-permute-start(f32[192,26]{0,1:T(8,128)} %pad_maximum_fusion.21), channel_id=1, source_target_pairs={{0,2},{1,3},{2,0},{3,1},{4,6},{5,7},{6,4},{7,5},{8,10},{9,11},{10,... | collective-permute-start | bytes 59912 | tf_op jit(solution)/shard_map/ppermute | solution.py:856
  629.9 8.6 %collective-permute-start.56 = (f32[192,26]{0,1:T(8,128)}, f32[192,26]{0,1:T(8,128)}, u32[]{:S(2)}, u32[]{:S(2)}) collective-permute-start(f32[192,26]{0,1:T(8,128)} %pad_maximum_fusion.21), channel_id=1, source_target_pairs={{0,1},{1,2},{2,3},{3,0},{4,5},{5,6},{6,7},{7,4},{8,9},{9,10},{10,1... | collective-permute-start | bytes 59912 | tf_op jit(solution)/shard_map/ppermute | solution.py:856
  (57 other events, 434.2 us)
Sparse Core Ops, SparseCore 0:
  27.9 63.7 all-gather.6
  93.9 29.0 all-gather.12
  154.4 63.1 all-gather.10
  238.5 62.2 all-gather.8
  315.6 57.9 reduce-scatter.3
  429.6 57.4 reduce-scatter.5
  539.4 58.3 reduce-scatter.7

commit v3 on v2

--- a/solution.py
+++ b/solution.py
@@ -317,7 +317,6 @@
             flops=2 * length * width * cols * parts,
             transcendentals=length * 128,
             bytes_accessed=10 * length * width + 2 * width * cols * parts,
-            scale=100,
         ),
         name="mid_fwd",
     )(att_all, wo_rows, tokens, gain, pack, routes)
@@ -441,7 +440,7 @@
         gact_ref[:, 128 * k : 128 * k + 128] = (cols[k] * act).astype(BF16)
 
 
-def moe_fwd(base, x, w_in, gates, rows):
+def moe_fwd(base, x, w_in, gates, rows, scale):
     length, width = x.shape
     cols = w_in.shape[1]
     return pl.pallas_call(
@@ -470,16 +469,55 @@
             flops=2 * length * width * cols,
             transcendentals=length * cols // 2,
             bytes_accessed=2 * length * (width + cols + cols // 2) + 4 * width * cols,
-            scale=100,
+            scale=scale,
         ),
         name="moe_fwd",
     )(base, x, w_in, gates)
 
 
-def moe_bwd_kernel(base_ref, g_ref, w_ref, gate_ref, h_ref, gug_ref, choice_ref):
+def combine_kernel(*refs):
+    gact_ref, pieces, out_ref, w_scr = refs[0], refs[1:-2], refs[-2], refs[-1]
+
+    @pl.when(pl.program_id(0) == 0)
+    def _():
+        at = 0
+        for piece in pieces:
+            w_scr[at : at + piece.shape[0], :] = piece[...]
+            at += piece.shape[0]
+
+    out_ref[...] = nt(gact_ref[...], w_scr[...]).astype(BF16)
+
+
+def combine(gact, pieces, rows):
+    length, cols = gact.shape
+    width = sum(p.shape[0] for p in pieces)
+    return pl.pallas_call(
+        combine_kernel,
+        grid=(length // rows,),
+        in_specs=[pl.BlockSpec((rows, cols), lambda i: (i, 0))]
+        + [pl.BlockSpec(p.shape, lambda i: (0, 0)) for p in pieces],
+        out_specs=pl.BlockSpec((rows, width), lambda i: (i, 0)),
+        out_shape=jax.ShapeDtypeStruct((length, width), BF16),
+        scratch_shapes=[pltpu.VMEM((width, cols), BF16)],
+        compiler_params=pltpu.CompilerParams(
+            dimension_semantics=("arbitrary",), vmem_limit_bytes=VMEM_CAP
+        ),
+        cost_estimate=cost(
+            flops=2 * length * width * cols,
+            transcendentals=0,
+            bytes_accessed=2 * (length * width + length * cols + width * cols),
+        ),
+        name="combine",
+    )(gact, *pieces)
+
+
+def moe_bwd_kernel(*refs):
+    base_ref, g_ref, gate_ref, h_ref = refs[:4]
+    pieces, gug_ref, choice_ref = refs[4:-2], refs[-2], refs[-1]
     p = pl.program_id(1)
     first = base_ref[0] + 2 * p
-    plain = nn(g_ref[...], w_ref[...])
+    weights = [piece[...] for piece in pieces]
+    plain = nn(g_ref[...], weights[0] if len(weights) == 1 else jnp.concatenate(weights, 0))
     cols = gate_cols(gate_ref[...], first)
 
     @pl.when(p == 0)
@@ -503,7 +541,7 @@
     choice_ref[...] += add
 
 
-def moe_bwd(base, g, w_out, gates, h, rows):
+def moe_bwd(base, g, pieces, gates, h, rows):
     length, width = g.shape
     cols = h.shape[1]
     return pl.pallas_call(
@@ -513,10 +551,10 @@
             grid=(length // rows, cols // 512),
             in_specs=[
                 pl.BlockSpec((rows, width), lambda i, p, b: (i, 0)),
-                pl.BlockSpec((width, 256), lambda i, p, b: (0, p)),
                 pl.BlockSpec((rows, 128), lambda i, p, b: (i, 0)),
                 pl.BlockSpec((rows, 512), lambda i, p, b: (i, p)),
-            ],
+            ]
+            + [pl.BlockSpec((w.shape[0], 256), lambda i, p, b: (0, p)) for w in pieces],
             out_specs=[
                 pl.BlockSpec((rows, 512), lambda i, p, b: (i, p)),
                 pl.BlockSpec((rows, 128), lambda i, p, b: (i, 0)),
@@ -535,39 +573,63 @@
             bytes_accessed=2 * length * (width + 2 * cols) + 2 * width * cols,
         ),
         name="moe_bwd",
-    )(base, g, w_out, gates, h)
-
-
-def tn_pair_kernel(left_ref, left2_ref, right_ref, right2_ref, out_ref):
-    out_ref[...] = (tn(left_ref[...], right_ref[...]) + tn(left2_ref[...], right2_ref[...])).astype(BF16)
-
-
-def tn_pair(left, left2, right, right2):
+    )(base, g, gates, h, *pieces)
+
+
+def segment_kernel(*refs, count):
+    lefts, rights, outs = refs[:4], refs[4:6], refs[6:]
+    first = tn(jnp.concatenate([lefts[0][...], lefts[1][...]], 1), rights[0][...])
+    second = tn(jnp.concatenate([lefts[2][...], lefts[3][...]], 1), rights[1][...])
+    value = (first + second).astype(BF16)
+    for k in range(count):
+
+        @pl.when(pl.program_id(0) == k)
+        def _(k=k):
+            outs[k][...] = value
+
+
+def pick(s, values):
+    out = values[0]
+    for k in range(1, len(values)):
+        out = jnp.where(s == k, values[k], out)
+    return out
+
+
+def weight_grad(left, left2, right, right2, segments):
     length, width = left.shape
-    cols = right.shape[1]
-    tall, wide = width // 2, 512
+    cols = right.shape[1] // 2
+    quarter = width // 4
+    wide = min(cols, 768)
+    steps = cols // wide
+    count = len(segments)
+    firsts, seconds, halves = zip(*segments, strict=True)
+    one = pl.BlockSpec((length, quarter), lambda s, j: (0, pick(s, firsts)))
+    two = pl.BlockSpec((length, quarter), lambda s, j: (0, pick(s, seconds)))
+    side = pl.BlockSpec((length, wide), lambda s, j: (0, pick(s, halves) * steps + j))
+
+    def place(k):
+        return pl.BlockSpec(
+            (2 * quarter, wide),
+            lambda s, j: (0, jnp.where(s == k, j, jnp.where(s < k, 0, steps - 1))),
+        )
+
     return pl.pallas_call(
-        tn_pair_kernel,
-        grid=(width // tall, cols // wide),
-        in_specs=[
-            pl.BlockSpec((length, tall), lambda i, j: (0, i)),
-            pl.BlockSpec((length, tall), lambda i, j: (0, i)),
-            pl.BlockSpec((length, wide), lambda i, j: (0, j)),
-            pl.BlockSpec((length, wide), lambda i, j: (0, j)),
-        ],
-        out_specs=pl.BlockSpec((tall, wide), lambda i, j: (i, j)),
-        out_shape=jax.ShapeDtypeStruct((width, cols), BF16),
+        functools.partial(segment_kernel, count=count),
+        grid=(count, steps),
+        in_specs=[one, two, one, two, side, side],
+        out_specs=[place(k) for k in range(count)],
+        out_shape=[jax.ShapeDtypeStruct((2 * quarter, cols), BF16)] * count,
         compiler_params=pltpu.CompilerParams(
             dimension_semantics=("arbitrary", "arbitrary"), vmem_limit_bytes=VMEM_CAP
         ),
         cost_estimate=cost(
-            flops=4 * length * width * cols,
+            flops=2 * count * length * width * cols,
             transcendentals=0,
             bytes_accessed=4 * length * (width + 2 * cols),
             scale=100,
         ),
         name="weight_grad",
-    )(left, left2, right, right2)
+    )(left, left, left2, left2, right, right2)
 
 
 def swap(value, axis, bit, size):
@@ -578,71 +640,96 @@
     if quads != 4:
         return value
     n = value.shape[-1] // 4
-    b = [value[..., k * n : (k + 1) * n] for k in range(4)]
+    b = [value[..., k * n : (k + 1) * n] for k in (0, 1, 3, 2)]
+    odd = (q & 1) == 1
+    far = (q & 2) == 2
+    c = [jnp.where(odd, b[k], b[j]) for j, k in ((0, 1), (1, 0), (2, 3), (3, 2))]
+    return jnp.concatenate([jnp.where(far, c[k], c[j]) for j, k in ((0, 3), (1, 2), (2, 1), (3, 0))], -1)
+
+
+def restore(value, q, quads):
+    if quads != 4:
+        return value
+    n = value.shape[-1] // 4
+    b = [value[..., k * n : (k + 1) * n] for k in (0, 1, 3, 2)]
     odd = (q & 1) == 1
     far = (q & 2) == 2
     c = [jnp.where(odd, b[k ^ 1], b[k]) for k in range(4)]
     return jnp.concatenate([jnp.where(far, c[k ^ 2], c[k]) for k in range(4)], -1)
 
 
-def gather_first(value, quads):
+def gather_first(low, high, quads):
     if quads != 4:
-        return (lax.all_gather(value, "q", axis=0, tiled=True),)
-    half = value.shape[0] // 2
-    return swap(value[:half], "q", 1, 4), swap(value[half:], "q", 2, 4)
-
-
-def gather_rest(value, quads):
+        return (lax.all_gather(jnp.concatenate([low, high], 0), "q", axis=0, tiled=True),)
+    return swap(low, "q", 1, 4), swap(high, "q", 2, 4)
+
+
+def gather_rest(low, high, quads):
     if quads != 4:
         return ()
-    half = value.shape[0] // 2
-    return swap(value[half:], "q", 1, 4), swap(value[:half], "q", 2, 4)
-
-
-def gather_last(value, first, rest, quads):
+    return swap(high, "q", 1, 4), swap(low, "q", 2, 4)
+
+
+def gather_diagonal(first, quads):
+    if quads != 4:
+        return ()
+    return swap(first[0], "q", 2, 4), swap(first[1], "q", 1, 4)
+
+
+def gather_join(low, high, first, rest, diagonal, quads):
     if quads != 4:
         return first[0]
-    diag_a = swap(first[0], "q", 2, 4)
-    diag_b = swap(first[1], "q", 1, 4)
-    return jnp.concatenate([value, first[0], rest[0], rest[1], first[1], diag_a, diag_b], 0)
-
-
-def gather_rows(value, quads):
-    return gather_last(value, gather_first(value, quads), gather_rest(value, quads), quads)
-
-
-def scatter_first(value, quads):
+    return jnp.concatenate(
+        [low, high, first[0], rest[0], diagonal[0], diagonal[1], rest[1], first[1]], 0
+    )
+
+
+def gather_pieces(low, high, first, rest, diagonal, quads):
     if quads != 4:
-        return (value,)
-    n = value.shape[0] // 8
-    part = [value[k * n : (k + 1) * n] for k in range(8)]
-    from_x = swap(jnp.concatenate([part[2], part[6]], 0), "q", 1, 4)
-    from_y = swap(jnp.concatenate([part[5], part[7]], 0), "q", 2, 4)
-    return value, from_x, from_y
-
-
-def scatter_second(first, quads):
-    if quads != 4:
-        return lax.psum_scatter(first[0], "q", scatter_dimension=0, tiled=True).astype(F32)
-    value, from_x, from_y = first
-    n = value.shape[0] // 8
-    give_y = (value[4 * n : 5 * n].astype(F32) + from_x[n:].astype(F32)).astype(BF16)
-    give_x = (value[3 * n : 4 * n].astype(F32) + from_y[n:].astype(F32)).astype(BF16)
+        return first
+    return (low, high, first[0], rest[0], diagonal[0], diagonal[1], rest[1], first[1])
+
+
+def gather_rows(low, high, quads):
+    first = gather_first(low, high, quads)
+    rest = gather_rest(low, high, quads)
+    return gather_join(low, high, first, rest, gather_diagonal(first, quads), quads)
+
+
+SEND_LEFT, SEND_RIGHT, KEEP_LEFT, KEEP_RIGHT = (2, 3, 0), (2, 1, 1), (0, 1, 0), (0, 3, 1)
+
+
+def cut(value, segment):
+    n, half = value.shape[0] // 4, (value.shape[1] // 2 + 127) // 128 * 128
+    side = value[:, half:] if segment[2] else value[:, :half]
+    return jnp.concatenate([side[k * n : (k + 1) * n] for k in segment[:2]], 0)
+
+
+def scatter_first(left, right):
+    return swap(left, "q", 2, 4), swap(right, "q", 1, 4)
+
+
+def scatter_second(keep_left, keep_right, from_y, from_x, tie=None):
+    n = keep_left.shape[0] // 2
+    give_x = (keep_left[n:].astype(F32) + from_y[:n].astype(F32)).astype(BF16)
+    give_y = (keep_right[n:].astype(F32) + from_x[:n].astype(F32)).astype(BF16)
     give_x, give_y = lax.optimization_barrier((give_x, give_y))
-    low = swap(give_y, "q", 2, 4)
-    high = swap(give_x, "q", 1, 4)
-    value, from_x, from_y = all_after((value, from_x, from_y), low, high)
-    return jnp.concatenate(
-        [
-            value[:n].astype(F32) + from_x[:n].astype(F32) + low.astype(F32),
-            value[n : 2 * n].astype(F32) + from_y[:n].astype(F32) + high.astype(F32),
-        ],
-        0,
-    )
-
-
-def scatter_rows(value, quads):
-    return scatter_second(scatter_first(value, quads), quads)
+    left = swap(give_x, "q", 1, 4)
+    right = swap(give_y, "q", 2, 4)
+    others = () if tie is None else tie(left, right)
+    keep_left, keep_right, from_y, from_x, left, right = all_after(
+        (keep_left, keep_right, from_y, from_x, left, right), *others
+    )
+    return (
+        (keep_left[:n].astype(F32) + from_y[n:].astype(F32) + left.astype(F32)).astype(BF16),
+        (keep_right[:n].astype(F32) + from_x[n:].astype(F32) + right.astype(F32)).astype(BF16),
+    )
+
+
+def scatter_plain(value):
+    total = lax.psum_scatter(value, "q", scatter_dimension=0, tiled=True)
+    half = total.shape[1] // 2
+    return total[:, :half], total[:, half:]
 
 
 def after(value, *others):
@@ -656,15 +743,18 @@
 def to_halves(mine, give, c):
     other = swap(give, "c", 1, 2)
     first = c == 0
-    return jnp.concatenate([jnp.where(first, mine, other), jnp.where(first, other, mine)], 0)
-
-
-def from_halves(total, rows, c):
-    mine = lax.dynamic_slice_in_dim(total, c * rows, rows, 0)
-    give = lax.dynamic_slice_in_dim(total, (1 - c) * rows, rows, 0)
-    other = swap(give, "c", 1, 2)
-    first = c == 0
-    return jnp.where(first, mine, other), jnp.where(first, other, mine), mine, other
+    return jnp.where(first, mine, other), jnp.where(first, other, mine)
+
+
+def from_halves(totals, rows, c):
+    def take(at):
+        return jnp.concatenate([lax.dynamic_slice_in_dim(t, at * rows, rows, 0) for t in totals], 1)
+
+    return take(c), swap(take(1 - c), "c", 1, 2)
+
+
+def in_order(mine, other, c):
+    return jnp.where(c == 0, mine, other), jnp.where(c == 0, other, mine)
 
 
 def column_halves(value, c):
@@ -701,13 +791,23 @@
     tok_own = reorder(tokens[0], q, quads)
     tok_all = lax.all_gather(tok_own, "mp", axis=0, tiled=True)
 
+    def half_rows(value):
+        mine = lax.dynamic_slice_in_dim(value, c * half_e, half_e, 1).reshape(rows, -1)
+        give = lax.dynamic_slice_in_dim(value, (1 - c) * half_e, half_e, 1).reshape(rows, -1)
+        return to_halves(mine, give, c), mine, give
+
+    in_pair, in_kept, in_gave = half_rows(w_in)
+
     pad = jnp.zeros((rows, 128 - experts - 2), BF16)
     pack = jnp.concatenate(
         [w_query, key_weight, value_weight, router, attn_gain[:, None], moe_gain[:, None], pad], 1
     )
-    pack_pair = to_halves(*column_halves(pack, c), c)
-    pack_first = gather_first(pack_pair, quads)
-    pack_half = gather_last(pack_pair, pack_first, gather_rest(pack_pair, quads), quads)
+    pack_pair = to_halves(*column_halves(after(pack, in_gave, in_kept), c), c)
+    pack_first = gather_first(*pack_pair, quads)
+    pack_rest = gather_rest(*pack_pair, quads)
+    pack_half = gather_join(
+        *pack_pair, pack_first, pack_rest, gather_diagonal(pack_first, quads), quads
+    )
     pack = jnp.concatenate(whole_columns(pack_half, c), 1)
     small_at = qkv_cols // 128
     gains = pack[:, qkv_cols + experts : qkv_cols + experts + 2].astype(F32)
@@ -723,37 +823,40 @@
     upper = (jnp.arange(128, dtype=jnp.int32) % HEAD) < (HEAD // 2)
     sine = jnp.where(upper[None, :], -jnp.sin(angles), jnp.sin(angles))
 
-    def half_rows(value):
-        mine = lax.dynamic_slice_in_dim(value, c * half_e, half_e, 1).reshape(rows, -1)
-        give = lax.dynamic_slice_in_dim(value, (1 - c) * half_e, half_e, 1).reshape(rows, -1)
-        return to_halves(mine, give, c), mine, give
-
-    in_pair, in_kept, in_gave = half_rows(after(w_in, pack_pair))
-    out_pair, _, _ = half_rows(after(w_out, in_pair))
-    in_src = after(in_pair, *pack_first)
-    in_got = gather_first(in_src, quads)
-    in_rest = gather_rest(after(in_src, *in_got), quads)
+    out_pair, _, _ = half_rows(after(w_out, *pack_pair))
+    in_src = in_pair
+    in_got = gather_first(*in_src, quads)
+    in_rest = gather_rest(*in_src, quads)
 
     normed_a, q_r, k_r, v_r, attended, lse = attn_fwd(
-        tok_all, attn_g, after(pack, *in_got), cosine, sine, doc_col, doc_row, q_heads, kv_heads
+        tok_all, attn_g, pack, cosine, sine, doc_col, doc_row, q_heads, kv_heads
     )
 
     wo_pad = jnp.concatenate([w_output, jnp.zeros((rows, 5 * 64), BF16)], 1)
-    wo_cols = lax.all_gather(after(wo_pad, tok_all, pack), "mp", axis=0, tiled=False)
+    wo_cols = lax.all_gather(after(wo_pad, pack), "mp", axis=0, tiled=False)
     wo_cols = jnp.concatenate([wo_cols[j, :, :q_cols] for j in range(mp)], 1)
     wo_pair = to_halves(*column_halves(after(wo_cols, attended), c), c)
-    in_full = gather_last(in_pair, in_got, in_rest, quads)
-    wo_src = after(wo_pair, in_full)
-    wo_got, wo_rest = gather_first(wo_src, quads), gather_rest(wo_src, quads)
-    out_src = after(out_pair, *wo_got, *wo_rest)
-    out_got, out_rest = gather_first(out_src, quads), gather_rest(out_src, quads)
-    wo_half = gather_last(wo_src, wo_got, wo_rest, quads)
-    wo_rows = jnp.concatenate(whole_columns(wo_half, c), 1)
-    out_full = gather_last(out_src, out_got, out_rest, quads)
-
-    att_all = lax.all_gather(after(attended, *in_rest), "mp", axis=0, tiled=False)
+    in_diag = gather_diagonal(in_got, quads)
+    wo_src = all_after(wo_pair, *in_diag)
+    wo_got, wo_rest = gather_first(*wo_src, quads), gather_rest(*wo_src, quads)
+    out_src = all_after(out_pair, *wo_got, *wo_rest)
+    out_got, out_rest = gather_first(*out_src, quads), gather_rest(*out_src, quads)
+    wo_half = gather_join(*wo_src, wo_got, wo_rest, gather_diagonal(wo_got, quads), quads)
+    step = width // 4
+    wo_other = jnp.concatenate(
+        [swap(wo_half[k * step : (k + 1) * step], "c", 1, 2) for k in range(4)], 0
+    )
+    wo_rows = jnp.concatenate(in_order(*lax.optimization_barrier((wo_half, wo_other)), c), 1)
+    join = (*in_src, *in_got, *in_rest, *in_diag)
+    join = all_after(join, *wo_got)
+    in_full = gather_join(
+        *join[:2], join[2 : 2 + len(in_got)], join[2 + len(in_got) : 2 + len(in_got) + len(in_rest)],
+        join[2 + len(in_got) + len(in_rest) :], quads,
+    )
+
+    att_all = lax.all_gather(after(attended, *in_got, *in_rest, *out_pair), "mp", axis=0, tiled=False)
     middle, normed_m, gates, att_flat = mid_fwd(
-        after(att_all, in_full, *out_got, *out_rest), wo_rows, tok_all, moe_g, pack, small_at, routes[0]
+        after(att_all, in_full, *out_got), wo_rows, tok_all, moe_g, pack, small_at, routes[0]
     )
 
     cot_own = lax.optimization_barrier(reorder(cotangent[0], q, quads))
@@ -764,54 +867,88 @@
     x_other = swap(normed_m, "c", 1, 2)
     gates_other = swap(gates, "c", 1, 2)
     base = (c * half_e).astype(jnp.int32).reshape(1)
-    hid_own, gact_own = moe_fwd(base, x_own, in_full, gates, length)
-    x_other, _ = lax.optimization_barrier((x_other, gact_own))
-    hid_other, gact_other = moe_fwd(base, x_other, in_full, gates_other, length)
-    comb_give = nt(gact_other, out_full).astype(BF16)
+    hid_own, gact_own = moe_fwd(
+        base, x_own, in_full, gates, length, 100
+    )
+    x_other = after(x_other, gact_own, *out_rest)
+    out_diag = all_after(gather_diagonal(out_got, quads), gact_own)
+    out_full = gather_pieces(*out_src, out_got, out_rest, out_diag, quads)
+    hid_other, gact_other = moe_fwd(base, x_other, in_full, gates_other, length, 1)
+    comb_give = combine(gact_other, out_full, length // 2)
     comb_recv = swap(comb_give, "c", 1, 2)
-    comb_own = nt(after(gact_own, comb_give), out_full)
-    combined = (comb_own + comb_recv.astype(F32)).astype(BF16)
+    comb_own = combine(after(gact_own, comb_give, grad_all), out_full, length // 2)
+    combined = (comb_own.astype(F32) + comb_recv.astype(F32)).astype(BF16)
     moe_branch = lax.psum_scatter(combined, "mp", scatter_dimension=0, tiled=True).astype(F32)
 
-    g_other = swap(grad_all, "c", 1, 2)
-    gug_own, choice_own = moe_bwd(base, grad_all, out_full, gates, after(hid_own, combined), length)
-    gug_other, choice_other = moe_bwd(
-        base, g_other, out_full, gates_other, after(hid_other, gug_own), length
-    )
+    g_other = swap(after(grad_all, comb_give), "c", 1, 2)
+    gacts = all_after((gact_own, gact_other), comb_own)
+    if quads == 4:
+        out_send = weight_grad(
+            grad_all, g_other, *gacts, (SEND_LEFT, SEND_RIGHT, KEEP_LEFT, KEEP_RIGHT)
+        )
+        out_keep = out_send[2:]
+        out_move = scatter_first(*out_send[:2])
+    else:
+        g2, gact2 = jnp.concatenate([grad_all, g_other], 0), jnp.concatenate(gacts, 0)
+        out_move = out_keep = (tn(g2, gact2).astype(BF16),)
+    gug_own, choice_own = moe_bwd(
+        base, grad_all, out_full, gates, after(hid_own, *out_keep), length
+    )
+    gug_other, choice_other = moe_bwd(base, g_other, out_full, gates_other, after(hid_other, gug_own), length)
     choice = choice_own + swap(choice_other, "c", 1, 2)
-    out_part = tn_pair(grad_all, g_other, *all_after((gact_own, gact_other), gug_other))
-    out_first = scatter_first(out_part, quads)
-    back_give = nt(after(gug_other, out_part), in_full).astype(BF16)
+    back_give = nt(after(gug_other, *out_move), in_full).astype(BF16)
     back_recv = swap(back_give, "c", 1, 2)
-    back_own = nt(after(gug_own, back_give), in_full).astype(BF16)
+    gug_late = after(gug_own, back_give)
+    back_own = nt(gug_late, in_full).astype(BF16)
     gates_c = gates * choice
     logit_grad = (gates_c - gates * jnp.sum(gates_c, -1, keepdims=True)).astype(BF16)
-    ag, p_part = back_mid(
-        m.astype(jnp.int32).reshape(1), back_own, back_recv, logit_grad, pack, small_at,
-        after(middle, moe_branch, *out_first[1:]), moe_g, cot_own, wo_rows, mp,
-    )
+    def middle_back(*arrived):
+        return back_mid(
+            m.astype(jnp.int32).reshape(1), back_own, back_recv, logit_grad, pack, small_at,
+            after(middle, moe_branch, *arrived), moe_g, cot_own, wo_rows, mp,
+        )
+
+    made = []
+
+    def tie(left, right):
+        made.extend(middle_back(left, right))
+        return (made[0],)
+
+    if quads == 4:
+        out_sum = scatter_second(*out_keep, *out_move, tie)
+    else:
+        out_sum = scatter_plain(*out_keep)
+        made.extend(middle_back())
+    ag, p_part = made
     attended_grad = lax.psum_scatter(p_part, "mp", scatter_dimension=0, tiled=False)
 
-    out_sum = scatter_second(all_after(out_first, ag), quads).astype(BF16)
-    in_part = tn_pair(x_own, x_other, *all_after((gug_own, gug_other), ag))
-    att_late = after(att_flat, in_part)
+    gugs = all_after((gug_own, gug_other), ag)
+    if quads == 4:
+        in_send = weight_grad(x_own, x_other, *gugs, (SEND_LEFT, SEND_RIGHT))
+        in_move = scatter_first(*in_send)
+        in_keep = weight_grad(
+            x_own, x_other, *all_after(gugs, *in_send), (KEEP_LEFT, KEEP_RIGHT)
+        )
+    else:
+        in_move = in_keep = (tn(jnp.concatenate([x_own, x_other], 0), jnp.concatenate(gugs, 0)).astype(BF16),)
+    att_late = after(att_flat, *in_send) if quads == 4 else att_flat
     half_cols = att_flat.shape[1] // 2
-    wo_mine = tn(ag, jnp.where(c == 0, att_late[:, :half_cols], att_late[:, half_cols:]))
-    wo_give = tn(ag, jnp.where(c == 0, att_late[:, half_cols:], att_late[:, :half_cols]))
-    wo_part = (wo_mine + swap(wo_give.astype(BF16), "c", 1, 2).astype(F32)).astype(BF16)
-    in_first = scatter_first(in_part, quads)
+    low_att, high_att = att_late[:, :half_cols], att_late[:, half_cols:]
+    wo_give = tn(ag, jnp.where(c == 0, high_att, low_att)).astype(BF16)
+    wo_mine = tn(ag, after(jnp.where(c == 0, low_att, high_att), wo_give)).astype(BF16)
+    wo_part = (wo_mine.astype(F32) + swap(wo_give, "c", 1, 2).astype(F32)).astype(BF16)
+    if quads == 4:
+        wo_keep = (cut(wo_part, KEEP_LEFT), cut(wo_part, KEEP_RIGHT))
+        wo_move = scatter_first(cut(wo_part, SEND_LEFT), cut(wo_part, SEND_RIGHT))
     layer_out = (
-        lax.dynamic_slice_in_dim(middle, m * (length // mp), length // mp, 0) + RESID * moe_branch
+        lax.dynamic_slice_in_dim(middle, m * (length // mp), length // mp, 0) + RESID * after(moe_branch, ag)
     ).astype(BF16)
 
     dq, dkv = attn_bwd(
-        after(attended_grad, out_sum), q_r, k_r, v_r, attended, lse, cosine, sine, doc_col, doc_row
+        attended_grad, q_r, k_r, v_r, attended, lse, cosine, sine, doc_col, doc_row
     )
     end_part = back_end(dq, dkv, pack, tok_all, attn_g, ag)
     grad_tokens = lax.psum_scatter(end_part, "mp", scatter_dimension=0, tiled=True).astype(F32)
-
-    in_sum = scatter_second(all_after(in_first, end_part), quads).astype(BF16)
-    wo_sum = scatter_rows(after(wo_part, end_part), quads).astype(BF16)
 
     dq_late, dkv_late = after(dq, end_part), after(dkv, end_part)
     part = jnp.concatenate(
@@ -819,26 +956,35 @@
     ).astype(BF16)
     mine, give = column_halves(part, c)
     pair = (mine.astype(F32) + swap(give, "c", 1, 2).astype(F32)).astype(BF16)
-    pair_sum = scatter_second(all_after(scatter_first(pair, quads), in_sum), quads).astype(BF16)
-    sums = jnp.concatenate(from_halves(after(pair_sum, wo_sum), rows, c)[:2], 1)
-    sums = sums.astype(F32)
+    if quads == 4:
+        in_sum = scatter_second(*in_keep, *all_after(in_move, end_part))
+        wo_sum = scatter_second(*wo_keep, *all_after(wo_move, end_part))
+        pair_keep = (cut(pair, KEEP_LEFT), cut(pair, KEEP_RIGHT))
+        pair_move = scatter_first(cut(pair, SEND_LEFT), cut(pair, SEND_RIGHT))
+        *pair_move, in_left, in_right = lax.optimization_barrier((*pair_move, *in_sum))
+        in_sum = (in_left, in_right)
+        pair_sum = scatter_second(*pair_keep, *pair_move)
+        late_sum = (*wo_sum, *pair_sum)
+    else:
+        in_sum, wo_sum, pair_sum = (scatter_plain(v) for v in (in_keep[0], wo_part, pair))
+        late_sum = (*wo_sum, *pair_sum)
+    late_mine, late_other = from_halves(late_sum, rows, c)
+    wo_cols_here = wo_part.shape[1]
+    wo_own_rows = jnp.concatenate(
+        in_order(late_mine[:, :wo_cols_here], late_other[:, :wo_cols_here], c), 1
+    )
+    sums = jnp.concatenate(
+        in_order(late_mine[:, wo_cols_here:], late_other[:, wo_cols_here:], c), 1
+    ).astype(F32)
     grad_query = sums[:, :q_cols]
     grad_key = sums[:, q_cols : q_cols + kv_cols]
     grad_value = sums[:, q_cols + kv_cols : qkv_cols]
     router_part = sums[:, qkv_cols : qkv_cols + experts]
 
-    wo_own_rows = jnp.concatenate(from_halves(wo_sum, rows, c)[:2], 1)
-    grad_output = lax.dynamic_slice_in_dim(wo_own_rows, m * q_cols, q_cols, 1).astype(F32)
-    for k in range(1, mp):
-        send = lax.dynamic_slice_in_dim(wo_own_rows, ((m + k) % mp) * q_cols, q_cols, 1)
-        grad_output = grad_output + lax.ppermute(
-            send, "mp", [(i, (i + k) % mp) for i in range(mp)]
-        ).astype(F32)
-
-    in_0, in_1, in_mine, in_other = from_halves(in_sum, rows, c)
-    out_0, out_1, _, _ = from_halves(out_sum, rows, c)
-    grad_in = jnp.concatenate([in_0, in_1], 1).astype(F32)
-    grad_out = jnp.concatenate([out_0, out_1], 1).astype(F32)
+    in_mine, in_other = from_halves(in_sum, rows, c)
+    out_mine, out_other = from_halves(all_after(out_sum, ag), rows, c)
+    grad_in = jnp.concatenate(in_order(in_mine, in_other, c), 1).astype(F32)
+    grad_out = jnp.concatenate(in_order(out_mine, out_other, c), 1).astype(F32)
 
     attn_gain_part = (
         jnp.sum(grad_query * w_query.astype(F32), 1)
@@ -850,14 +996,22 @@
         + jnp.sum(in_other.astype(F32) * in_gave.astype(F32), 1)
         + jnp.sum(router_part * router.astype(F32), 1)
     ) / moe_gain.astype(F32)
-    tiny = jnp.concatenate([router_part, attn_gain_part[:, None], moe_gain_part[:, None]], 1)
-    total = tiny
+    total = jnp.concatenate(
+        [router_part, attn_gain_part[:, None], moe_gain_part[:, None], jnp.zeros((rows, 128 - experts - 2), F32)], 1
+    )
+    tiny = total.astype(BF16)
+    grad_output = lax.dynamic_slice_in_dim(wo_own_rows, m * q_cols, q_cols, 1).astype(F32)
     for k in range(1, mp):
-        total = total + lax.ppermute(tiny, "mp", [(i, (i + k) % mp) for i in range(mp)])
+        send = lax.dynamic_slice_in_dim(wo_own_rows, ((m + k) % mp) * q_cols, q_cols, 1)
+        got = lax.ppermute(
+            jnp.concatenate([send, tiny], 1), "mp", [(i, (i + k) % mp) for i in range(mp)]
+        ).astype(F32)
+        grad_output = grad_output + got[:, :q_cols]
+        total = total + got[:, q_cols:]
 
     return (
-        reorder(layer_out, q, quads)[None],
-        reorder(grad_tokens, q, quads)[None],
+        restore(layer_out, q, quads)[None],
+        restore(grad_tokens, q, quads)[None],
         total[:, experts],
         grad_query,
         grad_key,

time: 656 us -> 603 us (0.919)
  waiting for transfers between devices: 201 us -> 125 us
  Pallas kernels: 178 us -> 213 us
  other arithmetic: 66.1 us -> 85.5 us
  matrix products: 62.6 us -> 47 us
  starting transfers between devices: 62.8 us -> 50.7 us
    ppermute x58 -> x60, waiting for transfers between devices: 176 us -> 105 us  [swap(): return lax.ppermute(value, axis, [(i, i ^ bit) for i in range(size)])]
    pallas_call x2 -> x5, Pallas kernels: 42.8 us -> 75.8 us  [the longest x3 56.7 us: weight_grad(): pl.pallas_call(functools.partial(segment_kernel, count=count), grid=(coun...]
    convert_element_type x7 -> x24, other arithmetic: 13.2 us -> 38.5 us  [the longest x1 5.36 us: body(): combined = (comb_own.astype(F32) + comb_recv.astype(F32)).astype(BF16)]
    dot_general x4 -> x2, matrix products: 46.7 us -> 29.7 us  [nt(): lax.dot_general(left, right, (((1,), (1,)), ((), ())), preferred_element_...]
    reduce_scatter x1, starting transfers between devices: 10.5 us -> 0.04 us  [body(): lax.psum_scatter(p_part, 'mp', scatter_dimension=0, tiled=False)]
    all_gather x1, waiting for transfers between devices: 7.68 us -> 14.7 us  [body(): tok_all = lax.all_gather(tok_own, 'mp', axis=0, tiled=True)]
    unnamed x125 -> x169, local copies, waits for them, and re-layouts: 34.4 us -> 31.7 us
    ppermute x58 -> x60, starting transfers between devices: 46 us -> 45.4 us  [swap(): return lax.ppermute(value, axis, [(i, i ^ bit) for i in range(size)])]
  transfers between devices with their start and end apart: 71 -> 70, of which waited for: 35 -> 22; matrix products, arithmetic and copies ran while one was open for 26% -> 30% of each run, Pallas kernels for 25% -> 33%
where the time goes in v3:
time: 603 us; the launch traced here: 596 us
  Pallas kernels  213 us (35%)
  waiting for transfers between devices  125 us (21%)
  other arithmetic  85.5 us (14%)
  local copies, waits for them, and re-layouts  59.7 us (10%)
  starting transfers between devices  50.7 us (8%)
  matrix products  47 us (8%)
  between operations  15.8 us (3%)
    ppermute x60, waiting for transfers between devices, swap(): return lax.ppermute(value, axis, [(i, i ^ bit) for i in range(size)])  105 us
    pallas_call x3, Pallas kernels, weight_grad(): pl.pallas_call(functools.partial(segment_kernel, count=count), grid=(coun...  56.7 us
    ppermute x60, starting transfers between devices, swap(): return lax.ppermute(value, axis, [(i, i ^ bit) for i in range(size)])  45.4 us
    unnamed x169, local copies, waits for them, and re-layouts  31.7 us
    pallas_call x2, Pallas kernels, moe_fwd(): pl.pallas_call(moe_fwd_kernel, grid_spec=pltpu.PrefetchScalarGridSpec(num...  30 us
    dot_general x2, matrix products, nt(): lax.dot_general(left, right, (((1,), (1,)), ((), ())), preferred_element_...  29.7 us
    pallas_call x2, Pallas kernels, moe_bwd(): pl.pallas_call(moe_bwd_kernel, grid_spec=pltpu.PrefetchScalarGridSpec(num...  29.4 us
    pallas_call x1, Pallas kernels, attn_fwd(): pl.pallas_call(functools.partial(attn_fwd_kernel, q_heads=q_heads, kv_hea...  20.9 us
  transfers between devices with their start and end apart: 70, of which 22 were waited for; matrix products, arithmetic and copies ran while one was open for 30% of the time, Pallas kernels for 33%

profile of v3, /device:TPU:0, one launch (start us, length us, event | category | flops | bytes accessed | tf_op | source)
XLA Modules:
  0.0 596.4 jit_solution(10096741387346319612)
XLA Ops:
  11.8 3.2 constant_dynamic-slice_fusion.18
  16.0 1.7 reshape.80
  20.2 2.9 collective-permute-start.1
  27.3 2.5 collective-permute-start.3
  32.7 3.1 collective-permute-done.3
  44.0 1.9 broadcast_select_fusion.8
  47.6 1.8 broadcast_select_fusion.5
  53.6 3.1 negate_select_fusion
  57.7 2.5 bitcast_select_fusion
  61.7 14.7 %all-gather.7.cloned.1.call-done.tok_ref = bf16[1024,1536]{1,0:T(8,128)(2,1)} async-done(((bf16[256,1536]{1,0:T(8,128)(2,1)}), bf16[1024,1536]{1,0:T(8,128)(2,1)}) %all-gather.7.cloned.1.call-update) | async-done | bytes 3145744 | tf_op jit(solution)/shard_map/all_gather | solution.py:792
  76.4 20.9 %attn_fwd.1 = (bf16[1024,1536]{1,0:T(8,128)(2,1)}, bf16[6,1024,64]{2,1,0:T(8,128)(2,1)}, bf16[2,1024,64]{2,1,0:T(8,128)(2,1)}, bf16[2,1024,64]{2,1,0:T(8,128)(2,...) custom-call(bf16[1024,1536]{1,0:T(8,128)(2,1)} %all-gather.7.cloned.1.call-done.tok_ref, ...), custom_call_target="tpu_custom_call" | custom-call | flops 44291848 | bytes 82575 | tf_op jit(solution)/shard_map/attn_fwd/pallas_call | solution.py:121
  97.3 7.2 %collective-permute-done.9 = bf16[192,3072]{1,0:T(8,128)(2,1)} collective-permute-done((bf16[192,3072]{1,0:T(8,128)(2,1)S(1)}, bf16[192,3072]{1,0:T(8,128)(2,1)}, u32[]{:S(2)}, u32[]{:S(2)}) %collective-permute-start.9) | collective-permute-done | bytes 1179680 | tf_op jit(solution)/shard_map/ppermute | solution.py:636
  111.0 22.4 %collective-permute-done.14 = bf16[192,3072]{1,0:T(8,128)(2,1)} collective-permute-done((bf16[192,3072]{1,0:T(8,128)(2,1)}, bf16[192,3072]{1,0:T(8,128)(2,1)}, u32[]{:S(2)}, u32[]{:S(2)}) %collective-permute-start.14) | collective-permute-done | bytes 1179680 | tf_op jit(solution)/shard_map/ppermute | solution.py:636
  137.9 10.3 %collective-permute-done.17 = bf16[192,768]{1,0:T(8,128)(2,1)S(1)} collective-permute-done((bf16[192,768]{1,0:T(8,128)(2,1)S(1)}, bf16[192,768]{1,0:T(8,128)(2,1)S(1)}, u32[]{:S(2)}, u32[]{:S(2)}) %collective-permute-start.17) | collective-permute-done | bytes 294944 | tf_op jit(solution)/shard_map/ppermute | solution.py:636
  151.3 2.4 constant_dynamic-update-slice_fusion.13
  153.7 2.4 constant_dynamic-update-slice_fusion.12
  156.1 2.4 constant_dynamic-update-slice_fusion.11
  158.6 2.4 constant_dynamic-update-slice_fusion.10
  161.0 2.4 constant_dynamic-update-slice_fusion.9
  165.5 2.4 constant_dynamic-update-slice_fusion.8.w_ref
  167.9 4.9 collective-permute-done.23
  176.1 2.6 pad_maximum_fusion.wo_ref
  178.7 10.9 %collective-permute-done.22.refs_8_.refs_11_ = bf16[192,1536]{1,0:T(8,128)(2,1)S(1)} collective-permute-done((bf16[192,1536]{1,0:T(8,128)(2,1)S(1)}, bf16[192,1536]{1,0:T(8,128)(2,1)S(1)}, u32[]{:S(2)}, u32[]{:S(2)}) %collective-permute-start.22) | collective-permute-done | bytes 589856 | tf_op jit(solution)/shard_map/ppermute | solution.py:636
  189.7 13.2 %mid_fwd.1 = (f32[1024,1536]{1,0:T(8,128)}, bf16[1024,1536]{1,0:T(8,128)(2,1)}, f32[1024,128]{1,0:T(8,128)}, bf16[1024,1536]{1,0:T(8,128)(2,1)}) custom-call(bf16[4,1024,384]{2,1,0:T(8,128)(2,1)} %bitcast.55, bf16[1536,1536]{1,0:T(8,128)(2,1)} %pad_maximum_fusion.wo_ref, bf16[1024,1536]{1,0:T(8,128)(2,1)} %all-gather.7.cloned.1.call-done.tok_ref, ...), custom_call_target="tpu_custom_call" | custom-call | flops 4831838208 | bytes 20447232 | tf_op jit(solution)/shard_map/mid_fwd/pallas_call | solution.py:290
  207.0 12.4 %collective-permute-done.33.refs_5_.refs_8_ = bf16[192,1536]{1,0:T(8,128)(2,1)} collective-permute-done((bf16[192,1536]{1,0:T(8,128)(2,1)}, bf16[192,1536]{1,0:T(8,128)(2,1)}, u32[]{:S(2)}, u32[]{:S(2)}) %collective-permute-start.33) | collective-permute-done | bytes 589856 | tf_op jit(solution)/shard_map/ppermute | solution.py:636
  219.4 15.0 %moe_fwd.2 = (bf16[1024,3072]{1,0:T(8,128)(2,1)}, bf16[1024,1536]{1,0:T(8,128)(2,1)}) custom-call(s32[1]{0:T(128)} %bitcast.9.base_ref.refs_0_, bf16[1024,1536]{1,0:T(8,128)(2,1)} %get-tuple-element.147.x_ref.refs_0_.refs_1_, bf16[1536,3072]{1,0:T(8,128)(2,1)} %constant_dynamic-update-slice_fusion.8.w_ref, f32[1024,128]{1,0:T(8,128)} %get-tuple-element.148.gate_ref.refs_2_), custom_call_target="tpu_custom_call" | custom-call | flops 96636768 | bytes 314572 | tf_op jit(solution)/shard_map/moe_fwd/pallas_call | solution.py:446
  236.0 15.0 %moe_fwd.3 = (bf16[1024,3072]{1,0:T(8,128)(2,1)}, bf16[1024,1536]{1,0:T(8,128)(2,1)}) custom-call(s32[1]{0:T(128)} %bitcast.9.base_ref.refs_0_, bf16[1024,1536]{1,0:T(8,128)(2,1)} %copy-done.1, bf16[1536,3072]{1,0:T(8,128)(2,1)} %constant_dynamic-update-slice_fusion.8.w_ref, f32[1024,128]{1,0:T(8,128)} %collective-permute-done.32.gate_ref.refs_2_), custom_call_target="tpu_custom_call" | custom-call | flops 9663676416 | bytes 31457280 | tf_op jit(solution)/shard_map/moe_fwd/pallas_call | solution.py:446
  251.0 9.6 %combine.2 = bf16[1024,1536]{1,0:T(8,128)(2,1)} custom-call(bf16[1024,1536]{1,0:T(8,128)(2,1)} %get-tuple-element.159.refs_0_.refs_5_, bf16[192,1536]{1,0:T(8,128)(2,1)} %get-tuple-element.141.refs_1_.refs_4_, bf16[192,1536]{1,0:T(8,128)(2,1)} %get-tuple-element.142.refs_2_.refs_5_, bf16[192,1536]{1,0:T(8,128)(2,1)} %copy-done.71, ...), custom_call_target="tpu_custom_call" | custom-call | flops 4831838208 | bytes 11010048 | tf_op jit(solution)/shard_map/combine/pallas_call | solution.py:494
  261.2 9.6 %combine.3 = bf16[1024,1536]{1,0:T(8,128)(2,1)} custom-call(bf16[1024,1536]{1,0:T(8,128)(2,1)} %get-tuple-element.158.refs_0_.refs_4_, bf16[192,1536]{1,0:T(8,128)(2,1)} %get-tuple-element.141.refs_1_.refs_4_, bf16[192,1536]{1,0:T(8,128)(2,1)} %get-tuple-element.142.refs_2_.refs_5_, bf16[192,1536]{1,0:T(8,128)(2,1)} %copy-done.71, ...), custom_call_target="tpu_custom_call" | custom-call | flops 4831838208 | bytes 11010048 | tf_op jit(solution)/shard_map/combine/pallas_call | solution.py:494
  272.4 25.1 %weight_grad.3 = (bf16[768,768]{1,0:T(8,128)(2,1)}, bf16[768,768]{1,0:T(8,128)(2,1)}, bf16[768,768]{1,0:T(8,128)(2,1)}, bf16[768,768]{1,0:T(8,128)(2,1)}) custom-call(bf16[1024,1536]{1,0:T(8,128)(2,1)} %all-gather.9.cloned.1.call-done.refs_0_.refs_1_, bf16[1024,1536]{1,0:T(8,128)(2,1)} %all-gather.9.cloned.1.call-done.refs_0_.refs_1_, ...), custom_call_target="tpu_custom_call" | custom-call | flops 96636768 | bytes 125829 | tf_op jit(solution)/shard_map/weight_grad/pallas_call | solution.py:616
  299.9 5.4 add_convert_fusion
  305.4 14.8 %moe_bwd.2 = (bf16[1024,3072]{1,0:T(8,128)(2,1)}, f32[1024,128]{1,0:T(8,128)}) custom-call(s32[1]{0:T(128)} %bitcast.9.base_ref.refs_0_, bf16[1024,1536]{1,0:T(8,128)(2,1)} %all-gather.9.cloned.1.call-done.refs_0_.refs_1_, f32[1024,128]{1,0:T(8,128)} %get-tuple-element.148.gate_ref.refs_2_, bf16[1024,3072]{1,0:T(8,128)(2,1)} %get-tuple-element.162.refs_3_, ...), custom_call_target="tpu_custom_call" | custom-call | flops 4831838208 | bytes 25165824 | tf_op jit(solution)/shard_map/moe_bwd/pallas_call | solution.py:547
  320.2 14.5 %moe_bwd.3 = (bf16[1024,3072]{1,0:T(8,128)(2,1)}, f32[1024,128]{1,0:T(8,128)}) custom-call(s32[1]{0:T(128)} %bitcast.9.base_ref.refs_0_, bf16[1024,1536]{1,0:T(8,128)(2,1)} %copy-done.3, f32[1024,128]{1,0:T(8,128)} %collective-permute-done.32.gate_ref.refs_2_, bf16[1024,3072]{1,0:T(8,128)(2,1)} %get-tuple-element.165.refs_3_, ...), custom_call_target="tpu_custom_call" | custom-call | flops 4831838208 | bytes 25165824 | tf_op jit(solution)/shard_map/moe_bwd/pallas_call | solution.py:547
  335.9 15.8 %convolution_convert_fusion.1 = bf16[1024,1536]{1,0:T(8,128)(2,1)} fusion(bf16[1024,3072]{1,0:T(8,128)(2,1)} %get-tuple-element.193.refs_5_, bf16[1536,3072]{1,0:T(8,128)(2,1)} %constant_dynamic-update-slice_fusion.8.w_ref), kind=kOutput, calls=%fused_computation.4 | convolution fusion | flops 9665249280 | bytes 18874368 | tf_op jit(solution)/shard_map/dot_general | solution.py:24
  353.3 2.0 add_convert_fusion.11
  358.3 13.9 %convolution_convert_fusion.back_ref = bf16[1024,1536]{1,0:T(8,128)(2,1)} fusion(bf16[1024,3072]{1,0:T(8,128)(2,1)S(1)} %copy-done.2, bf16[1536,3072]{1,0:T(8,128)(2,1)} %constant_dynamic-update-slice_fusion.8.w_ref), kind=kOutput, calls=%fused_computation.3 | convolution fusion | flops 9665249280 | bytes 18874368 | tf_op jit(solution)/shard_map/dot_general | solution.py:24
  372.2 2.5 convert_element_type.321
  374.8 13.9 %back_mid.1 = (bf16[1024,1536]{1,0:T(8,128)(2,1)}, bf16[4,1024,384]{2,1,0:T(8,128)(2,1)}) custom-call(s32[1]{0:T(128)} %bitcast.11.own_ref, bf16[1024,1536]{1,0:T(8,128)(2,1)} %convolution_convert_fusion.back_ref, bf16[1024,1536]{1,0:T(8,128)(2,1)} %collective-permute-done.39.recv_ref, bf16[1024,128]{1,0:T(8,128)(2,1)} %subtract_convert_fusion.lg_ref, ...), custom_call_target="tpu_custom_call" | custom-call | flops 4831838208 | bytes 23592960 | tf_op jit(solution)/shard_map/back_mid/pallas_call | solution.py:351
  390.6 1.8 convolution_convert_fusion.6
  392.3 15.9 %weight_grad.4 = (bf16[768,1536]{1,0:T(8,128)(2,1)}, bf16[768,1536]{1,0:T(8,128)(2,1)}) custom-call(bf16[1024,1536]{1,0:T(8,128)(2,1)} %get-tuple-element.147.x_ref.refs_0_.refs_1_, bf16[1024,1536]{1,0:T(8,128)(2,1)} %get-tuple-element.147.x_ref.refs_0_.refs_1_, bf16[1024,1536]{1,0:T(8,128)(2,1)} %copy-done.1, bf16[1024,1536]{1,0:T(8,128)(2,1)} %copy-done.1, ...), custom_call_target="tpu_custom_call" | custom-call | flops 96636768 | bytes 188743 | tf_op jit(solution)/shard_map/weight_grad/pallas_call | solution.py:616
  410.6 6.2 %convolution_convert_fusion.3 = bf16[1536,768]{1,0:T(8,128)(2,1)} fusion(bf16[1024,1536]{1,0:T(8,128)(2,1)} %get-tuple-element.176.ag_ref, pred[]{:T(512)S(6)} %eq.14, bf16[1024,1536]{1,0:T(8,128)(2,1)S(1)} %copy-done.13), kind=kOutput, calls=%fused_computation.6 | convolution fusion | flops 2417885184 | bytes 8650753 | tf_op jit(solution)/shard_map/dot_general | solution.py:28
  421.8 15.7 %weight_grad.5 = (bf16[768,1536]{1,0:T(8,128)(2,1)}, bf16[768,1536]{1,0:T(8,128)(2,1)}) custom-call(bf16[1024,1536]{1,0:T(8,128)(2,1)} %get-tuple-element.147.x_ref.refs_0_.refs_1_, bf16[1024,1536]{1,0:T(8,128)(2,1)} %get-tuple-element.147.x_ref.refs_0_.refs_1_, bf16[1024,1536]{1,0:T(8,128)(2,1)} %copy-done.1, bf16[1024,1536]{1,0:T(8,128)(2,1)} %copy-done.1, ...), custom_call_target="tpu_custom_call" | custom-call | flops 96636768 | bytes 188743 | tf_op jit(solution)/shard_map/weight_grad/pallas_call | solution.py:616
  437.5 1.8 add_convert_fusion.7
  441.5 4.3 convolution_convert_fusion.2
  448.8 1.8 maximum_convert_fusion.1
  451.4 2.2 add_convert_fusion.1
  457.2 20.4 %attn_bwd.1 = (bf16[1024,384]{1,0:T(8,128)(2,1)}, bf16[1024,256]{1,0:T(8,128)(2,1)}) custom-call(bf16[1024,384]{1,0:T(8,128)(2,1)} %bitcast.56, bf16[6,1024,64]{2,1,0:T(8,128)(2,1)} %get-tuple-element.179.q_ref, bf16[2,1024,64]{2,1,0:T(8,128)(2,1)} %get-tuple-element.180.k_ref, bf16[2,1024,64]{2,1,0:T(8,128)(2,1)} %get-tuple-element.181.v_ref, ...), custom_call_target="tpu_custom_call" | custom-call | flops 6039797760 | bytes 3145728 | tf_op jit(solution)/shard_map/attn_bwd/pallas_call | solution.py:224
  477.6 9.0 %back_end.1 = bf16[1024,1536]{1,0:T(8,128)(2,1)} custom-call(bf16[1024,384]{1,0:T(8,128)(2,1)} %get-tuple-element.186.dq_ref, bf16[1024,256]{1,0:T(8,128)(2,1)} %get-tuple-element.187.dkv_ref, bf16[1536,768]{1,0:T(8,128)(2,1)} %pad_maximum_fusion.1.w_ref.small_ref, bf16[1024,1536]{1,0:T(8,128)(2,1)} %all-gather.7.cloned.1.call-done.tok_ref, ...), custom_call_target="tpu_custom_call" | custom-call | flops 2013265920 | bytes 11403264 | tf_op jit(solution)/shard_map/back_end/pallas_call | solution.py:399
  486.7 3.2 convolution_convert_fusion.5
  490.1 1.8 broadcast_select_fusion.7
  495.9 2.2 add_convert_fusion.4
  499.7 3.4 collective-permute-done.55
  510.4 18.0 %collective-permute-done.48 = bf16[384,1536]{1,0:T(8,128)(2,1)S(1)} collective-permute-done((bf16[384,1536]{1,0:T(8,128)(2,1)S(1)}, bf16[384,1536]{1,0:T(8,128)(2,1)S(1)}, u32[]{:S(2)}, u32[]{:S(2)}) %collective-permute-start.48) | collective-permute-done | bytes 1179680 | tf_op jit(solution)/shard_map/ppermute | solution.py:636
  529.5 1.7 add_convert_fusion.3
  531.2 1.7 add_convert_fusion.2
  533.6 3.6 collective-permute-done.44
  542.2 2.3 collective-permute-done.51
  548.6 2.5 multiply_reduce_fusion.1
  557.1 1.7 fusion.14
  558.8 1.9 pad_maximum_fusion.20
  560.7 3.8 collective-permute-start.61
  566.9 3.5 concatenate.184
  571.3 4.6 maximum_convert_fusion
  577.0 5.3 collective-permute-done.60
  (395 shorter events, 126.7 us)
Async XLA Ops:
  7.2 69.2 %all-gather.7.cloned.1.call-start = ((), (), s32[]{:S(2)}) async-start(), calls=%async_computation.3 | async-start | bytes 3932160 | tf_op jit(solution)/shard_map/all_gather | solution.py:792
  9.6 98.1 %all-gather.13.cloned.1.call-start = ((), (), s32[]{:S(2)}) async-start(), calls=%async_computation.9 | async-start | bytes 1474560 | tf_op jit(solution)/shard_map/all_gather | solution.py:836
  20.2 7.1 %collective-permute-start.1 = (bf16[192,384]{1,0:T(8,128)(2,1)S(1)}, bf16[192,384]{1,0:T(8,128)(2,1)S(1)}, u32[]{:S(2)}, u32[]{:S(2)}) collective-permute-start(bf16[192,384]{1,0:T(8,128)(2,1)S(1)} %get-tuple-element.289), channel_id=1, source_target_pairs={{0,8},{8,0},{16,24},{24,16},{1,9},{9,1},{17,25},{25,17},{2,10},{10... | collective-permute-start | bytes 442376 | tf_op jit(solution)/shard_map/ppermute | solution.py:636
  23.8 6.7 %collective-permute-start.4 = (bf16[192,384]{1,0:T(8,128)(2,1)S(1)}, bf16[192,384]{1,0:T(8,128)(2,1)S(1)}, u32[]{:S(2)}, u32[]{:S(2)}) collective-permute-start(bf16[192,384]{1,0:T(8,128)(2,1)S(1)} %get-tuple-element.287), channel_id=1, source_target_pairs={{0,16},{8,24},{16,0},{24,8},{1,17},{9,25},{17,1},{25,9},{2,18},{10... | collective-permute-start | bytes 442376 | tf_op jit(solution)/shard_map/ppermute | solution.py:636
  25.3 6.7 %collective-permute-start.2 = (bf16[192,384]{1,0:T(8,128)(2,1)S(1)}, bf16[192,384]{1,0:T(8,128)(2,1)S(1)}, u32[]{:S(2)}, u32[]{:S(2)}) collective-permute-start(bf16[192,384]{1,0:T(8,128)(2,1)S(1)} %get-tuple-element.287), channel_id=1, source_target_pairs={{0,8},{8,0},{16,24},{24,16},{1,9},{9,1},{17,25},{25,17},{2,10},{10... | collective-permute-start | bytes 442376 | tf_op jit(solution)/shard_map/ppermute | solution.py:636
  25.9 11.2 %collective-permute-start.6 = (bf16[192,384]{1,0:T(8,128)(2,1)S(1)}, bf16[192,384]{1,0:T(8,128)(2,1)S(1)}, u32[]{:S(2)}, u32[]{:S(2)}) collective-permute-start(bf16[192,384]{1,0:T(8,128)(2,1)S(1)} %get-tuple-element.289), channel_id=1, source_target_pairs={{0,16},{8,24},{16,0},{24,8},{1,17},{9,25},{17,1},{25,9},{2,18},{10... | collective-permute-start | bytes 442376 | tf_op jit(solution)/shard_map/ppermute | solution.py:636
  27.3 8.4 %collective-permute-start.3 = (bf16[192,384]{1,0:T(8,128)(2,1)S(1)}, bf16[192,384]{1,0:T(8,128)(2,1)S(1)}, u32[]{:S(2)}, u32[]{:S(2)}) collective-permute-start(bf16[192,384]{1,0:T(8,128)(2,1)S(1)} %collective-permute-done.1), channel_id=1, source_target_pairs={{0,16},{8,24},{16,0},{24,8},{1,17},{9,25},{17,1},{25,9},{2,18},{10... | collective-permute-start | bytes 442376 | tf_op jit(solution)/shard_map/ppermute | solution.py:636
  30.5 5.9 collective-permute-start.5
  38.5 5.5 collective-permute-start.7
  38.5 9.1 %collective-permute-start.8 = (bf16[192,3072]{1,0:T(8,128)(2,1)S(1)}, bf16[192,3072]{1,0:T(8,128)(2,1)}, u32[]{:S(2)}, u32[]{:S(2)}) collective-permute-start(bf16[192,3072]{1,0:T(8,128)(2,1)S(1)} %reshape.79), channel_id=1, source_target_pairs={{0,4},{4,0},{1,5},{5,1},{2,6},{6,2},{3,7},{7,3},{8,12},{12,8},{9,1... | collective-permute-start | bytes 3538952 | tf_op jit(solution)/shard_map/ppermute | solution.py:636
  44.0 13.7 %collective-permute-start.13 = (bf16[192,1536]{1,0:T(8,128)(2,1)}, bf16[192,1536]{1,0:T(8,128)(2,1)}, u32[]{:S(2)}, u32[]{:S(2)}) collective-permute-start(bf16[192,1536]{1,0:T(8,128)(2,1)} %bitcast.43), channel_id=1, source_target_pairs={{0,4},{4,0},{1,5},{5,1},{2,6},{6,2},{3,7},{7,3},{8,12},{12,8},{9,1... | collective-permute-start | bytes 1769480 | tf_op jit(solution)/shard_map/ppermute | solution.py:636
  47.5 142.1 %all-gather.11.cloned.1.call-start = ((), (), s32[]{:S(2)}) async-start(), calls=%async_computation.8 | async-start | bytes 3932160 | tf_op jit(solution)/shard_map/all_gather | solution.py:857
  49.4 55.0 %collective-permute-start.10 = (bf16[192,3072]{1,0:T(8,128)(2,1)S(1)}, bf16[192,3072]{1,0:T(8,128)(2,1)}, u32[]{:S(2)}, u32[]{:S(2)}) collective-permute-start(bf16[192,3072]{1,0:T(8,128)(2,1)S(1)} %get-tuple-element.134), channel_id=1, source_target_pairs={{0,16},{8,24},{16,0},{24,8},{1,17},{9,25},{17,1},{25,9},{2,18},{10... | collective-permute-start | bytes 3538952 | tf_op jit(solution)/shard_map/ppermute | solution.py:636
  51.0 53.5 %collective-permute-start.11 = (bf16[192,3072]{1,0:T(8,128)(2,1)S(1)}, bf16[192,3072]{1,0:T(8,128)(2,1)}, u32[]{:S(2)}, u32[]{:S(2)}) collective-permute-start(bf16[192,3072]{1,0:T(8,128)(2,1)S(1)} %get-tuple-element.134), channel_id=1, source_target_pairs={{0,8},{8,0},{16,24},{24,16},{1,9},{9,1},{17,25},{25,17},{2,10},{10... | collective-permute-start | bytes 3538952 | tf_op jit(solution)/shard_map/ppermute | solution.py:636
  51.5 52.9 %collective-permute-start.9 = (bf16[192,3072]{1,0:T(8,128)(2,1)S(1)}, bf16[192,3072]{1,0:T(8,128)(2,1)}, u32[]{:S(2)}, u32[]{:S(2)}) collective-permute-start(bf16[192,3072]{1,0:T(8,128)(2,1)S(1)} %get-tuple-element.133), channel_id=1, source_target_pairs={{0,8},{8,0},{16,24},{24,16},{1,9},{9,1},{17,25},{25,17},{2,10},{10... | collective-permute-start | bytes 3538952 | tf_op jit(solution)/shard_map/ppermute | solution.py:636
  53.0 51.4 %collective-permute-start.12 = (bf16[192,3072]{1,0:T(8,128)(2,1)S(1)}, bf16[192,3072]{1,0:T(8,128)(2,1)}, u32[]{:S(2)}, u32[]{:S(2)}) collective-permute-start(bf16[192,3072]{1,0:T(8,128)(2,1)S(1)} %get-tuple-element.133), channel_id=1, source_target_pairs={{0,16},{8,24},{16,0},{24,8},{1,17},{9,25},{17,1},{25,9},{2,18},{10... | collective-permute-start | bytes 3538952 | tf_op jit(solution)/shard_map/ppermute | solution.py:636
  104.5 156.1 %all-gather.9.cloned.1.call-start = ((), (), s32[]{:S(2)}) async-start(), calls=%async_computation.4 | async-start | bytes 3932160 | tf_op jit(solution)/shard_map/all_gather | solution.py:864
  105.8 27.6 %collective-permute-start.14 = (bf16[192,3072]{1,0:T(8,128)(2,1)}, bf16[192,3072]{1,0:T(8,128)(2,1)}, u32[]{:S(2)}, u32[]{:S(2)}) collective-permute-start(bf16[192,3072]{1,0:T(8,128)(2,1)} %collective-permute-done.9), channel_id=1, source_target_pairs={{0,16},{8,24},{16,0},{24,8},{1,17},{9,25},{17,1},{25,9},{2,18},{10... | collective-permute-start | bytes 3538952 | tf_op jit(solution)/shard_map/ppermute | solution.py:636
  106.3 27.4 %collective-permute-start.15 = (bf16[192,3072]{1,0:T(8,128)(2,1)}, bf16[192,3072]{1,0:T(8,128)(2,1)}, u32[]{:S(2)}, u32[]{:S(2)}) collective-permute-start(bf16[192,3072]{1,0:T(8,128)(2,1)} %collective-permute-done.10), channel_id=1, source_target_pairs={{0,8},{8,0},{16,24},{24,16},{1,9},{9,1},{17,25},{25,17},{2,10},{10... | collective-permute-start | bytes 3538952 | tf_op jit(solution)/shard_map/ppermute | solution.py:636
  110.7 261.6 %reduce-scatter.4.cloned.1.call-start = ((), (), s32[]{:S(2)}) async-start(), calls=%async_computation.5 | async-start | bytes 3932160 | tf_op jit(solution)/shard_map/reduce_scatter | solution.py:881
  133.7 14.6 %collective-permute-start.18 = (bf16[192,768]{1,0:T(8,128)(2,1)S(1)}, bf16[192,768]{1,0:T(8,128)(2,1)S(1)}, u32[]{:S(2)}, u32[]{:S(2)}) collective-permute-start(bf16[192,768]{1,0:T(8,128)(2,1)S(1)} %get-tuple-element.132), channel_id=1, source_target_pairs={{0,16},{8,24},{16,0},{24,8},{1,17},{9,25},{17,1},{25,9},{2,18},{10... | collective-permute-start | bytes 884744 | tf_op jit(solution)/shard_map/ppermute | solution.py:636
  135.1 14.2 %collective-permute-start.19 = (bf16[192,768]{1,0:T(8,128)(2,1)S(1)}, bf16[192,768]{1,0:T(8,128)(2,1)S(1)}, u32[]{:S(2)}, u32[]{:S(2)}) collective-permute-start(bf16[192,768]{1,0:T(8,128)(2,1)S(1)} %get-tuple-element.132), channel_id=1, source_target_pairs={{0,8},{8,0},{16,24},{24,16},{1,9},{9,1},{17,25},{25,17},{2,10},{10... | collective-permute-start | bytes 884744 | tf_op jit(solution)/shard_map/ppermute | solution.py:636
  135.8 12.5 %collective-permute-start.17 = (bf16[192,768]{1,0:T(8,128)(2,1)S(1)}, bf16[192,768]{1,0:T(8,128)(2,1)S(1)}, u32[]{:S(2)}, u32[]{:S(2)}) collective-permute-start(bf16[192,768]{1,0:T(8,128)(2,1)S(1)} %get-tuple-element.131), channel_id=1, source_target_pairs={{0,8},{8,0},{16,24},{24,16},{1,9},{9,1},{17,25},{25,17},{2,10},{10... | collective-permute-start | bytes 884744 | tf_op jit(solution)/shard_map/ppermute | solution.py:636
  137.2 12.2 %collective-permute-start.20 = (bf16[192,768]{1,0:T(8,128)(2,1)S(1)}, bf16[192,768]{1,0:T(8,128)(2,1)S(1)}, u32[]{:S(2)}, u32[]{:S(2)}) collective-permute-start(bf16[192,768]{1,0:T(8,128)(2,1)S(1)} %get-tuple-element.131), channel_id=1, source_target_pairs={{0,16},{8,24},{16,0},{24,8},{1,17},{9,25},{17,1},{25,9},{2,18},{10... | collective-permute-start | bytes 884744 | tf_op jit(solution)/shard_map/ppermute | solution.py:636
  137.8 35.8 %collective-permute-start.25 = (bf16[384,768]{1,0:T(8,128)(2,1)S(1)}, bf16[384,768]{1,0:T(8,128)(2,1)S(1)}, u32[]{:S(2)}, u32[]{:S(2)}) collective-permute-start(bf16[384,768]{1,0:T(8,128)(2,1)S(1)} %pad_maximum_fusion.9), channel_id=1, source_target_pairs={{0,4},{4,0},{1,5},{5,1},{2,6},{6,2},{3,7},{7,3},{8,12},{12,8},{9,1... | collective-permute-start | bytes 1769480 | tf_op jit(solution)/shard_map/ppermute | solution.py:636
  149.4 29.3 %collective-permute-start.21 = (bf16[192,1536]{1,0:T(8,128)(2,1)S(1)}, bf16[192,1536]{1,0:T(8,128)(2,1)S(1)}, u32[]{:S(2)}, u32[]{:S(2)}) collective-permute-start(bf16[192,1536]{1,0:T(8,128)(2,1)S(1)} %copy-done.40), channel_id=1, source_target_pairs={{0,8},{8,0},{16,24},{24,16},{1,9},{9,1},{17,25},{25,17},{2,10},{10... | collective-permute-start | bytes 1769480 | tf_op jit(solution)/shard_map/ppermute | solution.py:636
  150.2 25.5 %collective-permute-start.28 = (bf16[384,768]{1,0:T(8,128)(2,1)S(1)}, bf16[384,768]{1,0:T(8,128)(2,1)S(1)}, u32[]{:S(2)}, u32[]{:S(2)}) collective-permute-start(bf16[384,768]{1,0:T(8,128)(2,1)S(1)} %pad_maximum_fusion.12), channel_id=1, source_target_pairs={{0,4},{4,0},{1,5},{5,1},{2,6},{6,2},{3,7},{7,3},{8,12},{12,8},{9,1... | collective-permute-start | bytes 1769480 | tf_op jit(solution)/shard_map/ppermute | solution.py:636
  163.4 9.4 %collective-permute-start.23 = (bf16[192,768]{1,0:T(8,128)(2,1)S(1)}, bf16[192,768]{1,0:T(8,128)(2,1)S(1)}, u32[]{:S(2)}, u32[]{:S(2)}) collective-permute-start(bf16[192,768]{1,0:T(8,128)(2,1)S(1)} %collective-permute-done.17), channel_id=1, source_target_pairs={{0,16},{8,24},{16,0},{24,8},{1,17},{9,25},{17,1},{25,9},{2,18},{10... | collective-permute-start | bytes 884744 | tf_op jit(solution)/shard_map/ppermute | solution.py:636
  164.0 9.1 %collective-permute-start.24 = (bf16[192,768]{1,0:T(8,128)(2,1)S(1)}, bf16[192,768]{1,0:T(8,128)(2,1)S(1)}, u32[]{:S(2)}, u32[]{:S(2)}) collective-permute-start(bf16[192,768]{1,0:T(8,128)(2,1)S(1)} %collective-permute-done.18), channel_id=1, source_target_pairs={{0,8},{8,0},{16,24},{24,16},{1,9},{9,1},{17,25},{25,17},{2,10},{10... | collective-permute-start | bytes 884744 | tf_op jit(solution)/shard_map/ppermute | solution.py:636
  174.3 15.4 %collective-permute-start.22 = (bf16[192,1536]{1,0:T(8,128)(2,1)S(1)}, bf16[192,1536]{1,0:T(8,128)(2,1)S(1)}, u32[]{:S(2)}, u32[]{:S(2)}) collective-permute-start(bf16[192,1536]{1,0:T(8,128)(2,1)S(1)} %copy-done.39), channel_id=1, source_target_pairs={{0,16},{8,24},{16,0},{24,8},{1,17},{9,25},{17,1},{25,9},{2,18},{10... | collective-permute-start | bytes 1769480 | tf_op jit(solution)/shard_map/ppermute | solution.py:636
  202.8 31.6 %collective-permute-start.29 = (bf16[1024,1536]{1,0:T(8,128)(2,1)}, bf16[1024,1536]{1,0:T(8,128)(2,1)S(1)}, u32[]{:S(2)}, u32[]{:S(2)}) collective-permute-start(bf16[1024,1536]{1,0:T(8,128)(2,1)} %get-tuple-element.147.x_ref.refs_0_.refs_1_), channel_id=1, source_target_pairs={{0,4},{4,0},{1,5},{5,1},{2,6},{6,2},{3,7},{7,3},{8,12},{12,8},{9,1... | collective-permute-start | bytes 9437192 | tf_op jit(solution)/shard_map/ppermute | solution.py:636
  202.9 16.5 %collective-permute-start.33 = (bf16[192,1536]{1,0:T(8,128)(2,1)}, bf16[192,1536]{1,0:T(8,128)(2,1)}, u32[]{:S(2)}, u32[]{:S(2)}) collective-permute-start(bf16[192,1536]{1,0:T(8,128)(2,1)} %copy-done.71), channel_id=1, source_target_pairs={{0,16},{8,24},{16,0},{24,8},{1,17},{9,25},{17,1},{25,9},{2,18},{10... | collective-permute-start | bytes 1769480 | tf_op jit(solution)/shard_map/ppermute | solution.py:636
  203.9 30.5 %collective-permute-start.34 = (bf16[192,1536]{1,0:T(8,128)(2,1)}, bf16[192,1536]{1,0:T(8,128)(2,1)}, u32[]{:S(2)}, u32[]{:S(2)}) collective-permute-start(bf16[192,1536]{1,0:T(8,128)(2,1)} %copy-done.72), channel_id=1, source_target_pairs={{0,8},{8,0},{16,24},{24,16},{1,9},{9,1},{17,25},{25,17},{2,10},{10... | collective-permute-start | bytes 1769480 | tf_op jit(solution)/shard_map/ppermute | solution.py:636
  205.3 29.1 %collective-permute-start.30 = (bf16[192,1536]{1,0:T(8,128)(2,1)S(1)}, bf16[192,1536]{1,0:T(8,128)(2,1)}, u32[]{:S(2)}, u32[]{:S(2)}) collective-permute-start(bf16[192,1536]{1,0:T(8,128)(2,1)S(1)} %copy-done.39), channel_id=1, source_target_pairs={{0,8},{8,0},{16,24},{24,16},{1,9},{9,1},{17,25},{25,17},{2,10},{10... | collective-permute-start | bytes 1769480 | tf_op jit(solution)/shard_map/ppermute | solution.py:636
  206.0 28.5 %collective-permute-start.31 = (bf16[192,1536]{1,0:T(8,128)(2,1)}, bf16[192,1536]{1,0:T(8,128)(2,1)}, u32[]{:S(2)}, u32[]{:S(2)}) collective-permute-start(bf16[192,1536]{1,0:T(8,128)(2,1)} %get-tuple-element.141.refs_1_.refs_4_), channel_id=1, source_target_pairs={{0,16},{8,24},{16,0},{24,8},{1,17},{9,25},{17,1},{25,9},{2,18},{10... | collective-permute-start | bytes 1769480 | tf_op jit(solution)/shard_map/ppermute | solution.py:636
  219.4 15.0 %collective-permute-start.32 = (f32[1024,128]{1,0:T(8,128)}, f32[1024,128]{1,0:T(8,128)}, u32[]{:S(2)}, u32[]{:S(2)}) collective-permute-start(f32[1024,128]{1,0:T(8,128)} %get-tuple-element.148.gate_ref.refs_2_), channel_id=1, source_target_pairs={{0,4},{4,0},{1,5},{5,1},{2,6},{6,2},{3,7},{7,3},{8,12},{12,8},{9,1... | collective-permute-start | bytes 1572872 | tf_op jit(solution)/shard_map/ppermute | solution.py:636
  260.6 10.1 %collective-permute-start.36 = (bf16[1024,1536]{1,0:T(8,128)(2,1)}, bf16[1024,1536]{1,0:T(8,128)(2,1)S(1)}, u32[]{:S(2)}, u32[]{:S(2)}) collective-permute-start(bf16[1024,1536]{1,0:T(8,128)(2,1)} %all-gather.9.cloned.1.call-done.refs_0_.refs_1_), channel_id=1, source_target_pairs={{0,4},{4,0},{1,5},{5,1},{2,6},{6,2},{3,7},{7,3},{8,12},{12,8},{9,1... | collective-permute-start | bytes 9437192 | tf_op jit(solution)/shard_map/ppermute | solution.py:636
  261.1 38.9 %collective-permute-start.35 = (bf16[1024,1536]{1,0:T(8,128)(2,1)}, bf16[1024,1536]{1,0:T(8,128)(2,1)}, u32[]{:S(2)}, u32[]{:S(2)}) collective-permute-start(bf16[1024,1536]{1,0:T(8,128)(2,1)} %combine.2), channel_id=1, source_target_pairs={{0,4},{4,0},{1,5},{5,1},{2,6},{6,2},{3,7},{7,3},{8,12},{12,8},{9,1... | collective-permute-start | bytes 9437192 | tf_op jit(solution)/shard_map/ppermute | solution.py:636
  297.5 37.3 %collective-permute-start.37 = (bf16[768,768]{1,0:T(8,128)(2,1)}, bf16[768,768]{1,0:T(8,128)(2,1)S(1)}, u32[]{:S(2)}, u32[]{:S(2)}) collective-permute-start(bf16[768,768]{1,0:T(8,128)(2,1)} %get-tuple-element.167), channel_id=1, source_target_pairs={{0,16},{8,24},{16,0},{24,8},{1,17},{9,25},{17,1},{25,9},{2,18},{10... | collective-permute-start | bytes 3538952 | tf_op jit(solution)/shard_map/ppermute | solution.py:636
  298.6 36.3 %collective-permute-start.38 = (bf16[768,768]{1,0:T(8,128)(2,1)}, bf16[768,768]{1,0:T(8,128)(2,1)}, u32[]{:S(2)}, u32[]{:S(2)}) collective-permute-start(bf16[768,768]{1,0:T(8,128)(2,1)} %get-tuple-element.168), channel_id=1, source_target_pairs={{0,8},{8,0},{16,24},{24,16},{1,9},{9,1},{17,25},{25,17},{2,10},{10... | collective-permute-start | bytes 3538952 | tf_op jit(solution)/shard_map/ppermute | solution.py:636
  305.3 151.9 %reduce-scatter.6.cloned.1.call-start = ((), (), s32[]{:S(2)}) async-start(), calls=%async_computation.6 | async-start | bytes 3932160 | tf_op jit(solution)/shard_map/reduce_scatter | solution.py:923
  334.7 17.4 %collective-permute-start.40 = (f32[1024,128]{1,0:T(8,128)}, f32[1024,128]{1,0:T(8,128)S(1)}, u32[]{:S(2)}, u32[]{:S(2)}) collective-permute-start(f32[1024,128]{1,0:T(8,128)} %get-tuple-element.172), channel_id=1, source_target_pairs={{0,4},{4,0},{1,5},{5,1},{2,6},{6,2},{3,7},{7,3},{8,12},{12,8},{9,1... | collective-permute-start | bytes 1572872 | tf_op jit(solution)/shard_map/ppermute | solution.py:636
  351.7 23.1 %collective-permute-start.39 = (bf16[1024,1536]{1,0:T(8,128)(2,1)}, bf16[1024,1536]{1,0:T(8,128)(2,1)}, u32[]{:S(2)}, u32[]{:S(2)}) collective-permute-start(bf16[1024,1536]{1,0:T(8,128)(2,1)} %convolution_convert_fusion.1), channel_id=1, source_target_pairs={{0,4},{4,0},{1,5},{5,1},{2,6},{6,2},{3,7},{7,3},{8,12},{12,8},{9,1... | collective-permute-start | bytes 9437192 | tf_op jit(solution)/shard_map/ppermute | solution.py:636
  356.5 18.2 %collective-permute-start.41 = (bf16[384,768]{1,0:T(8,128)(2,1)S(1)}, bf16[384,768]{1,0:T(8,128)(2,1)S(1)}, u32[]{:S(2)}, u32[]{:S(2)}) collective-permute-start(bf16[384,768]{1,0:T(8,128)(2,1)S(1)} %add_convert_fusion.11), channel_id=1, source_target_pairs={{0,8},{8,0},{16,24},{24,16},{1,9},{9,1},{17,25},{25,17},{2,10},{10... | collective-permute-start | bytes 1769480 | tf_op jit(solution)/shard_map/ppermute | solution.py:636
  357.1 17.6 %collective-permute-start.42 = (bf16[384,768]{1,0:T(8,128)(2,1)S(1)}, bf16[384,768]{1,0:T(8,128)(2,1)S(1)}, u32[]{:S(2)}, u32[]{:S(2)}) collective-permute-start(bf16[384,768]{1,0:T(8,128)(2,1)S(1)} %add_convert_fusion.10), channel_id=1, source_target_pairs={{0,16},{8,24},{16,0},{24,8},{1,17},{9,25},{17,1},{25,9},{2,18},{10... | collective-permute-start | bytes 1769480 | tf_op jit(solution)/shard_map/ppermute | solution.py:636
  388.7 197.9 %reduce-scatter.8.cloned.1.call-start = ((), (), s32[]{:S(2)}) async-start(), calls=%async_computation.7 | async-start | bytes 3932160 | tf_op jit(solution)/shard_map/reduce_scatter | solution.py:951
  408.2 83.8 %collective-permute-start.46 = (bf16[768,1536]{1,0:T(8,128)(2,1)}, bf16[768,1536]{1,0:T(8,128)(2,1)}, u32[]{:S(2)}, u32[]{:S(2)}) collective-permute-start(bf16[768,1536]{1,0:T(8,128)(2,1)} %get-tuple-element.190), channel_id=1, source_target_pairs={{0,16},{8,24},{16,0},{24,8},{1,17},{9,25},{17,1},{25,9},{2,18},{10... | collective-permute-start | bytes 7077896 | tf_op jit(solution)/shard_map/ppermute | solution.py:636
  409.1 83.0 %collective-permute-start.47 = (bf16[768,1536]{1,0:T(8,128)(2,1)}, bf16[768,1536]{1,0:T(8,128)(2,1)}, u32[]{:S(2)}, u32[]{:S(2)}) collective-permute-start(bf16[768,1536]{1,0:T(8,128)(2,1)} %get-tuple-element.191), channel_id=1, source_target_pairs={{0,8},{8,0},{16,24},{24,16},{1,9},{9,1},{17,25},{25,17},{2,10},{10... | collective-permute-start | bytes 7077896 | tf_op jit(solution)/shard_map/ppermute | solution.py:636
  416.8 33.8 %collective-permute-start.52 = (bf16[1536,768]{1,0:T(8,128)(2,1)}, bf16[1536,768]{1,0:T(8,128)(2,1)}, u32[]{:S(2)}, u32[]{:S(2)}) collective-permute-start(bf16[1536,768]{1,0:T(8,128)(2,1)} %convolution_convert_fusion.3), channel_id=1, source_target_pairs={{0,4},{4,0},{1,5},{5,1},{2,6},{6,2},{3,7},{7,3},{8,12},{12,8},{9,1... | collective-permute-start | bytes 7077896 | tf_op jit(solution)/shard_map/ppermute | solution.py:636
  421.8 24.1 %collective-permute-start.62 = (bf16[192,1536]{1,0:T(8,128)(2,1)}, bf16[192,1536]{1,0:T(8,128)(2,1)S(1)}, u32[]{:S(2)}, u32[]{:S(2)}) collective-permute-start(bf16[192,1536]{1,0:T(8,128)(2,1)} %pad_maximum_fusion.16), channel_id=1, source_target_pairs={{0,4},{4,0},{1,5},{5,1},{2,6},{6,2},{3,7},{7,3},{8,12},{12,8},{9,1... | collective-permute-start | bytes 1769480 | tf_op jit(solution)/shard_map/ppermute | solution.py:636
  454.6 37.4 %collective-permute-start.53 = (bf16[768,384]{1,0:T(8,128)(2,1)}, bf16[768,384]{1,0:T(8,128)(2,1)}, u32[]{:S(2)}, u32[]{:S(2)}) collective-permute-start(bf16[768,384]{1,0:T(8,128)(2,1)} %get-tuple-element.300), channel_id=1, source_target_pairs={{0,16},{8,24},{16,0},{24,8},{1,17},{9,25},{17,1},{25,9},{2,18},{10... | collective-permute-start | bytes 1769480 | tf_op jit(solution)/shard_map/ppermute | solution.py:636
  456.1 35.9 %collective-permute-start.54 = (bf16[768,384]{1,0:T(8,128)(2,1)}, bf16[768,384]{1,0:T(8,128)(2,1)}, u32[]{:S(2)}, u32[]{:S(2)}) collective-permute-start(bf16[768,384]{1,0:T(8,128)(2,1)} %pad_maximum_fusion.14), channel_id=1, source_target_pairs={{0,8},{8,0},{16,24},{24,16},{1,9},{9,1},{17,25},{25,17},{2,10},{10... | collective-permute-start | bytes 1769480 | tf_op jit(solution)/shard_map/ppermute | solution.py:636
  491.9 15.3 %collective-permute-start.43 = (bf16[1536,384]{1,0:T(8,128)(2,1)S(1)}, bf16[1536,384]{1,0:T(8,128)(2,1)S(1)}, u32[]{:S(2)}, u32[]{:S(2)}) collective-permute-start(bf16[1536,384]{1,0:T(8,128)(2,1)S(1)} %get-tuple-element.372), channel_id=1, source_target_pairs={{0,4},{4,0},{1,5},{5,1},{2,6},{6,2},{3,7},{7,3},{8,12},{12,8},{9,1... | collective-permute-start | bytes 3538952 | tf_op jit(solution)/shard_map/ppermute | solution.py:636
  493.2 9.9 %collective-permute-start.55 = (bf16[384,384]{1,0:T(8,128)(2,1)S(1)}, bf16[384,384]{1,0:T(8,128)(2,1)S(1)}, u32[]{:S(2)}, u32[]{:S(2)}) collective-permute-start(bf16[384,384]{1,0:T(8,128)(2,1)S(1)} %get-tuple-element.221), channel_id=1, source_target_pairs={{0,8},{8,0},{16,24},{24,16},{1,9},{9,1},{17,25},{25,17},{2,10},{10... | collective-permute-start | bytes 884744 | tf_op jit(solution)/shard_map/ppermute | solution.py:636
  494.3 9.9 %collective-permute-start.56 = (bf16[384,384]{1,0:T(8,128)(2,1)S(1)}, bf16[384,384]{1,0:T(8,128)(2,1)S(1)}, u32[]{:S(2)}, u32[]{:S(2)}) collective-permute-start(bf16[384,384]{1,0:T(8,128)(2,1)S(1)} %get-tuple-element.222), channel_id=1, source_target_pairs={{0,16},{8,24},{16,0},{24,8},{1,17},{9,25},{17,1},{25,9},{2,18},{10... | collective-permute-start | bytes 884744 | tf_op jit(solution)/shard_map/ppermute | solution.py:636
  498.1 30.3 %collective-permute-start.48 = (bf16[384,1536]{1,0:T(8,128)(2,1)S(1)}, bf16[384,1536]{1,0:T(8,128)(2,1)S(1)}, u32[]{:S(2)}, u32[]{:S(2)}) collective-permute-start(bf16[384,1536]{1,0:T(8,128)(2,1)S(1)} %get-tuple-element.198), channel_id=1, source_target_pairs={{0,8},{8,0},{16,24},{24,16},{1,9},{9,1},{17,25},{25,17},{2,10},{10... | collective-permute-start | bytes 3538952 | tf_op jit(solution)/shard_map/ppermute | solution.py:636
  498.5 31.0 %collective-permute-start.49 = (bf16[384,1536]{1,0:T(8,128)(2,1)S(1)}, bf16[384,1536]{1,0:T(8,128)(2,1)S(1)}, u32[]{:S(2)}, u32[]{:S(2)}) collective-permute-start(bf16[384,1536]{1,0:T(8,128)(2,1)S(1)} %get-tuple-element.199), channel_id=1, source_target_pairs={{0,16},{8,24},{16,0},{24,8},{1,17},{9,25},{17,1},{25,9},{2,18},{10... | collective-permute-start | bytes 3538952 | tf_op jit(solution)/shard_map/ppermute | solution.py:636
  508.5 28.6 %collective-permute-start.44 = (bf16[768,256]{1,0:T(8,128)(2,1)S(1)}, bf16[768,256]{1,0:T(8,128)(2,1)S(1)}, u32[]{:S(2)}, u32[]{:S(2)}) collective-permute-start(bf16[768,256]{1,0:T(8,128)(2,1)S(1)} %get-tuple-element.324), channel_id=1, source_target_pairs={{0,16},{8,24},{16,0},{24,8},{1,17},{9,25},{17,1},{25,9},{2,18},{10... | collective-permute-start | bytes 1179656 | tf_op jit(solution)/shard_map/ppermute | solution.py:636
  510.1 23.5 %collective-permute-start.45 = (bf16[768,128]{1,0:T(8,128)(2,1)S(1)}, bf16[768,128]{1,0:T(8,128)(2,1)S(1)}, u32[]{:S(2)}, u32[]{:S(2)}) collective-permute-start(bf16[768,128]{1,0:T(8,128)(2,1)S(1)} %pad_maximum_fusion.23), channel_id=1, source_target_pairs={{0,8},{8,0},{16,24},{24,16},{1,9},{9,1},{17,25},{25,17},{2,10},{10... | collective-permute-start | bytes 589832 | tf_op jit(solution)/shard_map/ppermute | solution.py:636
  538.6 6.6 %collective-permute-start.50 = (bf16[384,256]{1,0:T(8,128)(2,1)}, bf16[384,256]{1,0:T(8,128)(2,1)}, u32[]{:S(2)}, u32[]{:S(2)}) collective-permute-start(bf16[384,256]{1,0:T(8,128)(2,1)} %add_convert_fusion.17), channel_id=1, source_target_pairs={{0,8},{8,0},{16,24},{24,16},{1,9},{9,1},{17,25},{25,17},{2,10},{10... | collective-permute-start | bytes 589832 | tf_op jit(solution)/shard_map/ppermute | solution.py:636
  542.2 14.4 %collective-permute-start.58 = (bf16[192,3072]{1,0:T(8,128)(2,1)}, bf16[192,3072]{1,0:T(8,128)(2,1)S(1)}, u32[]{:S(2)}, u32[]{:S(2)}) collective-permute-start(bf16[192,3072]{1,0:T(8,128)(2,1)} %pad_maximum_fusion.4), channel_id=1, source_target_pairs={{0,4},{4,0},{1,5},{5,1},{2,6},{6,2},{3,7},{7,3},{8,12},{12,8},{9,1... | collective-permute-start | bytes 3538952 | tf_op jit(solution)/shard_map/ppermute | solution.py:636
  560.7 15.2 %collective-permute-start.61 = (bf16[192,512]{1,0:T(8,128)(2,1)}, bf16[192,512]{1,0:T(8,128)(2,1)}, u32[]{:S(2)}, u32[]{:S(2)}) collective-permute-start(bf16[192,512]{1,0:T(8,128)(2,1)} %get-tuple-element.369), channel_id=1, source_target_pairs={{0,3},{1,0},{2,1},{3,2},{4,7},{5,4},{6,5},{7,6},{8,11},{9,8},{10,9... | collective-permute-start | bytes 589832 | tf_op jit(solution)/shard_map/ppermute | solution.py:1006
  564.5 17.7 %collective-permute-start.60 = (bf16[192,512]{1,0:T(8,128)(2,1)}, bf16[192,512]{1,0:T(8,128)(2,1)}, u32[]{:S(2)}, u32[]{:S(2)}) collective-permute-start(bf16[192,512]{1,0:T(8,128)(2,1)} %get-tuple-element.368), channel_id=1, source_target_pairs={{0,2},{1,3},{2,0},{3,1},{4,6},{5,7},{6,4},{7,5},{8,10},{9,11},{10,... | collective-permute-start | bytes 589832 | tf_op jit(solution)/shard_map/ppermute | solution.py:1006
  564.5 18.7 %collective-permute-start.59 = (bf16[192,512]{1,0:T(8,128)(2,1)}, bf16[192,512]{1,0:T(8,128)(2,1)}, u32[]{:S(2)}, u32[]{:S(2)}) collective-permute-start(bf16[192,512]{1,0:T(8,128)(2,1)} %get-tuple-element.367), channel_id=1, source_target_pairs={{0,1},{1,2},{2,3},{3,0},{4,5},{5,6},{6,7},{7,4},{8,9},{9,10},{10,1... | collective-permute-start | bytes 589832 | tf_op jit(solution)/shard_map/ppermute | solution.py:1006
  (79 other events, 529.3 us)
Sparse Core Ops, SparseCore 0:
  10.2 66.1 all-gather.6
  78.5 29.0 all-gather.12
  109.2 62.6 all-gather.10
  173.9 62.1 all-gather.8
  305.4 60.1 reduce-scatter.3
  388.8 60.9 reduce-scatter.5
  486.8 60.8 reduce-scatter.7

commit v4 on v3

--- a/solution.py
+++ b/solution.py
@@ -82,29 +82,43 @@
         v_ref[g, rows, :] = vals[:, g * HEAD : (g + 1) * HEAD]
     lo = jnp.maximum(i - 2, 0)
     qdoc = qdoc_ref[...]
-    for g in range(kv_heads):
-        qs = jnp.concatenate(heads[g * group : (g + 1) * group], 0)
-
-        def scores(kc, top, g=g, qs=qs):
-            keys = k_ref[g, pl.ds(pl.multiple_of(kc * BLK, BLK), BLK), :]
-            bias = seen(kc, i, kdoc_ref, qdoc, group)
-            s = nt(keys, qs) * ATTN_MULT + jnp.concatenate([bias] * group, 1)
-            s_scr[kc - lo] = s
-            return jnp.maximum(top, jnp.max(s, 0, keepdims=True))
-
-        top = lax.fori_loop(lo, i + 1, scores, jnp.full((1, group * BLK), NEG, F32))
-
-        def mix(kc, carry, g=g, top=top):
-            total, out = carry
-            e = jnp.exp(s_scr[kc - lo] - top)
-            vv = v_ref[g, pl.ds(pl.multiple_of(kc * BLK, BLK), BLK), :]
-            return total + jnp.sum(e, 0, keepdims=True), out + tn(vv, e.astype(BF16))
-
-        total, out = lax.fori_loop(
-            lo, i + 1, mix, (jnp.zeros((1, group * BLK), F32), jnp.zeros((HEAD, group * BLK), F32))
-        )
+    groups = range(kv_heads)
+    queries = [jnp.concatenate(heads[g * group : (g + 1) * group], 0) for g in groups]
+
+    def scores(kc, tops):
+        bias = seen(kc, i, kdoc_ref, qdoc, group)
+        bias = jnp.concatenate([bias] * group, 1)
+        rows = pl.ds(pl.multiple_of(kc * BLK, BLK), BLK)
+        out = []
+        for g in groups:
+            s = nt(k_ref[g, rows, :], queries[g]) * ATTN_MULT + bias
+            s_scr[g, kc - lo] = s
+            out.append(jnp.maximum(tops[g], jnp.max(s, 0, keepdims=True)))
+        return tuple(out)
+
+    start = tuple(jnp.full((1, group * BLK), NEG, F32) for _ in groups)
+    tops = lax.fori_loop(lo, i + 1, scores, start)
+
+    def mix(kc, carry):
+        rows = pl.ds(pl.multiple_of(kc * BLK, BLK), BLK)
+        out = []
+        for g in groups:
+            total, mixed = carry[g]
+            e = jnp.exp(s_scr[g, kc - lo] - tops[g])
+            out.append(
+                (
+                    total + jnp.sum(e, 0, keepdims=True),
+                    mixed + tn(v_ref[g, rows, :], e.astype(BF16)),
+                )
+            )
+        return tuple(out)
+
+    zero = (jnp.zeros((1, group * BLK), F32), jnp.zeros((HEAD, group * BLK), F32))
+    sums = lax.fori_loop(lo, i + 1, mix, tuple(zero for _ in groups))
+    for g in groups:
+        total, out = sums[g]
         out = out / total
-        lse_ref[0, g : g + 1, :] = top + jnp.log(total)
+        lse_ref[0, g : g + 1, :] = tops[g] + jnp.log(total)
         for j in range(group):
             h = g * group + j
             att_ref[:, h * HEAD : (h + 1) * HEAD] = out[:, j * BLK : (j + 1) * BLK].T.astype(BF16)
@@ -146,7 +160,7 @@
             jax.ShapeDtypeStruct((length, q_heads * HEAD), BF16),
             jax.ShapeDtypeStruct((blocks, kv_heads, group * BLK), F32),
         ],
-        scratch_shapes=[pltpu.VMEM((3, BLK, group * BLK), F32)],
+        scratch_shapes=[pltpu.VMEM((kv_heads, 3, BLK, group * BLK), F32)],
         compiler_params=pltpu.CompilerParams(
             dimension_semantics=("arbitrary",), vmem_limit_bytes=VMEM_CAP
         ),
@@ -176,31 +190,36 @@
     lo = jnp.maximum(i - 2, 0)
     qdoc = qdoc_ref[...]
     att = att_ref[...]
-    dq_heads = []
-    for g in range(kv_heads):
+    groups = range(kv_heads)
+    queries, gives, dot_rows, lses = [], [], [], []
+    for g in groups:
         span = range(g * group, (g + 1) * group)
-        qs = jnp.concatenate([q_ref[h] for h in span], 0)
-        dos = jnp.concatenate([do[:, h * HEAD : (h + 1) * HEAD] for h in span], 0)
+        queries.append(jnp.concatenate([q_ref[h] for h in span], 0))
+        gives.append(jnp.concatenate([do[:, h * HEAD : (h + 1) * HEAD] for h in span], 0))
         outs = jnp.concatenate([att[:, h * HEAD : (h + 1) * HEAD] for h in span], 0)
-        dot_row = jnp.sum((dos.astype(F32) * outs.astype(F32)).T, 0, keepdims=True)
-        lse = lse_ref[0, g : g + 1, :]
-
-        def chunk(kc, dq, g=g, qs=qs, dos=dos, dot_row=dot_row, lse=lse):
-            rows = pl.ds(pl.multiple_of(kc * BLK, BLK), BLK)
+        dot_rows.append(
+            jnp.sum((gives[g].astype(F32) * outs.astype(F32)).T, 0, keepdims=True)
+        )
+        lses.append(lse_ref[0, g : g + 1, :])
+
+    def chunk(kc, dqs):
+        rows = pl.ds(pl.multiple_of(kc * BLK, BLK), BLK)
+        bias = seen(kc, i, kdoc_ref, qdoc, group)
+        bias = jnp.concatenate([bias] * group, 1)
+        out = []
+        for g in groups:
             keys = k_ref[g, rows, :]
-            vals = v_ref[g, rows, :]
-            bias = seen(kc, i, kdoc_ref, qdoc, group)
-            s = nt(keys, qs) * ATTN_MULT + jnp.concatenate([bias] * group, 1)
-            prob = jnp.exp(s - lse)
-            dprob = nt(vals, dos)
-            ds = (prob * (dprob - dot_row)).astype(BF16)
-            dv_scr[g, rows, :] += nn(prob.astype(BF16), dos)
-            dk_scr[g, rows, :] += nn(ds, qs)
-            return dq + tn(keys, ds)
-
-        dq = lax.fori_loop(lo, i + 1, chunk, jnp.zeros((HEAD, group * BLK), F32))
-        for j in range(group):
-            dq_heads.append(dq[:, j * BLK : (j + 1) * BLK].T)
+            prob = jnp.exp(nt(keys, queries[g]) * ATTN_MULT + bias - lses[g])
+            dprob = nt(v_ref[g, rows, :], gives[g])
+            ds = (prob * (dprob - dot_rows[g])).astype(BF16)
+            dv_scr[g, rows, :] += nn(prob.astype(BF16), gives[g])
+            dk_scr[g, rows, :] += nn(ds, queries[g])
+            out.append(dqs[g] + tn(keys, ds))
+        return tuple(out)
+
+    zero = jnp.zeros((HEAD, group * BLK), F32)
+    dqs = lax.fori_loop(lo, i + 1, chunk, tuple(zero for _ in groups))
+    dq_heads = [dqs[g][:, j * BLK : (j + 1) * BLK].T for g in groups for j in range(group)]
     rows = pl.ds(pl.multiple_of(i * BLK, BLK), BLK)
     dq_all = jnp.concatenate(dq_heads, 1) * ATTN_MULT
     dq_ref[...] = rope_cols(dq_all, cos_ref[rows, :], -sin_ref[rows, :]).astype(BF16)
@@ -421,6 +440,10 @@
     )(dq, dkv, pack, tokens, gain, ag)
 
 
+def sigmoid(value):
+    return 0.5 * jnp.tanh(0.5 * value) + 0.5
+
+
 def gate_cols(gates, first):
     lane = lax.broadcasted_iota(jnp.int32, gates.shape, 1)
     return [
@@ -436,7 +459,7 @@
     for k in range(2):
         gate = h[:, 256 * k : 256 * k + 128]
         up = h[:, 256 * k + 128 : 256 * k + 256]
-        act = gate * jax.nn.sigmoid(gate) * up
+        act = gate * sigmoid(gate) * up
         gact_ref[:, 128 * k : 128 * k + 128] = (cols[k] * act).astype(BF16)
 
 
@@ -513,52 +536,54 @@
 
 def moe_bwd_kernel(*refs):
     base_ref, g_ref, gate_ref, h_ref = refs[:4]
-    pieces, gug_ref, choice_ref = refs[4:-2], refs[-2], refs[-1]
+    pieces, gug_ref, choice_ref, plain_scr = refs[4:-3], refs[-3], refs[-2], refs[-1]
     p = pl.program_id(1)
-    first = base_ref[0] + 2 * p
-    weights = [piece[...] for piece in pieces]
-    plain = nn(g_ref[...], weights[0] if len(weights) == 1 else jnp.concatenate(weights, 0))
+    first = base_ref[0] + 2 * (p - 1)
+    plain = plain_scr[1 - p % 2]
     cols = gate_cols(gate_ref[...], first)
-
-    @pl.when(p == 0)
-    def _():
-        choice_ref[...] = jnp.zeros_like(choice_ref)
-
     lane = lax.broadcasted_iota(jnp.int32, choice_ref.shape, 1)
     add = jnp.zeros(choice_ref.shape, F32)
     for k in range(2):
         gate = h_ref[:, 256 * k : 256 * k + 128].astype(F32)
         up = h_ref[:, 256 * k + 128 : 256 * k + 256].astype(F32)
         part = plain[:, 128 * k : 128 * k + 128]
-        sig = jax.nn.sigmoid(gate)
+        sig = sigmoid(gate)
         silu = gate * sig
         add = jnp.where(lane == first + k, jnp.sum(silu * up * part, -1, keepdims=True), add)
         act_grad = cols[k] * part
-        gug_ref[:, 256 * k : 256 * k + 128] = (
-            act_grad * up * sig * (1.0 + gate * (1.0 - sig))
-        ).astype(BF16)
+        gug_ref[:, 256 * k : 256 * k + 128] = (act_grad * up * (sig + silu * (1.0 - sig))).astype(
+            BF16
+        )
         gug_ref[:, 256 * k + 128 : 256 * k + 256] = (act_grad * silu).astype(BF16)
-    choice_ref[...] += add
+    choice_ref[...] = jnp.where(p > 1, choice_ref[...], 0.0) + jnp.where(p > 0, add, 0.0)
+    weights = [piece[...] for piece in pieces]
+    plain_scr[p % 2] = nn(g_ref[...], weights[0] if len(weights) == 1 else jnp.concatenate(weights, 0))
 
 
 def moe_bwd(base, g, pieces, gates, h, rows):
     length, width = g.shape
     cols = h.shape[1]
+    steps = cols // 512
+    behind = lambda i, p, b: (i, jnp.maximum(p - 1, 0))
     return pl.pallas_call(
         moe_bwd_kernel,
         grid_spec=pltpu.PrefetchScalarGridSpec(
             num_scalar_prefetch=1,
-            grid=(length // rows, cols // 512),
+            grid=(length // rows, steps + 1),
             in_specs=[
                 pl.BlockSpec((rows, width), lambda i, p, b: (i, 0)),
                 pl.BlockSpec((rows, 128), lambda i, p, b: (i, 0)),
-                pl.BlockSpec((rows, 512), lambda i, p, b: (i, p)),
+                pl.BlockSpec((rows, 512), behind),
             ]
-            + [pl.BlockSpec((w.shape[0], 256), lambda i, p, b: (0, p)) for w in pieces],
+            + [
+                pl.BlockSpec((w.shape[0], 256), lambda i, p, b: (0, jnp.minimum(p, steps - 1)))
+                for w in pieces
+            ],
             out_specs=[
-                pl.BlockSpec((rows, 512), lambda i, p, b: (i, p)),
+                pl.BlockSpec((rows, 512), behind),
                 pl.BlockSpec((rows, 128), lambda i, p, b: (i, 0)),
             ],
+            scratch_shapes=[pltpu.VMEM((2, rows, 256), F32)],
         ),
         out_shape=[
             jax.ShapeDtypeStruct((length, cols), BF16),
@@ -709,16 +734,19 @@
     return swap(left, "q", 2, 4), swap(right, "q", 1, 4)
 
 
-def scatter_second(keep_left, keep_right, from_y, from_x, tie=None):
+def scatter_second(keep_left, keep_right, from_y, from_x):
     n = keep_left.shape[0] // 2
     give_x = (keep_left[n:].astype(F32) + from_y[:n].astype(F32)).astype(BF16)
     give_y = (keep_right[n:].astype(F32) + from_x[:n].astype(F32)).astype(BF16)
     give_x, give_y = lax.optimization_barrier((give_x, give_y))
-    left = swap(give_x, "q", 1, 4)
-    right = swap(give_y, "q", 2, 4)
-    others = () if tie is None else tie(left, right)
+    arrived = swap(give_x, "q", 1, 4), swap(give_y, "q", 2, 4)
+    return arrived, (give_x, give_y)
+
+
+def scatter_last(keep_left, keep_right, from_y, from_x, arrived, *others):
+    n = keep_left.shape[0] // 2
     keep_left, keep_right, from_y, from_x, left, right = all_after(
-        (keep_left, keep_right, from_y, from_x, left, right), *others
+        (keep_left, keep_right, from_y, from_x, *arrived), *others
     )
     return (
         (keep_left[:n].astype(F32) + from_y[n:].astype(F32) + left.astype(F32)).astype(BF16),
@@ -803,6 +831,7 @@
         [w_query, key_weight, value_weight, router, attn_gain[:, None], moe_gain[:, None], pad], 1
     )
     pack_pair = to_halves(*column_halves(after(pack, in_gave, in_kept), c), c)
+    pack_pair = all_after(pack_pair, *in_pair)
     pack_first = gather_first(*pack_pair, quads)
     pack_rest = gather_rest(*pack_pair, quads)
     pack_half = gather_join(
@@ -871,7 +900,7 @@
         base, x_own, in_full, gates, length, 100
     )
     x_other = after(x_other, gact_own, *out_rest)
-    out_diag = all_after(gather_diagonal(out_got, quads), gact_own)
+    out_diag = gather_diagonal(all_after(out_got, gact_own), quads)
     out_full = gather_pieces(*out_src, out_got, out_rest, out_diag, quads)
     hid_other, gact_other = moe_fwd(base, x_other, in_full, gates_other, length, 1)
     comb_give = combine(gact_other, out_full, length // 2)
@@ -902,24 +931,11 @@
     back_own = nt(gug_late, in_full).astype(BF16)
     gates_c = gates * choice
     logit_grad = (gates_c - gates * jnp.sum(gates_c, -1, keepdims=True)).astype(BF16)
-    def middle_back(*arrived):
-        return back_mid(
-            m.astype(jnp.int32).reshape(1), back_own, back_recv, logit_grad, pack, small_at,
-            after(middle, moe_branch, *arrived), moe_g, cot_own, wo_rows, mp,
-        )
-
-    made = []
-
-    def tie(left, right):
-        made.extend(middle_back(left, right))
-        return (made[0],)
-
-    if quads == 4:
-        out_sum = scatter_second(*out_keep, *out_move, tie)
-    else:
-        out_sum = scatter_plain(*out_keep)
-        made.extend(middle_back())
-    ag, p_part = made
+    out_late = scatter_second(*out_keep, *out_move)[0] if quads == 4 else ()
+    ag, p_part = back_mid(
+        m.astype(jnp.int32).reshape(1), back_own, back_recv, logit_grad, pack, small_at,
+        after(middle, moe_branch, *out_late), moe_g, cot_own, wo_rows, mp,
+    )
     attended_grad = lax.psum_scatter(p_part, "mp", scatter_dimension=0, tiled=False)
 
     gugs = all_after((gug_own, gug_other), ag)
@@ -940,34 +956,43 @@
     if quads == 4:
         wo_keep = (cut(wo_part, KEEP_LEFT), cut(wo_part, KEEP_RIGHT))
         wo_move = scatter_first(cut(wo_part, SEND_LEFT), cut(wo_part, SEND_RIGHT))
-    layer_out = (
-        lax.dynamic_slice_in_dim(middle, m * (length // mp), length // mp, 0) + RESID * after(moe_branch, ag)
-    ).astype(BF16)
-
     dq, dkv = attn_bwd(
         attended_grad, q_r, k_r, v_r, attended, lse, cosine, sine, doc_col, doc_row
     )
     end_part = back_end(dq, dkv, pack, tok_all, attn_g, ag)
     grad_tokens = lax.psum_scatter(end_part, "mp", scatter_dimension=0, tiled=True).astype(F32)
 
-    dq_late, dkv_late = after(dq, end_part), after(dkv, end_part)
+    layer_out = (
+        lax.dynamic_slice_in_dim(middle, m * (length // mp), length // mp, 0) + RESID * after(moe_branch, end_part)
+    ).astype(BF16)
+
+    given = (end_part,)
+    if quads == 4:
+        in_move = all_after(in_move, end_part)
+        in_late, given = scatter_second(*in_keep, *in_move)
+        wo_move = all_after(wo_move, *given)
+        wo_late, _ = scatter_second(*wo_keep, *wo_move)
+    dq_late, dkv_late = after(dq, *given), after(dkv, *given)
     part = jnp.concatenate(
-        [tn(normed_a, dq_late), tn(normed_a, dkv_late), tn(normed_m, logit_grad)], 1
+        [tn(normed_a, dq_late), tn(normed_a, dkv_late), tn(normed_m, after(logit_grad, *given))], 1
     ).astype(BF16)
     mine, give = column_halves(part, c)
     pair = (mine.astype(F32) + swap(give, "c", 1, 2).astype(F32)).astype(BF16)
     if quads == 4:
-        in_sum = scatter_second(*in_keep, *all_after(in_move, end_part))
-        wo_sum = scatter_second(*wo_keep, *all_after(wo_move, end_part))
         pair_keep = (cut(pair, KEEP_LEFT), cut(pair, KEEP_RIGHT))
         pair_move = scatter_first(cut(pair, SEND_LEFT), cut(pair, SEND_RIGHT))
-        *pair_move, in_left, in_right = lax.optimization_barrier((*pair_move, *in_sum))
-        in_sum = (in_left, in_right)
-        pair_sum = scatter_second(*pair_keep, *pair_move)
-        late_sum = (*wo_sum, *pair_sum)
+        *pair_move, in_left, in_right = lax.optimization_barrier((*pair_move, *in_late))
+        in_late = (in_left, in_right)
+        pair_late, _ = scatter_second(*pair_keep, *pair_move)
+        in_sum = scatter_last(*in_keep, *in_move, in_late)
+        wo_sum = scatter_last(*wo_keep, *wo_move, wo_late)
+        pair_sum = scatter_last(*pair_keep, *pair_move, pair_late)
+        out_sum = scatter_last(*out_keep, *out_move, out_late, end_part)
     else:
-        in_sum, wo_sum, pair_sum = (scatter_plain(v) for v in (in_keep[0], wo_part, pair))
-        late_sum = (*wo_sum, *pair_sum)
+        in_sum, wo_sum, pair_sum, out_sum = (
+            scatter_plain(v) for v in (in_keep[0], wo_part, pair, out_keep[0])
+        )
+    late_sum = (*wo_sum, *pair_sum)
     late_mine, late_other = from_halves(late_sum, rows, c)
     wo_cols_here = wo_part.shape[1]
     wo_own_rows = jnp.concatenate(
@@ -982,7 +1007,7 @@
     router_part = sums[:, qkv_cols : qkv_cols + experts]
 
     in_mine, in_other = from_halves(in_sum, rows, c)
-    out_mine, out_other = from_halves(all_after(out_sum, ag), rows, c)
+    out_mine, out_other = from_halves(out_sum, rows, c)
     grad_in = jnp.concatenate(in_order(in_mine, in_other, c), 1).astype(F32)
     grad_out = jnp.concatenate(in_order(out_mine, out_other, c), 1).astype(F32)
 

time: 603 us -> 584 us (0.968)
  waiting for transfers between devices: 125 us -> 117 us
  Pallas kernels: 213 us -> 206 us
    ppermute x60, waiting for transfers between devices: 105 us -> 72.5 us  [swap(): return lax.ppermute(value, axis, [(i, i ^ bit) for i in range(size)])]
    reduce_scatter x1, waiting for transfers between devices: 0.02 us -> 8.86 us  [body(): lax.psum_scatter(p_part, 'mp', scatter_dimension=0, tiled=False)]
    all_gather x1, waiting for transfers between devices: 0.57 us -> 8.3 us  [body(): wo_cols = lax.all_gather(after(wo_pad, pack), 'mp', axis=0, tiled=False)]
    all_gather x1, waiting for transfers between devices: 14.7 us -> 22.1 us  [body(): tok_all = lax.all_gather(tok_own, 'mp', axis=0, tiled=True)]
    unnamed x169 -> x157, local copies, waits for them, and re-layouts: 31.7 us -> 30.7 us
  transfers between devices with their start and end apart: 70 -> 70, of which waited for: 22 -> 20; matrix products, arithmetic and copies ran while one was open for 30% -> 29% of each run, Pallas kernels for 33% -> 33%
where the time goes in v4:
time: 584 us; the launch traced here: 578 us
  Pallas kernels  206 us (35%)
  waiting for transfers between devices  117 us (20%)
  other arithmetic  82.5 us (14%)
  local copies, waits for them, and re-layouts  57.9 us (10%)
  starting transfers between devices  53.9 us (9%)
  matrix products  44.7 us (8%)
  between operations  15.7 us (3%)
    ppermute x60, waiting for transfers between devices, swap(): return lax.ppermute(value, axis, [(i, i ^ bit) for i in range(size)])  72.5 us
    pallas_call x3, Pallas kernels, weight_grad(): pl.pallas_call(functools.partial(segment_kernel, count=count), grid=(coun...  56.5 us
    ppermute x60, starting transfers between devices, swap(): return lax.ppermute(value, axis, [(i, i ^ bit) for i in range(size)])  48.7 us
    unnamed x157, local copies, waits for them, and re-layouts  30.7 us
    pallas_call x2, Pallas kernels, moe_fwd(): pl.pallas_call(moe_fwd_kernel, grid_spec=pltpu.PrefetchScalarGridSpec(num...  30.2 us
    dot_general x2, matrix products, nt(): lax.dot_general(left, right, (((1,), (1,)), ((), ())), preferred_element_...  29.5 us
    pallas_call x2, Pallas kernels, moe_bwd(): pl.pallas_call(moe_bwd_kernel, grid_spec=pltpu.PrefetchScalarGridSpec(num...  27.7 us
    all_gather x1, waiting for transfers between devices, body(): tok_all = lax.all_gather(tok_own, 'mp', axis=0, tiled=True)  22.1 us
  transfers between devices with their start and end apart: 70, of which 20 were waited for; matrix products, arithmetic and copies ran while one was open for 29% of the time, Pallas kernels for 33%

profile of v4, /device:TPU:0, one launch (start us, length us, event | category | flops | bytes accessed | tf_op | source)
XLA Modules:
  0.0 577.7 jit_solution(17662212342725993450)
XLA Ops:
  7.2 3.3 constant_dynamic-slice_fusion.18
  10.5 1.7 reshape.79
  18.3 2.7 collective-permute-start.2
  21.7 2.0 collective-permute-start.5
  25.7 2.0 collective-permute-start.4
  28.4 2.0 collective-permute-start.6
  31.1 2.7 collective-permute-done.4
  41.0 1.8 broadcast_select_fusion.8
  44.5 1.8 collective-permute-start.9
  48.6 3.7 negate_select_fusion
  53.4 2.5 bitcast_select_fusion
  57.8 22.1 %all-gather.7.cloned.1.call-done.tok_ref = bf16[1024,1536]{1,0:T(8,128)(2,1)} async-done(((bf16[256,1536]{1,0:T(8,128)(2,1)}), bf16[1024,1536]{1,0:T(8,128)(2,1)}) %all-gather.7.cloned.1.call-update) | async-done | bytes 3145744 | tf_op jit(solution)/shard_map/all_gather | solution.py:820
  79.9 17.3 %attn_fwd.1 = (bf16[1024,1536]{1,0:T(8,128)(2,1)}, bf16[6,1024,64]{2,1,0:T(8,128)(2,1)}, bf16[2,1024,64]{2,1,0:T(8,128)(2,1)}, bf16[2,1024,64]{2,1,0:T(8,128)(2,...) custom-call(bf16[1024,1536]{1,0:T(8,128)(2,1)} %all-gather.7.cloned.1.call-done.tok_ref, ...), custom_call_target="tpu_custom_call" | custom-call | flops 44291848 | bytes 82575 | tf_op jit(solution)/shard_map/attn_fwd/pallas_call | solution.py:135
  102.8 8.3 %all-gather.13.cloned.1.call-done = bf16[768,704]{1,0:T(8,128)(2,1)} async-done(((bf16[192,704]{1,0:T(8,128)(2,1)}), bf16[768,704]{1,0:T(8,128)(2,1)}) %all-gather.13.cloned.1.call-update) | async-done | bytes 1081360 | tf_op jit(solution)/shard_map/all_gather | solution.py:865
  114.5 13.3 %collective-permute-done.14 = bf16[192,3072]{1,0:T(8,128)(2,1)} collective-permute-done((bf16[192,3072]{1,0:T(8,128)(2,1)}, bf16[192,3072]{1,0:T(8,128)(2,1)}, u32[]{:S(2)}, u32[]{:S(2)}) %collective-permute-start.14) | collective-permute-done | bytes 1179680 | tf_op jit(solution)/shard_map/ppermute | solution.py:661
  133.2 8.9 %collective-permute-done.17 = bf16[192,768]{1,0:T(8,128)(2,1)S(1)} collective-permute-done((bf16[192,768]{1,0:T(8,128)(2,1)S(1)}, bf16[192,768]{1,0:T(8,128)(2,1)S(1)}, u32[]{:S(2)}, u32[]{:S(2)}) %collective-permute-start.17) | collective-permute-done | bytes 294944 | tf_op jit(solution)/shard_map/ppermute | solution.py:661
  145.4 2.4 constant_dynamic-update-slice_fusion.13
  147.8 2.4 constant_dynamic-update-slice_fusion.12
  150.2 2.4 constant_dynamic-update-slice_fusion.11
  152.6 2.5 constant_dynamic-update-slice_fusion.10
  155.0 2.4 constant_dynamic-update-slice_fusion.9
  160.2 2.4 constant_dynamic-update-slice_fusion.8.w_ref
  162.5 4.3 collective-permute-done.23
  170.5 2.6 pad_maximum_fusion.wo_ref
  173.0 10.9 %collective-permute-done.22.refs_8_.refs_11_ = bf16[192,1536]{1,0:T(8,128)(2,1)S(1)} collective-permute-done((bf16[192,1536]{1,0:T(8,128)(2,1)S(1)}, bf16[192,1536]{1,0:T(8,128)(2,1)S(1)}, u32[]{:S(2)}, u32[]{:S(2)}) %collective-permute-start.22) | collective-permute-done | bytes 589856 | tf_op jit(solution)/shard_map/ppermute | solution.py:661
  184.0 13.4 %mid_fwd.1 = (f32[1024,1536]{1,0:T(8,128)}, bf16[1024,1536]{1,0:T(8,128)(2,1)}, f32[1024,128]{1,0:T(8,128)}, bf16[1024,1536]{1,0:T(8,128)(2,1)}) custom-call(bf16[4,1024,384]{2,1,0:T(8,128)(2,1)} %bitcast.55, bf16[1536,1536]{1,0:T(8,128)(2,1)} %pad_maximum_fusion.wo_ref, bf16[1024,1536]{1,0:T(8,128)(2,1)} %all-gather.7.cloned.1.call-done.tok_ref, ...), custom_call_target="tpu_custom_call" | custom-call | flops 4831838208 | bytes 20447232 | tf_op jit(solution)/shard_map/mid_fwd/pallas_call | solution.py:309
  200.0 15.1 %moe_fwd.2 = (bf16[1024,3072]{1,0:T(8,128)(2,1)}, bf16[1024,1536]{1,0:T(8,128)(2,1)}) custom-call(s32[1]{0:T(128)} %bitcast.9.base_ref.refs_0_, bf16[1024,1536]{1,0:T(8,128)(2,1)} %get-tuple-element.150.x_ref.refs_0_.refs_1_, bf16[1536,3072]{1,0:T(8,128)(2,1)} %constant_dynamic-update-slice_fusion.8.w_ref, f32[1024,128]{1,0:T(8,128)} %get-tuple-element.151.gate_ref.refs_2_), custom_call_target="tpu_custom_call" | custom-call | flops 96636768 | bytes 314572 | tf_op jit(solution)/shard_map/moe_fwd/pallas_call | solution.py:469
  218.3 15.1 %moe_fwd.3 = (bf16[1024,3072]{1,0:T(8,128)(2,1)}, bf16[1024,1536]{1,0:T(8,128)(2,1)}) custom-call(s32[1]{0:T(128)} %bitcast.9.base_ref.refs_0_, bf16[1024,1536]{1,0:T(8,128)(2,1)} %copy-done.1, bf16[1536,3072]{1,0:T(8,128)(2,1)} %constant_dynamic-update-slice_fusion.8.w_ref, f32[1024,128]{1,0:T(8,128)} %collective-permute-done.32.gate_ref.refs_2_), custom_call_target="tpu_custom_call" | custom-call | flops 9663676416 | bytes 31457280 | tf_op jit(solution)/shard_map/moe_fwd/pallas_call | solution.py:469
  234.3 9.6 %combine.2 = bf16[1024,1536]{1,0:T(8,128)(2,1)} custom-call(bf16[1024,1536]{1,0:T(8,128)(2,1)} %get-tuple-element.162.refs_0_.refs_5_, bf16[192,1536]{1,0:T(8,128)(2,1)} %get-tuple-element.144.refs_1_.refs_4_, bf16[192,1536]{1,0:T(8,128)(2,1)} %get-tuple-element.145.refs_2_.refs_5_, bf16[192,1536]{1,0:T(8,128)(2,1)} %copy-done.63, ...), custom_call_target="tpu_custom_call" | custom-call | flops 4831838208 | bytes 11010048 | tf_op jit(solution)/shard_map/combine/pallas_call | solution.py:517
  244.4 9.6 %combine.3 = bf16[1024,1536]{1,0:T(8,128)(2,1)} custom-call(bf16[1024,1536]{1,0:T(8,128)(2,1)} %get-tuple-element.161.refs_0_.refs_4_, bf16[192,1536]{1,0:T(8,128)(2,1)} %get-tuple-element.144.refs_1_.refs_4_, bf16[192,1536]{1,0:T(8,128)(2,1)} %get-tuple-element.145.refs_2_.refs_5_, bf16[192,1536]{1,0:T(8,128)(2,1)} %copy-done.63, ...), custom_call_target="tpu_custom_call" | custom-call | flops 4831838208 | bytes 11010048 | tf_op jit(solution)/shard_map/combine/pallas_call | solution.py:517
  254.0 1.7 copy-done.3
  255.7 25.0 %weight_grad.3 = (bf16[768,768]{1,0:T(8,128)(2,1)}, bf16[768,768]{1,0:T(8,128)(2,1)}, bf16[768,768]{1,0:T(8,128)(2,1)}, bf16[768,768]{1,0:T(8,128)(2,1)}) custom-call(bf16[1024,1536]{1,0:T(8,128)(2,1)} %all-gather.9.cloned.1.call-done.refs_0_.refs_1_, bf16[1024,1536]{1,0:T(8,128)(2,1)} %all-gather.9.cloned.1.call-done.refs_0_.refs_1_, ...), custom_call_target="tpu_custom_call" | custom-call | flops 96636768 | bytes 125829 | tf_op jit(solution)/shard_map/weight_grad/pallas_call | solution.py:641
  283.3 5.4 add_convert_fusion
  288.7 14.0 %moe_bwd.2 = (bf16[1024,3072]{1,0:T(8,128)(2,1)}, f32[1024,128]{1,0:T(8,128)}) custom-call(s32[1]{0:T(128)} %bitcast.9.base_ref.refs_0_, bf16[1024,1536]{1,0:T(8,128)(2,1)} %all-gather.9.cloned.1.call-done.refs_0_.refs_1_, f32[1024,128]{1,0:T(8,128)} %get-tuple-element.151.gate_ref.refs_2_, bf16[1024,3072]{1,0:T(8,128)(2,1)} %get-tuple-element.165.refs_3_, ...), custom_call_target="tpu_custom_call" | custom-call | flops 4831838208 | bytes 25165824 | tf_op jit(solution)/shard_map/moe_bwd/pallas_call | solution.py:568
  302.7 13.7 %moe_bwd.3 = (bf16[1024,3072]{1,0:T(8,128)(2,1)}, f32[1024,128]{1,0:T(8,128)}) custom-call(s32[1]{0:T(128)} %bitcast.9.base_ref.refs_0_, bf16[1024,1536]{1,0:T(8,128)(2,1)} %copy-done.3, f32[1024,128]{1,0:T(8,128)} %collective-permute-done.32.gate_ref.refs_2_, bf16[1024,3072]{1,0:T(8,128)(2,1)} %get-tuple-element.168.refs_3_, ...), custom_call_target="tpu_custom_call" | custom-call | flops 4831838208 | bytes 25165824 | tf_op jit(solution)/shard_map/moe_bwd/pallas_call | solution.py:568
  317.5 15.8 %convolution_convert_fusion.1 = bf16[1024,1536]{1,0:T(8,128)(2,1)} fusion(bf16[1024,3072]{1,0:T(8,128)(2,1)} %get-tuple-element.194.refs_5_, bf16[1536,3072]{1,0:T(8,128)(2,1)} %constant_dynamic-update-slice_fusion.8.w_ref), kind=kOutput, calls=%fused_computation.4 | convolution fusion | flops 9665249280 | bytes 18874368 | tf_op jit(solution)/shard_map/dot_general | solution.py:24
  335.0 1.8 add_convert_fusion.11
  340.1 13.7 %convolution_convert_fusion.back_ref = bf16[1024,1536]{1,0:T(8,128)(2,1)} fusion(bf16[1024,3072]{1,0:T(8,128)(2,1)S(1)} %copy-done.2, bf16[1536,3072]{1,0:T(8,128)(2,1)} %constant_dynamic-update-slice_fusion.8.w_ref), kind=kOutput, calls=%fused_computation.3 | convolution fusion | flops 9665249280 | bytes 18874368 | tf_op jit(solution)/shard_map/dot_general | solution.py:24
  353.8 2.5 convert_element_type.321
  356.3 13.8 %back_mid.1 = (bf16[1024,1536]{1,0:T(8,128)(2,1)}, bf16[4,1024,384]{2,1,0:T(8,128)(2,1)}) custom-call(s32[1]{0:T(128)} %bitcast.11.own_ref, bf16[1024,1536]{1,0:T(8,128)(2,1)} %convolution_convert_fusion.back_ref, bf16[1024,1536]{1,0:T(8,128)(2,1)} %collective-permute-done.39.recv_ref, bf16[1024,128]{1,0:T(8,128)(2,1)} %subtract_convert_fusion.lg_ref, ...), custom_call_target="tpu_custom_call" | custom-call | flops 4831838208 | bytes 23592960 | tf_op jit(solution)/shard_map/back_mid/pallas_call | solution.py:370
  370.2 15.9 %weight_grad.4 = (bf16[768,1536]{1,0:T(8,128)(2,1)}, bf16[768,1536]{1,0:T(8,128)(2,1)}) custom-call(bf16[1024,1536]{1,0:T(8,128)(2,1)} %get-tuple-element.150.x_ref.refs_0_.refs_1_, bf16[1024,1536]{1,0:T(8,128)(2,1)} %get-tuple-element.150.x_ref.refs_0_.refs_1_, bf16[1024,1536]{1,0:T(8,128)(2,1)} %copy-done.1, bf16[1024,1536]{1,0:T(8,128)(2,1)} %copy-done.1, ...), custom_call_target="tpu_custom_call" | custom-call | flops 96636768 | bytes 188743 | tf_op jit(solution)/shard_map/weight_grad/pallas_call | solution.py:641
  386.1 6.0 %convolution_convert_fusion.3 = bf16[1536,768]{1,0:T(8,128)(2,1)} fusion(bf16[1024,1536]{1,0:T(8,128)(2,1)} %get-tuple-element.186.ag_ref, pred[]{:T(512)S(6)} %eq.14, bf16[1024,1536]{1,0:T(8,128)(2,1)S(1)} %copy-done.11), kind=kOutput, calls=%fused_computation.6 | convolution fusion | flops 2417885184 | bytes 8650753 | tf_op jit(solution)/shard_map/dot_general | solution.py:28
  395.8 3.9 convolution_convert_fusion.2
  399.7 15.5 %weight_grad.5 = (bf16[768,1536]{1,0:T(8,128)(2,1)}, bf16[768,1536]{1,0:T(8,128)(2,1)}) custom-call(bf16[1024,1536]{1,0:T(8,128)(2,1)} %get-tuple-element.150.x_ref.refs_0_.refs_1_, bf16[1024,1536]{1,0:T(8,128)(2,1)} %get-tuple-element.150.x_ref.refs_0_.refs_1_, bf16[1024,1536]{1,0:T(8,128)(2,1)} %copy-done.1, bf16[1024,1536]{1,0:T(8,128)(2,1)} %copy-done.1, ...), custom_call_target="tpu_custom_call" | custom-call | flops 96636768 | bytes 188743 | tf_op jit(solution)/shard_map/weight_grad/pallas_call | solution.py:641
  415.2 3.0 add_convert_fusion.1
  422.2 8.9 %reduce-scatter.6.cloned.1.call-done = bf16[1,1024,384]{2,1,0:T(8,128)(2,1)} async-done(((bf16[4,1024,384]{2,1,0:T(8,128)(2,1)}), bf16[1,1024,384]{2,1,0:T(8,128)(2,1)}) %reduce-scatter.6.cloned.1.call-update) | async-done | bytes 786448 | tf_op jit(solution)/shard_map/reduce_scatter | solution.py:939
  431.0 19.3 %attn_bwd.1 = (bf16[1024,384]{1,0:T(8,128)(2,1)}, bf16[1024,256]{1,0:T(8,128)(2,1)}) custom-call(bf16[1024,384]{1,0:T(8,128)(2,1)} %bitcast.56, bf16[6,1024,64]{2,1,0:T(8,128)(2,1)} %get-tuple-element.180.q_ref, bf16[2,1024,64]{2,1,0:T(8,128)(2,1)} %get-tuple-element.181.k_ref, bf16[2,1024,64]{2,1,0:T(8,128)(2,1)} %get-tuple-element.182.v_ref, ...), custom_call_target="tpu_custom_call" | custom-call | flops 6039797760 | bytes 3145728 | tf_op jit(solution)/shard_map/attn_bwd/pallas_call | solution.py:243
  450.3 8.9 %back_end.1 = bf16[1024,1536]{1,0:T(8,128)(2,1)} custom-call(bf16[1024,384]{1,0:T(8,128)(2,1)} %get-tuple-element.201.dq_ref, bf16[1024,256]{1,0:T(8,128)(2,1)} %get-tuple-element.202.dkv_ref, bf16[1536,768]{1,0:T(8,128)(2,1)} %pad_maximum_fusion.1.w_ref.small_ref, bf16[1024,1536]{1,0:T(8,128)(2,1)} %all-gather.7.cloned.1.call-done.tok_ref, ...), custom_call_target="tpu_custom_call" | custom-call | flops 2013265920 | bytes 11403264 | tf_op jit(solution)/shard_map/back_end/pallas_call | solution.py:418
  459.3 4.5 add_convert_fusion.5
  469.0 3.2 broadcast_select_fusion.7
  472.2 1.7 add_convert_fusion.7
  479.4 18.5 %collective-permute-done.55 = bf16[384,384]{1,0:T(8,128)(2,1)S(1)} collective-permute-done((bf16[384,384]{1,0:T(8,128)(2,1)S(1)}, bf16[384,384]{1,0:T(8,128)(2,1)S(1)}, u32[]{:S(2)}, u32[]{:S(2)}) %collective-permute-start.55) | collective-permute-done | bytes 294944 | tf_op jit(solution)/shard_map/ppermute | solution.py:661
  504.1 2.1 add_convert_fusion.4
  509.2 1.8 maximum_convert_fusion.1
  511.7 2.6 collective-permute-done.47
  514.3 2.7 collective-permute-done.46
  521.5 2.1 add_convert_fusion.2
  525.2 2.1 add_convert_fusion.3
  532.8 2.7 multiply_reduce_fusion.1
  542.7 2.6 collective-permute-start.61
  545.3 2.0 collective-permute-start.59
  548.9 3.3 concatenate.184
  553.1 4.6 maximum_convert_fusion
  558.8 4.7 collective-permute-done.60
  (383 shorter events, 120.8 us)
Async XLA Ops:
  7.2 72.7 %all-gather.7.cloned.1.call-start = ((), (), s32[]{:S(2)}) async-start(), calls=%async_computation.3 | async-start | bytes 3932160 | tf_op jit(solution)/shard_map/all_gather | solution.py:820
  12.2 4.6 collective-permute-start.1
  13.8 97.3 %all-gather.13.cloned.1.call-start = ((), (), s32[]{:S(2)}) async-start(), calls=%async_computation.9 | async-start | bytes 1474560 | tf_op jit(solution)/shard_map/all_gather | solution.py:865
  18.3 7.4 %collective-permute-start.2 = (bf16[192,384]{1,0:T(8,128)(2,1)S(1)}, bf16[192,384]{1,0:T(8,128)(2,1)S(1)}, u32[]{:S(2)}, u32[]{:S(2)}) collective-permute-start(bf16[192,384]{1,0:T(8,128)(2,1)S(1)} %get-tuple-element.127), channel_id=1, source_target_pairs={{0,8},{8,0},{16,24},{24,16},{1,9},{9,1},{17,25},{25,17},{2,10},{10... | collective-permute-start | bytes 442376 | tf_op jit(solution)/shard_map/ppermute | solution.py:661
  21.7 8.8 %collective-permute-start.3 = (bf16[192,384]{1,0:T(8,128)(2,1)S(1)}, bf16[192,384]{1,0:T(8,128)(2,1)S(1)}, u32[]{:S(2)}, u32[]{:S(2)}) collective-permute-start(bf16[192,384]{1,0:T(8,128)(2,1)S(1)} %get-tuple-element.128), channel_id=1, source_target_pairs={{0,8},{8,0},{16,24},{24,16},{1,9},{9,1},{17,25},{25,17},{2,10},{10... | collective-permute-start | bytes 442376 | tf_op jit(solution)/shard_map/ppermute | solution.py:661
  21.7 6.7 %collective-permute-start.5 = (bf16[192,384]{1,0:T(8,128)(2,1)S(1)}, bf16[192,384]{1,0:T(8,128)(2,1)S(1)}, u32[]{:S(2)}, u32[]{:S(2)}) collective-permute-start(bf16[192,384]{1,0:T(8,128)(2,1)S(1)} %get-tuple-element.128), channel_id=1, source_target_pairs={{0,16},{8,24},{16,0},{24,8},{1,17},{9,25},{17,1},{25,9},{2,18},{10... | collective-permute-start | bytes 442376 | tf_op jit(solution)/shard_map/ppermute | solution.py:661
  23.7 11.5 %collective-permute-start.7 = (bf16[192,384]{1,0:T(8,128)(2,1)S(1)}, bf16[192,384]{1,0:T(8,128)(2,1)S(1)}, u32[]{:S(2)}, u32[]{:S(2)}) collective-permute-start(bf16[192,384]{1,0:T(8,128)(2,1)S(1)} %get-tuple-element.127), channel_id=1, source_target_pairs={{0,16},{8,24},{16,0},{24,8},{1,17},{9,25},{17,1},{25,9},{2,18},{10... | collective-permute-start | bytes 442376 | tf_op jit(solution)/shard_map/ppermute | solution.py:661
  25.7 8.2 %collective-permute-start.4 = (bf16[192,384]{1,0:T(8,128)(2,1)S(1)}, bf16[192,384]{1,0:T(8,128)(2,1)S(1)}, u32[]{:S(2)}, u32[]{:S(2)}) collective-permute-start(bf16[192,384]{1,0:T(8,128)(2,1)S(1)} %collective-permute-done.2), channel_id=1, source_target_pairs={{0,16},{8,24},{16,0},{24,8},{1,17},{9,25},{17,1},{25,9},{2,18},{10... | collective-permute-start | bytes 442376 | tf_op jit(solution)/shard_map/ppermute | solution.py:661
  28.4 6.1 %collective-permute-start.6 = (bf16[192,384]{1,0:T(8,128)(2,1)S(1)}, bf16[192,384]{1,0:T(8,128)(2,1)S(1)}, u32[]{:S(2)}, u32[]{:S(2)}) collective-permute-start(bf16[192,384]{1,0:T(8,128)(2,1)S(1)} %collective-permute-done.5), channel_id=1, source_target_pairs={{0,8},{8,0},{16,24},{24,16},{1,9},{9,1},{17,25},{25,17},{2,10},{10... | collective-permute-start | bytes 442376 | tf_op jit(solution)/shard_map/ppermute | solution.py:661
  40.5 13.0 %collective-permute-start.13 = (bf16[192,1536]{1,0:T(8,128)(2,1)}, bf16[192,1536]{1,0:T(8,128)(2,1)}, u32[]{:S(2)}, u32[]{:S(2)}) collective-permute-start(bf16[192,1536]{1,0:T(8,128)(2,1)} %bitcast.43), channel_id=1, source_target_pairs={{0,4},{4,0},{1,5},{5,1},{2,6},{6,2},{3,7},{7,3},{8,12},{12,8},{9,1... | collective-permute-start | bytes 1769480 | tf_op jit(solution)/shard_map/ppermute | solution.py:661
  44.5 139.5 %all-gather.11.cloned.1.call-start = ((), (), s32[]{:S(2)}) async-start(), calls=%async_computation.8 | async-start | bytes 3932160 | tf_op jit(solution)/shard_map/all_gather | solution.py:886
  44.5 52.7 %collective-permute-start.9 = (bf16[192,3072]{1,0:T(8,128)(2,1)S(1)}, bf16[192,3072]{1,0:T(8,128)(2,1)}, u32[]{:S(2)}, u32[]{:S(2)}) collective-permute-start(bf16[192,3072]{1,0:T(8,128)(2,1)S(1)} %get-tuple-element.136), channel_id=1, source_target_pairs={{0,8},{8,0},{16,24},{24,16},{1,9},{9,1},{17,25},{25,17},{2,10},{10... | collective-permute-start | bytes 3538952 | tf_op jit(solution)/shard_map/ppermute | solution.py:661
  46.3 50.9 %collective-permute-start.10 = (bf16[192,3072]{1,0:T(8,128)(2,1)S(1)}, bf16[192,3072]{1,0:T(8,128)(2,1)}, u32[]{:S(2)}, u32[]{:S(2)}) collective-permute-start(bf16[192,3072]{1,0:T(8,128)(2,1)S(1)} %get-tuple-element.137), channel_id=1, source_target_pairs={{0,16},{8,24},{16,0},{24,8},{1,17},{9,25},{17,1},{25,9},{2,18},{10... | collective-permute-start | bytes 3538952 | tf_op jit(solution)/shard_map/ppermute | solution.py:661
  47.8 50.0 %collective-permute-start.11 = (bf16[192,3072]{1,0:T(8,128)(2,1)S(1)}, bf16[192,3072]{1,0:T(8,128)(2,1)}, u32[]{:S(2)}, u32[]{:S(2)}) collective-permute-start(bf16[192,3072]{1,0:T(8,128)(2,1)S(1)} %get-tuple-element.137), channel_id=1, source_target_pairs={{0,8},{8,0},{16,24},{24,16},{1,9},{9,1},{17,25},{25,17},{2,10},{10... | collective-permute-start | bytes 3538952 | tf_op jit(solution)/shard_map/ppermute | solution.py:661
  48.4 50.9 %collective-permute-start.12 = (bf16[192,3072]{1,0:T(8,128)(2,1)S(1)}, bf16[192,3072]{1,0:T(8,128)(2,1)}, u32[]{:S(2)}, u32[]{:S(2)}) collective-permute-start(bf16[192,3072]{1,0:T(8,128)(2,1)S(1)} %get-tuple-element.136), channel_id=1, source_target_pairs={{0,16},{8,24},{16,0},{24,8},{1,17},{9,25},{17,1},{25,9},{2,18},{10... | collective-permute-start | bytes 3538952 | tf_op jit(solution)/shard_map/ppermute | solution.py:661
  99.3 144.6 %all-gather.9.cloned.1.call-start = ((), (), s32[]{:S(2)}) async-start(), calls=%async_computation.4 | async-start | bytes 3932160 | tf_op jit(solution)/shard_map/all_gather | solution.py:893
  100.6 27.1 %collective-permute-start.14 = (bf16[192,3072]{1,0:T(8,128)(2,1)}, bf16[192,3072]{1,0:T(8,128)(2,1)}, u32[]{:S(2)}, u32[]{:S(2)}) collective-permute-start(bf16[192,3072]{1,0:T(8,128)(2,1)} %collective-permute-done.9), channel_id=1, source_target_pairs={{0,16},{8,24},{16,0},{24,8},{1,17},{9,25},{17,1},{25,9},{2,18},{10... | collective-permute-start | bytes 3538952 | tf_op jit(solution)/shard_map/ppermute | solution.py:661
  102.2 26.8 %collective-permute-start.15 = (bf16[192,3072]{1,0:T(8,128)(2,1)}, bf16[192,3072]{1,0:T(8,128)(2,1)}, u32[]{:S(2)}, u32[]{:S(2)}) collective-permute-start(bf16[192,3072]{1,0:T(8,128)(2,1)} %collective-permute-done.10), channel_id=1, source_target_pairs={{0,8},{8,0},{16,24},{24,16},{1,9},{9,1},{17,25},{25,17},{2,10},{10... | collective-permute-start | bytes 3538952 | tf_op jit(solution)/shard_map/ppermute | solution.py:661
  114.1 239.7 %reduce-scatter.4.cloned.1.call-start = ((), (), s32[]{:S(2)}) async-start(), calls=%async_computation.5 | async-start | bytes 3932160 | tf_op jit(solution)/shard_map/reduce_scatter | solution.py:910
  129.0 13.2 %collective-permute-start.18 = (bf16[192,768]{1,0:T(8,128)(2,1)S(1)}, bf16[192,768]{1,0:T(8,128)(2,1)S(1)}, u32[]{:S(2)}, u32[]{:S(2)}) collective-permute-start(bf16[192,768]{1,0:T(8,128)(2,1)S(1)} %get-tuple-element.135), channel_id=1, source_target_pairs={{0,16},{8,24},{16,0},{24,8},{1,17},{9,25},{17,1},{25,9},{2,18},{10... | collective-permute-start | bytes 884744 | tf_op jit(solution)/shard_map/ppermute | solution.py:661
  129.5 13.8 %collective-permute-start.19 = (bf16[192,768]{1,0:T(8,128)(2,1)S(1)}, bf16[192,768]{1,0:T(8,128)(2,1)S(1)}, u32[]{:S(2)}, u32[]{:S(2)}) collective-permute-start(bf16[192,768]{1,0:T(8,128)(2,1)S(1)} %get-tuple-element.135), channel_id=1, source_target_pairs={{0,8},{8,0},{16,24},{24,16},{1,9},{9,1},{17,25},{25,17},{2,10},{10... | collective-permute-start | bytes 884744 | tf_op jit(solution)/shard_map/ppermute | solution.py:661
  130.1 12.0 %collective-permute-start.17 = (bf16[192,768]{1,0:T(8,128)(2,1)S(1)}, bf16[192,768]{1,0:T(8,128)(2,1)S(1)}, u32[]{:S(2)}, u32[]{:S(2)}) collective-permute-start(bf16[192,768]{1,0:T(8,128)(2,1)S(1)} %get-tuple-element.134), channel_id=1, source_target_pairs={{0,8},{8,0},{16,24},{24,16},{1,9},{9,1},{17,25},{25,17},{2,10},{10... | collective-permute-start | bytes 884744 | tf_op jit(solution)/shard_map/ppermute | solution.py:661
  131.5 11.8 %collective-permute-start.20 = (bf16[192,768]{1,0:T(8,128)(2,1)S(1)}, bf16[192,768]{1,0:T(8,128)(2,1)S(1)}, u32[]{:S(2)}, u32[]{:S(2)}) collective-permute-start(bf16[192,768]{1,0:T(8,128)(2,1)S(1)} %get-tuple-element.134), channel_id=1, source_target_pairs={{0,16},{8,24},{16,0},{24,8},{1,17},{9,25},{17,1},{25,9},{2,18},{10... | collective-permute-start | bytes 884744 | tf_op jit(solution)/shard_map/ppermute | solution.py:661
  133.1 35.1 %collective-permute-start.25 = (bf16[384,768]{1,0:T(8,128)(2,1)S(1)}, bf16[384,768]{1,0:T(8,128)(2,1)S(1)}, u32[]{:S(2)}, u32[]{:S(2)}) collective-permute-start(bf16[384,768]{1,0:T(8,128)(2,1)S(1)} %pad_maximum_fusion.9), channel_id=1, source_target_pairs={{0,4},{4,0},{1,5},{5,1},{2,6},{6,2},{3,7},{7,3},{8,12},{12,8},{9,1... | collective-permute-start | bytes 1769480 | tf_op jit(solution)/shard_map/ppermute | solution.py:661
  143.3 29.8 %collective-permute-start.21 = (bf16[192,1536]{1,0:T(8,128)(2,1)S(1)}, bf16[192,1536]{1,0:T(8,128)(2,1)S(1)}, u32[]{:S(2)}, u32[]{:S(2)}) collective-permute-start(bf16[192,1536]{1,0:T(8,128)(2,1)S(1)} %copy-done.34), channel_id=1, source_target_pairs={{0,8},{8,0},{16,24},{24,16},{1,9},{9,1},{17,25},{25,17},{2,10},{10... | collective-permute-start | bytes 1769480 | tf_op jit(solution)/shard_map/ppermute | solution.py:661
  144.2 25.5 %collective-permute-start.28 = (bf16[384,768]{1,0:T(8,128)(2,1)S(1)}, bf16[384,768]{1,0:T(8,128)(2,1)S(1)}, u32[]{:S(2)}, u32[]{:S(2)}) collective-permute-start(bf16[384,768]{1,0:T(8,128)(2,1)S(1)} %pad_maximum_fusion.12), channel_id=1, source_target_pairs={{0,4},{4,0},{1,5},{5,1},{2,6},{6,2},{3,7},{7,3},{8,12},{12,8},{9,1... | collective-permute-start | bytes 1769480 | tf_op jit(solution)/shard_map/ppermute | solution.py:661
  157.4 9.4 %collective-permute-start.23 = (bf16[192,768]{1,0:T(8,128)(2,1)S(1)}, bf16[192,768]{1,0:T(8,128)(2,1)S(1)}, u32[]{:S(2)}, u32[]{:S(2)}) collective-permute-start(bf16[192,768]{1,0:T(8,128)(2,1)S(1)} %collective-permute-done.17), channel_id=1, source_target_pairs={{0,16},{8,24},{16,0},{24,8},{1,17},{9,25},{17,1},{25,9},{2,18},{10... | collective-permute-start | bytes 884744 | tf_op jit(solution)/shard_map/ppermute | solution.py:661
  158.8 9.1 %collective-permute-start.24 = (bf16[192,768]{1,0:T(8,128)(2,1)S(1)}, bf16[192,768]{1,0:T(8,128)(2,1)S(1)}, u32[]{:S(2)}, u32[]{:S(2)}) collective-permute-start(bf16[192,768]{1,0:T(8,128)(2,1)S(1)} %collective-permute-done.18), channel_id=1, source_target_pairs={{0,8},{8,0},{16,24},{24,16},{1,9},{9,1},{17,25},{25,17},{2,10},{10... | collective-permute-start | bytes 884744 | tf_op jit(solution)/shard_map/ppermute | solution.py:661
  169.0 15.0 %collective-permute-start.22 = (bf16[192,1536]{1,0:T(8,128)(2,1)S(1)}, bf16[192,1536]{1,0:T(8,128)(2,1)S(1)}, u32[]{:S(2)}, u32[]{:S(2)}) collective-permute-start(bf16[192,1536]{1,0:T(8,128)(2,1)S(1)} %copy-done.33), channel_id=1, source_target_pairs={{0,16},{8,24},{16,0},{24,8},{1,17},{9,25},{17,1},{25,9},{2,18},{10... | collective-permute-start | bytes 1769480 | tf_op jit(solution)/shard_map/ppermute | solution.py:661
  197.4 19.3 %collective-permute-start.29 = (bf16[1024,1536]{1,0:T(8,128)(2,1)}, bf16[1024,1536]{1,0:T(8,128)(2,1)S(1)}, u32[]{:S(2)}, u32[]{:S(2)}) collective-permute-start(bf16[1024,1536]{1,0:T(8,128)(2,1)} %get-tuple-element.150.x_ref.refs_0_.refs_1_), channel_id=1, source_target_pairs={{0,4},{4,0},{1,5},{5,1},{2,6},{6,2},{3,7},{7,3},{8,12},{12,8},{9,1... | collective-permute-start | bytes 9437192 | tf_op jit(solution)/shard_map/ppermute | solution.py:661
  197.4 18.6 %collective-permute-start.30 = (bf16[192,1536]{1,0:T(8,128)(2,1)S(1)}, bf16[192,1536]{1,0:T(8,128)(2,1)}, u32[]{:S(2)}, u32[]{:S(2)}) collective-permute-start(bf16[192,1536]{1,0:T(8,128)(2,1)S(1)} %copy-done.33), channel_id=1, source_target_pairs={{0,8},{8,0},{16,24},{24,16},{1,9},{9,1},{17,25},{25,17},{2,10},{10... | collective-permute-start | bytes 1769480 | tf_op jit(solution)/shard_map/ppermute | solution.py:661
  198.9 17.8 %collective-permute-start.31 = (bf16[192,1536]{1,0:T(8,128)(2,1)}, bf16[192,1536]{1,0:T(8,128)(2,1)}, u32[]{:S(2)}, u32[]{:S(2)}) collective-permute-start(bf16[192,1536]{1,0:T(8,128)(2,1)} %get-tuple-element.144.refs_1_.refs_4_), channel_id=1, source_target_pairs={{0,16},{8,24},{16,0},{24,8},{1,17},{9,25},{17,1},{25,9},{2,18},{10... | collective-permute-start | bytes 1769480 | tf_op jit(solution)/shard_map/ppermute | solution.py:661
  200.0 16.7 %collective-permute-start.32 = (f32[1024,128]{1,0:T(8,128)}, f32[1024,128]{1,0:T(8,128)}, u32[]{:S(2)}, u32[]{:S(2)}) collective-permute-start(f32[1024,128]{1,0:T(8,128)} %get-tuple-element.151.gate_ref.refs_2_), channel_id=1, source_target_pairs={{0,4},{4,0},{1,5},{5,1},{2,6},{6,2},{3,7},{7,3},{8,12},{12,8},{9,1... | collective-permute-start | bytes 1572872 | tf_op jit(solution)/shard_map/ppermute | solution.py:661
  215.2 18.3 %collective-permute-start.33 = (bf16[192,1536]{1,0:T(8,128)(2,1)}, bf16[192,1536]{1,0:T(8,128)(2,1)}, u32[]{:S(2)}, u32[]{:S(2)}) collective-permute-start(bf16[192,1536]{1,0:T(8,128)(2,1)} %copy-done.63), channel_id=1, source_target_pairs={{0,16},{8,24},{16,0},{24,8},{1,17},{9,25},{17,1},{25,9},{2,18},{10... | collective-permute-start | bytes 1769480 | tf_op jit(solution)/shard_map/ppermute | solution.py:661
  216.0 17.4 %collective-permute-start.34 = (bf16[192,1536]{1,0:T(8,128)(2,1)}, bf16[192,1536]{1,0:T(8,128)(2,1)S(1)}, u32[]{:S(2)}, u32[]{:S(2)}) collective-permute-start(bf16[192,1536]{1,0:T(8,128)(2,1)} %copy-done.64), channel_id=1, source_target_pairs={{0,8},{8,0},{16,24},{24,16},{1,9},{9,1},{17,25},{25,17},{2,10},{10... | collective-permute-start | bytes 1769480 | tf_op jit(solution)/shard_map/ppermute | solution.py:661
  243.9 10.1 %collective-permute-start.36 = (bf16[1024,1536]{1,0:T(8,128)(2,1)}, bf16[1024,1536]{1,0:T(8,128)(2,1)S(1)}, u32[]{:S(2)}, u32[]{:S(2)}) collective-permute-start(bf16[1024,1536]{1,0:T(8,128)(2,1)} %all-gather.9.cloned.1.call-done.refs_0_.refs_1_), channel_id=1, source_target_pairs={{0,4},{4,0},{1,5},{5,1},{2,6},{6,2},{3,7},{7,3},{8,12},{12,8},{9,1... | collective-permute-start | bytes 9437192 | tf_op jit(solution)/shard_map/ppermute | solution.py:661
  243.9 39.4 %collective-permute-start.35 = (bf16[1024,1536]{1,0:T(8,128)(2,1)}, bf16[1024,1536]{1,0:T(8,128)(2,1)}, u32[]{:S(2)}, u32[]{:S(2)}) collective-permute-start(bf16[1024,1536]{1,0:T(8,128)(2,1)} %combine.2), channel_id=1, source_target_pairs={{0,4},{4,0},{1,5},{5,1},{2,6},{6,2},{3,7},{7,3},{8,12},{12,8},{9,1... | collective-permute-start | bytes 9437192 | tf_op jit(solution)/shard_map/ppermute | solution.py:661
  280.7 35.8 %collective-permute-start.37 = (bf16[768,768]{1,0:T(8,128)(2,1)}, bf16[768,768]{1,0:T(8,128)(2,1)S(1)}, u32[]{:S(2)}, u32[]{:S(2)}) collective-permute-start(bf16[768,768]{1,0:T(8,128)(2,1)} %get-tuple-element.170), channel_id=1, source_target_pairs={{0,16},{8,24},{16,0},{24,8},{1,17},{9,25},{17,1},{25,9},{2,18},{10... | collective-permute-start | bytes 3538952 | tf_op jit(solution)/shard_map/ppermute | solution.py:661
  281.9 34.6 %collective-permute-start.38 = (bf16[768,768]{1,0:T(8,128)(2,1)}, bf16[768,768]{1,0:T(8,128)(2,1)}, u32[]{:S(2)}, u32[]{:S(2)}) collective-permute-start(bf16[768,768]{1,0:T(8,128)(2,1)} %get-tuple-element.171), channel_id=1, source_target_pairs={{0,8},{8,0},{16,24},{24,16},{1,9},{9,1},{17,25},{25,17},{2,10},{10... | collective-permute-start | bytes 3538952 | tf_op jit(solution)/shard_map/ppermute | solution.py:661
  288.6 142.4 %reduce-scatter.6.cloned.1.call-start = ((), (), s32[]{:S(2)}) async-start(), calls=%async_computation.6 | async-start | bytes 3932160 | tf_op jit(solution)/shard_map/reduce_scatter | solution.py:939
  316.4 17.4 %collective-permute-start.40 = (f32[1024,128]{1,0:T(8,128)}, f32[1024,128]{1,0:T(8,128)S(1)}, u32[]{:S(2)}, u32[]{:S(2)}) collective-permute-start(f32[1024,128]{1,0:T(8,128)} %get-tuple-element.175), channel_id=1, source_target_pairs={{0,4},{4,0},{1,5},{5,1},{2,6},{6,2},{3,7},{7,3},{8,12},{12,8},{9,1... | collective-permute-start | bytes 1572872 | tf_op jit(solution)/shard_map/ppermute | solution.py:661
  333.3 23.0 %collective-permute-start.39 = (bf16[1024,1536]{1,0:T(8,128)(2,1)}, bf16[1024,1536]{1,0:T(8,128)(2,1)}, u32[]{:S(2)}, u32[]{:S(2)}) collective-permute-start(bf16[1024,1536]{1,0:T(8,128)(2,1)} %convolution_convert_fusion.1), channel_id=1, source_target_pairs={{0,4},{4,0},{1,5},{5,1},{2,6},{6,2},{3,7},{7,3},{8,12},{12,8},{9,1... | collective-permute-start | bytes 9437192 | tf_op jit(solution)/shard_map/ppermute | solution.py:661
  338.2 18.1 %collective-permute-start.41 = (bf16[384,768]{1,0:T(8,128)(2,1)S(1)}, bf16[384,768]{1,0:T(8,128)(2,1)S(1)}, u32[]{:S(2)}, u32[]{:S(2)}) collective-permute-start(bf16[384,768]{1,0:T(8,128)(2,1)S(1)} %add_convert_fusion.11), channel_id=1, source_target_pairs={{0,8},{8,0},{16,24},{24,16},{1,9},{9,1},{17,25},{25,17},{2,10},{10... | collective-permute-start | bytes 1769480 | tf_op jit(solution)/shard_map/ppermute | solution.py:661
  338.8 17.5 %collective-permute-start.42 = (bf16[384,768]{1,0:T(8,128)(2,1)S(1)}, bf16[384,768]{1,0:T(8,128)(2,1)S(1)}, u32[]{:S(2)}, u32[]{:S(2)}) collective-permute-start(bf16[384,768]{1,0:T(8,128)(2,1)S(1)} %add_convert_fusion.10), channel_id=1, source_target_pairs={{0,16},{8,24},{16,0},{24,8},{1,17},{9,25},{17,1},{25,9},{2,18},{10... | collective-permute-start | bytes 1769480 | tf_op jit(solution)/shard_map/ppermute | solution.py:661
  370.1 197.7 %reduce-scatter.8.cloned.1.call-start = ((), (), s32[]{:S(2)}) async-start(), calls=%async_computation.7 | async-start | bytes 3932160 | tf_op jit(solution)/shard_map/reduce_scatter | solution.py:963
  392.1 23.1 %collective-permute-start.52 = (bf16[1536,768]{1,0:T(8,128)(2,1)}, bf16[1536,768]{1,0:T(8,128)(2,1)}, u32[]{:S(2)}, u32[]{:S(2)}) collective-permute-start(bf16[1536,768]{1,0:T(8,128)(2,1)} %convolution_convert_fusion.3), channel_id=1, source_target_pairs={{0,4},{4,0},{1,5},{5,1},{2,6},{6,2},{3,7},{7,3},{8,12},{12,8},{9,1... | collective-permute-start | bytes 7077896 | tf_op jit(solution)/shard_map/ppermute | solution.py:661
  392.9 66.3 %collective-permute-start.43 = (bf16[768,1536]{1,0:T(8,128)(2,1)}, bf16[768,1536]{1,0:T(8,128)(2,1)}, u32[]{:S(2)}, u32[]{:S(2)}) collective-permute-start(bf16[768,1536]{1,0:T(8,128)(2,1)} %get-tuple-element.191), channel_id=1, source_target_pairs={{0,16},{8,24},{16,0},{24,8},{1,17},{9,25},{17,1},{25,9},{2,18},{10... | collective-permute-start | bytes 7077896 | tf_op jit(solution)/shard_map/ppermute | solution.py:661
  394.1 65.2 %collective-permute-start.44 = (bf16[768,1536]{1,0:T(8,128)(2,1)}, bf16[768,1536]{1,0:T(8,128)(2,1)}, u32[]{:S(2)}, u32[]{:S(2)}) collective-permute-start(bf16[768,1536]{1,0:T(8,128)(2,1)} %get-tuple-element.192), channel_id=1, source_target_pairs={{0,8},{8,0},{16,24},{24,16},{1,9},{9,1},{17,25},{25,17},{2,10},{10... | collective-permute-start | bytes 7077896 | tf_op jit(solution)/shard_map/ppermute | solution.py:661
  419.3 54.8 %collective-permute-start.53 = (bf16[768,384]{1,0:T(8,128)(2,1)}, bf16[768,384]{1,0:T(8,128)(2,1)}, u32[]{:S(2)}, u32[]{:S(2)}) collective-permute-start(bf16[768,384]{1,0:T(8,128)(2,1)} %get-tuple-element.298), channel_id=1, source_target_pairs={{0,16},{8,24},{16,0},{24,8},{1,17},{9,25},{17,1},{25,9},{2,18},{10... | collective-permute-start | bytes 1769480 | tf_op jit(solution)/shard_map/ppermute | solution.py:661
  421.3 52.8 %collective-permute-start.54 = (bf16[768,384]{1,0:T(8,128)(2,1)}, bf16[768,384]{1,0:T(8,128)(2,1)}, u32[]{:S(2)}, u32[]{:S(2)}) collective-permute-start(bf16[768,384]{1,0:T(8,128)(2,1)} %pad_maximum_fusion.14), channel_id=1, source_target_pairs={{0,8},{8,0},{16,24},{24,16},{1,9},{9,1},{17,25},{25,17},{2,10},{10... | collective-permute-start | bytes 1769480 | tf_op jit(solution)/shard_map/ppermute | solution.py:661
  463.8 47.9 %collective-permute-start.48 = (bf16[384,1536]{1,0:T(8,128)(2,1)}, bf16[384,1536]{1,0:T(8,128)(2,1)}, u32[]{:S(2)}, u32[]{:S(2)}) collective-permute-start(bf16[384,1536]{1,0:T(8,128)(2,1)} %get-tuple-element.199), channel_id=1, source_target_pairs={{0,8},{8,0},{16,24},{24,16},{1,9},{9,1},{17,25},{25,17},{2,10},{10... | collective-permute-start | bytes 3538952 | tf_op jit(solution)/shard_map/ppermute | solution.py:661
  465.3 46.4 %collective-permute-start.49 = (bf16[384,1536]{1,0:T(8,128)(2,1)}, bf16[384,1536]{1,0:T(8,128)(2,1)}, u32[]{:S(2)}, u32[]{:S(2)}) collective-permute-start(bf16[384,1536]{1,0:T(8,128)(2,1)} %get-tuple-element.200), channel_id=1, source_target_pairs={{0,16},{8,24},{16,0},{24,8},{1,17},{9,25},{17,1},{25,9},{2,18},{10... | collective-permute-start | bytes 3538952 | tf_op jit(solution)/shard_map/ppermute | solution.py:661
  472.2 31.6 %collective-permute-start.45 = (bf16[1536,384]{1,0:T(8,128)(2,1)}, bf16[1536,384]{1,0:T(8,128)(2,1)}, u32[]{:S(2)}, u32[]{:S(2)}) collective-permute-start(bf16[1536,384]{1,0:T(8,128)(2,1)} %get-tuple-element.372), channel_id=1, source_target_pairs={{0,4},{4,0},{1,5},{5,1},{2,6},{6,2},{3,7},{7,3},{8,12},{12,8},{9,1... | collective-permute-start | bytes 3538952 | tf_op jit(solution)/shard_map/ppermute | solution.py:661
  475.5 22.4 %collective-permute-start.55 = (bf16[384,384]{1,0:T(8,128)(2,1)S(1)}, bf16[384,384]{1,0:T(8,128)(2,1)S(1)}, u32[]{:S(2)}, u32[]{:S(2)}) collective-permute-start(bf16[384,384]{1,0:T(8,128)(2,1)S(1)} %get-tuple-element.219), channel_id=1, source_target_pairs={{0,8},{8,0},{16,24},{24,16},{1,9},{9,1},{17,25},{25,17},{2,10},{10... | collective-permute-start | bytes 884744 | tf_op jit(solution)/shard_map/ppermute | solution.py:661
  476.1 23.0 %collective-permute-start.56 = (bf16[384,384]{1,0:T(8,128)(2,1)S(1)}, bf16[384,384]{1,0:T(8,128)(2,1)S(1)}, u32[]{:S(2)}, u32[]{:S(2)}) collective-permute-start(bf16[384,384]{1,0:T(8,128)(2,1)S(1)} %get-tuple-element.220), channel_id=1, source_target_pairs={{0,16},{8,24},{16,0},{24,8},{1,17},{9,25},{17,1},{25,9},{2,18},{10... | collective-permute-start | bytes 884744 | tf_op jit(solution)/shard_map/ppermute | solution.py:661
  497.9 4.9 collective-permute-start.62
  507.0 10.0 %collective-permute-start.46 = (bf16[768,256]{1,0:T(8,128)(2,1)S(1)}, bf16[768,256]{1,0:T(8,128)(2,1)S(1)}, u32[]{:S(2)}, u32[]{:S(2)}) collective-permute-start(bf16[768,256]{1,0:T(8,128)(2,1)S(1)} %get-tuple-element.322), channel_id=1, source_target_pairs={{0,16},{8,24},{16,0},{24,8},{1,17},{9,25},{17,1},{25,9},{2,18},{10... | collective-permute-start | bytes 1179656 | tf_op jit(solution)/shard_map/ppermute | solution.py:661
  508.6 5.7 collective-permute-start.47
  518.5 10.4 %collective-permute-start.50 = (bf16[384,256]{1,0:T(8,128)(2,1)}, bf16[384,256]{1,0:T(8,128)(2,1)}, u32[]{:S(2)}, u32[]{:S(2)}) collective-permute-start(bf16[384,256]{1,0:T(8,128)(2,1)} %add_convert_fusion.17), channel_id=1, source_target_pairs={{0,8},{8,0},{16,24},{24,16},{1,9},{9,1},{17,25},{25,17},{2,10},{10... | collective-permute-start | bytes 589832 | tf_op jit(solution)/shard_map/ppermute | solution.py:661
  520.0 8.9 %collective-permute-start.51 = (bf16[384,128]{1,0:T(8,128)(2,1)}, bf16[384,128]{1,0:T(8,128)(2,1)}, u32[]{:S(2)}, u32[]{:S(2)}) collective-permute-start(bf16[384,128]{1,0:T(8,128)(2,1)} %add_convert_fusion.19), channel_id=1, source_target_pairs={{0,16},{8,24},{16,0},{24,8},{1,17},{9,25},{17,1},{25,9},{2,18},{10... | collective-permute-start | bytes 294920 | tf_op jit(solution)/shard_map/ppermute | solution.py:661
  528.8 10.5 %collective-permute-start.58 = (bf16[192,3072]{1,0:T(8,128)(2,1)}, bf16[192,3072]{1,0:T(8,128)(2,1)S(1)}, u32[]{:S(2)}, u32[]{:S(2)}) collective-permute-start(bf16[192,3072]{1,0:T(8,128)(2,1)} %pad_maximum_fusion.4), channel_id=1, source_target_pairs={{0,4},{4,0},{1,5},{5,1},{2,6},{6,2},{3,7},{7,3},{8,12},{12,8},{9,1... | collective-permute-start | bytes 3538952 | tf_op jit(solution)/shard_map/ppermute | solution.py:661
  542.7 15.0 %collective-permute-start.61 = (bf16[192,512]{1,0:T(8,128)(2,1)}, bf16[192,512]{1,0:T(8,128)(2,1)}, u32[]{:S(2)}, u32[]{:S(2)}) collective-permute-start(bf16[192,512]{1,0:T(8,128)(2,1)} %get-tuple-element.369), channel_id=1, source_target_pairs={{0,3},{1,0},{2,1},{3,2},{4,7},{5,4},{6,5},{7,6},{8,11},{9,8},{10,9... | collective-permute-start | bytes 589832 | tf_op jit(solution)/shard_map/ppermute | solution.py:1031
  545.2 18.2 %collective-permute-start.60 = (bf16[192,512]{1,0:T(8,128)(2,1)}, bf16[192,512]{1,0:T(8,128)(2,1)}, u32[]{:S(2)}, u32[]{:S(2)}) collective-permute-start(bf16[192,512]{1,0:T(8,128)(2,1)} %get-tuple-element.368), channel_id=1, source_target_pairs={{0,2},{1,3},{2,0},{3,1},{4,6},{5,7},{6,4},{7,5},{8,10},{9,11},{10,... | collective-permute-start | bytes 589832 | tf_op jit(solution)/shard_map/ppermute | solution.py:1031
  545.3 19.1 %collective-permute-start.59 = (bf16[192,512]{1,0:T(8,128)(2,1)}, bf16[192,512]{1,0:T(8,128)(2,1)}, u32[]{:S(2)}, u32[]{:S(2)}) collective-permute-start(bf16[192,512]{1,0:T(8,128)(2,1)} %get-tuple-element.367), channel_id=1, source_target_pairs={{0,1},{1,2},{2,3},{3,0},{4,5},{5,6},{6,7},{7,4},{8,9},{9,10},{10,1... | collective-permute-start | bytes 589832 | tf_op jit(solution)/shard_map/ppermute | solution.py:1031
  (72 other events, 469.6 us)
Sparse Core Ops, SparseCore 0:
  13.9 65.8 all-gather.6
  82.0 29.0 all-gather.12
  113.2 62.6 all-gather.10
  177.4 62.1 all-gather.8
  288.8 60.0 reduce-scatter.3
  370.3 60.7 reduce-scatter.5
  459.4 60.2 reduce-scatter.7

commit v5 on v4

--- a/solution.py
+++ b/solution.py
@@ -754,6 +754,23 @@
     )
 
 
+def small_first(value):
+    n = value.shape[0] // 4
+    return swap(value[n : 3 * n], "q", 1, 4)
+
+
+def small_second(value, got):
+    n = value.shape[0] // 4
+    give = (value[3 * n :].astype(F32) + got[n:].astype(F32)).astype(BF16)
+    return swap(lax.optimization_barrier(give), "q", 2, 4)
+
+
+def small_last(value, got, late):
+    n = value.shape[0] // 4
+    value, got, late = lax.optimization_barrier((value, got, late))
+    return (value[:n].astype(F32) + got[:n].astype(F32) + late.astype(F32)).astype(BF16)
+
+
 def scatter_plain(value):
     total = lax.psum_scatter(value, "q", scatter_dimension=0, tiled=True)
     half = total.shape[1] // 2
@@ -774,11 +791,16 @@
     return jnp.where(first, mine, other), jnp.where(first, other, mine)
 
 
-def from_halves(totals, rows, c):
+def part_halves(totals, rows, c):
     def take(at):
         return jnp.concatenate([lax.dynamic_slice_in_dim(t, at * rows, rows, 0) for t in totals], 1)
 
-    return take(c), swap(take(1 - c), "c", 1, 2)
+    return take(c), take(1 - c)
+
+
+def from_halves(totals, rows, c):
+    mine, give = part_halves(totals, rows, c)
+    return mine, swap(give, "c", 1, 2)
 
 
 def in_order(mine, other, c):
@@ -907,7 +929,7 @@
     comb_recv = swap(comb_give, "c", 1, 2)
     comb_own = combine(after(gact_own, comb_give, grad_all), out_full, length // 2)
     combined = (comb_own.astype(F32) + comb_recv.astype(F32)).astype(BF16)
-    moe_branch = lax.psum_scatter(combined, "mp", scatter_dimension=0, tiled=True).astype(F32)
+    moe_low = lax.psum_scatter(combined, "mp", scatter_dimension=0, tiled=True)
 
     g_other = swap(after(grad_all, comb_give), "c", 1, 2)
     gacts = all_after((gact_own, gact_other), comb_own)
@@ -934,7 +956,7 @@
     out_late = scatter_second(*out_keep, *out_move)[0] if quads == 4 else ()
     ag, p_part = back_mid(
         m.astype(jnp.int32).reshape(1), back_own, back_recv, logit_grad, pack, small_at,
-        after(middle, moe_branch, *out_late), moe_g, cot_own, wo_rows, mp,
+        after(middle, moe_low, *out_late), moe_g, cot_own, wo_rows, mp,
     )
     attended_grad = lax.psum_scatter(p_part, "mp", scatter_dimension=0, tiled=False)
 
@@ -963,7 +985,7 @@
     grad_tokens = lax.psum_scatter(end_part, "mp", scatter_dimension=0, tiled=True).astype(F32)
 
     layer_out = (
-        lax.dynamic_slice_in_dim(middle, m * (length // mp), length // mp, 0) + RESID * after(moe_branch, end_part)
+        lax.dynamic_slice_in_dim(middle, m * (length // mp), length // mp, 0) + RESID * after(moe_low, end_part).astype(F32)
     ).astype(BF16)
 
     given = (end_part,)
@@ -979,19 +1001,20 @@
     mine, give = column_halves(part, c)
     pair = (mine.astype(F32) + swap(give, "c", 1, 2).astype(F32)).astype(BF16)
     if quads == 4:
-        pair_keep = (cut(pair, KEEP_LEFT), cut(pair, KEEP_RIGHT))
-        pair_move = scatter_first(cut(pair, SEND_LEFT), cut(pair, SEND_RIGHT))
-        *pair_move, in_left, in_right = lax.optimization_barrier((*pair_move, *in_late))
-        in_late = (in_left, in_right)
-        pair_late, _ = scatter_second(*pair_keep, *pair_move)
+        pair_move = small_first(pair)
         in_sum = scatter_last(*in_keep, *in_move, in_late)
-        wo_sum = scatter_last(*wo_keep, *wo_move, wo_late)
-        pair_sum = scatter_last(*pair_keep, *pair_move, pair_late)
+        in_mine, in_give = part_halves(in_sum, rows, c)
+        pair_move, in_give = lax.optimization_barrier((pair_move, in_give))
+        in_other = swap(in_give, "c", 1, 2)
+        pair_late = small_second(pair, pair_move)
+        wo_sum = scatter_last(*wo_keep, *wo_move, wo_late, pair_move)
+        pair_sum = (small_last(pair, pair_move, pair_late),)
         out_sum = scatter_last(*out_keep, *out_move, out_late, end_part)
     else:
         in_sum, wo_sum, pair_sum, out_sum = (
             scatter_plain(v) for v in (in_keep[0], wo_part, pair, out_keep[0])
         )
+        in_mine, in_other = from_halves(in_sum, rows, c)
     late_sum = (*wo_sum, *pair_sum)
     late_mine, late_other = from_halves(late_sum, rows, c)
     wo_cols_here = wo_part.shape[1]
@@ -1006,7 +1029,6 @@
     grad_value = sums[:, q_cols + kv_cols : qkv_cols]
     router_part = sums[:, qkv_cols : qkv_cols + experts]
 
-    in_mine, in_other = from_halves(in_sum, rows, c)
     out_mine, out_other = from_halves(out_sum, rows, c)
     grad_in = jnp.concatenate(in_order(in_mine, in_other, c), 1).astype(F32)
     grad_out = jnp.concatenate(in_order(out_mine, out_other, c), 1).astype(F32)

time: 584 us -> 571 us (0.978)
  waiting for transfers between devices: 117 us -> 107 us
    ppermute x60 -> x58, waiting for transfers between devices: 72.5 us -> 63.9 us  [swap(): return lax.ppermute(value, axis, [(i, i ^ bit) for i in range(size)])]
    unnamed x157 -> x147, local copies, waits for them, and re-layouts: 30.7 us -> 32.5 us
    ppermute x60 -> x58, starting transfers between devices: 48.7 us -> 47 us  [swap(): return lax.ppermute(value, axis, [(i, i ^ bit) for i in range(size)])]
  transfers between devices with their start and end apart: 70 -> 68, of which waited for: 20 -> 20; matrix products, arithmetic and copies ran while one was open for 29% -> 29% of each run, Pallas kernels for 33% -> 34%
where the time goes in v5:
time: 571 us; the launch traced here: 565 us
  Pallas kernels  206 us (36%)
  waiting for transfers between devices  107 us (19%)
  other arithmetic  78.7 us (14%)
  local copies, waits for them, and re-layouts  59.6 us (10%)
  starting transfers between devices  52.5 us (9%)
  matrix products  44.9 us (8%)
  between operations  15.6 us (3%)
    ppermute x58, waiting for transfers between devices, swap(): return lax.ppermute(value, axis, [(i, i ^ bit) for i in range(size)])  63.9 us
    pallas_call x3, Pallas kernels, weight_grad(): pl.pallas_call(functools.partial(segment_kernel, count=count), grid=(coun...  56.7 us
    ppermute x58, starting transfers between devices, swap(): return lax.ppermute(value, axis, [(i, i ^ bit) for i in range(size)])  47 us
    unnamed x147, local copies, waits for them, and re-layouts  32.5 us
    pallas_call x2, Pallas kernels, moe_fwd(): pl.pallas_call(moe_fwd_kernel, grid_spec=pltpu.PrefetchScalarGridSpec(num...  30.3 us
    dot_general x2, matrix products, nt(): lax.dot_general(left, right, (((1,), (1,)), ((), ())), preferred_element_...  29.7 us
    pallas_call x2, Pallas kernels, moe_bwd(): pl.pallas_call(moe_bwd_kernel, grid_spec=pltpu.PrefetchScalarGridSpec(num...  27.7 us
    all_gather x1, waiting for transfers between devices, body(): tok_all = lax.all_gather(tok_own, 'mp', axis=0, tiled=True)  22.1 us
  transfers between devices with their start and end apart: 68, of which 20 were waited for; matrix products, arithmetic and copies ran while one was open for 29% of the time, Pallas kernels for 34%

profile of v5, /device:TPU:0, one launch (start us, length us, event | category | flops | bytes accessed | tf_op | source)
XLA Modules:
  0.0 564.6 jit_solution(12656551725383089071)
XLA Ops:
  7.2 3.3 constant_dynamic-slice_fusion.15
  10.5 1.7 reshape.79
  18.3 2.7 collective-permute-start.2
  21.7 2.0 collective-permute-start.5
  25.7 2.0 collective-permute-start.4
  28.4 2.0 collective-permute-start.6
  31.1 2.7 collective-permute-done.4
  41.0 1.8 broadcast_select_fusion.8
  44.5 1.8 collective-permute-start.9
  48.7 3.8 negate_select_fusion
  53.5 2.5 bitcast_select_fusion
  57.8 22.1 %all-gather.7.cloned.1.call-done.tok_ref = bf16[1024,1536]{1,0:T(8,128)(2,1)} async-done(((bf16[256,1536]{1,0:T(8,128)(2,1)}), bf16[1024,1536]{1,0:T(8,128)(2,1)}) %all-gather.7.cloned.1.call-update) | async-done | bytes 3145744 | tf_op jit(solution)/shard_map/all_gather | solution.py:842
  79.9 17.3 %attn_fwd.1 = (bf16[1024,1536]{1,0:T(8,128)(2,1)}, bf16[6,1024,64]{2,1,0:T(8,128)(2,1)}, bf16[2,1024,64]{2,1,0:T(8,128)(2,1)}, bf16[2,1024,64]{2,1,0:T(8,128)(2,...) custom-call(bf16[1024,1536]{1,0:T(8,128)(2,1)} %all-gather.7.cloned.1.call-done.tok_ref, ...), custom_call_target="tpu_custom_call" | custom-call | flops 44291848 | bytes 82575 | tf_op jit(solution)/shard_map/attn_fwd/pallas_call | solution.py:135
  102.7 8.3 %all-gather.13.cloned.1.call-done = bf16[768,704]{1,0:T(8,128)(2,1)} async-done(((bf16[192,704]{1,0:T(8,128)(2,1)}), bf16[768,704]{1,0:T(8,128)(2,1)}) %all-gather.13.cloned.1.call-update) | async-done | bytes 1081360 | tf_op jit(solution)/shard_map/all_gather | solution.py:887
  114.5 13.2 %collective-permute-done.14 = bf16[192,3072]{1,0:T(8,128)(2,1)} collective-permute-done((bf16[192,3072]{1,0:T(8,128)(2,1)}, bf16[192,3072]{1,0:T(8,128)(2,1)}, u32[]{:S(2)}, u32[]{:S(2)}) %collective-permute-start.14) | collective-permute-done | bytes 1179680 | tf_op jit(solution)/shard_map/ppermute | solution.py:661
  133.2 8.9 %collective-permute-done.17 = bf16[192,768]{1,0:T(8,128)(2,1)S(1)} collective-permute-done((bf16[192,768]{1,0:T(8,128)(2,1)S(1)}, bf16[192,768]{1,0:T(8,128)(2,1)S(1)}, u32[]{:S(2)}, u32[]{:S(2)}) %collective-permute-start.17) | collective-permute-done | bytes 294944 | tf_op jit(solution)/shard_map/ppermute | solution.py:661
  145.3 2.4 constant_dynamic-update-slice_fusion.13
  147.7 2.4 constant_dynamic-update-slice_fusion.12
  150.1 2.4 constant_dynamic-update-slice_fusion.11
  152.5 2.5 constant_dynamic-update-slice_fusion.10
  154.9 2.4 constant_dynamic-update-slice_fusion.9
  160.1 2.4 constant_dynamic-update-slice_fusion.8.w_ref
  162.5 4.3 collective-permute-done.23
  170.4 2.6 pad_maximum_fusion.wo_ref
  172.9 10.9 %collective-permute-done.22.refs_8_.refs_11_ = bf16[192,1536]{1,0:T(8,128)(2,1)S(1)} collective-permute-done((bf16[192,1536]{1,0:T(8,128)(2,1)S(1)}, bf16[192,1536]{1,0:T(8,128)(2,1)S(1)}, u32[]{:S(2)}, u32[]{:S(2)}) %collective-permute-start.22) | collective-permute-done | bytes 589856 | tf_op jit(solution)/shard_map/ppermute | solution.py:661
  183.9 13.3 %mid_fwd.1 = (f32[1024,1536]{1,0:T(8,128)}, bf16[1024,1536]{1,0:T(8,128)(2,1)}, f32[1024,128]{1,0:T(8,128)}, bf16[1024,1536]{1,0:T(8,128)(2,1)}) custom-call(bf16[4,1024,384]{2,1,0:T(8,128)(2,1)} %bitcast.55, bf16[1536,1536]{1,0:T(8,128)(2,1)} %pad_maximum_fusion.wo_ref, bf16[1024,1536]{1,0:T(8,128)(2,1)} %all-gather.7.cloned.1.call-done.tok_ref, ...), custom_call_target="tpu_custom_call" | custom-call | flops 4831838208 | bytes 20447232 | tf_op jit(solution)/shard_map/mid_fwd/pallas_call | solution.py:309
  199.9 15.1 %moe_fwd.2 = (bf16[1024,3072]{1,0:T(8,128)(2,1)}, bf16[1024,1536]{1,0:T(8,128)(2,1)}) custom-call(s32[1]{0:T(128)} %bitcast.9.base_ref.refs_0_, bf16[1024,1536]{1,0:T(8,128)(2,1)} %get-tuple-element.143.x_ref.refs_0_.refs_1_, bf16[1536,3072]{1,0:T(8,128)(2,1)} %constant_dynamic-update-slice_fusion.8.w_ref, f32[1024,128]{1,0:T(8,128)} %get-tuple-element.144.gate_ref.refs_2_), custom_call_target="tpu_custom_call" | custom-call | flops 96636768 | bytes 314572 | tf_op jit(solution)/shard_map/moe_fwd/pallas_call | solution.py:469
  218.1 15.2 %moe_fwd.3 = (bf16[1024,3072]{1,0:T(8,128)(2,1)}, bf16[1024,1536]{1,0:T(8,128)(2,1)}) custom-call(s32[1]{0:T(128)} %bitcast.9.base_ref.refs_0_, bf16[1024,1536]{1,0:T(8,128)(2,1)} %copy-done.1, bf16[1536,3072]{1,0:T(8,128)(2,1)} %constant_dynamic-update-slice_fusion.8.w_ref, f32[1024,128]{1,0:T(8,128)} %collective-permute-done.32.gate_ref.refs_2_), custom_call_target="tpu_custom_call" | custom-call | flops 9663676416 | bytes 31457280 | tf_op jit(solution)/shard_map/moe_fwd/pallas_call | solution.py:469
  234.2 9.6 %combine.2 = bf16[1024,1536]{1,0:T(8,128)(2,1)} custom-call(bf16[1024,1536]{1,0:T(8,128)(2,1)} %get-tuple-element.155.refs_0_.refs_5_, bf16[192,1536]{1,0:T(8,128)(2,1)} %get-tuple-element.137.refs_1_.refs_4_, bf16[192,1536]{1,0:T(8,128)(2,1)} %get-tuple-element.138.refs_2_.refs_5_, bf16[192,1536]{1,0:T(8,128)(2,1)} %copy-done.58, ...), custom_call_target="tpu_custom_call" | custom-call | flops 4831838208 | bytes 11010048 | tf_op jit(solution)/shard_map/combine/pallas_call | solution.py:517
  244.3 9.5 %combine.3 = bf16[1024,1536]{1,0:T(8,128)(2,1)} custom-call(bf16[1024,1536]{1,0:T(8,128)(2,1)} %get-tuple-element.154.refs_0_.refs_4_, bf16[192,1536]{1,0:T(8,128)(2,1)} %get-tuple-element.137.refs_1_.refs_4_, bf16[192,1536]{1,0:T(8,128)(2,1)} %get-tuple-element.138.refs_2_.refs_5_, bf16[192,1536]{1,0:T(8,128)(2,1)} %copy-done.58, ...), custom_call_target="tpu_custom_call" | custom-call | flops 4831838208 | bytes 11010048 | tf_op jit(solution)/shard_map/combine/pallas_call | solution.py:517
  253.8 1.7 copy-done.3
  255.5 24.9 %weight_grad.3 = (bf16[768,768]{1,0:T(8,128)(2,1)}, bf16[768,768]{1,0:T(8,128)(2,1)}, bf16[768,768]{1,0:T(8,128)(2,1)}, bf16[768,768]{1,0:T(8,128)(2,1)}) custom-call(bf16[1024,1536]{1,0:T(8,128)(2,1)} %all-gather.9.cloned.1.call-done.refs_0_.refs_1_, bf16[1024,1536]{1,0:T(8,128)(2,1)} %all-gather.9.cloned.1.call-done.refs_0_.refs_1_, ...), custom_call_target="tpu_custom_call" | custom-call | flops 96636768 | bytes 125829 | tf_op jit(solution)/shard_map/weight_grad/pallas_call | solution.py:641
  283.0 5.3 add_convert_fusion
  288.4 14.0 %moe_bwd.2 = (bf16[1024,3072]{1,0:T(8,128)(2,1)}, f32[1024,128]{1,0:T(8,128)}) custom-call(s32[1]{0:T(128)} %bitcast.9.base_ref.refs_0_, bf16[1024,1536]{1,0:T(8,128)(2,1)} %all-gather.9.cloned.1.call-done.refs_0_.refs_1_, f32[1024,128]{1,0:T(8,128)} %get-tuple-element.144.gate_ref.refs_2_, bf16[1024,3072]{1,0:T(8,128)(2,1)} %get-tuple-element.158.refs_3_, ...), custom_call_target="tpu_custom_call" | custom-call | flops 4831838208 | bytes 25165824 | tf_op jit(solution)/shard_map/moe_bwd/pallas_call | solution.py:568
  302.4 13.7 %moe_bwd.3 = (bf16[1024,3072]{1,0:T(8,128)(2,1)}, f32[1024,128]{1,0:T(8,128)}) custom-call(s32[1]{0:T(128)} %bitcast.9.base_ref.refs_0_, bf16[1024,1536]{1,0:T(8,128)(2,1)} %copy-done.3, f32[1024,128]{1,0:T(8,128)} %collective-permute-done.32.gate_ref.refs_2_, bf16[1024,3072]{1,0:T(8,128)(2,1)} %get-tuple-element.161.refs_3_, ...), custom_call_target="tpu_custom_call" | custom-call | flops 4831838208 | bytes 25165824 | tf_op jit(solution)/shard_map/moe_bwd/pallas_call | solution.py:568
  317.3 16.0 %convolution_convert_fusion.1 = bf16[1024,1536]{1,0:T(8,128)(2,1)} fusion(bf16[1024,3072]{1,0:T(8,128)(2,1)} %get-tuple-element.187.refs_5_, bf16[1536,3072]{1,0:T(8,128)(2,1)} %constant_dynamic-update-slice_fusion.8.w_ref), kind=kOutput, calls=%fused_computation.4 | convolution fusion | flops 9665249280 | bytes 18874368 | tf_op jit(solution)/shard_map/dot_general | solution.py:24
  334.9 1.9 add_convert_fusion.11
  340.0 13.7 %convolution_convert_fusion.back_ref = bf16[1024,1536]{1,0:T(8,128)(2,1)} fusion(bf16[1024,3072]{1,0:T(8,128)(2,1)S(1)} %copy-done.2, bf16[1536,3072]{1,0:T(8,128)(2,1)} %constant_dynamic-update-slice_fusion.8.w_ref), kind=kOutput, calls=%fused_computation.3 | convolution fusion | flops 9665249280 | bytes 18874368 | tf_op jit(solution)/shard_map/dot_general | solution.py:24
  354.6 13.8 %back_mid.1 = (bf16[1024,1536]{1,0:T(8,128)(2,1)}, bf16[4,1024,384]{2,1,0:T(8,128)(2,1)}) custom-call(s32[1]{0:T(128)} %bitcast.11.own_ref, bf16[1024,1536]{1,0:T(8,128)(2,1)} %convolution_convert_fusion.back_ref, bf16[1024,1536]{1,0:T(8,128)(2,1)} %collective-permute-done.39.recv_ref, bf16[1024,128]{1,0:T(8,128)(2,1)} %subtract_convert_fusion.lg_ref, ...), custom_call_target="tpu_custom_call" | custom-call | flops 4831838208 | bytes 23592960 | tf_op jit(solution)/shard_map/back_mid/pallas_call | solution.py:370
  368.5 15.9 %weight_grad.4 = (bf16[768,1536]{1,0:T(8,128)(2,1)}, bf16[768,1536]{1,0:T(8,128)(2,1)}) custom-call(bf16[1024,1536]{1,0:T(8,128)(2,1)} %get-tuple-element.143.x_ref.refs_0_.refs_1_, bf16[1024,1536]{1,0:T(8,128)(2,1)} %get-tuple-element.143.x_ref.refs_0_.refs_1_, bf16[1024,1536]{1,0:T(8,128)(2,1)} %copy-done.1, bf16[1024,1536]{1,0:T(8,128)(2,1)} %copy-done.1, ...), custom_call_target="tpu_custom_call" | custom-call | flops 96636768 | bytes 188743 | tf_op jit(solution)/shard_map/weight_grad/pallas_call | solution.py:641
  384.4 6.0 %convolution_convert_fusion.3 = bf16[1536,768]{1,0:T(8,128)(2,1)} fusion(bf16[1024,1536]{1,0:T(8,128)(2,1)} %get-tuple-element.179.ag_ref, pred[]{:T(512)S(6)} %eq.14, bf16[1024,1536]{1,0:T(8,128)(2,1)S(1)} %copy-done.10), kind=kOutput, calls=%fused_computation.6 | convolution fusion | flops 2417885184 | bytes 8650753 | tf_op jit(solution)/shard_map/dot_general | solution.py:28
  394.1 3.9 convolution_convert_fusion.2
  398.0 15.9 %weight_grad.5 = (bf16[768,1536]{1,0:T(8,128)(2,1)}, bf16[768,1536]{1,0:T(8,128)(2,1)}) custom-call(bf16[1024,1536]{1,0:T(8,128)(2,1)} %get-tuple-element.143.x_ref.refs_0_.refs_1_, bf16[1024,1536]{1,0:T(8,128)(2,1)} %get-tuple-element.143.x_ref.refs_0_.refs_1_, bf16[1024,1536]{1,0:T(8,128)(2,1)} %copy-done.1, bf16[1024,1536]{1,0:T(8,128)(2,1)} %copy-done.1, ...), custom_call_target="tpu_custom_call" | custom-call | flops 96636768 | bytes 188743 | tf_op jit(solution)/shard_map/weight_grad/pallas_call | solution.py:641
  413.9 3.0 add_convert_fusion.1
  421.6 7.7 %reduce-scatter.6.cloned.1.call-done = bf16[1,1024,384]{2,1,0:T(8,128)(2,1)} async-done(((bf16[4,1024,384]{2,1,0:T(8,128)(2,1)}), bf16[1,1024,384]{2,1,0:T(8,128)(2,1)}) %reduce-scatter.6.cloned.1.call-update) | async-done | bytes 786448 | tf_op jit(solution)/shard_map/reduce_scatter | solution.py:961
  429.4 19.3 %attn_bwd.1 = (bf16[1024,384]{1,0:T(8,128)(2,1)}, bf16[1024,256]{1,0:T(8,128)(2,1)}) custom-call(bf16[1024,384]{1,0:T(8,128)(2,1)} %bitcast.56, bf16[6,1024,64]{2,1,0:T(8,128)(2,1)} %get-tuple-element.173.q_ref, bf16[2,1024,64]{2,1,0:T(8,128)(2,1)} %get-tuple-element.174.k_ref, bf16[2,1024,64]{2,1,0:T(8,128)(2,1)} %get-tuple-element.175.v_ref, ...), custom_call_target="tpu_custom_call" | custom-call | flops 6039797760 | bytes 3145728 | tf_op jit(solution)/shard_map/attn_bwd/pallas_call | solution.py:243
  448.6 8.9 %back_end.1 = bf16[1024,1536]{1,0:T(8,128)(2,1)} custom-call(bf16[1024,384]{1,0:T(8,128)(2,1)} %get-tuple-element.194.dq_ref, bf16[1024,256]{1,0:T(8,128)(2,1)} %get-tuple-element.195.dkv_ref, bf16[1536,768]{1,0:T(8,128)(2,1)} %pad_maximum_fusion.1.w_ref.small_ref, bf16[1024,1536]{1,0:T(8,128)(2,1)} %all-gather.7.cloned.1.call-done.tok_ref, ...), custom_call_target="tpu_custom_call" | custom-call | flops 2013265920 | bytes 11403264 | tf_op jit(solution)/shard_map/back_end/pallas_call | solution.py:418
  457.6 4.6 add_convert_fusion.5
  468.1 3.2 broadcast_select_fusion.7
  471.4 2.1 add_convert_fusion.14
  481.8 1.8 maximum_convert_fusion.1
  483.6 1.9 add_convert_fusion.4
  487.4 4.0 collective-permute-done.47
  492.8 2.1 add_convert_fusion.2
  496.6 2.1 add_convert_fusion.3
  500.2 8.7 %collective-permute-done.46 = bf16[768,384]{1,0:T(8,128)(2,1)} collective-permute-done((bf16[768,384]{1,0:T(8,128)(2,1)}, bf16[768,384]{1,0:T(8,128)(2,1)}, u32[]{:S(2)}, u32[]{:S(2)}) %collective-permute-start.46) | collective-permute-done | bytes 589856 | tf_op jit(solution)/shard_map/ppermute | solution.py:661
  515.4 2.3 collective-permute-done.49
  519.0 2.7 multiply_reduce_fusion.1
  526.0 1.7 multiply_reduce_fusion
  529.4 2.9 collective-permute-start.59
  532.4 2.0 collective-permute-start.57
  535.9 3.3 concatenate.163
  540.1 4.6 maximum_convert_fusion
  545.7 4.6 collective-permute-done.58
  (362 shorter events, 117.9 us)
Async XLA Ops:
  7.2 72.7 %all-gather.7.cloned.1.call-start = ((), (), s32[]{:S(2)}) async-start(), calls=%async_computation.3 | async-start | bytes 3932160 | tf_op jit(solution)/shard_map/all_gather | solution.py:842
  12.2 4.6 collective-permute-start.1
  13.8 97.3 %all-gather.13.cloned.1.call-start = ((), (), s32[]{:S(2)}) async-start(), calls=%async_computation.9 | async-start | bytes 1474560 | tf_op jit(solution)/shard_map/all_gather | solution.py:887
  18.3 7.4 %collective-permute-start.2 = (bf16[192,384]{1,0:T(8,128)(2,1)S(1)}, bf16[192,384]{1,0:T(8,128)(2,1)S(1)}, u32[]{:S(2)}, u32[]{:S(2)}) collective-permute-start(bf16[192,384]{1,0:T(8,128)(2,1)S(1)} %get-tuple-element.120), channel_id=1, source_target_pairs={{0,8},{8,0},{16,24},{24,16},{1,9},{9,1},{17,25},{25,17},{2,10},{10... | collective-permute-start | bytes 442376 | tf_op jit(solution)/shard_map/ppermute | solution.py:661
  21.7 8.8 %collective-permute-start.3 = (bf16[192,384]{1,0:T(8,128)(2,1)S(1)}, bf16[192,384]{1,0:T(8,128)(2,1)S(1)}, u32[]{:S(2)}, u32[]{:S(2)}) collective-permute-start(bf16[192,384]{1,0:T(8,128)(2,1)S(1)} %get-tuple-element.121), channel_id=1, source_target_pairs={{0,8},{8,0},{16,24},{24,16},{1,9},{9,1},{17,25},{25,17},{2,10},{10... | collective-permute-start | bytes 442376 | tf_op jit(solution)/shard_map/ppermute | solution.py:661
  21.7 6.7 %collective-permute-start.5 = (bf16[192,384]{1,0:T(8,128)(2,1)S(1)}, bf16[192,384]{1,0:T(8,128)(2,1)S(1)}, u32[]{:S(2)}, u32[]{:S(2)}) collective-permute-start(bf16[192,384]{1,0:T(8,128)(2,1)S(1)} %get-tuple-element.121), channel_id=1, source_target_pairs={{0,16},{8,24},{16,0},{24,8},{1,17},{9,25},{17,1},{25,9},{2,18},{10... | collective-permute-start | bytes 442376 | tf_op jit(solution)/shard_map/ppermute | solution.py:661
  23.7 11.5 %collective-permute-start.7 = (bf16[192,384]{1,0:T(8,128)(2,1)S(1)}, bf16[192,384]{1,0:T(8,128)(2,1)S(1)}, u32[]{:S(2)}, u32[]{:S(2)}) collective-permute-start(bf16[192,384]{1,0:T(8,128)(2,1)S(1)} %get-tuple-element.120), channel_id=1, source_target_pairs={{0,16},{8,24},{16,0},{24,8},{1,17},{9,25},{17,1},{25,9},{2,18},{10... | collective-permute-start | bytes 442376 | tf_op jit(solution)/shard_map/ppermute | solution.py:661
  25.7 8.2 %collective-permute-start.4 = (bf16[192,384]{1,0:T(8,128)(2,1)S(1)}, bf16[192,384]{1,0:T(8,128)(2,1)S(1)}, u32[]{:S(2)}, u32[]{:S(2)}) collective-permute-start(bf16[192,384]{1,0:T(8,128)(2,1)S(1)} %collective-permute-done.2), channel_id=1, source_target_pairs={{0,16},{8,24},{16,0},{24,8},{1,17},{9,25},{17,1},{25,9},{2,18},{10... | collective-permute-start | bytes 442376 | tf_op jit(solution)/shard_map/ppermute | solution.py:661
  28.4 6.1 %collective-permute-start.6 = (bf16[192,384]{1,0:T(8,128)(2,1)S(1)}, bf16[192,384]{1,0:T(8,128)(2,1)S(1)}, u32[]{:S(2)}, u32[]{:S(2)}) collective-permute-start(bf16[192,384]{1,0:T(8,128)(2,1)S(1)} %collective-permute-done.5), channel_id=1, source_target_pairs={{0,8},{8,0},{16,24},{24,16},{1,9},{9,1},{17,25},{25,17},{2,10},{10... | collective-permute-start | bytes 442376 | tf_op jit(solution)/shard_map/ppermute | solution.py:661
  36.6 4.4 collective-permute-start.8
  40.5 13.0 %collective-permute-start.13 = (bf16[192,1536]{1,0:T(8,128)(2,1)}, bf16[192,1536]{1,0:T(8,128)(2,1)}, u32[]{:S(2)}, u32[]{:S(2)}) collective-permute-start(bf16[192,1536]{1,0:T(8,128)(2,1)} %bitcast.43), channel_id=1, source_target_pairs={{0,4},{4,0},{1,5},{5,1},{2,6},{6,2},{3,7},{7,3},{8,12},{12,8},{9,1... | collective-permute-start | bytes 1769480 | tf_op jit(solution)/shard_map/ppermute | solution.py:661
  44.5 139.4 %all-gather.11.cloned.1.call-start = ((), (), s32[]{:S(2)}) async-start(), calls=%async_computation.8 | async-start | bytes 3932160 | tf_op jit(solution)/shard_map/all_gather | solution.py:908
  44.5 52.7 %collective-permute-start.9 = (bf16[192,3072]{1,0:T(8,128)(2,1)S(1)}, bf16[192,3072]{1,0:T(8,128)(2,1)}, u32[]{:S(2)}, u32[]{:S(2)}) collective-permute-start(bf16[192,3072]{1,0:T(8,128)(2,1)S(1)} %get-tuple-element.129), channel_id=1, source_target_pairs={{0,8},{8,0},{16,24},{24,16},{1,9},{9,1},{17,25},{25,17},{2,10},{10... | collective-permute-start | bytes 3538952 | tf_op jit(solution)/shard_map/ppermute | solution.py:661
  46.3 50.9 %collective-permute-start.10 = (bf16[192,3072]{1,0:T(8,128)(2,1)S(1)}, bf16[192,3072]{1,0:T(8,128)(2,1)}, u32[]{:S(2)}, u32[]{:S(2)}) collective-permute-start(bf16[192,3072]{1,0:T(8,128)(2,1)S(1)} %get-tuple-element.130), channel_id=1, source_target_pairs={{0,16},{8,24},{16,0},{24,8},{1,17},{9,25},{17,1},{25,9},{2,18},{10... | collective-permute-start | bytes 3538952 | tf_op jit(solution)/shard_map/ppermute | solution.py:661
  47.8 50.0 %collective-permute-start.11 = (bf16[192,3072]{1,0:T(8,128)(2,1)S(1)}, bf16[192,3072]{1,0:T(8,128)(2,1)}, u32[]{:S(2)}, u32[]{:S(2)}) collective-permute-start(bf16[192,3072]{1,0:T(8,128)(2,1)S(1)} %get-tuple-element.130), channel_id=1, source_target_pairs={{0,8},{8,0},{16,24},{24,16},{1,9},{9,1},{17,25},{25,17},{2,10},{10... | collective-permute-start | bytes 3538952 | tf_op jit(solution)/shard_map/ppermute | solution.py:661
  48.4 50.9 %collective-permute-start.12 = (bf16[192,3072]{1,0:T(8,128)(2,1)S(1)}, bf16[192,3072]{1,0:T(8,128)(2,1)}, u32[]{:S(2)}, u32[]{:S(2)}) collective-permute-start(bf16[192,3072]{1,0:T(8,128)(2,1)S(1)} %get-tuple-element.129), channel_id=1, source_target_pairs={{0,16},{8,24},{16,0},{24,8},{1,17},{9,25},{17,1},{25,9},{2,18},{10... | collective-permute-start | bytes 3538952 | tf_op jit(solution)/shard_map/ppermute | solution.py:661
  99.3 144.5 %all-gather.9.cloned.1.call-start = ((), (), s32[]{:S(2)}) async-start(), calls=%async_computation.4 | async-start | bytes 3932160 | tf_op jit(solution)/shard_map/all_gather | solution.py:915
  100.6 27.1 %collective-permute-start.14 = (bf16[192,3072]{1,0:T(8,128)(2,1)}, bf16[192,3072]{1,0:T(8,128)(2,1)}, u32[]{:S(2)}, u32[]{:S(2)}) collective-permute-start(bf16[192,3072]{1,0:T(8,128)(2,1)} %collective-permute-done.9), channel_id=1, source_target_pairs={{0,16},{8,24},{16,0},{24,8},{1,17},{9,25},{17,1},{25,9},{2,18},{10... | collective-permute-start | bytes 3538952 | tf_op jit(solution)/shard_map/ppermute | solution.py:661
  102.2 26.8 %collective-permute-start.15 = (bf16[192,3072]{1,0:T(8,128)(2,1)}, bf16[192,3072]{1,0:T(8,128)(2,1)}, u32[]{:S(2)}, u32[]{:S(2)}) collective-permute-start(bf16[192,3072]{1,0:T(8,128)(2,1)} %collective-permute-done.10), channel_id=1, source_target_pairs={{0,8},{8,0},{16,24},{24,16},{1,9},{9,1},{17,25},{25,17},{2,10},{10... | collective-permute-start | bytes 3538952 | tf_op jit(solution)/shard_map/ppermute | solution.py:661
  114.1 240.4 %reduce-scatter.4.cloned.1.call-start = ((), (), s32[]{:S(2)}) async-start(), calls=%async_computation.5 | async-start | bytes 3932160 | tf_op jit(solution)/shard_map/reduce_scatter | solution.py:932
  129.0 13.2 %collective-permute-start.18 = (bf16[192,768]{1,0:T(8,128)(2,1)S(1)}, bf16[192,768]{1,0:T(8,128)(2,1)S(1)}, u32[]{:S(2)}, u32[]{:S(2)}) collective-permute-start(bf16[192,768]{1,0:T(8,128)(2,1)S(1)} %get-tuple-element.128), channel_id=1, source_target_pairs={{0,16},{8,24},{16,0},{24,8},{1,17},{9,25},{17,1},{25,9},{2,18},{10... | collective-permute-start | bytes 884744 | tf_op jit(solution)/shard_map/ppermute | solution.py:661
  129.5 13.8 %collective-permute-start.19 = (bf16[192,768]{1,0:T(8,128)(2,1)S(1)}, bf16[192,768]{1,0:T(8,128)(2,1)S(1)}, u32[]{:S(2)}, u32[]{:S(2)}) collective-permute-start(bf16[192,768]{1,0:T(8,128)(2,1)S(1)} %get-tuple-element.128), channel_id=1, source_target_pairs={{0,8},{8,0},{16,24},{24,16},{1,9},{9,1},{17,25},{25,17},{2,10},{10... | collective-permute-start | bytes 884744 | tf_op jit(solution)/shard_map/ppermute | solution.py:661
  130.1 12.0 %collective-permute-start.17 = (bf16[192,768]{1,0:T(8,128)(2,1)S(1)}, bf16[192,768]{1,0:T(8,128)(2,1)S(1)}, u32[]{:S(2)}, u32[]{:S(2)}) collective-permute-start(bf16[192,768]{1,0:T(8,128)(2,1)S(1)} %get-tuple-element.127), channel_id=1, source_target_pairs={{0,8},{8,0},{16,24},{24,16},{1,9},{9,1},{17,25},{25,17},{2,10},{10... | collective-permute-start | bytes 884744 | tf_op jit(solution)/shard_map/ppermute | solution.py:661
  131.5 11.8 %collective-permute-start.20 = (bf16[192,768]{1,0:T(8,128)(2,1)S(1)}, bf16[192,768]{1,0:T(8,128)(2,1)S(1)}, u32[]{:S(2)}, u32[]{:S(2)}) collective-permute-start(bf16[192,768]{1,0:T(8,128)(2,1)S(1)} %get-tuple-element.127), channel_id=1, source_target_pairs={{0,16},{8,24},{16,0},{24,8},{1,17},{9,25},{17,1},{25,9},{2,18},{10... | collective-permute-start | bytes 884744 | tf_op jit(solution)/shard_map/ppermute | solution.py:661
  133.0 35.0 %collective-permute-start.25 = (bf16[384,768]{1,0:T(8,128)(2,1)S(1)}, bf16[384,768]{1,0:T(8,128)(2,1)S(1)}, u32[]{:S(2)}, u32[]{:S(2)}) collective-permute-start(bf16[384,768]{1,0:T(8,128)(2,1)S(1)} %pad_maximum_fusion.9), channel_id=1, source_target_pairs={{0,4},{4,0},{1,5},{5,1},{2,6},{6,2},{3,7},{7,3},{8,12},{12,8},{9,1... | collective-permute-start | bytes 1769480 | tf_op jit(solution)/shard_map/ppermute | solution.py:661
  143.2 29.7 %collective-permute-start.21 = (bf16[192,1536]{1,0:T(8,128)(2,1)S(1)}, bf16[192,1536]{1,0:T(8,128)(2,1)S(1)}, u32[]{:S(2)}, u32[]{:S(2)}) collective-permute-start(bf16[192,1536]{1,0:T(8,128)(2,1)S(1)} %copy-done.33), channel_id=1, source_target_pairs={{0,8},{8,0},{16,24},{24,16},{1,9},{9,1},{17,25},{25,17},{2,10},{10... | collective-permute-start | bytes 1769480 | tf_op jit(solution)/shard_map/ppermute | solution.py:661
  144.1 25.4 %collective-permute-start.28 = (bf16[384,768]{1,0:T(8,128)(2,1)S(1)}, bf16[384,768]{1,0:T(8,128)(2,1)S(1)}, u32[]{:S(2)}, u32[]{:S(2)}) collective-permute-start(bf16[384,768]{1,0:T(8,128)(2,1)S(1)} %pad_maximum_fusion.12), channel_id=1, source_target_pairs={{0,4},{4,0},{1,5},{5,1},{2,6},{6,2},{3,7},{7,3},{8,12},{12,8},{9,1... | collective-permute-start | bytes 1769480 | tf_op jit(solution)/shard_map/ppermute | solution.py:661
  157.3 9.4 %collective-permute-start.23 = (bf16[192,768]{1,0:T(8,128)(2,1)S(1)}, bf16[192,768]{1,0:T(8,128)(2,1)S(1)}, u32[]{:S(2)}, u32[]{:S(2)}) collective-permute-start(bf16[192,768]{1,0:T(8,128)(2,1)S(1)} %collective-permute-done.17), channel_id=1, source_target_pairs={{0,16},{8,24},{16,0},{24,8},{1,17},{9,25},{17,1},{25,9},{2,18},{10... | collective-permute-start | bytes 884744 | tf_op jit(solution)/shard_map/ppermute | solution.py:661
  158.6 9.1 %collective-permute-start.24 = (bf16[192,768]{1,0:T(8,128)(2,1)S(1)}, bf16[192,768]{1,0:T(8,128)(2,1)S(1)}, u32[]{:S(2)}, u32[]{:S(2)}) collective-permute-start(bf16[192,768]{1,0:T(8,128)(2,1)S(1)} %collective-permute-done.18), channel_id=1, source_target_pairs={{0,8},{8,0},{16,24},{24,16},{1,9},{9,1},{17,25},{25,17},{2,10},{10... | collective-permute-start | bytes 884744 | tf_op jit(solution)/shard_map/ppermute | solution.py:661
  168.9 15.0 %collective-permute-start.22 = (bf16[192,1536]{1,0:T(8,128)(2,1)S(1)}, bf16[192,1536]{1,0:T(8,128)(2,1)S(1)}, u32[]{:S(2)}, u32[]{:S(2)}) collective-permute-start(bf16[192,1536]{1,0:T(8,128)(2,1)S(1)} %copy-done.32), channel_id=1, source_target_pairs={{0,16},{8,24},{16,0},{24,8},{1,17},{9,25},{17,1},{25,9},{2,18},{10... | collective-permute-start | bytes 1769480 | tf_op jit(solution)/shard_map/ppermute | solution.py:661
  197.2 19.3 %collective-permute-start.29 = (bf16[1024,1536]{1,0:T(8,128)(2,1)}, bf16[1024,1536]{1,0:T(8,128)(2,1)S(1)}, u32[]{:S(2)}, u32[]{:S(2)}) collective-permute-start(bf16[1024,1536]{1,0:T(8,128)(2,1)} %get-tuple-element.143.x_ref.refs_0_.refs_1_), channel_id=1, source_target_pairs={{0,4},{4,0},{1,5},{5,1},{2,6},{6,2},{3,7},{7,3},{8,12},{12,8},{9,1... | collective-permute-start | bytes 9437192 | tf_op jit(solution)/shard_map/ppermute | solution.py:661
  197.3 18.6 %collective-permute-start.30 = (bf16[192,1536]{1,0:T(8,128)(2,1)S(1)}, bf16[192,1536]{1,0:T(8,128)(2,1)}, u32[]{:S(2)}, u32[]{:S(2)}) collective-permute-start(bf16[192,1536]{1,0:T(8,128)(2,1)S(1)} %copy-done.32), channel_id=1, source_target_pairs={{0,8},{8,0},{16,24},{24,16},{1,9},{9,1},{17,25},{25,17},{2,10},{10... | collective-permute-start | bytes 1769480 | tf_op jit(solution)/shard_map/ppermute | solution.py:661
  198.7 17.8 %collective-permute-start.31 = (bf16[192,1536]{1,0:T(8,128)(2,1)}, bf16[192,1536]{1,0:T(8,128)(2,1)}, u32[]{:S(2)}, u32[]{:S(2)}) collective-permute-start(bf16[192,1536]{1,0:T(8,128)(2,1)} %get-tuple-element.137.refs_1_.refs_4_), channel_id=1, source_target_pairs={{0,16},{8,24},{16,0},{24,8},{1,17},{9,25},{17,1},{25,9},{2,18},{10... | collective-permute-start | bytes 1769480 | tf_op jit(solution)/shard_map/ppermute | solution.py:661
  199.9 16.6 %collective-permute-start.32 = (f32[1024,128]{1,0:T(8,128)}, f32[1024,128]{1,0:T(8,128)}, u32[]{:S(2)}, u32[]{:S(2)}) collective-permute-start(f32[1024,128]{1,0:T(8,128)} %get-tuple-element.144.gate_ref.refs_2_), channel_id=1, source_target_pairs={{0,4},{4,0},{1,5},{5,1},{2,6},{6,2},{3,7},{7,3},{8,12},{12,8},{9,1... | collective-permute-start | bytes 1572872 | tf_op jit(solution)/shard_map/ppermute | solution.py:661
  215.0 18.4 %collective-permute-start.33 = (bf16[192,1536]{1,0:T(8,128)(2,1)}, bf16[192,1536]{1,0:T(8,128)(2,1)}, u32[]{:S(2)}, u32[]{:S(2)}) collective-permute-start(bf16[192,1536]{1,0:T(8,128)(2,1)} %copy-done.58), channel_id=1, source_target_pairs={{0,16},{8,24},{16,0},{24,8},{1,17},{9,25},{17,1},{25,9},{2,18},{10... | collective-permute-start | bytes 1769480 | tf_op jit(solution)/shard_map/ppermute | solution.py:661
  215.9 17.5 %collective-permute-start.34 = (bf16[192,1536]{1,0:T(8,128)(2,1)}, bf16[192,1536]{1,0:T(8,128)(2,1)S(1)}, u32[]{:S(2)}, u32[]{:S(2)}) collective-permute-start(bf16[192,1536]{1,0:T(8,128)(2,1)} %copy-done.59), channel_id=1, source_target_pairs={{0,8},{8,0},{16,24},{24,16},{1,9},{9,1},{17,25},{25,17},{2,10},{10... | collective-permute-start | bytes 1769480 | tf_op jit(solution)/shard_map/ppermute | solution.py:661
  243.8 10.1 %collective-permute-start.36 = (bf16[1024,1536]{1,0:T(8,128)(2,1)}, bf16[1024,1536]{1,0:T(8,128)(2,1)S(1)}, u32[]{:S(2)}, u32[]{:S(2)}) collective-permute-start(bf16[1024,1536]{1,0:T(8,128)(2,1)} %all-gather.9.cloned.1.call-done.refs_0_.refs_1_), channel_id=1, source_target_pairs={{0,4},{4,0},{1,5},{5,1},{2,6},{6,2},{3,7},{7,3},{8,12},{12,8},{9,1... | collective-permute-start | bytes 9437192 | tf_op jit(solution)/shard_map/ppermute | solution.py:661
  243.8 39.2 %collective-permute-start.35 = (bf16[1024,1536]{1,0:T(8,128)(2,1)}, bf16[1024,1536]{1,0:T(8,128)(2,1)}, u32[]{:S(2)}, u32[]{:S(2)}) collective-permute-start(bf16[1024,1536]{1,0:T(8,128)(2,1)} %combine.2), channel_id=1, source_target_pairs={{0,4},{4,0},{1,5},{5,1},{2,6},{6,2},{3,7},{7,3},{8,12},{12,8},{9,1... | collective-permute-start | bytes 9437192 | tf_op jit(solution)/shard_map/ppermute | solution.py:661
  280.4 35.8 %collective-permute-start.37 = (bf16[768,768]{1,0:T(8,128)(2,1)}, bf16[768,768]{1,0:T(8,128)(2,1)S(1)}, u32[]{:S(2)}, u32[]{:S(2)}) collective-permute-start(bf16[768,768]{1,0:T(8,128)(2,1)} %get-tuple-element.163), channel_id=1, source_target_pairs={{0,16},{8,24},{16,0},{24,8},{1,17},{9,25},{17,1},{25,9},{2,18},{10... | collective-permute-start | bytes 3538952 | tf_op jit(solution)/shard_map/ppermute | solution.py:661
  281.7 34.6 %collective-permute-start.38 = (bf16[768,768]{1,0:T(8,128)(2,1)}, bf16[768,768]{1,0:T(8,128)(2,1)}, u32[]{:S(2)}, u32[]{:S(2)}) collective-permute-start(bf16[768,768]{1,0:T(8,128)(2,1)} %get-tuple-element.164), channel_id=1, source_target_pairs={{0,8},{8,0},{16,24},{24,16},{1,9},{9,1},{17,25},{25,17},{2,10},{10... | collective-permute-start | bytes 3538952 | tf_op jit(solution)/shard_map/ppermute | solution.py:661
  288.4 141.0 %reduce-scatter.6.cloned.1.call-start = ((), (), s32[]{:S(2)}) async-start(), calls=%async_computation.6 | async-start | bytes 3932160 | tf_op jit(solution)/shard_map/reduce_scatter | solution.py:961
  316.2 17.6 %collective-permute-start.40 = (f32[1024,128]{1,0:T(8,128)}, f32[1024,128]{1,0:T(8,128)S(1)}, u32[]{:S(2)}, u32[]{:S(2)}) collective-permute-start(f32[1024,128]{1,0:T(8,128)} %get-tuple-element.168), channel_id=1, source_target_pairs={{0,4},{4,0},{1,5},{5,1},{2,6},{6,2},{3,7},{7,3},{8,12},{12,8},{9,1... | collective-permute-start | bytes 1572872 | tf_op jit(solution)/shard_map/ppermute | solution.py:661
  333.3 21.3 %collective-permute-start.39 = (bf16[1024,1536]{1,0:T(8,128)(2,1)}, bf16[1024,1536]{1,0:T(8,128)(2,1)}, u32[]{:S(2)}, u32[]{:S(2)}) collective-permute-start(bf16[1024,1536]{1,0:T(8,128)(2,1)} %convolution_convert_fusion.1), channel_id=1, source_target_pairs={{0,4},{4,0},{1,5},{5,1},{2,6},{6,2},{3,7},{7,3},{8,12},{12,8},{9,1... | collective-permute-start | bytes 9437192 | tf_op jit(solution)/shard_map/ppermute | solution.py:661
  338.1 15.6 %collective-permute-start.41 = (bf16[384,768]{1,0:T(8,128)(2,1)S(1)}, bf16[384,768]{1,0:T(8,128)(2,1)S(1)}, u32[]{:S(2)}, u32[]{:S(2)}) collective-permute-start(bf16[384,768]{1,0:T(8,128)(2,1)S(1)} %add_convert_fusion.11), channel_id=1, source_target_pairs={{0,8},{8,0},{16,24},{24,16},{1,9},{9,1},{17,25},{25,17},{2,10},{10... | collective-permute-start | bytes 1769480 | tf_op jit(solution)/shard_map/ppermute | solution.py:661
  338.7 15.9 %collective-permute-start.42 = (bf16[384,768]{1,0:T(8,128)(2,1)S(1)}, bf16[384,768]{1,0:T(8,128)(2,1)}, u32[]{:S(2)}, u32[]{:S(2)}) collective-permute-start(bf16[384,768]{1,0:T(8,128)(2,1)S(1)} %add_convert_fusion.10), channel_id=1, source_target_pairs={{0,16},{8,24},{16,0},{24,8},{1,17},{9,25},{17,1},{25,9},{2,18},{10... | collective-permute-start | bytes 1769480 | tf_op jit(solution)/shard_map/ppermute | solution.py:661
  368.4 186.3 %reduce-scatter.8.cloned.1.call-start = ((), (), s32[]{:S(2)}) async-start(), calls=%async_computation.7 | async-start | bytes 3932160 | tf_op jit(solution)/shard_map/reduce_scatter | solution.py:985
  390.4 23.5 %collective-permute-start.50 = (bf16[1536,768]{1,0:T(8,128)(2,1)}, bf16[1536,768]{1,0:T(8,128)(2,1)}, u32[]{:S(2)}, u32[]{:S(2)}) collective-permute-start(bf16[1536,768]{1,0:T(8,128)(2,1)} %convolution_convert_fusion.3), channel_id=1, source_target_pairs={{0,4},{4,0},{1,5},{5,1},{2,6},{6,2},{3,7},{7,3},{8,12},{12,8},{9,1... | collective-permute-start | bytes 7077896 | tf_op jit(solution)/shard_map/ppermute | solution.py:661
  391.2 66.3 %collective-permute-start.43 = (bf16[768,1536]{1,0:T(8,128)(2,1)}, bf16[768,1536]{1,0:T(8,128)(2,1)}, u32[]{:S(2)}, u32[]{:S(2)}) collective-permute-start(bf16[768,1536]{1,0:T(8,128)(2,1)} %get-tuple-element.184), channel_id=1, source_target_pairs={{0,16},{8,24},{16,0},{24,8},{1,17},{9,25},{17,1},{25,9},{2,18},{10... | collective-permute-start | bytes 7077896 | tf_op jit(solution)/shard_map/ppermute | solution.py:661
  392.4 65.2 %collective-permute-start.44 = (bf16[768,1536]{1,0:T(8,128)(2,1)}, bf16[768,1536]{1,0:T(8,128)(2,1)}, u32[]{:S(2)}, u32[]{:S(2)}) collective-permute-start(bf16[768,1536]{1,0:T(8,128)(2,1)} %get-tuple-element.185), channel_id=1, source_target_pairs={{0,8},{8,0},{16,24},{24,16},{1,9},{9,1},{17,25},{25,17},{2,10},{10... | collective-permute-start | bytes 7077896 | tf_op jit(solution)/shard_map/ppermute | solution.py:661
  418.0 53.3 %collective-permute-start.51 = (bf16[768,384]{1,0:T(8,128)(2,1)}, bf16[768,384]{1,0:T(8,128)(2,1)}, u32[]{:S(2)}, u32[]{:S(2)}) collective-permute-start(bf16[768,384]{1,0:T(8,128)(2,1)} %get-tuple-element.284), channel_id=1, source_target_pairs={{0,16},{8,24},{16,0},{24,8},{1,17},{9,25},{17,1},{25,9},{2,18},{10... | collective-permute-start | bytes 1769480 | tf_op jit(solution)/shard_map/ppermute | solution.py:661
  419.9 51.5 %collective-permute-start.52 = (bf16[768,384]{1,0:T(8,128)(2,1)}, bf16[768,384]{1,0:T(8,128)(2,1)}, u32[]{:S(2)}, u32[]{:S(2)}) collective-permute-start(bf16[768,384]{1,0:T(8,128)(2,1)} %pad_maximum_fusion.14), channel_id=1, source_target_pairs={{0,8},{8,0},{16,24},{24,16},{1,9},{9,1},{17,25},{25,17},{2,10},{10... | collective-permute-start | bytes 1769480 | tf_op jit(solution)/shard_map/ppermute | solution.py:661
  462.1 29.2 %collective-permute-start.47 = (bf16[384,1536]{1,0:T(8,128)(2,1)}, bf16[384,1536]{1,0:T(8,128)(2,1)}, u32[]{:S(2)}, u32[]{:S(2)}) collective-permute-start(bf16[384,1536]{1,0:T(8,128)(2,1)} %get-tuple-element.192), channel_id=1, source_target_pairs={{0,8},{8,0},{16,24},{24,16},{1,9},{9,1},{17,25},{25,17},{2,10},{10... | collective-permute-start | bytes 3538952 | tf_op jit(solution)/shard_map/ppermute | solution.py:661
  463.6 29.2 %collective-permute-start.48 = (bf16[384,1536]{1,0:T(8,128)(2,1)}, bf16[384,1536]{1,0:T(8,128)(2,1)}, u32[]{:S(2)}, u32[]{:S(2)}) collective-permute-start(bf16[384,1536]{1,0:T(8,128)(2,1)} %get-tuple-element.193), channel_id=1, source_target_pairs={{0,16},{8,24},{16,0},{24,8},{1,17},{9,25},{17,1},{25,9},{2,18},{10... | collective-permute-start | bytes 3538952 | tf_op jit(solution)/shard_map/ppermute | solution.py:661
  471.3 12.2 %collective-permute-start.45 = (bf16[1536,384]{1,0:T(8,128)(2,1)}, bf16[1536,384]{1,0:T(8,128)(2,1)}, u32[]{:S(2)}, u32[]{:S(2)}) collective-permute-start(bf16[1536,384]{1,0:T(8,128)(2,1)} %get-tuple-element.348), channel_id=1, source_target_pairs={{0,4},{4,0},{1,5},{5,1},{2,6},{6,2},{3,7},{7,3},{8,12},{12,8},{9,1... | collective-permute-start | bytes 3538952 | tf_op jit(solution)/shard_map/ppermute | solution.py:661
  473.5 38.0 %collective-permute-start.53 = (bf16[384,384]{1,0:T(8,128)(2,1)}, bf16[384,384]{1,0:T(8,128)(2,1)}, u32[]{:S(2)}, u32[]{:S(2)}) collective-permute-start(bf16[384,384]{1,0:T(8,128)(2,1)} %get-tuple-element.212), channel_id=1, source_target_pairs={{0,8},{8,0},{16,24},{24,16},{1,9},{9,1},{17,25},{25,17},{2,10},{10... | collective-permute-start | bytes 884744 | tf_op jit(solution)/shard_map/ppermute | solution.py:661
  476.1 3.7 collective-permute-start.60
  479.8 31.7 %collective-permute-start.54 = (bf16[384,384]{1,0:T(8,128)(2,1)}, bf16[384,384]{1,0:T(8,128)(2,1)}, u32[]{:S(2)}, u32[]{:S(2)}) collective-permute-start(bf16[384,384]{1,0:T(8,128)(2,1)} %get-tuple-element.213), channel_id=1, source_target_pairs={{0,16},{8,24},{16,0},{24,8},{1,17},{9,25},{17,1},{25,9},{2,18},{10... | collective-permute-start | bytes 884744 | tf_op jit(solution)/shard_map/ppermute | solution.py:661
  486.3 22.6 %collective-permute-start.46 = (bf16[768,384]{1,0:T(8,128)(2,1)}, bf16[768,384]{1,0:T(8,128)(2,1)}, u32[]{:S(2)}, u32[]{:S(2)}) collective-permute-start(bf16[768,384]{1,0:T(8,128)(2,1)} %slice.366), channel_id=1, source_target_pairs={{0,8},{8,0},{16,24},{24,16},{1,9},{9,1},{17,25},{25,17},{2,10},{10... | collective-permute-start | bytes 1769480 | tf_op jit(solution)/shard_map/ppermute | solution.py:661
  510.0 7.7 %collective-permute-start.49 = (bf16[384,384]{1,0:T(8,128)(2,1)S(1)}, bf16[384,384]{1,0:T(8,128)(2,1)S(1)}, u32[]{:S(2)}, u32[]{:S(2)}) collective-permute-start(bf16[384,384]{1,0:T(8,128)(2,1)S(1)} %add_convert_fusion.17), channel_id=1, source_target_pairs={{0,16},{8,24},{16,0},{24,8},{1,17},{9,25},{17,1},{25,9},{2,18},{10... | collective-permute-start | bytes 884744 | tf_op jit(solution)/shard_map/ppermute | solution.py:661
  518.9 3.4 collective-permute-start.55
  521.7 4.3 collective-permute-start.56
  529.4 15.3 %collective-permute-start.59 = (bf16[192,512]{1,0:T(8,128)(2,1)}, bf16[192,512]{1,0:T(8,128)(2,1)}, u32[]{:S(2)}, u32[]{:S(2)}) collective-permute-start(bf16[192,512]{1,0:T(8,128)(2,1)} %get-tuple-element.345), channel_id=1, source_target_pairs={{0,3},{1,0},{2,1},{3,2},{4,7},{5,4},{6,5},{7,6},{8,11},{9,8},{10,9... | collective-permute-start | bytes 589832 | tf_op jit(solution)/shard_map/ppermute | solution.py:1053
  532.3 18.1 %collective-permute-start.58 = (bf16[192,512]{1,0:T(8,128)(2,1)}, bf16[192,512]{1,0:T(8,128)(2,1)}, u32[]{:S(2)}, u32[]{:S(2)}) collective-permute-start(bf16[192,512]{1,0:T(8,128)(2,1)} %get-tuple-element.344), channel_id=1, source_target_pairs={{0,2},{1,3},{2,0},{3,1},{4,6},{5,7},{6,4},{7,5},{8,10},{9,11},{10,... | collective-permute-start | bytes 589832 | tf_op jit(solution)/shard_map/ppermute | solution.py:1053
  532.4 19.0 %collective-permute-start.57 = (bf16[192,512]{1,0:T(8,128)(2,1)}, bf16[192,512]{1,0:T(8,128)(2,1)}, u32[]{:S(2)}, u32[]{:S(2)}) collective-permute-start(bf16[192,512]{1,0:T(8,128)(2,1)} %get-tuple-element.343), channel_id=1, source_target_pairs={{0,1},{1,2},{2,3},{3,0},{4,5},{5,6},{6,7},{7,4},{8,9},{9,10},{10,1... | collective-permute-start | bytes 589832 | tf_op jit(solution)/shard_map/ppermute | solution.py:1053
  (65 other events, 404.8 us)
Sparse Core Ops, SparseCore 0:
  13.9 65.8 all-gather.6
  82.0 29.0 all-gather.12
  113.2 62.6 all-gather.10
  177.4 62.1 all-gather.8
  288.5 60.0 reduce-scatter.3
  368.5 60.7 reduce-scatter.5
  457.6 60.2 reduce-scatter.7

commit v6 on v5

--- a/solution.py
+++ b/solution.py
@@ -907,7 +907,7 @@
 
     att_all = lax.all_gather(after(attended, *in_got, *in_rest, *out_pair), "mp", axis=0, tiled=False)
     middle, normed_m, gates, att_flat = mid_fwd(
-        after(att_all, in_full, *out_got), wo_rows, tok_all, moe_g, pack, small_at, routes[0]
+        after(att_all, in_full, out_got[0]), wo_rows, tok_all, moe_g, pack, small_at, routes[0]
     )
 
     cot_own = lax.optimization_barrier(reorder(cotangent[0], q, quads))
@@ -921,7 +921,7 @@
     hid_own, gact_own = moe_fwd(
         base, x_own, in_full, gates, length, 100
     )
-    x_other = after(x_other, gact_own, *out_rest)
+    x_other = after(x_other, gact_own, out_got[-1])
     out_diag = gather_diagonal(all_after(out_got, gact_own), quads)
     out_full = gather_pieces(*out_src, out_got, out_rest, out_diag, quads)
     hid_other, gact_other = moe_fwd(base, x_other, in_full, gates_other, length, 1)

time: 571 us -> 564 us (0.988)
    unnamed x147 -> x143, local copies, waits for them, and re-layouts: 32.5 us -> 30.2 us
  transfers between devices with their start and end apart: 68 -> 68, of which waited for: 20 -> 22; matrix products, arithmetic and copies ran while one was open for 29% -> 29% of each run, Pallas kernels for 34% -> 34%
where the time goes in v6:
time: 564 us; the launch traced here: 558 us
  Pallas kernels  206 us (37%)
  waiting for transfers between devices  103 us (18%)
  other arithmetic  78.7 us (14%)
  local copies, waits for them, and re-layouts  57.3 us (10%)
  starting transfers between devices  53.5 us (9%)
  matrix products  44.7 us (8%)
  between operations  15.6 us (3%)
    ppermute x58, waiting for transfers between devices, swap(): return lax.ppermute(value, axis, [(i, i ^ bit) for i in range(size)])  58.4 us
    pallas_call x3, Pallas kernels, weight_grad(): pl.pallas_call(functools.partial(segment_kernel, count=count), grid=(coun...  56.2 us
    ppermute x58, starting transfers between devices, swap(): return lax.ppermute(value, axis, [(i, i ^ bit) for i in range(size)])  48 us
    pallas_call x2, Pallas kernels, moe_fwd(): pl.pallas_call(moe_fwd_kernel, grid_spec=pltpu.PrefetchScalarGridSpec(num...  30.3 us
    unnamed x143, local copies, waits for them, and re-layouts  30.2 us
    dot_general x2, matrix products, nt(): lax.dot_general(left, right, (((1,), (1,)), ((), ())), preferred_element_...  29.5 us
    pallas_call x2, Pallas kernels, moe_bwd(): pl.pallas_call(moe_bwd_kernel, grid_spec=pltpu.PrefetchScalarGridSpec(num...  27.5 us
    all_gather x1, waiting for transfers between devices, body(): tok_all = lax.all_gather(tok_own, 'mp', axis=0, tiled=True)  22.1 us
  transfers between devices with their start and end apart: 68, of which 22 were waited for; matrix products, arithmetic and copies ran while one was open for 29% of the time, Pallas kernels for 34%

profile of v6, /device:TPU:0, one launch (start us, length us, event | category | flops | bytes accessed | tf_op | source)
XLA Modules:
  0.0 558.3 jit_solution(13215004637257886795)
XLA Ops:
  7.2 3.3 constant_dynamic-slice_fusion.15
  10.5 1.7 reshape.79
  18.3 2.7 collective-permute-start.2
  21.7 2.0 collective-permute-start.5
  25.7 2.0 collective-permute-start.4
  28.4 2.0 collective-permute-start.6
  31.1 2.7 collective-permute-done.4
  40.9 1.8 broadcast_select_fusion.8
  44.5 1.8 collective-permute-start.9
  48.6 3.8 negate_select_fusion
  53.4 2.5 bitcast_select_fusion
  57.8 22.1 %all-gather.7.cloned.1.call-done.tok_ref = bf16[1024,1536]{1,0:T(8,128)(2,1)} async-done(((bf16[256,1536]{1,0:T(8,128)(2,1)}), bf16[1024,1536]{1,0:T(8,128)(2,1)}) %all-gather.7.cloned.1.call-update) | async-done | bytes 3145744 | tf_op jit(solution)/shard_map/all_gather | solution.py:842
  79.9 17.3 %attn_fwd.1 = (bf16[1024,1536]{1,0:T(8,128)(2,1)}, bf16[6,1024,64]{2,1,0:T(8,128)(2,1)}, bf16[2,1024,64]{2,1,0:T(8,128)(2,1)}, bf16[2,1024,64]{2,1,0:T(8,128)(2,...) custom-call(bf16[1024,1536]{1,0:T(8,128)(2,1)} %all-gather.7.cloned.1.call-done.tok_ref, ...), custom_call_target="tpu_custom_call" | custom-call | flops 44291848 | bytes 82575 | tf_op jit(solution)/shard_map/attn_fwd/pallas_call | solution.py:135
  102.7 8.4 %all-gather.13.cloned.1.call-done = bf16[768,704]{1,0:T(8,128)(2,1)} async-done(((bf16[192,704]{1,0:T(8,128)(2,1)}), bf16[768,704]{1,0:T(8,128)(2,1)}) %all-gather.13.cloned.1.call-update) | async-done | bytes 1081360 | tf_op jit(solution)/shard_map/all_gather | solution.py:887
  114.6 13.1 %collective-permute-done.14 = bf16[192,3072]{1,0:T(8,128)(2,1)} collective-permute-done((bf16[192,3072]{1,0:T(8,128)(2,1)}, bf16[192,3072]{1,0:T(8,128)(2,1)}, u32[]{:S(2)}, u32[]{:S(2)}) %collective-permute-start.14) | collective-permute-done | bytes 1179680 | tf_op jit(solution)/shard_map/ppermute | solution.py:661
  133.2 8.9 %collective-permute-done.17 = bf16[192,768]{1,0:T(8,128)(2,1)S(1)} collective-permute-done((bf16[192,768]{1,0:T(8,128)(2,1)S(1)}, bf16[192,768]{1,0:T(8,128)(2,1)S(1)}, u32[]{:S(2)}, u32[]{:S(2)}) %collective-permute-start.17) | collective-permute-done | bytes 294944 | tf_op jit(solution)/shard_map/ppermute | solution.py:661
  145.3 2.4 constant_dynamic-update-slice_fusion.13
  147.7 2.4 constant_dynamic-update-slice_fusion.12
  150.1 2.4 constant_dynamic-update-slice_fusion.11
  152.5 2.5 constant_dynamic-update-slice_fusion.10
  154.9 2.3 constant_dynamic-update-slice_fusion.9
  160.0 2.4 constant_dynamic-update-slice_fusion.8.w_ref
  162.4 4.3 collective-permute-done.22
  170.4 2.6 pad_maximum_fusion.wo_ref
  172.9 3.0 all-gather.11.cloned.1.call-done
  175.9 13.1 %mid_fwd.1 = (f32[1024,1536]{1,0:T(8,128)}, bf16[1024,1536]{1,0:T(8,128)(2,1)}, f32[1024,128]{1,0:T(8,128)}, bf16[1024,1536]{1,0:T(8,128)(2,1)}) custom-call(bf16[4,1024,384]{2,1,0:T(8,128)(2,1)} %bitcast.55, bf16[1536,1536]{1,0:T(8,128)(2,1)} %pad_maximum_fusion.wo_ref, bf16[1024,1536]{1,0:T(8,128)(2,1)} %all-gather.7.cloned.1.call-done.tok_ref, ...), custom_call_target="tpu_custom_call" | custom-call | flops 4831838208 | bytes 20447232 | tf_op jit(solution)/shard_map/mid_fwd/pallas_call | solution.py:309
  192.8 15.1 %moe_fwd.2 = (bf16[1024,3072]{1,0:T(8,128)(2,1)}, bf16[1024,1536]{1,0:T(8,128)(2,1)}) custom-call(s32[1]{0:T(128)} %bitcast.9.base_ref.refs_0_, bf16[1024,1536]{1,0:T(8,128)(2,1)} %get-tuple-element.142.x_ref.refs_0_.refs_1_, bf16[1536,3072]{1,0:T(8,128)(2,1)} %constant_dynamic-update-slice_fusion.8.w_ref, f32[1024,128]{1,0:T(8,128)} %get-tuple-element.143.gate_ref.refs_2_), custom_call_target="tpu_custom_call" | custom-call | flops 96636768 | bytes 314572 | tf_op jit(solution)/shard_map/moe_fwd/pallas_call | solution.py:469
  211.1 15.1 %moe_fwd.3 = (bf16[1024,3072]{1,0:T(8,128)(2,1)}, bf16[1024,1536]{1,0:T(8,128)(2,1)}) custom-call(s32[1]{0:T(128)} %bitcast.9.base_ref.refs_0_, bf16[1024,1536]{1,0:T(8,128)(2,1)} %copy-done.1, bf16[1536,3072]{1,0:T(8,128)(2,1)} %constant_dynamic-update-slice_fusion.8.w_ref, f32[1024,128]{1,0:T(8,128)} %collective-permute-done.30.gate_ref.refs_2_), custom_call_target="tpu_custom_call" | custom-call | flops 9663676416 | bytes 31457280 | tf_op jit(solution)/shard_map/moe_fwd/pallas_call | solution.py:469
  226.2 4.1 collective-permute-done.32.refs_5_.refs_8_
  230.3 9.6 %combine.2 = bf16[1024,1536]{1,0:T(8,128)(2,1)} custom-call(bf16[1024,1536]{1,0:T(8,128)(2,1)} %get-tuple-element.155.refs_0_.refs_5_, bf16[192,1536]{1,0:T(8,128)(2,1)} %get-tuple-element.137.refs_1_.refs_4_, bf16[192,1536]{1,0:T(8,128)(2,1)} %get-tuple-element.145.refs_2_.refs_5_, bf16[192,1536]{1,0:T(8,128)(2,1)} %copy-done.58, ...), custom_call_target="tpu_custom_call" | custom-call | flops 4831838208 | bytes 11010048 | tf_op jit(solution)/shard_map/combine/pallas_call | solution.py:517
  240.4 9.5 %combine.3 = bf16[1024,1536]{1,0:T(8,128)(2,1)} custom-call(bf16[1024,1536]{1,0:T(8,128)(2,1)} %get-tuple-element.154.refs_0_.refs_4_, bf16[192,1536]{1,0:T(8,128)(2,1)} %get-tuple-element.137.refs_1_.refs_4_, bf16[192,1536]{1,0:T(8,128)(2,1)} %get-tuple-element.145.refs_2_.refs_5_, bf16[192,1536]{1,0:T(8,128)(2,1)} %copy-done.58, ...), custom_call_target="tpu_custom_call" | custom-call | flops 4831838208 | bytes 11010048 | tf_op jit(solution)/shard_map/combine/pallas_call | solution.py:517
  251.6 24.9 %weight_grad.3 = (bf16[768,768]{1,0:T(8,128)(2,1)}, bf16[768,768]{1,0:T(8,128)(2,1)}, bf16[768,768]{1,0:T(8,128)(2,1)}, bf16[768,768]{1,0:T(8,128)(2,1)}) custom-call(bf16[1024,1536]{1,0:T(8,128)(2,1)} %all-gather.9.cloned.1.call-done.refs_0_.refs_1_, bf16[1024,1536]{1,0:T(8,128)(2,1)} %all-gather.9.cloned.1.call-done.refs_0_.refs_1_, ...), custom_call_target="tpu_custom_call" | custom-call | flops 96636768 | bytes 125829 | tf_op jit(solution)/shard_map/weight_grad/pallas_call | solution.py:641
  279.5 5.3 add_convert_fusion
  284.9 13.8 %moe_bwd.2 = (bf16[1024,3072]{1,0:T(8,128)(2,1)}, f32[1024,128]{1,0:T(8,128)}) custom-call(s32[1]{0:T(128)} %bitcast.9.base_ref.refs_0_, bf16[1024,1536]{1,0:T(8,128)(2,1)} %all-gather.9.cloned.1.call-done.refs_0_.refs_1_, f32[1024,128]{1,0:T(8,128)} %get-tuple-element.143.gate_ref.refs_2_, bf16[1024,3072]{1,0:T(8,128)(2,1)} %get-tuple-element.158.refs_3_, ...), custom_call_target="tpu_custom_call" | custom-call | flops 4831838208 | bytes 25165824 | tf_op jit(solution)/shard_map/moe_bwd/pallas_call | solution.py:568
  298.7 13.8 %moe_bwd.3 = (bf16[1024,3072]{1,0:T(8,128)(2,1)}, f32[1024,128]{1,0:T(8,128)}) custom-call(s32[1]{0:T(128)} %bitcast.9.base_ref.refs_0_, bf16[1024,1536]{1,0:T(8,128)(2,1)} %copy-done.3, f32[1024,128]{1,0:T(8,128)} %collective-permute-done.30.gate_ref.refs_2_, bf16[1024,3072]{1,0:T(8,128)(2,1)} %get-tuple-element.161.refs_3_, ...), custom_call_target="tpu_custom_call" | custom-call | flops 4831838208 | bytes 25165824 | tf_op jit(solution)/shard_map/moe_bwd/pallas_call | solution.py:568
  313.5 15.7 %convolution_convert_fusion.1 = bf16[1024,1536]{1,0:T(8,128)(2,1)} fusion(bf16[1024,3072]{1,0:T(8,128)(2,1)} %get-tuple-element.187.refs_5_, bf16[1536,3072]{1,0:T(8,128)(2,1)} %constant_dynamic-update-slice_fusion.8.w_ref), kind=kOutput, calls=%fused_computation.4 | convolution fusion | flops 9665249280 | bytes 18874368 | tf_op jit(solution)/shard_map/dot_general | solution.py:24
  330.8 1.8 add_convert_fusion.11
  336.0 13.8 %convolution_convert_fusion.back_ref = bf16[1024,1536]{1,0:T(8,128)(2,1)} fusion(bf16[1024,3072]{1,0:T(8,128)(2,1)S(1)} %copy-done.2, bf16[1536,3072]{1,0:T(8,128)(2,1)} %constant_dynamic-update-slice_fusion.8.w_ref), kind=kOutput, calls=%fused_computation.3 | convolution fusion | flops 9665249280 | bytes 18874368 | tf_op jit(solution)/shard_map/dot_general | solution.py:24
  350.6 13.8 %back_mid.1 = (bf16[1024,1536]{1,0:T(8,128)(2,1)}, bf16[4,1024,384]{2,1,0:T(8,128)(2,1)}) custom-call(s32[1]{0:T(128)} %bitcast.11.own_ref, bf16[1024,1536]{1,0:T(8,128)(2,1)} %convolution_convert_fusion.back_ref, bf16[1024,1536]{1,0:T(8,128)(2,1)} %collective-permute-done.39.recv_ref, bf16[1024,128]{1,0:T(8,128)(2,1)} %subtract_convert_fusion.lg_ref, ...), custom_call_target="tpu_custom_call" | custom-call | flops 4831838208 | bytes 23592960 | tf_op jit(solution)/shard_map/back_mid/pallas_call | solution.py:370
  364.6 15.7 %weight_grad.4 = (bf16[768,1536]{1,0:T(8,128)(2,1)}, bf16[768,1536]{1,0:T(8,128)(2,1)}) custom-call(bf16[1024,1536]{1,0:T(8,128)(2,1)} %get-tuple-element.142.x_ref.refs_0_.refs_1_, bf16[1024,1536]{1,0:T(8,128)(2,1)} %get-tuple-element.142.x_ref.refs_0_.refs_1_, bf16[1024,1536]{1,0:T(8,128)(2,1)} %copy-done.1, bf16[1024,1536]{1,0:T(8,128)(2,1)} %copy-done.1, ...), custom_call_target="tpu_custom_call" | custom-call | flops 96636768 | bytes 188743 | tf_op jit(solution)/shard_map/weight_grad/pallas_call | solution.py:641
  380.2 6.0 %convolution_convert_fusion.3 = bf16[1536,768]{1,0:T(8,128)(2,1)} fusion(bf16[1024,1536]{1,0:T(8,128)(2,1)} %get-tuple-element.179.ag_ref, pred[]{:T(512)S(6)} %eq.14, bf16[1024,1536]{1,0:T(8,128)(2,1)S(1)} %copy-done.10), kind=kOutput, calls=%fused_computation.6 | convolution fusion | flops 2417885184 | bytes 8650753 | tf_op jit(solution)/shard_map/dot_general | solution.py:28
  389.3 3.9 convolution_convert_fusion.2
  393.3 15.6 %weight_grad.5 = (bf16[768,1536]{1,0:T(8,128)(2,1)}, bf16[768,1536]{1,0:T(8,128)(2,1)}) custom-call(bf16[1024,1536]{1,0:T(8,128)(2,1)} %get-tuple-element.142.x_ref.refs_0_.refs_1_, bf16[1024,1536]{1,0:T(8,128)(2,1)} %get-tuple-element.142.x_ref.refs_0_.refs_1_, bf16[1024,1536]{1,0:T(8,128)(2,1)} %copy-done.1, bf16[1024,1536]{1,0:T(8,128)(2,1)} %copy-done.1, ...), custom_call_target="tpu_custom_call" | custom-call | flops 96636768 | bytes 188743 | tf_op jit(solution)/shard_map/weight_grad/pallas_call | solution.py:641
  408.9 3.0 add_convert_fusion.1
  416.8 6.2 %reduce-scatter.6.cloned.1.call-done = bf16[1,1024,384]{2,1,0:T(8,128)(2,1)} async-done(((bf16[4,1024,384]{2,1,0:T(8,128)(2,1)}), bf16[1,1024,384]{2,1,0:T(8,128)(2,1)}) %reduce-scatter.6.cloned.1.call-update) | async-done | bytes 786448 | tf_op jit(solution)/shard_map/reduce_scatter | solution.py:961
  423.0 19.3 %attn_bwd.1 = (bf16[1024,384]{1,0:T(8,128)(2,1)}, bf16[1024,256]{1,0:T(8,128)(2,1)}) custom-call(bf16[1024,384]{1,0:T(8,128)(2,1)} %bitcast.56, bf16[6,1024,64]{2,1,0:T(8,128)(2,1)} %get-tuple-element.173.q_ref, bf16[2,1024,64]{2,1,0:T(8,128)(2,1)} %get-tuple-element.174.k_ref, bf16[2,1024,64]{2,1,0:T(8,128)(2,1)} %get-tuple-element.175.v_ref, ...), custom_call_target="tpu_custom_call" | custom-call | flops 6039797760 | bytes 3145728 | tf_op jit(solution)/shard_map/attn_bwd/pallas_call | solution.py:243
  442.3 8.9 %back_end.1 = bf16[1024,1536]{1,0:T(8,128)(2,1)} custom-call(bf16[1024,384]{1,0:T(8,128)(2,1)} %get-tuple-element.194.dq_ref, bf16[1024,256]{1,0:T(8,128)(2,1)} %get-tuple-element.195.dkv_ref, bf16[1536,768]{1,0:T(8,128)(2,1)} %pad_maximum_fusion.1.w_ref.small_ref, bf16[1024,1536]{1,0:T(8,128)(2,1)} %all-gather.7.cloned.1.call-done.tok_ref, ...), custom_call_target="tpu_custom_call" | custom-call | flops 2013265920 | bytes 11403264 | tf_op jit(solution)/shard_map/back_end/pallas_call | solution.py:418
  451.2 4.5 add_convert_fusion.5
  461.7 3.2 broadcast_select_fusion.7
  465.0 2.1 add_convert_fusion.14
  475.4 1.8 maximum_convert_fusion.1
  477.2 1.9 add_convert_fusion.4
  481.0 3.9 collective-permute-done.47
  486.5 2.1 add_convert_fusion.2
  490.2 2.1 add_convert_fusion.3
  493.8 8.8 %collective-permute-done.46 = bf16[768,384]{1,0:T(8,128)(2,1)} collective-permute-done((bf16[768,384]{1,0:T(8,128)(2,1)}, bf16[768,384]{1,0:T(8,128)(2,1)}, u32[]{:S(2)}, u32[]{:S(2)}) %collective-permute-start.46) | collective-permute-done | bytes 589856 | tf_op jit(solution)/shard_map/ppermute | solution.py:661
  509.0 2.3 collective-permute-done.49
  512.6 2.7 multiply_reduce_fusion.1
  519.7 1.7 multiply_reduce_fusion
  523.1 2.9 collective-permute-start.59
  526.0 2.0 collective-permute-start.57
  529.6 3.3 concatenate.163
  533.8 4.6 maximum_convert_fusion
  539.4 4.6 collective-permute-done.58
  (358 shorter events, 119.6 us)
Async XLA Ops:
  7.2 72.7 %all-gather.7.cloned.1.call-start = ((), (), s32[]{:S(2)}) async-start(), calls=%async_computation.3 | async-start | bytes 3932160 | tf_op jit(solution)/shard_map/all_gather | solution.py:842
  12.2 4.6 collective-permute-start.1
  13.8 97.3 %all-gather.13.cloned.1.call-start = ((), (), s32[]{:S(2)}) async-start(), calls=%async_computation.9 | async-start | bytes 1474560 | tf_op jit(solution)/shard_map/all_gather | solution.py:887
  18.3 7.4 %collective-permute-start.2 = (bf16[192,384]{1,0:T(8,128)(2,1)S(1)}, bf16[192,384]{1,0:T(8,128)(2,1)S(1)}, u32[]{:S(2)}, u32[]{:S(2)}) collective-permute-start(bf16[192,384]{1,0:T(8,128)(2,1)S(1)} %get-tuple-element.120), channel_id=1, source_target_pairs={{0,8},{8,0},{16,24},{24,16},{1,9},{9,1},{17,25},{25,17},{2,10},{10... | collective-permute-start | bytes 442376 | tf_op jit(solution)/shard_map/ppermute | solution.py:661
  21.7 8.8 %collective-permute-start.3 = (bf16[192,384]{1,0:T(8,128)(2,1)S(1)}, bf16[192,384]{1,0:T(8,128)(2,1)S(1)}, u32[]{:S(2)}, u32[]{:S(2)}) collective-permute-start(bf16[192,384]{1,0:T(8,128)(2,1)S(1)} %get-tuple-element.121), channel_id=1, source_target_pairs={{0,8},{8,0},{16,24},{24,16},{1,9},{9,1},{17,25},{25,17},{2,10},{10... | collective-permute-start | bytes 442376 | tf_op jit(solution)/shard_map/ppermute | solution.py:661
  21.7 6.7 %collective-permute-start.5 = (bf16[192,384]{1,0:T(8,128)(2,1)S(1)}, bf16[192,384]{1,0:T(8,128)(2,1)S(1)}, u32[]{:S(2)}, u32[]{:S(2)}) collective-permute-start(bf16[192,384]{1,0:T(8,128)(2,1)S(1)} %get-tuple-element.121), channel_id=1, source_target_pairs={{0,16},{8,24},{16,0},{24,8},{1,17},{9,25},{17,1},{25,9},{2,18},{10... | collective-permute-start | bytes 442376 | tf_op jit(solution)/shard_map/ppermute | solution.py:661
  23.7 11.5 %collective-permute-start.7 = (bf16[192,384]{1,0:T(8,128)(2,1)S(1)}, bf16[192,384]{1,0:T(8,128)(2,1)S(1)}, u32[]{:S(2)}, u32[]{:S(2)}) collective-permute-start(bf16[192,384]{1,0:T(8,128)(2,1)S(1)} %get-tuple-element.120), channel_id=1, source_target_pairs={{0,16},{8,24},{16,0},{24,8},{1,17},{9,25},{17,1},{25,9},{2,18},{10... | collective-permute-start | bytes 442376 | tf_op jit(solution)/shard_map/ppermute | solution.py:661
  25.7 8.2 %collective-permute-start.4 = (bf16[192,384]{1,0:T(8,128)(2,1)S(1)}, bf16[192,384]{1,0:T(8,128)(2,1)S(1)}, u32[]{:S(2)}, u32[]{:S(2)}) collective-permute-start(bf16[192,384]{1,0:T(8,128)(2,1)S(1)} %collective-permute-done.2), channel_id=1, source_target_pairs={{0,16},{8,24},{16,0},{24,8},{1,17},{9,25},{17,1},{25,9},{2,18},{10... | collective-permute-start | bytes 442376 | tf_op jit(solution)/shard_map/ppermute | solution.py:661
  28.4 6.1 %collective-permute-start.6 = (bf16[192,384]{1,0:T(8,128)(2,1)S(1)}, bf16[192,384]{1,0:T(8,128)(2,1)S(1)}, u32[]{:S(2)}, u32[]{:S(2)}) collective-permute-start(bf16[192,384]{1,0:T(8,128)(2,1)S(1)} %collective-permute-done.5), channel_id=1, source_target_pairs={{0,8},{8,0},{16,24},{24,16},{1,9},{9,1},{17,25},{25,17},{2,10},{10... | collective-permute-start | bytes 442376 | tf_op jit(solution)/shard_map/ppermute | solution.py:661
  36.6 4.4 collective-permute-start.8
  40.4 13.0 %collective-permute-start.13 = (bf16[192,1536]{1,0:T(8,128)(2,1)}, bf16[192,1536]{1,0:T(8,128)(2,1)}, u32[]{:S(2)}, u32[]{:S(2)}) collective-permute-start(bf16[192,1536]{1,0:T(8,128)(2,1)} %bitcast.43), channel_id=1, source_target_pairs={{0,4},{4,0},{1,5},{5,1},{2,6},{6,2},{3,7},{7,3},{8,12},{12,8},{9,1... | collective-permute-start | bytes 1769480 | tf_op jit(solution)/shard_map/ppermute | solution.py:661
  44.4 131.5 %all-gather.11.cloned.1.call-start = ((), (), s32[]{:S(2)}) async-start(), calls=%async_computation.8 | async-start | bytes 3932160 | tf_op jit(solution)/shard_map/all_gather | solution.py:908
  44.5 52.7 %collective-permute-start.9 = (bf16[192,3072]{1,0:T(8,128)(2,1)S(1)}, bf16[192,3072]{1,0:T(8,128)(2,1)}, u32[]{:S(2)}, u32[]{:S(2)}) collective-permute-start(bf16[192,3072]{1,0:T(8,128)(2,1)S(1)} %get-tuple-element.129), channel_id=1, source_target_pairs={{0,8},{8,0},{16,24},{24,16},{1,9},{9,1},{17,25},{25,17},{2,10},{10... | collective-permute-start | bytes 3538952 | tf_op jit(solution)/shard_map/ppermute | solution.py:661
  46.3 50.9 %collective-permute-start.10 = (bf16[192,3072]{1,0:T(8,128)(2,1)S(1)}, bf16[192,3072]{1,0:T(8,128)(2,1)}, u32[]{:S(2)}, u32[]{:S(2)}) collective-permute-start(bf16[192,3072]{1,0:T(8,128)(2,1)S(1)} %get-tuple-element.130), channel_id=1, source_target_pairs={{0,16},{8,24},{16,0},{24,8},{1,17},{9,25},{17,1},{25,9},{2,18},{10... | collective-permute-start | bytes 3538952 | tf_op jit(solution)/shard_map/ppermute | solution.py:661
  47.8 50.0 %collective-permute-start.11 = (bf16[192,3072]{1,0:T(8,128)(2,1)S(1)}, bf16[192,3072]{1,0:T(8,128)(2,1)}, u32[]{:S(2)}, u32[]{:S(2)}) collective-permute-start(bf16[192,3072]{1,0:T(8,128)(2,1)S(1)} %get-tuple-element.130), channel_id=1, source_target_pairs={{0,8},{8,0},{16,24},{24,16},{1,9},{9,1},{17,25},{25,17},{2,10},{10... | collective-permute-start | bytes 3538952 | tf_op jit(solution)/shard_map/ppermute | solution.py:661
  48.3 50.9 %collective-permute-start.12 = (bf16[192,3072]{1,0:T(8,128)(2,1)S(1)}, bf16[192,3072]{1,0:T(8,128)(2,1)}, u32[]{:S(2)}, u32[]{:S(2)}) collective-permute-start(bf16[192,3072]{1,0:T(8,128)(2,1)S(1)} %get-tuple-element.129), channel_id=1, source_target_pairs={{0,16},{8,24},{16,0},{24,8},{1,17},{9,25},{17,1},{25,9},{2,18},{10... | collective-permute-start | bytes 3538952 | tf_op jit(solution)/shard_map/ppermute | solution.py:661
  99.3 140.6 %all-gather.9.cloned.1.call-start = ((), (), s32[]{:S(2)}) async-start(), calls=%async_computation.4 | async-start | bytes 3932160 | tf_op jit(solution)/shard_map/all_gather | solution.py:915
  100.6 27.1 %collective-permute-start.14 = (bf16[192,3072]{1,0:T(8,128)(2,1)}, bf16[192,3072]{1,0:T(8,128)(2,1)}, u32[]{:S(2)}, u32[]{:S(2)}) collective-permute-start(bf16[192,3072]{1,0:T(8,128)(2,1)} %collective-permute-done.9), channel_id=1, source_target_pairs={{0,16},{8,24},{16,0},{24,8},{1,17},{9,25},{17,1},{25,9},{2,18},{10... | collective-permute-start | bytes 3538952 | tf_op jit(solution)/shard_map/ppermute | solution.py:661
  102.2 26.8 %collective-permute-start.15 = (bf16[192,3072]{1,0:T(8,128)(2,1)}, bf16[192,3072]{1,0:T(8,128)(2,1)}, u32[]{:S(2)}, u32[]{:S(2)}) collective-permute-start(bf16[192,3072]{1,0:T(8,128)(2,1)} %collective-permute-done.10), channel_id=1, source_target_pairs={{0,8},{8,0},{16,24},{24,16},{1,9},{9,1},{17,25},{25,17},{2,10},{10... | collective-permute-start | bytes 3538952 | tf_op jit(solution)/shard_map/ppermute | solution.py:661
  114.2 236.4 %reduce-scatter.4.cloned.1.call-start = ((), (), s32[]{:S(2)}) async-start(), calls=%async_computation.5 | async-start | bytes 3932160 | tf_op jit(solution)/shard_map/reduce_scatter | solution.py:932
  128.9 13.2 %collective-permute-start.18 = (bf16[192,768]{1,0:T(8,128)(2,1)S(1)}, bf16[192,768]{1,0:T(8,128)(2,1)S(1)}, u32[]{:S(2)}, u32[]{:S(2)}) collective-permute-start(bf16[192,768]{1,0:T(8,128)(2,1)S(1)} %get-tuple-element.128), channel_id=1, source_target_pairs={{0,16},{8,24},{16,0},{24,8},{1,17},{9,25},{17,1},{25,9},{2,18},{10... | collective-permute-start | bytes 884744 | tf_op jit(solution)/shard_map/ppermute | solution.py:661
  129.4 13.8 %collective-permute-start.19 = (bf16[192,768]{1,0:T(8,128)(2,1)S(1)}, bf16[192,768]{1,0:T(8,128)(2,1)S(1)}, u32[]{:S(2)}, u32[]{:S(2)}) collective-permute-start(bf16[192,768]{1,0:T(8,128)(2,1)S(1)} %get-tuple-element.128), channel_id=1, source_target_pairs={{0,8},{8,0},{16,24},{24,16},{1,9},{9,1},{17,25},{25,17},{2,10},{10... | collective-permute-start | bytes 884744 | tf_op jit(solution)/shard_map/ppermute | solution.py:661
  130.0 12.0 %collective-permute-start.17 = (bf16[192,768]{1,0:T(8,128)(2,1)S(1)}, bf16[192,768]{1,0:T(8,128)(2,1)S(1)}, u32[]{:S(2)}, u32[]{:S(2)}) collective-permute-start(bf16[192,768]{1,0:T(8,128)(2,1)S(1)} %get-tuple-element.127), channel_id=1, source_target_pairs={{0,8},{8,0},{16,24},{24,16},{1,9},{9,1},{17,25},{25,17},{2,10},{10... | collective-permute-start | bytes 884744 | tf_op jit(solution)/shard_map/ppermute | solution.py:661
  131.4 11.7 %collective-permute-start.20 = (bf16[192,768]{1,0:T(8,128)(2,1)S(1)}, bf16[192,768]{1,0:T(8,128)(2,1)S(1)}, u32[]{:S(2)}, u32[]{:S(2)}) collective-permute-start(bf16[192,768]{1,0:T(8,128)(2,1)S(1)} %get-tuple-element.127), channel_id=1, source_target_pairs={{0,16},{8,24},{16,0},{24,8},{1,17},{9,25},{17,1},{25,9},{2,18},{10... | collective-permute-start | bytes 884744 | tf_op jit(solution)/shard_map/ppermute | solution.py:661
  133.0 35.0 %collective-permute-start.24 = (bf16[384,768]{1,0:T(8,128)(2,1)S(1)}, bf16[384,768]{1,0:T(8,128)(2,1)S(1)}, u32[]{:S(2)}, u32[]{:S(2)}) collective-permute-start(bf16[384,768]{1,0:T(8,128)(2,1)S(1)} %pad_maximum_fusion.9), channel_id=1, source_target_pairs={{0,4},{4,0},{1,5},{5,1},{2,6},{6,2},{3,7},{7,3},{8,12},{12,8},{9,1... | collective-permute-start | bytes 1769480 | tf_op jit(solution)/shard_map/ppermute | solution.py:661
  143.2 29.7 %collective-permute-start.21 = (bf16[192,1536]{1,0:T(8,128)(2,1)S(1)}, bf16[192,1536]{1,0:T(8,128)(2,1)S(1)}, u32[]{:S(2)}, u32[]{:S(2)}) collective-permute-start(bf16[192,1536]{1,0:T(8,128)(2,1)S(1)} %copy-done.33), channel_id=1, source_target_pairs={{0,8},{8,0},{16,24},{24,16},{1,9},{9,1},{17,25},{25,17},{2,10},{10... | collective-permute-start | bytes 1769480 | tf_op jit(solution)/shard_map/ppermute | solution.py:661
  144.1 23.9 %collective-permute-start.27 = (bf16[384,768]{1,0:T(8,128)(2,1)S(1)}, bf16[384,768]{1,0:T(8,128)(2,1)S(1)}, u32[]{:S(2)}, u32[]{:S(2)}) collective-permute-start(bf16[384,768]{1,0:T(8,128)(2,1)S(1)} %pad_maximum_fusion.12), channel_id=1, source_target_pairs={{0,4},{4,0},{1,5},{5,1},{2,6},{6,2},{3,7},{7,3},{8,12},{12,8},{9,1... | collective-permute-start | bytes 1769480 | tf_op jit(solution)/shard_map/ppermute | solution.py:661
  157.3 9.4 %collective-permute-start.22 = (bf16[192,768]{1,0:T(8,128)(2,1)S(1)}, bf16[192,768]{1,0:T(8,128)(2,1)S(1)}, u32[]{:S(2)}, u32[]{:S(2)}) collective-permute-start(bf16[192,768]{1,0:T(8,128)(2,1)S(1)} %collective-permute-done.17), channel_id=1, source_target_pairs={{0,16},{8,24},{16,0},{24,8},{1,17},{9,25},{17,1},{25,9},{2,18},{10... | collective-permute-start | bytes 884744 | tf_op jit(solution)/shard_map/ppermute | solution.py:661
  158.6 9.1 %collective-permute-start.23 = (bf16[192,768]{1,0:T(8,128)(2,1)S(1)}, bf16[192,768]{1,0:T(8,128)(2,1)S(1)}, u32[]{:S(2)}, u32[]{:S(2)}) collective-permute-start(bf16[192,768]{1,0:T(8,128)(2,1)S(1)} %collective-permute-done.18), channel_id=1, source_target_pairs={{0,8},{8,0},{16,24},{24,16},{1,9},{9,1},{17,25},{25,17},{2,10},{10... | collective-permute-start | bytes 884744 | tf_op jit(solution)/shard_map/ppermute | solution.py:661
  189.1 20.4 %collective-permute-start.28 = (bf16[1024,1536]{1,0:T(8,128)(2,1)}, bf16[1024,1536]{1,0:T(8,128)(2,1)S(1)}, u32[]{:S(2)}, u32[]{:S(2)}) collective-permute-start(bf16[1024,1536]{1,0:T(8,128)(2,1)} %get-tuple-element.142.x_ref.refs_0_.refs_1_), channel_id=1, source_target_pairs={{0,4},{4,0},{1,5},{5,1},{2,6},{6,2},{3,7},{7,3},{8,12},{12,8},{9,1... | collective-permute-start | bytes 9437192 | tf_op jit(solution)/shard_map/ppermute | solution.py:661
  189.2 18.8 %collective-permute-start.29 = (bf16[192,1536]{1,0:T(8,128)(2,1)S(1)}, bf16[192,1536]{1,0:T(8,128)(2,1)}, u32[]{:S(2)}, u32[]{:S(2)}) collective-permute-start(bf16[192,1536]{1,0:T(8,128)(2,1)S(1)} %copy-done.32), channel_id=1, source_target_pairs={{0,16},{8,24},{16,0},{24,8},{1,17},{9,25},{17,1},{25,9},{2,18},{10... | collective-permute-start | bytes 1769480 | tf_op jit(solution)/shard_map/ppermute | solution.py:661
  190.6 19.3 %collective-permute-start.30 = (f32[1024,128]{1,0:T(8,128)}, f32[1024,128]{1,0:T(8,128)}, u32[]{:S(2)}, u32[]{:S(2)}) collective-permute-start(f32[1024,128]{1,0:T(8,128)} %get-tuple-element.143.gate_ref.refs_2_), channel_id=1, source_target_pairs={{0,4},{4,0},{1,5},{5,1},{2,6},{6,2},{3,7},{7,3},{8,12},{12,8},{9,1... | collective-permute-start | bytes 1572872 | tf_op jit(solution)/shard_map/ppermute | solution.py:661
  190.8 35.4 %collective-permute-start.31 = (bf16[192,1536]{1,0:T(8,128)(2,1)S(1)}, bf16[192,1536]{1,0:T(8,128)(2,1)}, u32[]{:S(2)}, u32[]{:S(2)}) collective-permute-start(bf16[192,1536]{1,0:T(8,128)(2,1)S(1)} %copy-done.32), channel_id=1, source_target_pairs={{0,8},{8,0},{16,24},{24,16},{1,9},{9,1},{17,25},{25,17},{2,10},{10... | collective-permute-start | bytes 1769480 | tf_op jit(solution)/shard_map/ppermute | solution.py:661
  192.3 33.9 %collective-permute-start.34 = (bf16[192,1536]{1,0:T(8,128)(2,1)}, bf16[192,1536]{1,0:T(8,128)(2,1)}, u32[]{:S(2)}, u32[]{:S(2)}) collective-permute-start(bf16[192,1536]{1,0:T(8,128)(2,1)} %get-tuple-element.137.refs_1_.refs_4_), channel_id=1, source_target_pairs={{0,16},{8,24},{16,0},{24,8},{1,17},{9,25},{17,1},{25,9},{2,18},{10... | collective-permute-start | bytes 1769480 | tf_op jit(solution)/shard_map/ppermute | solution.py:661
  208.0 22.3 %collective-permute-start.32 = (bf16[192,1536]{1,0:T(8,128)(2,1)}, bf16[192,1536]{1,0:T(8,128)(2,1)}, u32[]{:S(2)}, u32[]{:S(2)}) collective-permute-start(bf16[192,1536]{1,0:T(8,128)(2,1)} %copy-done.58), channel_id=1, source_target_pairs={{0,16},{8,24},{16,0},{24,8},{1,17},{9,25},{17,1},{25,9},{2,18},{10... | collective-permute-start | bytes 1769480 | tf_op jit(solution)/shard_map/ppermute | solution.py:661
  209.5 20.8 %collective-permute-start.33 = (bf16[192,1536]{1,0:T(8,128)(2,1)}, bf16[192,1536]{1,0:T(8,128)(2,1)}, u32[]{:S(2)}, u32[]{:S(2)}) collective-permute-start(bf16[192,1536]{1,0:T(8,128)(2,1)} %collective-permute-done.29.refs_8_.refs_11_), channel_id=1, source_target_pairs={{0,8},{8,0},{16,24},{24,16},{1,9},{9,1},{17,25},{25,17},{2,10},{10... | collective-permute-start | bytes 1769480 | tf_op jit(solution)/shard_map/ppermute | solution.py:661
  239.9 10.1 %collective-permute-start.36 = (bf16[1024,1536]{1,0:T(8,128)(2,1)}, bf16[1024,1536]{1,0:T(8,128)(2,1)S(1)}, u32[]{:S(2)}, u32[]{:S(2)}) collective-permute-start(bf16[1024,1536]{1,0:T(8,128)(2,1)} %all-gather.9.cloned.1.call-done.refs_0_.refs_1_), channel_id=1, source_target_pairs={{0,4},{4,0},{1,5},{5,1},{2,6},{6,2},{3,7},{7,3},{8,12},{12,8},{9,1... | collective-permute-start | bytes 9437192 | tf_op jit(solution)/shard_map/ppermute | solution.py:661
  239.9 39.6 %collective-permute-start.35 = (bf16[1024,1536]{1,0:T(8,128)(2,1)}, bf16[1024,1536]{1,0:T(8,128)(2,1)}, u32[]{:S(2)}, u32[]{:S(2)}) collective-permute-start(bf16[1024,1536]{1,0:T(8,128)(2,1)} %combine.2), channel_id=1, source_target_pairs={{0,4},{4,0},{1,5},{5,1},{2,6},{6,2},{3,7},{7,3},{8,12},{12,8},{9,1... | collective-permute-start | bytes 9437192 | tf_op jit(solution)/shard_map/ppermute | solution.py:661
  276.5 36.0 %collective-permute-start.37 = (bf16[768,768]{1,0:T(8,128)(2,1)}, bf16[768,768]{1,0:T(8,128)(2,1)S(1)}, u32[]{:S(2)}, u32[]{:S(2)}) collective-permute-start(bf16[768,768]{1,0:T(8,128)(2,1)} %get-tuple-element.163), channel_id=1, source_target_pairs={{0,16},{8,24},{16,0},{24,8},{1,17},{9,25},{17,1},{25,9},{2,18},{10... | collective-permute-start | bytes 3538952 | tf_op jit(solution)/shard_map/ppermute | solution.py:661
  278.0 34.5 %collective-permute-start.38 = (bf16[768,768]{1,0:T(8,128)(2,1)}, bf16[768,768]{1,0:T(8,128)(2,1)}, u32[]{:S(2)}, u32[]{:S(2)}) collective-permute-start(bf16[768,768]{1,0:T(8,128)(2,1)} %get-tuple-element.164), channel_id=1, source_target_pairs={{0,8},{8,0},{16,24},{24,16},{1,9},{9,1},{17,25},{25,17},{2,10},{10... | collective-permute-start | bytes 3538952 | tf_op jit(solution)/shard_map/ppermute | solution.py:661
  284.8 138.1 %reduce-scatter.6.cloned.1.call-start = ((), (), s32[]{:S(2)}) async-start(), calls=%async_computation.6 | async-start | bytes 3932160 | tf_op jit(solution)/shard_map/reduce_scatter | solution.py:961
  312.4 17.3 %collective-permute-start.40 = (f32[1024,128]{1,0:T(8,128)}, f32[1024,128]{1,0:T(8,128)S(1)}, u32[]{:S(2)}, u32[]{:S(2)}) collective-permute-start(f32[1024,128]{1,0:T(8,128)} %get-tuple-element.168), channel_id=1, source_target_pairs={{0,4},{4,0},{1,5},{5,1},{2,6},{6,2},{3,7},{7,3},{8,12},{12,8},{9,1... | collective-permute-start | bytes 1572872 | tf_op jit(solution)/shard_map/ppermute | solution.py:661
  329.2 21.4 %collective-permute-start.39 = (bf16[1024,1536]{1,0:T(8,128)(2,1)}, bf16[1024,1536]{1,0:T(8,128)(2,1)}, u32[]{:S(2)}, u32[]{:S(2)}) collective-permute-start(bf16[1024,1536]{1,0:T(8,128)(2,1)} %convolution_convert_fusion.1), channel_id=1, source_target_pairs={{0,4},{4,0},{1,5},{5,1},{2,6},{6,2},{3,7},{7,3},{8,12},{12,8},{9,1... | collective-permute-start | bytes 9437192 | tf_op jit(solution)/shard_map/ppermute | solution.py:661
  334.1 15.7 %collective-permute-start.41 = (bf16[384,768]{1,0:T(8,128)(2,1)S(1)}, bf16[384,768]{1,0:T(8,128)(2,1)S(1)}, u32[]{:S(2)}, u32[]{:S(2)}) collective-permute-start(bf16[384,768]{1,0:T(8,128)(2,1)S(1)} %add_convert_fusion.11), channel_id=1, source_target_pairs={{0,8},{8,0},{16,24},{24,16},{1,9},{9,1},{17,25},{25,17},{2,10},{10... | collective-permute-start | bytes 1769480 | tf_op jit(solution)/shard_map/ppermute | solution.py:661
  334.8 15.8 %collective-permute-start.42 = (bf16[384,768]{1,0:T(8,128)(2,1)S(1)}, bf16[384,768]{1,0:T(8,128)(2,1)}, u32[]{:S(2)}, u32[]{:S(2)}) collective-permute-start(bf16[384,768]{1,0:T(8,128)(2,1)S(1)} %add_convert_fusion.10), channel_id=1, source_target_pairs={{0,16},{8,24},{16,0},{24,8},{1,17},{9,25},{17,1},{25,9},{2,18},{10... | collective-permute-start | bytes 1769480 | tf_op jit(solution)/shard_map/ppermute | solution.py:661
  364.5 183.9 %reduce-scatter.8.cloned.1.call-start = ((), (), s32[]{:S(2)}) async-start(), calls=%async_computation.7 | async-start | bytes 3932160 | tf_op jit(solution)/shard_map/reduce_scatter | solution.py:985
  386.2 22.7 %collective-permute-start.50 = (bf16[1536,768]{1,0:T(8,128)(2,1)}, bf16[1536,768]{1,0:T(8,128)(2,1)}, u32[]{:S(2)}, u32[]{:S(2)}) collective-permute-start(bf16[1536,768]{1,0:T(8,128)(2,1)} %convolution_convert_fusion.3), channel_id=1, source_target_pairs={{0,4},{4,0},{1,5},{5,1},{2,6},{6,2},{3,7},{7,3},{8,12},{12,8},{9,1... | collective-permute-start | bytes 7077896 | tf_op jit(solution)/shard_map/ppermute | solution.py:661
  387.1 64.1 %collective-permute-start.43 = (bf16[768,1536]{1,0:T(8,128)(2,1)}, bf16[768,1536]{1,0:T(8,128)(2,1)}, u32[]{:S(2)}, u32[]{:S(2)}) collective-permute-start(bf16[768,1536]{1,0:T(8,128)(2,1)} %get-tuple-element.184), channel_id=1, source_target_pairs={{0,16},{8,24},{16,0},{24,8},{1,17},{9,25},{17,1},{25,9},{2,18},{10... | collective-permute-start | bytes 7077896 | tf_op jit(solution)/shard_map/ppermute | solution.py:661
  387.8 63.4 %collective-permute-start.44 = (bf16[768,1536]{1,0:T(8,128)(2,1)}, bf16[768,1536]{1,0:T(8,128)(2,1)}, u32[]{:S(2)}, u32[]{:S(2)}) collective-permute-start(bf16[768,1536]{1,0:T(8,128)(2,1)} %get-tuple-element.185), channel_id=1, source_target_pairs={{0,8},{8,0},{16,24},{24,16},{1,9},{9,1},{17,25},{25,17},{2,10},{10... | collective-permute-start | bytes 7077896 | tf_op jit(solution)/shard_map/ppermute | solution.py:661
  413.1 51.9 %collective-permute-start.51 = (bf16[768,384]{1,0:T(8,128)(2,1)}, bf16[768,384]{1,0:T(8,128)(2,1)}, u32[]{:S(2)}, u32[]{:S(2)}) collective-permute-start(bf16[768,384]{1,0:T(8,128)(2,1)} %get-tuple-element.284), channel_id=1, source_target_pairs={{0,16},{8,24},{16,0},{24,8},{1,17},{9,25},{17,1},{25,9},{2,18},{10... | collective-permute-start | bytes 1769480 | tf_op jit(solution)/shard_map/ppermute | solution.py:661
  414.7 50.3 %collective-permute-start.52 = (bf16[768,384]{1,0:T(8,128)(2,1)}, bf16[768,384]{1,0:T(8,128)(2,1)}, u32[]{:S(2)}, u32[]{:S(2)}) collective-permute-start(bf16[768,384]{1,0:T(8,128)(2,1)} %pad_maximum_fusion.14), channel_id=1, source_target_pairs={{0,8},{8,0},{16,24},{24,16},{1,9},{9,1},{17,25},{25,17},{2,10},{10... | collective-permute-start | bytes 1769480 | tf_op jit(solution)/shard_map/ppermute | solution.py:661
  455.8 29.2 %collective-permute-start.47 = (bf16[384,1536]{1,0:T(8,128)(2,1)}, bf16[384,1536]{1,0:T(8,128)(2,1)}, u32[]{:S(2)}, u32[]{:S(2)}) collective-permute-start(bf16[384,1536]{1,0:T(8,128)(2,1)} %get-tuple-element.192), channel_id=1, source_target_pairs={{0,8},{8,0},{16,24},{24,16},{1,9},{9,1},{17,25},{25,17},{2,10},{10... | collective-permute-start | bytes 3538952 | tf_op jit(solution)/shard_map/ppermute | solution.py:661
  457.2 29.2 %collective-permute-start.48 = (bf16[384,1536]{1,0:T(8,128)(2,1)}, bf16[384,1536]{1,0:T(8,128)(2,1)}, u32[]{:S(2)}, u32[]{:S(2)}) collective-permute-start(bf16[384,1536]{1,0:T(8,128)(2,1)} %get-tuple-element.193), channel_id=1, source_target_pairs={{0,16},{8,24},{16,0},{24,8},{1,17},{9,25},{17,1},{25,9},{2,18},{10... | collective-permute-start | bytes 3538952 | tf_op jit(solution)/shard_map/ppermute | solution.py:661
  465.0 12.2 %collective-permute-start.45 = (bf16[1536,384]{1,0:T(8,128)(2,1)}, bf16[1536,384]{1,0:T(8,128)(2,1)}, u32[]{:S(2)}, u32[]{:S(2)}) collective-permute-start(bf16[1536,384]{1,0:T(8,128)(2,1)} %get-tuple-element.348), channel_id=1, source_target_pairs={{0,4},{4,0},{1,5},{5,1},{2,6},{6,2},{3,7},{7,3},{8,12},{12,8},{9,1... | collective-permute-start | bytes 3538952 | tf_op jit(solution)/shard_map/ppermute | solution.py:661
  467.1 38.0 %collective-permute-start.53 = (bf16[384,384]{1,0:T(8,128)(2,1)}, bf16[384,384]{1,0:T(8,128)(2,1)}, u32[]{:S(2)}, u32[]{:S(2)}) collective-permute-start(bf16[384,384]{1,0:T(8,128)(2,1)} %get-tuple-element.212), channel_id=1, source_target_pairs={{0,8},{8,0},{16,24},{24,16},{1,9},{9,1},{17,25},{25,17},{2,10},{10... | collective-permute-start | bytes 884744 | tf_op jit(solution)/shard_map/ppermute | solution.py:661
  469.7 3.7 collective-permute-start.60
  473.4 31.8 %collective-permute-start.54 = (bf16[384,384]{1,0:T(8,128)(2,1)}, bf16[384,384]{1,0:T(8,128)(2,1)}, u32[]{:S(2)}, u32[]{:S(2)}) collective-permute-start(bf16[384,384]{1,0:T(8,128)(2,1)} %get-tuple-element.213), channel_id=1, source_target_pairs={{0,16},{8,24},{16,0},{24,8},{1,17},{9,25},{17,1},{25,9},{2,18},{10... | collective-permute-start | bytes 884744 | tf_op jit(solution)/shard_map/ppermute | solution.py:661
  479.9 22.6 %collective-permute-start.46 = (bf16[768,384]{1,0:T(8,128)(2,1)}, bf16[768,384]{1,0:T(8,128)(2,1)}, u32[]{:S(2)}, u32[]{:S(2)}) collective-permute-start(bf16[768,384]{1,0:T(8,128)(2,1)} %slice.366), channel_id=1, source_target_pairs={{0,8},{8,0},{16,24},{24,16},{1,9},{9,1},{17,25},{25,17},{2,10},{10... | collective-permute-start | bytes 1769480 | tf_op jit(solution)/shard_map/ppermute | solution.py:661
  503.6 7.7 %collective-permute-start.49 = (bf16[384,384]{1,0:T(8,128)(2,1)S(1)}, bf16[384,384]{1,0:T(8,128)(2,1)S(1)}, u32[]{:S(2)}, u32[]{:S(2)}) collective-permute-start(bf16[384,384]{1,0:T(8,128)(2,1)S(1)} %add_convert_fusion.17), channel_id=1, source_target_pairs={{0,16},{8,24},{16,0},{24,8},{1,17},{9,25},{17,1},{25,9},{2,18},{10... | collective-permute-start | bytes 884744 | tf_op jit(solution)/shard_map/ppermute | solution.py:661
  512.5 3.4 collective-permute-start.55
  515.4 4.3 collective-permute-start.56
  523.1 15.3 %collective-permute-start.59 = (bf16[192,512]{1,0:T(8,128)(2,1)}, bf16[192,512]{1,0:T(8,128)(2,1)}, u32[]{:S(2)}, u32[]{:S(2)}) collective-permute-start(bf16[192,512]{1,0:T(8,128)(2,1)} %get-tuple-element.345), channel_id=1, source_target_pairs={{0,3},{1,0},{2,1},{3,2},{4,7},{5,4},{6,5},{7,6},{8,11},{9,8},{10,9... | collective-permute-start | bytes 589832 | tf_op jit(solution)/shard_map/ppermute | solution.py:1053
  526.0 18.0 %collective-permute-start.58 = (bf16[192,512]{1,0:T(8,128)(2,1)}, bf16[192,512]{1,0:T(8,128)(2,1)}, u32[]{:S(2)}, u32[]{:S(2)}) collective-permute-start(bf16[192,512]{1,0:T(8,128)(2,1)} %get-tuple-element.344), channel_id=1, source_target_pairs={{0,2},{1,3},{2,0},{3,1},{4,6},{5,7},{6,4},{7,5},{8,10},{9,11},{10,... | collective-permute-start | bytes 589832 | tf_op jit(solution)/shard_map/ppermute | solution.py:1053
  526.0 19.0 %collective-permute-start.57 = (bf16[192,512]{1,0:T(8,128)(2,1)}, bf16[192,512]{1,0:T(8,128)(2,1)}, u32[]{:S(2)}, u32[]{:S(2)}) collective-permute-start(bf16[192,512]{1,0:T(8,128)(2,1)} %get-tuple-element.343), channel_id=1, source_target_pairs={{0,1},{1,2},{2,3},{3,0},{4,5},{5,6},{6,7},{7,4},{8,9},{9,10},{10,1... | collective-permute-start | bytes 589832 | tf_op jit(solution)/shard_map/ppermute | solution.py:1053
  (63 other events, 392.2 us)
Sparse Core Ops, SparseCore 0:
  13.9 65.8 all-gather.6
  82.0 29.0 all-gather.12
  113.3 62.6 all-gather.10
  177.4 62.1 all-gather.8
  285.0 57.0 reduce-scatter.3
  364.6 58.3 reduce-scatter.5
  451.3 60.2 reduce-scatter.7
